TPU v7x, 32 devices: a whole 2x2x4 slice. The times are simulated.
32 devices in a mesh: head: 4 (over z), tok: 8 (over y, x, core).
Axes of the slice: x: 2, y: 2, z: 4, core: 2. Of those that a mesh axis runs over, the one named last changes fastest.
Arguments:
- tokens: bfloat16 [8192, 2048], P('tok', 'head'), may hold values from -6 to 6
- mix_gain: float32 [2048], P('head'), may hold values from 0.5 to 1.5
- mix_bias: float32 [2048], P('head'), may hold values from -1.5 to 1.5
- query_weight: bfloat16 [2048, 2048], P(None, 'head'), may hold values from -0.125 to 0.125
- key_weight: bfloat16 [2048, 2048], P(None, 'head'), may hold values from -0.125 to 0.125
- value_weight: bfloat16 [2048, 4096], P(None, 'head'), may hold values from -0.125 to 0.125
- gate_weight: bfloat16 [2048, 4096], P(None, 'head'), may hold values from -0.125 to 0.125
- output_weight: bfloat16 [4096, 2048], P('head'), may hold values from -0.1875 to 0.1875
- feed_gain: float32 [2048], P('head'), may hold values from 0.5 to 1.5
- feed_bias: float32 [2048], P('head'), may hold values from -1.5 to 1.5
- up_weight: bfloat16 [2048, 4096], P(None, 'head'), may hold values from -0.125 to 0.125
- down_weight: bfloat16 [4096, 2048], P('head'), may hold values from -0.09375 to 0.09375
- doc_ids: int32 [8192], P('tok'), may hold values from 0 to 15, never falling along the last dimension, each value on 1 to 3072 neighbouring positions
- pad_mask: int32 [8192], P('tok'), may hold values 0 or 1
- out_grad: bfloat16 [8192, 2048], P('tok', 'head'), may hold values from -6 to 6
Outputs:
- layer_out: bfloat16 [8192, 2048], P('tok', 'head')
- tokens_grad: float32 [8192, 2048], P('tok', 'head')
- mix_gain_grad: float32 [2048], P('head')
- mix_bias_grad: float32 [2048], P('head')
- query_weight_grad: float32 [2048, 2048], P(None, 'head')
- key_weight_grad: float32 [2048, 2048], P(None, 'head')
- value_weight_grad: float32 [2048, 4096], P(None, 'head')
- gate_weight_grad: float32 [2048, 4096], P(None, 'head')
- output_weight_grad: float32 [4096, 2048], P('head')
- feed_gain_grad: float32 [2048], P('head')
- feed_bias_grad: float32 [2048], P('head')
- up_weight_grad: float32 [2048, 4096], P(None, 'head')
- down_weight_grad: float32 [4096, 2048], P('head')
Inputs may be any that keep to these rules, and one draw needn't show every extreme that they name: `doc_ids`: document numbers never fall along the stream; a document has 1 to 3072 tokens, and one has exactly that many.
All inputs are finite; a program needn't handle non-finite values. No bound on the sum of `pad_mask` on one device may be relied on, other than what follows from the above.
Results may differ from a plain program's by a relative error of at most 0.014.
Values may be sent and summed in bfloat16 or wider, within the bound.
No kernel may reach another device: no remote copies, remote signals or barrier semaphores. Data moves between devices by JAX's collectives and lax.ppermute only.
A program may use at most 256 MiB of HBM per device.

v0:
```python
from functools import partial

import jax
import jax.numpy as jnp
from jax import lax
from jax.sharding import PartitionSpec as P

KD = 256
VD = 512


EPSILON = 1e-05


def passed_along(shard, axis, by):
    length = lax.axis_size(axis)
    pairs = [(i, i + by) for i in range(length) if 0 <= i + by < length]
    return lax.ppermute(shard, axis, pairs)


def prefix(value, axis, join, neutral, backward):
    count, mine = (lax.axis_size(axis), lax.axis_index(axis))
    pieces = jax.tree.map(lambda part: lax.all_gather(part, axis), value)
    if backward:
        pieces = jax.tree.map(lambda part: part[::-1], pieces)
        mine = count - 1 - mine
    so_far = jax.tree.map(
        lambda part, zero: jnp.full_like(part, 0) + jnp.asarray(zero, part.dtype), value, neutral
    )

    def turn(position, so_far):
        longer = join(so_far, jax.tree.map(lambda part: part[position], pieces))
        return jax.tree.map(lambda new, old: jnp.where(position < mine, new, old), longer, so_far)

    return lax.fori_loop(0, count - 1, turn, so_far)


def gather_rows(values):
    return lax.all_gather(values, "head", axis=1, tiled=True)


def sum_rows(values):
    return lax.psum_scatter(values, "head", scatter_dimension=1, tiled=True)


def head_sums(sum_one, sum_two):
    return lax.psum((sum_one, sum_two), "head")


def norm_forward(values, gain_vec, bias_vec):
    full_width = values.shape[1] * lax.axis_size("head")
    totals, squares = head_sums(jnp.sum(values, axis=1), jnp.sum(values * values, axis=1))
    row_mean = totals / full_width
    row_scale = lax.rsqrt(squares / full_width - row_mean * row_mean + EPSILON)
    normed = (values - row_mean[:, None]) * row_scale[:, None]
    return (normed, row_scale, (normed * gain_vec + bias_vec).astype(jnp.bfloat16))


def norm_backward(upstream, normed, row_scale, gain_vec):
    full_width = normed.shape[1] * lax.axis_size("head")
    scaled = upstream * gain_vec
    sum_grad, sum_cross = head_sums(jnp.sum(scaled, axis=1), jnp.sum(scaled * normed, axis=1))
    back_rows = row_scale[:, None] * (
        scaled - sum_grad[:, None] / full_width - normed * sum_cross[:, None] / full_width
    )
    return (back_rows, jnp.sum(upstream * normed, axis=0), jnp.sum(upstream, axis=0))


def rotate(values, angles):
    half_dim = values.shape[-1] // 2
    cosine = jnp.cos(angles)[:, None, :]
    sine_vals = jnp.sin(angles)[:, None, :]
    front_half = values[..., :half_dim]
    back_half = values[..., half_dim:]
    return jnp.concatenate(
        [front_half * cosine - back_half * sine_vals, back_half * cosine + front_half * sine_vals],
        axis=-1,
    )


def unrotate(values, angles):
    half_dim = values.shape[-1] // 2
    cosine = jnp.cos(angles)[:, None, :]
    sine_vals = jnp.sin(angles)[:, None, :]
    front_half = values[..., :half_dim]
    back_half = values[..., half_dim:]
    return jnp.concatenate(
        [front_half * cosine + back_half * sine_vals, back_half * cosine - front_half * sine_vals],
        axis=-1,
    )


def group_norm(mixed):
    group_mean = jnp.mean(mixed, axis=-1, keepdims=True)
    group_var = jnp.mean(mixed * mixed, axis=-1, keepdims=True) - group_mean * group_mean
    return (mixed - group_mean) * lax.rsqrt(group_var + 1.0)


def compose(earlier_part, later_part):
    return (
        later_part[0] + later_part[1][:, None, None] * earlier_part[0],
        earlier_part[1] * later_part[1],
    )


def body(
    tokens,
    mix_gain,
    mix_bias,
    query_weight,
    key_weight,
    value_weight,
    gate_weight,
    output_weight,
    feed_gain,
    feed_bias,
    up_weight,
    down_weight,
    doc_ids,
    pad_mask,
    out_grad,
):
    row_count = tokens.shape[0]
    heads_here = query_weight.shape[1] // KD
    first_head = lax.axis_index("head") * heads_here
    log_decay = jnp.log(
        1.0
        - 2.0 ** (-5.0 - (first_head + jnp.arange(heads_here, dtype=jnp.int32)).astype(jnp.float32))
    )
    position = jnp.arange(row_count, dtype=jnp.int32)
    offset = lax.axis_index("tok") * row_count
    frequency = 10000.0 ** (-2.0 * jnp.arange(KD // 2, dtype=jnp.int32).astype(jnp.float32) / KD)
    angles = (offset + position).astype(jnp.float32)[:, None] * frequency[None, :]
    padding = pad_mask.astype(jnp.float32)
    before = passed_along(doc_ids[row_count - 1 :] + 1, "tok", 1)[0]
    last_doc = doc_ids[row_count - 1]
    distance = position[:, None] - position[None, :]
    allowed = ((doc_ids[:, None] == doc_ids[None, :]) & (distance >= 0)).astype(
        jnp.float32
    ) * padding[None, :]
    decay_mat = (
        jnp.exp(jnp.maximum(distance, 0).astype(jnp.float32)[None] * log_decay[:, None, None])
        * allowed[None]
    )
    carry_factor = (doc_ids + 1 == before).astype(jnp.float32)[:, None] * jnp.exp(
        (position + 1).astype(jnp.float32)[:, None] * log_decay[None, :]
    )
    end_factor = (padding * (doc_ids == last_doc).astype(jnp.float32))[:, None] * jnp.exp(
        (row_count - 1 - position).astype(jnp.float32)[:, None] * log_decay[None, :]
    )
    keep_factor = (last_doc + 1 == before).astype(jnp.float32) * jnp.exp(row_count * log_decay)
    norm_first, rstd_first, low_first = norm_forward(tokens.astype(jnp.float32), mix_gain, mix_bias)
    rows_first = gather_rows(low_first)
    queries = jnp.dot(rows_first, query_weight, preferred_element_type=jnp.float32).reshape(
        row_count, heads_here, KD
    )
    key_proj = jnp.dot(rows_first, key_weight, preferred_element_type=jnp.float32).reshape(
        row_count, heads_here, KD
    )
    values = (
        jnp.dot(rows_first, value_weight, preferred_element_type=jnp.float32)
        .astype(jnp.bfloat16)
        .reshape(row_count, heads_here, VD)
    )
    gate_pre = jnp.dot(rows_first, gate_weight, preferred_element_type=jnp.float32)
    query_rot = rotate(queries, angles).astype(jnp.bfloat16)
    key_rot = (rotate(key_proj, angles) * KD ** (-0.5)).astype(jnp.bfloat16)
    scores = jnp.einsum("nha,mha->hnm", query_rot, key_rot, preferred_element_type=jnp.float32)
    weights = (scores * decay_mat).astype(jnp.bfloat16)
    inner_part = jnp.einsum("hnm,mhb->nhb", weights, values, preferred_element_type=jnp.float32)
    key_end = (key_rot * end_factor[:, :, None]).astype(jnp.bfloat16)
    summary = jnp.einsum("nha,nhb->hab", key_end, values, preferred_element_type=jnp.float32)
    identity = (jnp.zeros_like(summary), jnp.ones_like(keep_factor))
    state_in = prefix((summary, keep_factor), "tok", compose, identity, False)[0]
    state_low = state_in.astype(jnp.bfloat16)
    query_carry = (query_rot * carry_factor[:, :, None]).astype(jnp.bfloat16)
    mixed = inner_part + jnp.einsum(
        "nha,hab->nhb", query_carry, state_low, preferred_element_type=jnp.float32
    )
    grouped, group_pull = jax.vjp(group_norm, mixed)
    gate_act, gate_pull = jax.vjp(jax.nn.silu, gate_pre)
    flat_group = grouped.reshape(row_count, heads_here * VD)
    gated = (padding[:, None] * gate_act * flat_group).astype(jnp.bfloat16)
    hidden = tokens.astype(jnp.float32) + sum_rows(
        jnp.dot(gated, output_weight, preferred_element_type=jnp.float32)
    )
    norm_second, rstd_second, low_second = norm_forward(hidden, feed_gain, feed_bias)
    rows_second = gather_rows(low_second)
    up_proj = jnp.dot(rows_second, up_weight, preferred_element_type=jnp.float32)
    activation, act_pull = jax.vjp(partial(jax.nn.gelu, approximate=False), up_proj)
    act_low = activation.astype(jnp.bfloat16)
    result = hidden + sum_rows(jnp.dot(act_low, down_weight, preferred_element_type=jnp.float32))
    layer_out = result.astype(jnp.bfloat16)
    grad_full = gather_rows(out_grad)
    grad_down = jnp.einsum("nf,nd->fd", act_low, grad_full, preferred_element_type=jnp.float32)
    grad_act = jnp.einsum("nd,fd->nf", grad_full, down_weight, preferred_element_type=jnp.float32)
    grad_up = act_pull(grad_act)[0].astype(jnp.bfloat16)
    grad_upw = jnp.einsum("nd,nf->df", rows_second, grad_up, preferred_element_type=jnp.float32)
    grad_ln2 = sum_rows(
        jnp.einsum("nf,df->nd", grad_up, up_weight, preferred_element_type=jnp.float32)
    )
    back_second, grad_gain2, grad_bias2 = norm_backward(
        grad_ln2, norm_second, rstd_second, feed_gain
    )
    grad_hidden = out_grad.astype(jnp.float32) + back_second
    grad_branch = grad_hidden.astype(jnp.bfloat16)
    grad_full_h = gather_rows(grad_branch)
    grad_outw = jnp.einsum("nc,nd->cd", gated, grad_full_h, preferred_element_type=jnp.float32)
    grad_gated = jnp.einsum(
        "nd,cd->nc", grad_full_h, output_weight, preferred_element_type=jnp.float32
    )
    grad_masked = grad_gated * padding[:, None]
    grad_gate = gate_pull(grad_masked * flat_group)[0].astype(jnp.bfloat16)
    grad_mixed = group_pull((grad_masked * gate_act).reshape(row_count, heads_here, VD))[0].astype(
        jnp.bfloat16
    )
    grad_weights = jnp.einsum(
        "nhb,mhb->hnm", grad_mixed, values, preferred_element_type=jnp.float32
    )
    grad_scores = (grad_weights * decay_mat).astype(jnp.bfloat16)
    grad_state = jnp.einsum(
        "nha,nhb->hab", query_carry, grad_mixed, preferred_element_type=jnp.float32
    )
    state_grad = prefix((grad_state, keep_factor), "tok", compose, identity, True)[0]
    state_grad_low = state_grad.astype(jnp.bfloat16)
    grad_query_rot = jnp.einsum(
        "hnm,mha->nha", grad_scores, key_rot, preferred_element_type=jnp.float32
    ) + carry_factor[:, :, None] * jnp.einsum(
        "nhb,hab->nha", grad_mixed, state_low, preferred_element_type=jnp.float32
    )
    grad_key_rot = jnp.einsum(
        "hnm,nha->mha", grad_scores, query_rot, preferred_element_type=jnp.float32
    ) + end_factor[:, :, None] * jnp.einsum(
        "nhb,hab->nha", values, state_grad_low, preferred_element_type=jnp.float32
    )
    grad_values = (
        (
            jnp.einsum("hnm,nhb->mhb", weights, grad_mixed, preferred_element_type=jnp.float32)
            + jnp.einsum(
                "nha,hab->nhb", key_end, state_grad_low, preferred_element_type=jnp.float32
            )
        )
        .astype(jnp.bfloat16)
        .reshape(row_count, heads_here * VD)
    )
    grad_queries = (
        unrotate(grad_query_rot, angles).astype(jnp.bfloat16).reshape(row_count, heads_here * KD)
    )
    grad_keys = (
        (unrotate(grad_key_rot, angles) * KD ** (-0.5))
        .astype(jnp.bfloat16)
        .reshape(row_count, heads_here * KD)
    )
    grad_qw = jnp.einsum("nd,nc->dc", rows_first, grad_queries, preferred_element_type=jnp.float32)
    grad_kw = jnp.einsum("nd,nc->dc", rows_first, grad_keys, preferred_element_type=jnp.float32)
    grad_vw = jnp.einsum("nd,nc->dc", rows_first, grad_values, preferred_element_type=jnp.float32)
    grad_gw = jnp.einsum("nd,nc->dc", rows_first, grad_gate, preferred_element_type=jnp.float32)
    grad_ln1_part = (
        jnp.einsum("nc,dc->nd", grad_queries, query_weight, preferred_element_type=jnp.float32)
        + jnp.einsum("nc,dc->nd", grad_keys, key_weight, preferred_element_type=jnp.float32)
        + jnp.einsum("nc,dc->nd", grad_values, value_weight, preferred_element_type=jnp.float32)
        + jnp.einsum("nc,dc->nd", grad_gate, gate_weight, preferred_element_type=jnp.float32)
    )
    grad_ln1 = sum_rows(grad_ln1_part)
    back_first, grad_gain1, grad_bias1 = norm_backward(grad_ln1, norm_first, rstd_first, mix_gain)
    tokens_grad = grad_hidden + back_first
    (
        grad_qw,
        grad_kw,
        grad_vw,
        grad_gw,
        grad_outw,
        grad_gain1,
        grad_bias1,
        grad_upw,
        grad_down,
        grad_gain2,
        grad_bias2,
    ) = lax.psum(
        (
            grad_qw,
            grad_kw,
            grad_vw,
            grad_gw,
            grad_outw,
            grad_gain1,
            grad_bias1,
            grad_upw,
            grad_down,
            grad_gain2,
            grad_bias2,
        ),
        "tok",
    )
    return (
        layer_out,
        tokens_grad,
        grad_gain1,
        grad_bias1,
        grad_qw,
        grad_kw,
        grad_vw,
        grad_gw,
        grad_outw,
        grad_gain2,
        grad_bias2,
        grad_upw,
        grad_down,
    )


def solution(mesh):
    return jax.shard_map(
        body,
        mesh=mesh,
        in_specs=(
            P("tok", "head"),
            P("head"),
            P("head"),
            P(None, "head"),
            P(None, "head"),
            P(None, "head"),
            P(None, "head"),
            P("head", None),
            P("head"),
            P("head"),
            P(None, "head"),
            P("head", None),
            P("tok"),
            P("tok"),
            P("tok", "head"),
        ),
        out_specs=(
            P("tok", "head"),
            P("tok", "head"),
            P("head"),
            P("head"),
            P(None, "head"),
            P(None, "head"),
            P(None, "head"),
            P(None, "head"),
            P("head", None),
            P("head"),
            P("head"),
            P(None, "head"),
            P("head", None),
        ),
        check_vma=False,
    )
```

profile of v0, /device:TPU:0, one launch (start us, length us, event | category | flops | bytes accessed | tf_op | source)
XLA Modules:
  0.0 1874.2 jit_solution(12761296357334139144)
XLA Ops:
  9.0 13.7 all-reduce.5
  32.9 72.3 %all-gather.10.cloned.1.call-done = bf16[1024,2048]{1,0:T(8,128)(2,1)} async-done(((bf16[1024,512]{1,0:T(8,128)(2,1)}), bf16[1024,2048]{1,0:T(8,128)(2,1)}) %all-gather.10.cloned.1.call-update) | async-done | bytes 4194320 | tf_op jit(solution)/shard_map/all_gather | solution.py:39
  105.1 4.6 fusion.54
  116.3 5.2 fusion.55
  133.3 4.8 convolution_convert_fusion
  144.6 5.5 copy.93
  152.7 5.3 copy.92
  159.2 8.7 all-gather.2
  168.1 6.4 multiply_convert_fusion.1
  180.9 13.7 all-gather.18.cloned.1.call-done
  194.6 11.6 while.28
  215.6 7.3 fusion.8
  222.9 8.5 fusion.57
  231.5 144.6 %reduce-scatter.5.cloned.1.call-done = f32[1024,512]{1,0:T(8,128)} async-done(((f32[1024,2048]{1,0:T(8,128)}), f32[1024,512]{1,0:T(8,128)}) %reduce-scatter.5.cloned.1.call-update) | async-done | bytes 2097168 | tf_op jit(solution)/shard_map/reduce_scatter | solution.py:43
  379.4 11.5 all-reduce.4
  394.6 78.7 %all-gather.12.cloned.1.call-done = bf16[1024,2048]{1,0:T(8,128)(2,1)} async-done(((bf16[1024,512]{1,0:T(8,128)(2,1)}), bf16[1024,2048]{1,0:T(8,128)(2,1)}) %all-gather.12.cloned.1.call-update) | async-done | bytes 4194320 | tf_op jit(solution)/shard_map/all_gather | solution.py:39
  473.2 10.0 fusion.58
  483.2 70.7 %all-gather.14.cloned.1.call-done = bf16[1024,2048]{1,0:T(8,128)(2,1)} async-done(((bf16[1024,512]{1,0:T(8,128)(2,1)}), bf16[1024,2048]{1,0:T(8,128)(2,1)}) %all-gather.14.cloned.1.call-update) | async-done | bytes 4194320 | tf_op jit(solution)/shard_map/all_gather | solution.py:39
  554.0 18.2 add_convert_fusion.1
  573.5 6.8 fusion.60
  580.5 4.7 multiply_convert_fusion.2
  586.6 6.9 fusion.59
  593.6 129.9 %reduce-scatter.9.cloned.1.call-done = f32[1024,512]{1,0:T(8,128)} async-done(((f32[1024,2048]{1,0:T(8,128)}), f32[1024,512]{1,0:T(8,128)}) %reduce-scatter.9.cloned.1.call-update) | async-done | bytes 2097168 | tf_op jit(solution)/shard_map/reduce_scatter | solution.py:43
  727.2 11.4 all-reduce.3
  738.6 133.0 %reduce-scatter.7.cloned.1.call-done = f32[1024,512]{1,0:T(8,128)} async-done(((f32[1024,2048]{1,0:T(8,128)}), f32[1024,512]{1,0:T(8,128)}) %reduce-scatter.7.cloned.1.call-update) | async-done | bytes 2097168 | tf_op jit(solution)/shard_map/reduce_scatter | solution.py:43
  871.6 5.0 fusion.50
  876.7 81.6 %all-gather.16.cloned.1.call-done = bf16[1024,2048]{1,0:T(8,128)(2,1)} async-done(((bf16[1024,512]{1,0:T(8,128)(2,1)}), bf16[1024,2048]{1,0:T(8,128)(2,1)}) %all-gather.16.cloned.1.call-update) | async-done | bytes 4194320 | tf_op jit(solution)/shard_map/all_gather | solution.py:39
  958.3 12.9 fusion.7
  981.7 7.5 multiply_convert_fusion
  998.6 7.4 fusion.64
  1006.1 25.2 %all-gather.20.cloned.1.call-done = f32[16,256,512]{2,1,0:T(8,128)} async-done(((f32[2,256,512]{2,1,0:T(8,128)}), f32[16,256,512]{2,1,0:T(8,128)}) %all-gather.20.cloned.1.call-update) | async-done | bytes 8388624 | tf_op jit(solution)/shard_map/all_gather | solution.py:23
  1031.3 8.2 rev.6
  1039.5 11.6 while.29
  1056.7 6.8 fusion.63
  1069.0 7.2 fusion.61
  1078.8 14.7 add_add_fusion
  1093.6 11.0 fusion.70
  1104.6 7.2 fusion.71
  1111.8 7.0 fusion.68
  1118.8 6.7 fusion.69
  1134.6 7.1 fusion.67
  1141.8 96.3 %reduce-scatter.11.cloned.1.call-done = f32[1024,512]{1,0:T(8,128)} async-done(((f32[1024,2048]{1,0:T(8,128)}), f32[1024,512]{1,0:T(8,128)}) %reduce-scatter.11.cloned.1.call-update) | async-done | bytes 2097168 | tf_op jit(solution)/shard_map/reduce_scatter | solution.py:43
  1240.9 14.4 all-reduce
  1255.2 11.7 all-reduce.2
  1270.6 560.9 %all-reduce.8.cloned.1.call-done = (f32[2048,512]{1,0:T(8,128)}, f32[2048,512]{1,0:T(8,128)}, f32[2048,1024]{1,0:T(8,128)}, f32[2048,1024]{1,0:T(8,128)}, f32[10...) async-done(((f32[2048,512]{1,0:T(8,128)}, f32[2048,512]{1,0:T(8,128)}, f32[2048,1024]{1,0:T(8,128)}, f32[2048,1024]{1,0:T(8,128)}, ...) | async-done | bytes 50331664 | tf_op jit(solution)/shard_map/psum | solution.py:279
  1831.5 4.9 copy.160
  1836.4 4.9 copy.161
  1850.8 8.0 copy.164
  (264 shorter events, 157.9 us)
Async XLA Ops:
  7.2 98.0 %copy-start = (bf16[2048,512]{1,0:T(8,128)(2,1)S(1)}, bf16[2048,512]{1,0:T(8,128)(2,1)}, u32[]{:S(2)}) copy-start(bf16[2048,512]{1,0:T(8,128)(2,1)} %param.22) | copy-start | bytes 6291460
  7.2 18.9 %copy-start.43 = (s32[1024]{0:T(1024)S(1)}, s32[1024]{0:T(1024)}, u32[]{:S(2)}) copy-start(s32[1024]{0:T(1024)} %param.31) | copy-start | bytes 12292
  7.2 22.4 %copy-start.46 = (s32[1024]{0:T(1024)S(1)}, s32[1024]{0:T(1024)}, u32[]{:S(2)}) copy-start(s32[1024]{0:T(1024)} %param.32) | copy-start | bytes 12292
  7.2 97.9 %all-gather.10.cloned.1.call-start = ((), (), s32[]{:S(2)}) async-start(), calls=%async_computation.4 | async-start | bytes 5242880 | tf_op jit(solution)/shard_map/all_gather | solution.py:39
  26.0 168.6 %all-gather.18.cloned.1.call-start = ((), (), s32[]{:S(2)}) async-start(), calls=%async_computation.12 | async-start | bytes 9437184 | tf_op jit(solution)/shard_map/all_gather | solution.py:23
  27.3 4.9 collective-permute-start
  32.1 96.1 %copy-start.21 = (f32[1024,128]{1,0:T(8,128)}, f32[1024,128]{1,0:T(8,128)S(1)}, u32[]{:S(2)}) copy-start(f32[1024,128]{1,0:T(8,128)S(1)} %get-tuple-element.351) | copy-start | bytes 1572868
  32.1 96.1 %copy-start.23 = (f32[1024,128]{1,0:T(8,128)}, f32[1024,128]{1,0:T(8,128)S(1)}, u32[]{:S(2)}) copy-start(f32[1024,128]{1,0:T(8,128)S(1)} %get-tuple-element.352) | copy-start | bytes 1572868
  32.9 105.3 %copy-start.37 = (f32[1024,2]{0,1:T(2,128)}, f32[1024,2]{0,1:T(2,128)S(1)}, u32[]{:S(2)}) copy-start(f32[1024,2]{0,1:T(2,128)S(1)} %get-tuple-element.357) | copy-start | bytes 24580
  141.6 234.5 %reduce-scatter.5.cloned.1.call-start = ((), (), s32[]{:S(2)}) async-start(), calls=%async_computation.5 | async-start | bytes 10485760 | tf_op jit(solution)/shard_map/reduce_scatter | solution.py:43
  168.1 8.4 copy-start.12
  215.6 7.3 copy-start.29
  215.6 7.3 copy-start.52
  231.4 159.5 %copy-start.44 = (f32[512]{0:T(512)S(1)}, f32[512]{0:T(512)}, u32[]{:S(2)}) copy-start(f32[512]{0:T(512)} %param.27) | copy-start | bytes 6148
  231.4 159.5 %copy-start.49 = (f32[512]{0:T(512)S(1)}, f32[512]{0:T(512)}, u32[]{:S(2)}) copy-start(f32[512]{0:T(512)} %param.28) | copy-start | bytes 6148
  231.4 241.8 %all-gather.12.cloned.1.call-start = ((), (), s32[]{:S(2)}) async-start(), calls=%async_computation.6 | async-start | bytes 5242880 | tf_op jit(solution)/shard_map/all_gather | solution.py:39
  393.9 160.0 %all-gather.14.cloned.1.call-start = ((), (), s32[]{:S(2)}) async-start(), calls=%async_computation.8 | async-start | bytes 5242880 | tf_op jit(solution)/shard_map/all_gather | solution.py:39
  394.5 328.9 %reduce-scatter.9.cloned.1.call-start = ((), (), s32[]{:S(2)}) async-start(), calls=%async_computation.9 | async-start | bytes 10485760 | tf_op jit(solution)/shard_map/reduce_scatter | solution.py:43
  553.9 19.5 %copy-start.50 = (bf16[2048,1024]{1,0:T(8,128)(2,1)S(1)}, bf16[2048,1024]{1,0:T(8,128)(2,1)}, u32[]{:S(2)}) copy-start(bf16[2048,1024]{1,0:T(8,128)(2,1)} %param.29) | copy-start | bytes 12582916
  580.3 291.4 %reduce-scatter.7.cloned.1.call-start = ((), (), s32[]{:S(2)}) async-start(), calls=%async_computation.7 | async-start | bytes 10485760 | tf_op jit(solution)/shard_map/reduce_scatter | solution.py:43
  593.5 364.8 %all-gather.16.cloned.1.call-start = ((), (), s32[]{:S(2)}) async-start(), calls=%async_computation.10 | async-start | bytes 5242880 | tf_op jit(solution)/shard_map/all_gather | solution.py:39
  876.6 154.6 %all-gather.20.cloned.1.call-start = ((), (), s32[]{:S(2)}) async-start(), calls=%async_computation.13 | async-start | bytes 9437184 | tf_op jit(solution)/shard_map/all_gather | solution.py:23
  958.3 12.9 copy-start.3
  958.3 12.9 copy-start.27
  978.2 259.9 %reduce-scatter.11.cloned.1.call-start = ((), (), s32[]{:S(2)}) async-start(), calls=%async_computation.11 | async-start | bytes 10485760 | tf_op jit(solution)/shard_map/reduce_scatter | solution.py:43
  981.7 7.5 copy-start.8
  1031.3 8.2 copy-start.4
  1039.5 14.3 copy-start.38
  1069.0 7.2 copy-start.30
  1069.0 7.2 copy-start.31
  1093.5 738.0 %all-reduce.8.cloned.1.call-start = ((), (), s32[]{:S(2)}) async-start(), calls=%async_computation.14 | async-start | bytes 100663296 | tf_op jit(solution)/shard_map/psum | solution.py:279
  1093.5 11.0 copy-start.33
  1093.6 11.0 copy-start.60
  1104.6 7.2 copy-start.59
  1104.6 7.2 copy-start.65
  1111.8 7.0 copy-start.61
  1111.8 7.0 copy-start.62
  1141.7 96.4 %copy-start.10 = (bf16[1024,512]{1,0:T(8,128)(2,1)S(1)}, bf16[1024,512]{1,0:T(8,128)(2,1)}, u32[]{:S(2)}) copy-start(bf16[1024,512]{1,0:T(8,128)(2,1)} %param.19) | copy-start | bytes 3145732
  1141.7 96.4 %copy-start.40 = (f32[1024]{0:T(1024)S(1)}, f32[1024]{0:T(1024)}, u32[]{:S(2)}) copy-start(f32[1024]{0:T(1024)} %copy-done.39) | copy-start | bytes 12292
  1141.7 96.4 %copy-start.42 = (f32[1024]{0:T(1024)S(1)}, f32[1024]{0:T(1024)}, u32[]{:S(2)}) copy-start(f32[1024]{0:T(1024)} %copy-done.41) | copy-start | bytes 12292
  1141.7 96.4 %copy-start.45 = (f32[512]{0:T(512)S(1)}, f32[512]{0:T(512)}, u32[]{:S(2)}) copy-start(f32[512]{0:T(512)} %param.20) | copy-start | bytes 6148
  1141.7 99.1 %copy-start.47 = (f32[512]{0:T(512)S(1)}, f32[512]{0:T(512)}, u32[]{:S(2)}) copy-start(f32[512]{0:T(512)} %get-tuple-element.269) | copy-start | bytes 6148
  1141.7 99.1 %copy-start.48 = (f32[512]{0:T(512)S(1)}, f32[512]{0:T(512)}, u32[]{:S(2)}) copy-start(f32[512]{0:T(512)} %get-tuple-element.279) | copy-start | bytes 6148
  1831.5 9.8 copy-start.19
  1836.4 9.2 slice-start.4
  1846.5 12.3 slice-start.2
  1850.8 8.0 slice-start.3
  1850.8 12.3 slice-start
  (36 other events, 121.6 us)
Sparse Core Ops, SparseCore 0:
  26.1 78.9 all-gather.9
  141.7 52.9 all-gather.17
  231.5 144.4 reduce-scatter.4
  394.0 79.1 all-gather.11
  474.6 79.2 all-gather.13
  580.4 142.9 reduce-scatter.8
  726.3 145.2 reduce-scatter.6
  876.7 81.4 all-gather.15
  978.3 52.9 all-gather.19
  1093.6 144.4 reduce-scatter.10
  1244.4 587.0 all-reduce.7
where the time goes:
time: 1880 us; the launch traced here: 1870 us
  waiting for transfers between devices  1410 us (75%)
  matrix products  211 us (11%)
  local copies, waits for them, and re-layouts  90.6 us (5%)
  other arithmetic  72.6 us (4%)
  blocking collectives  71.4 us (4%)
    psum x1, waiting for transfers between devices, body(): lax.psum((grad_qw, grad_kw, grad_vw, grad_gw, grad_outw, grad_gain1, grad...  561 us
    reduce_scatter x4, waiting for transfers between devices, sum_rows(): return lax.psum_scatter(values, 'head', scatter_dimension=1, tiled=True)  504 us
    all_gather x4, waiting for transfers between devices, gather_rows(): return lax.all_gather(values, 'head', axis=1, tiled=True)  303 us
    unnamed x157, local copies, waits for them, and re-layouts  64.6 us
    psum x4, blocking collectives, head_sums(): return lax.psum((sum_one, sum_two), 'head')  48.3 us
    all_gather x2, waiting for transfers between devices, prefix(): pieces = jax.tree.map(lambda part: lax.all_gather(part, axis), value)  38.9 us
  transfers between devices with their start and end apart: 12, of which 11 were waited for; matrix products, arithmetic and copies ran while one was open for 7% of the time, Pallas kernels for 0%

commit v1 on v0

v1 whole, which is shorter than its diff:
```python
from functools import partial

import jax
import jax.numpy as jnp
from jax import lax
from jax.sharding import PartitionSpec as P

KD = 256
VD = 512
EPSILON = 1e-05
BF = jnp.bfloat16
F32 = jnp.float32


def after(value, *others):
    return lax.optimization_barrier((value, *others))[0]


def shifted(value, by):
    length = lax.axis_size("tok")
    pairs = [(i, i + by) for i in range(length) if 0 <= i + by < length]
    return lax.ppermute(value, "tok", pairs)


def swapped(value, bit):
    length = lax.axis_size("tok")
    return lax.ppermute(value, "tok", [(i, i ^ (1 << bit)) for i in range(length)])


def my_bit(bit):
    return (lax.axis_index("tok") >> bit) & 1


def bit_orders():
    bits = lax.axis_size("tok").bit_length() - 1
    first = list(range(bits))
    second = [0, 2, 1] if bits == 3 else first[bits // 2 :] + first[: bits // 2]
    return first, second


def halves(value, bit):
    pieces = value.reshape(2, value.shape[0] // 2, value.shape[1])
    mine = my_bit(bit)
    keep = lax.dynamic_index_in_dim(pieces, mine, 0, keepdims=False)
    give = lax.dynamic_index_in_dim(pieces, 1 - mine, 0, keepdims=False)
    return keep, give


def scatter_sum(value, order):
    for bit in order:
        keep, give = halves(value, bit)
        value = keep.astype(F32) + swapped(give.astype(BF), bit).astype(F32)
    return value.astype(BF)


def gather_back(value, order):
    for bit in order[::-1]:
        other = swapped(value, bit)
        low_first = my_bit(bit) == 0
        value = jnp.where(
            low_first,
            jnp.concatenate([value, other], axis=0),
            jnp.concatenate([other, value], axis=0),
        )
    return value.astype(F32)


def token_sum(first, second):
    order_one, order_two = bit_orders()
    one = scatter_sum(first, order_one)
    two = scatter_sum(second, order_two)
    return gather_back(one, order_one), gather_back(two, order_two)


def gather_rows(values):
    return lax.all_gather(values, "head", axis=1, tiled=True)


def sum_rows(values):
    return lax.psum_scatter(values.astype(BF), "head", scatter_dimension=1, tiled=True)


def my_columns(full, width):
    return lax.dynamic_slice_in_dim(full, lax.axis_index("head") * width, width, axis=-1)


def row_norm(rows):
    mean = jnp.mean(rows, axis=1)
    scale = lax.rsqrt(jnp.mean(rows * rows, axis=1) - mean * mean + EPSILON)
    return mean, scale


def rotate(values, cosine, sine, sign):
    half_dim = values.shape[-1] // 2
    front = values[..., :half_dim]
    back = values[..., half_dim:]
    sine = sine * sign
    return jnp.concatenate([front * cosine - back * sine, back * cosine + front * sine], axis=-1)


def group_norm(mixed):
    group_mean = jnp.mean(mixed, axis=-1, keepdims=True)
    group_var = jnp.mean(mixed * mixed, axis=-1, keepdims=True) - group_mean * group_mean
    return (mixed - group_mean) * lax.rsqrt(group_var + 1.0)


def body(
    tokens,
    mix_gain,
    mix_bias,
    query_weight,
    key_weight,
    value_weight,
    gate_weight,
    output_weight,
    feed_gain,
    feed_bias,
    up_weight,
    down_weight,
    doc_ids,
    pad_mask,
    out_grad,
):
    row_count, width = tokens.shape
    heads_here = query_weight.shape[1] // KD
    full_width = width * lax.axis_size("head")
    block = lax.axis_index("tok")
    blocks = lax.axis_size("tok")

    rows_raw = gather_rows(tokens)
    grad_rows = gather_rows(after(out_grad, rows_raw))

    vectors = lax.all_gather(
        jnp.stack([mix_gain, mix_bias, feed_gain, feed_bias]), "head", axis=1, tiled=True
    )
    last_docs = lax.all_gather(doc_ids[row_count - 1 :], "tok", axis=0, tiled=True)

    first_head = lax.axis_index("head") * heads_here
    log_decay = jnp.log(
        1.0 - 2.0 ** (-5.0 - (first_head + jnp.arange(heads_here, dtype=jnp.int32)).astype(F32))
    )
    position = jnp.arange(row_count, dtype=jnp.int32)
    frequency = 10000.0 ** (-2.0 * jnp.arange(KD // 2, dtype=jnp.int32).astype(F32) / KD)
    angles = (block * row_count + position).astype(F32)[:, None] * frequency[None, :]
    cosine, sine = jnp.cos(angles)[:, None, :], jnp.sin(angles)[:, None, :]
    padding = pad_mask.astype(F32)
    last_doc = doc_ids[row_count - 1]

    def doc_of(index):
        return last_docs[jnp.clip(index, 0, blocks - 1)]

    before = doc_of(block - 1)
    block_decay = jnp.exp(row_count * log_decay)
    back_two = (doc_of(block - 2) == before).astype(F32) * block_decay
    back_three = (doc_of(block - 3) == before).astype(F32) * block_decay * block_decay
    ahead_two = (doc_of(block + 1) == last_doc).astype(F32) * block_decay
    ahead_three = (doc_of(block + 2) == last_doc).astype(F32) * block_decay * block_decay

    distance = position[:, None] - position[None, :]
    allowed = ((doc_ids[:, None] == doc_ids[None, :]) & (distance >= 0)).astype(F32) * padding[
        None, :
    ]
    decay_mat = (
        jnp.exp(jnp.maximum(distance, 0).astype(F32)[None] * log_decay[:, None, None])
        * allowed[None]
    )
    carry_factor = ((doc_ids == before) & (block > 0)).astype(F32)[:, None] * jnp.exp(
        (position + 1).astype(F32)[:, None] * log_decay[None, :]
    )
    end_factor = (padding * (doc_ids == last_doc).astype(F32))[:, None] * jnp.exp(
        (row_count - 1 - position).astype(F32)[:, None] * log_decay[None, :]
    )

    rows_f = rows_raw.astype(F32)
    mean_first, rstd_first = row_norm(rows_f)
    rows_first = (
        (rows_f - mean_first[:, None]) * rstd_first[:, None] * vectors[0] + vectors[1]
    ).astype(BF)
    queries = jnp.dot(rows_first, query_weight, preferred_element_type=F32).reshape(
        row_count, heads_here, KD
    )
    key_proj = jnp.dot(rows_first, key_weight, preferred_element_type=F32).reshape(
        row_count, heads_here, KD
    )
    values = (
        jnp.dot(rows_first, value_weight, preferred_element_type=F32)
        .astype(BF)
        .reshape(row_count, heads_here, VD)
    )
    gate_pre = jnp.dot(rows_first, gate_weight, preferred_element_type=F32)
    query_rot = rotate(queries, cosine, sine, 1.0).astype(BF)
    key_rot = (rotate(key_proj, cosine, sine, 1.0) * KD ** (-0.5)).astype(BF)
    key_end = (key_rot * end_factor[:, :, None]).astype(BF)
    summary = jnp.einsum("nha,nhb->hab", key_end, values, preferred_element_type=F32).astype(BF)
    state_in = (
        shifted(summary, 1).astype(F32)
        + shifted(summary, 2).astype(F32) * back_two[:, None, None]
        + shifted(summary, 3).astype(F32) * back_three[:, None, None]
    )
    state_low = state_in.astype(BF)
    scores = jnp.einsum("nha,mha->hnm", query_rot, key_rot, preferred_element_type=F32)
    weights = (scores * decay_mat).astype(BF)
    inner_part = jnp.einsum("hnm,mhb->nhb", weights, values, preferred_element_type=F32)
    query_carry = (query_rot * carry_factor[:, :, None]).astype(BF)
    mixed = inner_part + jnp.einsum(
        "nha,hab->nhb", query_carry, state_low, preferred_element_type=F32
    )
    grouped, group_pull = jax.vjp(group_norm, mixed)
    gate_act, gate_pull = jax.vjp(jax.nn.silu, gate_pre)
    flat_group = grouped.reshape(row_count, heads_here * VD)
    gated = (padding[:, None] * gate_act * flat_group).astype(BF)
    hidden = tokens.astype(F32) + sum_rows(
        jnp.dot(gated, output_weight, preferred_element_type=F32)
    ).astype(F32)
    hidden_rows = gather_rows(hidden.astype(BF))
    hidden_f = hidden_rows.astype(F32)
    mean_second, rstd_second = row_norm(hidden_f)
    norm_rows = (hidden_f - mean_second[:, None]) * rstd_second[:, None]
    rows_second = (norm_rows * vectors[2] + vectors[3]).astype(BF)
    up_proj = jnp.dot(rows_second, up_weight, preferred_element_type=F32)
    activation, act_pull = jax.vjp(partial(jax.nn.gelu, approximate=False), up_proj)
    act_low = activation.astype(BF)
    grad_act = jnp.einsum("nd,fd->nf", grad_rows, down_weight, preferred_element_type=F32)
    grad_up = act_pull(grad_act)[0].astype(BF)
    grad_ln2_part = jnp.einsum("nf,df->nd", grad_up, up_weight, preferred_element_type=F32)
    grad_ln2 = sum_rows(grad_ln2_part).astype(F32)
    scaled_part = grad_ln2_part * vectors[2]
    sums_second = lax.psum(
        jnp.stack([jnp.sum(scaled_part, axis=1), jnp.sum(scaled_part * norm_rows, axis=1)]), "head"
    )
    down_part = jnp.dot(act_low, down_weight, preferred_element_type=F32).astype(BF)
    grad_down = jnp.einsum("nf,nd->fd", act_low, grad_rows, preferred_element_type=F32).astype(BF)
    grad_upw = jnp.einsum("nd,nf->df", rows_second, grad_up, preferred_element_type=F32).astype(BF)

    norm_second = (hidden - mean_second[:, None]) * rstd_second[:, None]
    grad_hidden = out_grad.astype(F32) + rstd_second[:, None] * (
        grad_ln2 * feed_gain
        - sums_second[0][:, None] / full_width
        - norm_second * sums_second[1][:, None] / full_width
    )
    column_second = jnp.stack([jnp.sum(grad_ln2 * norm_second, axis=0), jnp.sum(grad_ln2, axis=0)])
    grad_branch = gather_rows(grad_hidden.astype(BF))
    result = hidden + sum_rows(after(down_part, grad_branch)).astype(F32)
    layer_out = result.astype(BF)

    grad_down, grad_upw = token_sum(grad_down, grad_upw)

    grad_outw = jnp.einsum("nc,nd->cd", gated, grad_branch, preferred_element_type=F32).astype(BF)
    grad_gated = jnp.einsum("nd,cd->nc", grad_branch, output_weight, preferred_element_type=F32)
    grad_masked = grad_gated * padding[:, None]
    grad_gate = gate_pull(grad_masked * flat_group)[0].astype(BF)
    grad_mixed = group_pull((grad_masked * gate_act).reshape(row_count, heads_here, VD))[0].astype(
        BF
    )
    grad_gw = jnp.einsum("nd,nc->dc", rows_first, grad_gate, preferred_element_type=F32).astype(BF)
    grad_outw, grad_gw = token_sum(grad_outw, grad_gw)

    grad_state = jnp.einsum(
        "nha,nhb->hab", query_carry, grad_mixed, preferred_element_type=F32
    ).astype(BF)
    state_grad = (
        shifted(grad_state, -1).astype(F32)
        + shifted(grad_state, -2).astype(F32) * ahead_two[:, None, None]
        + shifted(grad_state, -3).astype(F32) * ahead_three[:, None, None]
    )
    state_grad_low = state_grad.astype(BF)
    grad_weights = jnp.einsum("nhb,mhb->hnm", grad_mixed, values, preferred_element_type=F32)
    grad_scores = (grad_weights * decay_mat).astype(BF)
    grad_query_rot = jnp.einsum(
        "hnm,mha->nha", grad_scores, key_rot, preferred_element_type=F32
    ) + carry_factor[:, :, None] * jnp.einsum(
        "nhb,hab->nha", grad_mixed, state_low, preferred_element_type=F32
    )
    grad_key_rot = jnp.einsum(
        "hnm,nha->mha", grad_scores, query_rot, preferred_element_type=F32
    ) + end_factor[:, :, None] * jnp.einsum(
        "nhb,hab->nha", values, state_grad_low, preferred_element_type=F32
    )
    grad_values = (
        (
            jnp.einsum("hnm,nhb->mhb", weights, grad_mixed, preferred_element_type=F32)
            + jnp.einsum("nha,hab->nhb", key_end, state_grad_low, preferred_element_type=F32)
        )
        .astype(BF)
        .reshape(row_count, heads_here * VD)
    )
    grad_queries = (
        rotate(grad_query_rot, cosine, sine, -1.0).astype(BF).reshape(row_count, heads_here * KD)
    )
    grad_keys = (
        (rotate(grad_key_rot, cosine, sine, -1.0) * KD ** (-0.5))
        .astype(BF)
        .reshape(row_count, heads_here * KD)
    )
    grad_ln1_part = (
        jnp.einsum("nc,dc->nd", grad_queries, query_weight, preferred_element_type=F32)
        + jnp.einsum("nc,dc->nd", grad_keys, key_weight, preferred_element_type=F32)
        + jnp.einsum("nc,dc->nd", grad_values, value_weight, preferred_element_type=F32)
        + jnp.einsum("nc,dc->nd", grad_gate, gate_weight, preferred_element_type=F32)
    )
    grad_ln1 = sum_rows(grad_ln1_part).astype(F32)
    norm_full = (rows_f - mean_first[:, None]) * rstd_first[:, None]
    scaled_one = grad_ln1_part * vectors[0]
    sums_first = lax.psum(
        jnp.stack([jnp.sum(scaled_one, axis=1), jnp.sum(scaled_one * norm_full, axis=1)]), "head"
    )
    query_key = jnp.concatenate([grad_queries, grad_keys], axis=1)
    grad_vw = jnp.einsum("nd,nc->dc", rows_first, grad_values, preferred_element_type=F32)
    grad_qkw = jnp.einsum("nd,nc->dc", rows_first, query_key, preferred_element_type=F32)
    grad_vw, grad_qkw = token_sum(grad_vw.astype(BF), grad_qkw.astype(BF))
    grad_qw, grad_kw = grad_qkw[:, : heads_here * KD], grad_qkw[:, heads_here * KD :]

    norm_first = (tokens.astype(F32) - mean_first[:, None]) * rstd_first[:, None]
    tokens_grad = grad_hidden + rstd_first[:, None] * (
        grad_ln1 * mix_gain
        - sums_first[0][:, None] / full_width
        - norm_first * sums_first[1][:, None] / full_width
    )
    column_first = jnp.stack([jnp.sum(grad_ln1 * norm_first, axis=0), jnp.sum(grad_ln1, axis=0)])
    columns = lax.psum(jnp.concatenate([column_first, column_second]), "tok")
    return (
        layer_out,
        tokens_grad,
        columns[0],
        columns[1],
        grad_qw,
        grad_kw,
        grad_vw,
        grad_gw,
        grad_outw,
        columns[2],
        columns[3],
        grad_upw,
        grad_down,
    )


def solution(mesh):
    rows = P("tok", "head")
    columns = P(None, "head")
    return jax.shard_map(
        body,
        mesh=mesh,
        in_specs=(
            rows,
            P("head"),
            P("head"),
            columns,
            columns,
            columns,
            columns,
            P("head", None),
            P("head"),
            P("head"),
            columns,
            P("head", None),
            P("tok"),
            P("tok"),
            rows,
        ),
        out_specs=(
            rows,
            rows,
            P("head"),
            P("head"),
            columns,
            columns,
            columns,
            columns,
            P("head", None),
            P("head"),
            P("head"),
            columns,
            P("head", None),
        ),
        check_vma=False,
    )
```

time: 1880 us -> 1010 us (0.54)
  waiting for transfers between devices: 1410 us -> 464 us
  other arithmetic: 72.6 us -> 136 us
  starting transfers between devices: 3.76 us -> 54.6 us
  matrix products: 211 us -> 189 us
    psum x1 -> x0, waiting for transfers between devices: 561 us -> none  [body(): lax.psum((grad_qw, grad_kw, grad_vw, grad_gw, grad_outw, grad_gain1, grad...]
    reduce_scatter x4, waiting for transfers between devices: 504 us -> 126 us  [sum_rows(): lax.psum_scatter(values.astype(BF), 'head', scatter_dimension=1, tiled=True)]
    ppermute x1 -> x42, waiting for transfers between devices: 0.01 us -> 155 us  [the longest x36 144 us: swapped(): lax.ppermute(value, 'tok', [(i, i ^ 1 << bit) for i in range(length)])]
    all_gather x4, waiting for transfers between devices: 303 us -> 182 us  [gather_rows(): return lax.all_gather(values, 'head', axis=1, tiled=True)]
    ppermute x1 -> x42, starting transfers between devices: 2.23 us -> 53.9 us  [the longest x36 41 us: swapped(): lax.ppermute(value, 'tok', [(i, i ^ 1 << bit) for i in range(length)])]
    all_gather x2 -> x0, waiting for transfers between devices: 38.9 us -> none  [prefix(): pieces = jax.tree.map(lambda part: lax.all_gather(part, axis), value)]
    convert_element_type x11 -> x24, other arithmetic: 19.8 us -> 56.9 us  [the longest x6 36.3 us: gather_back(): return value.astype(F32)]
    psum x5 -> x3, blocking collectives: 62.7 us -> 33.6 us  [the longest x1 12.1 us: body(): columns = lax.psum(jnp.concatenate([column_first, column_second]), 'tok')]
  transfers between devices with their start and end apart: 12 -> 50, of which waited for: 11 -> 22; matrix products, arithmetic and copies ran while one was open for 7% -> 29% of each run, Pallas kernels for 0% -> 0%
where the time goes in v1:
time: 1010 us; the launch traced here: 1000 us
  waiting for transfers between devices  464 us (46%)
  matrix products  189 us (19%)
  other arithmetic  136 us (13%)
  local copies, waits for them, and re-layouts  77.1 us (8%)
  blocking collectives  57.8 us (6%)
  starting transfers between devices  54.6 us (5%)
  between operations  21.1 us (2%)
    all_gather x4, waiting for transfers between devices, gather_rows(): return lax.all_gather(values, 'head', axis=1, tiled=True)  182 us
    ppermute x36, waiting for transfers between devices, swapped(): lax.ppermute(value, 'tok', [(i, i ^ 1 << bit) for i in range(length)])  144 us
    reduce_scatter x4, waiting for transfers between devices, sum_rows(): lax.psum_scatter(values.astype(BF), 'head', scatter_dimension=1, tiled=True)  126 us
    ppermute x36, starting transfers between devices, swapped(): lax.ppermute(value, 'tok', [(i, i ^ 1 << bit) for i in range(length)])  41 us
    unnamed x205, local copies, waits for them, and re-layouts  40.9 us
    convert_element_type x6, other arithmetic, gather_back(): return value.astype(F32)  36.3 us
    select_n x12, other arithmetic, gather_back(): jnp.where(low_first, jnp.concatenate([value, other], axis=0), jnp.concate...  28.8 us
    add x12, other arithmetic, scatter_sum(): value = keep.astype(F32) + swapped(give.astype(BF), bit).astype(F32)  21.4 us
  transfers between devices with their start and end apart: 50, of which 22 were waited for; matrix products, arithmetic and copies ran while one was open for 29% of the time, Pallas kernels for 0%

profile of v1, /device:TPU:0, one launch (start us, length us, event | category | flops | bytes accessed | tf_op | source)
XLA Modules:
  0.0 1000.1 jit_solution(1467444606638663495)
XLA Ops:
  11.2 9.5 all-reduce
  24.6 5.3 copy.59
  32.6 5.4 copy.58
  41.2 14.7 %all_gather.19 = f32[4,2048]{1,0:T(4,128)S(1)} all-gather(f32[4,512]{1,0:T(4,128)S(1)} %pad_maximum_fusion.2), channel_id=1, replica_groups=mesh['head'=4,'tok'=8] {'head'}, dimensions={1}, use_global_device_ids=true | all-gather | bytes 40960 | tf_op jit(solution)/shard_map/all_gather | solution.py:133
  60.5 33.0 %all-gather.5.cloned.1.call-done = bf16[1024,2048]{1,0:T(8,128)(2,1)} async-done(((bf16[1024,512]{1,0:T(8,128)(2,1)}), bf16[1024,2048]{1,0:T(8,128)(2,1)}) %all-gather.5.cloned.1.call-update) | async-done | bytes 4194320 | tf_op jit(solution)/shard_map/all_gather | solution.py:76
  99.9 6.2 convolution_convert_fusion.8
  144.9 10.2 %collective-permute-done.1 = bf16[2,256,512]{2,1,0:T(8,128)(2,1)S(1)} collective-permute-done((bf16[2,256,512]{2,1,0:T(8,128)(2,1)}, bf16[2,256,512]{2,1,0:T(8,128)(2,1)S(1)}, u32[]{:S(2)}, u32[]{:S(2)}) %collective-permute-start.1) | collective-permute-done | bytes 524320 | tf_op jit(solution)/shard_map/ppermute | solution.py:22
  163.0 7.3 fusion.26
  170.4 7.8 convolution_convert_fusion.7
  178.2 84.2 %reduce-scatter.5.cloned.1.call-done = bf16[1024,512]{1,0:T(8,128)(2,1)} async-done(((bf16[1024,2048]{1,0:T(8,128)(2,1)}), bf16[1024,512]{1,0:T(8,128)(2,1)}) %reduce-scatter.5.cloned.1.call-update) | async-done | bytes 1048592 | tf_op jit(solution)/shard_map/reduce_scatter | solution.py:80
  265.5 80.8 %all-gather.7.cloned.1.call-done = bf16[1024,2048]{1,0:T(8,128)(2,1)} async-done(((bf16[1024,512]{1,0:T(8,128)(2,1)}), bf16[1024,2048]{1,0:T(8,128)(2,1)}) %all-gather.7.cloned.1.call-update) | async-done | bytes 4194320 | tf_op jit(solution)/shard_map/all_gather | solution.py:76
  349.9 9.1 fusion.82
  359.0 68.1 %all-gather.9.cloned.1.call-done = bf16[1024,2048]{1,0:T(8,128)(2,1)} async-done(((bf16[1024,512]{1,0:T(8,128)(2,1)}), bf16[1024,2048]{1,0:T(8,128)(2,1)}) %all-gather.9.cloned.1.call-update) | async-done | bytes 4194320 | tf_op jit(solution)/shard_map/all_gather | solution.py:76
  427.1 18.2 %add_convert_fusion.1 = (bf16[1024,1024]{0,1:T(8,128)(2,1)S(1)}, f32[1024,1024]{0,1:T(8,128)}) fusion(f32[1024,1024]{0,1:T(8,128)} %fusion.82, bf16[1024,2048]{1,0:T(8,128)(2,1)} %all-gather.9.cloned.1.call-done, bf16[1024,2048]{1,0:T(8,128)(2,1)} %param.26), kind=kOutput, calls=%fused_computation.63 | convolution fusion | flops 4370464768 | bytes 18874368 | tf_op jit(solution)/shard_map/nd,fd->nf/dot_general | solution.py:223
  445.3 8.2 multiply_reduce_fusion.1
  454.0 8.1 convolution_convert_fusion.1
  477.0 10.6 %psum.21 = f32[2,1024]{1,0:T(2,128)S(1)} all-reduce(f32[2,1024]{1,0:T(2,128)S(1)} %pad_maximum_fusion.3), channel_id=1, replica_groups=mesh['head'=4,'tok'=8] {'head'}, use_global_device_ids=true, to_apply=%region_10.11 | all-reduce | flops 2048 | bytes 16384 | tf_op jit(solution)/shard_map/psum | solution.py:228
  487.6 41.9 %reduce-scatter.7.cloned.1.call-done = bf16[1024,512]{1,0:T(8,128)(2,1)} async-done(((bf16[1024,2048]{1,0:T(8,128)(2,1)}), bf16[1024,512]{1,0:T(8,128)(2,1)}) %reduce-scatter.7.cloned.1.call-update) | async-done | bytes 1048592 | tf_op jit(solution)/shard_map/reduce_scatter | solution.py:80
  545.4 16.6 %collective-permute-done.31 = bf16[512,1024]{1,0:T(8,128)(2,1)} collective-permute-done((bf16[512,1024]{1,0:T(8,128)(2,1)S(1)}, bf16[512,1024]{1,0:T(8,128)(2,1)}, u32[]{:S(2)}, u32[]{:S(2)}) %collective-permute-start.31) | collective-permute-done | bytes 1048608 | tf_op jit(solution)/shard_map/ppermute | solution.py:27
  589.4 4.9 collective-permute-done.33
  598.3 8.5 convolution_convert_fusion.6
  611.5 10.0 collective-permute-done.34
  625.4 12.9 %fusion.19 = (bf16[1024,1024]{0,1:T(8,128)(2,1)}, f32[1024,1024]{0,1:T(8,128)S(1)}) fusion(f32[1024,1024]{0,1:T(8,128)} %get-tuple-element.94, f32[1024,2,512]{0,2,1:T(8,128)} %copy-done.42, f32[1024]{0:T(1024)S(1)} %convert_element_type.435, bf16[1024,2048]{1,0:T(8,128)(2,1)} %all-gather.11.cloned.1.call-done, bf16[1024,2048]{1,0:T(8,128)(2,1)} %param.22), kind=kOutput, calls=%fused_computation.34 | convolution fusion | flops 4307550208 | bytes 23072768 | tf_op jit(solution)/shard_map/nd,cd->nc/dot_general | solution.py:249
  648.2 5.6 multiply_convert_fusion
  662.4 7.6 convolution_convert_fusion.3
  674.7 5.2 convolution_convert_fusion.2
  684.4 6.8 fusion.99
  709.8 7.4 convolution_convert_fusion.5
  724.6 5.0 convolution_convert_fusion.4
  734.0 6.8 fusion.98
  740.9 5.8 fusion.96
  746.7 12.6 %multiply_reduce_fusion = (f32[1024]{0:T(1024)S(1)}, f32[1024]{0:T(1024)S(1)}, bf16[1024,2048]{1,0:T(8,128)(2,1)}) fusion(f32[2048]{0:T(1024)S(1)} %bitcast.285, f32[1024]{0:T(1024)S(1)} %copy-done.72, f32[1024]{0:T(1024)S(1)} %copy-done.70, bf16[1024,2048]{1,0:T(8,128)(2,1)S(1)} %copy-done.8, f32[1024,2048]{1,0:T(8,128)} %fusion.99, ...), kind=kOutput, calls=%fused_computation.24 | convolution fusion | flops 2170550272 | bytes 36724736 | tf_op jit(solution)/shard_map/nc,dc->nd/dot_general | solution.py:297
  778.4 13.2 %collective-permute-done.19 = bf16[512,1024]{1,0:T(8,128)(2,1)S(1)} collective-permute-done((bf16[512,1024]{1,0:T(8,128)(2,1)S(1)}, bf16[512,1024]{1,0:T(8,128)(2,1)S(1)}, u32[]{:S(2)}, u32[]{:S(2)}) %collective-permute-start.19) | collective-permute-done | bytes 1048608 | tf_op jit(solution)/shard_map/ppermute | solution.py:27
  799.1 14.9 %collective-permute-done.7 = bf16[512,1024]{1,0:T(8,128)(2,1)S(1)} collective-permute-done((bf16[512,1024]{1,0:T(8,128)(2,1)S(1)}, bf16[512,1024]{1,0:T(8,128)(2,1)S(1)}, u32[]{:S(2)}, u32[]{:S(2)}) %collective-permute-start.7) | collective-permute-done | bytes 1048608 | tf_op jit(solution)/shard_map/ppermute | solution.py:27
  821.7 8.8 collective-permute-done.20
  833.9 7.8 collective-permute-done.8
  842.8 9.7 collective-permute-done.21
  862.3 5.0 collective-permute-done.9
  867.8 22.3 %collective-permute-done.15 = bf16[256,1024]{1,0:T(8,128)(2,1)S(1)} collective-permute-done((bf16[256,1024]{1,0:T(8,128)(2,1)S(1)}, bf16[256,1024]{1,0:T(8,128)(2,1)S(1)}, u32[]{:S(2)}, u32[]{:S(2)}) %collective-permute-start.15) | collective-permute-done | bytes 524320 | tf_op jit(solution)/shard_map/ppermute | solution.py:27
  896.4 17.0 %collective-permute-done.10 = bf16[512,1024]{1,0:T(8,128)(2,1)S(1)} collective-permute-done((bf16[512,1024]{1,0:T(8,128)(2,1)S(1)}, bf16[512,1024]{1,0:T(8,128)(2,1)S(1)}, u32[]{:S(2)}, u32[]{:S(2)}) %collective-permute-start.10) | collective-permute-done | bytes 1048608 | tf_op jit(solution)/shard_map/ppermute | solution.py:27
  923.6 5.8 fusion.24
  929.5 6.8 fusion.25
  936.2 11.0 %psum.22 = f32[2,1024]{1,0:T(2,128)S(1)} all-reduce(f32[2,1024]{1,0:T(2,128)S(1)} %pad_maximum_fusion.4), channel_id=1, replica_groups=mesh['head'=4,'tok'=8] {'head'}, use_global_device_ids=true, to_apply=%region_17.18 | all-reduce | flops 2048 | bytes 16384 | tf_op jit(solution)/shard_map/psum | solution.py:304
  947.3 6.3 fusion.22
  953.5 6.8 fusion.23
  964.7 6.3 fusion.21
  975.5 4.9 fusion.50
  980.4 12.1 %psum.23 = f32[4,512]{1,0:T(4,128)S(1)} all-reduce(f32[4,512]{1,0:T(4,128)S(1)} %pad_maximum_fusion.5), channel_id=1, replica_groups=mesh['head'=4,'tok'=8] {'tok'}, use_global_device_ids=true, to_apply=%region_22.23 | all-reduce | flops 2048 | bytes 16384 | tf_op jit(solution)/shard_map/psum | solution.py:320
  (406 shorter events, 275.9 us)
Async XLA Ops:
  7.2 86.3 %all-gather.5.cloned.1.call-start = ((), (), s32[]{:S(2)}) async-start(), calls=%async_computation.4 | async-start | bytes 5242880 | tf_op jit(solution)/shard_map/all_gather | solution.py:76
  7.9 254.4 %reduce-scatter.5.cloned.1.call-start = ((), (), s32[]{:S(2)}) async-start(), calls=%async_computation.5 | async-start | bytes 5242880 | tf_op jit(solution)/shard_map/reduce_scatter | solution.py:80
  131.5 13.4 %collective-permute-start.2 = (bf16[2,256,512]{2,1,0:T(8,128)(2,1)}, bf16[2,256,512]{2,1,0:T(8,128)(2,1)S(1)}, u32[]{:S(2)}, u32[]{:S(2)}) collective-permute-start(bf16[2,256,512]{2,1,0:T(8,128)(2,1)} %convolution_convert_fusion.10), channel_id=1, source_target_pairs={{0,3},{1,4},{2,5},{3,6},{4,7},{8,11},{9,12},{10,13},{11,14},{12,15... | collective-permute-start | bytes 1572872 | tf_op jit(solution)/shard_map/ppermute | solution.py:22
  134.5 20.7 %collective-permute-start.1 = (bf16[2,256,512]{2,1,0:T(8,128)(2,1)}, bf16[2,256,512]{2,1,0:T(8,128)(2,1)S(1)}, u32[]{:S(2)}, u32[]{:S(2)}) collective-permute-start(bf16[2,256,512]{2,1,0:T(8,128)(2,1)} %convolution_convert_fusion.10), channel_id=1, source_target_pairs={{0,2},{1,3},{2,4},{3,5},{4,6},{5,7},{8,10},{9,11},{10,12},{11,13},... | collective-permute-start | bytes 1572872 | tf_op jit(solution)/shard_map/ppermute | solution.py:22
  137.9 17.3 %collective-permute-start = (bf16[2,256,512]{2,1,0:T(8,128)(2,1)}, bf16[2,256,512]{2,1,0:T(8,128)(2,1)S(1)}, u32[]{:S(2)}, u32[]{:S(2)}) collective-permute-start(bf16[2,256,512]{2,1,0:T(8,128)(2,1)} %convolution_convert_fusion.10), channel_id=1, source_target_pairs={{0,1},{1,2},{2,3},{3,4},{4,5},{5,6},{6,7},{8,9},{9,10},{10,11},{11... | collective-permute-start | bytes 1572872 | tf_op jit(solution)/shard_map/ppermute | solution.py:22
  178.2 168.1 %all-gather.7.cloned.1.call-start = ((), (), s32[]{:S(2)}) async-start(), calls=%async_computation.6 | async-start | bytes 5242880 | tf_op jit(solution)/shard_map/all_gather | solution.py:76
  264.9 162.3 %all-gather.9.cloned.1.call-start = ((), (), s32[]{:S(2)}) async-start(), calls=%async_computation.7 | async-start | bytes 5242880 | tf_op jit(solution)/shard_map/all_gather | solution.py:76
  265.4 264.1 %reduce-scatter.7.cloned.1.call-start = ((), (), s32[]{:S(2)}) async-start(), calls=%async_computation.8 | async-start | bytes 5242880 | tf_op jit(solution)/shard_map/reduce_scatter | solution.py:80
  453.6 171.8 %all-gather.11.cloned.1.call-start = ((), (), s32[]{:S(2)}) async-start(), calls=%async_computation.9 | async-start | bytes 5242880 | tf_op jit(solution)/shard_map/all_gather | solution.py:76
  463.6 69.8 %collective-permute-start.30 = (bf16[1024,1024]{1,0:T(8,128)(2,1)}, bf16[1024,1024]{1,0:T(8,128)(2,1)}, u32[]{:S(2)}, u32[]{:S(2)}) collective-permute-start(bf16[1024,1024]{1,0:T(8,128)(2,1)} %dynamic-slice_bitcast_fusion.1), channel_id=1, source_target_pairs={{0,1},{1,0},{2,3},{3,2},{4,5},{5,4},{6,7},{7,6},{8,9},{9,8},{10,11... | collective-permute-start | bytes 6291464 | tf_op jit(solution)/shard_map/ppermute | solution.py:27
  477.0 61.4 %collective-permute-start.36 = (bf16[512,2048]{1,0:T(8,128)(2,1)}, bf16[512,2048]{1,0:T(8,128)(2,1)}, u32[]{:S(2)}, u32[]{:S(2)}) collective-permute-start(bf16[512,2048]{1,0:T(8,128)(2,1)} %dynamic-slice_bitcast_fusion), channel_id=1, source_target_pairs={{0,1},{1,0},{2,3},{3,2},{4,5},{5,4},{6,7},{7,6},{8,9},{9,8},{10,11... | collective-permute-start | bytes 6291464 | tf_op jit(solution)/shard_map/ppermute | solution.py:27
  533.3 442.1 %reduce-scatter.9.cloned.1.call-start = ((), (), s32[]{:S(2)}) async-start(), calls=%async_computation.10 | async-start | bytes 5242880 | tf_op jit(solution)/shard_map/reduce_scatter | solution.py:80
  536.9 25.1 %collective-permute-start.31 = (bf16[512,1024]{1,0:T(8,128)(2,1)S(1)}, bf16[512,1024]{1,0:T(8,128)(2,1)}, u32[]{:S(2)}, u32[]{:S(2)}) collective-permute-start(bf16[512,1024]{1,0:T(8,128)(2,1)S(1)} %fusion.63), channel_id=1, source_target_pairs={{0,4},{1,5},{2,6},{3,7},{4,0},{5,1},{6,2},{7,3},{8,12},{9,13},{10,... | collective-permute-start | bytes 3145736 | tf_op jit(solution)/shard_map/ppermute | solution.py:27
  543.9 26.4 %collective-permute-start.37 = (bf16[256,2048]{1,0:T(8,128)(2,1)}, bf16[256,2048]{1,0:T(8,128)(2,1)}, u32[]{:S(2)}, u32[]{:S(2)}) collective-permute-start(bf16[256,2048]{1,0:T(8,128)(2,1)} %fusion.64), channel_id=1, source_target_pairs={{0,2},{1,3},{2,0},{3,1},{4,6},{5,7},{6,4},{7,5},{8,10},{9,11},{10,... | collective-permute-start | bytes 3145736 | tf_op jit(solution)/shard_map/ppermute | solution.py:27
  564.3 15.8 %collective-permute-start.32 = (bf16[256,1024]{1,0:T(8,128)(2,1)S(1)}, bf16[256,1024]{1,0:T(8,128)(2,1)}, u32[]{:S(2)}, u32[]{:S(2)}) collective-permute-start(bf16[256,1024]{1,0:T(8,128)(2,1)S(1)} %fusion.75), channel_id=1, source_target_pairs={{0,2},{1,3},{2,0},{3,1},{4,6},{5,7},{6,4},{7,5},{8,10},{9,11},{10,... | collective-permute-start | bytes 1572872 | tf_op jit(solution)/shard_map/ppermute | solution.py:27
  587.7 19.2 %collective-permute-start.39 = (bf16[128,2048]{1,0:T(8,128)(2,1)}, bf16[128,2048]{1,0:T(8,128)(2,1)}, u32[]{:S(2)}, u32[]{:S(2)}) collective-permute-start(bf16[128,2048]{1,0:T(8,128)(2,1)} %fusion.65), channel_id=1, source_target_pairs={{0,4},{1,5},{2,6},{3,7},{4,0},{5,1},{6,2},{7,3},{8,12},{9,13},{10,... | collective-permute-start | bytes 1572872 | tf_op jit(solution)/shard_map/ppermute | solution.py:27
  596.4 25.1 %collective-permute-start.34 = (bf16[512,1024]{1,0:T(8,128)(2,1)S(1)}, bf16[512,1024]{1,0:T(8,128)(2,1)}, u32[]{:S(2)}, u32[]{:S(2)}) collective-permute-start(bf16[512,1024]{1,0:T(8,128)(2,1)S(1)} %maximum_select_fusion.16), channel_id=1, source_target_pairs={{0,4},{1,5},{2,6},{3,7},{4,0},{5,1},{6,2},{7,3},{8,12},{9,13},{10,... | collective-permute-start | bytes 3145736 | tf_op jit(solution)/shard_map/ppermute | solution.py:27
  610.0 247.3 %collective-permute-start.40 = (bf16[256,2048]{1,0:T(8,128)(2,1)}, bf16[256,2048]{1,0:T(8,128)(2,1)}, u32[]{:S(2)}, u32[]{:S(2)}) collective-permute-start(bf16[256,2048]{1,0:T(8,128)(2,1)} %maximum_select_fusion.17), channel_id=1, source_target_pairs={{0,2},{1,3},{2,0},{3,1},{4,6},{5,7},{6,4},{7,5},{8,10},{9,11},{10,... | collective-permute-start | bytes 3145736 | tf_op jit(solution)/shard_map/ppermute | solution.py:27
  643.9 51.7 %collective-permute-start.5 = (bf16[2,256,512]{2,1,0:T(8,128)(2,1)}, bf16[2,256,512]{2,1,0:T(8,128)(2,1)}, u32[]{:S(2)}, u32[]{:S(2)}) collective-permute-start(bf16[2,256,512]{2,1,0:T(8,128)(2,1)} %convolution_convert_fusion.9), channel_id=1, source_target_pairs={{3,0},{4,1},{5,2},{6,3},{7,4},{11,8},{12,9},{13,10},{14,11},{15,12... | collective-permute-start | bytes 1572872 | tf_op jit(solution)/shard_map/ppermute | solution.py:22
  645.3 51.5 %collective-permute-start.4 = (bf16[2,256,512]{2,1,0:T(8,128)(2,1)}, bf16[2,256,512]{2,1,0:T(8,128)(2,1)}, u32[]{:S(2)}, u32[]{:S(2)}) collective-permute-start(bf16[2,256,512]{2,1,0:T(8,128)(2,1)} %convolution_convert_fusion.9), channel_id=1, source_target_pairs={{2,0},{3,1},{4,2},{5,3},{6,4},{7,5},{10,8},{11,9},{12,10},{13,11},... | collective-permute-start | bytes 1572872 | tf_op jit(solution)/shard_map/ppermute | solution.py:22
  646.6 50.2 %collective-permute-start.3 = (bf16[2,256,512]{2,1,0:T(8,128)(2,1)}, bf16[2,256,512]{2,1,0:T(8,128)(2,1)}, u32[]{:S(2)}, u32[]{:S(2)}) collective-permute-start(bf16[2,256,512]{2,1,0:T(8,128)(2,1)} %convolution_convert_fusion.9), channel_id=1, source_target_pairs={{1,0},{2,1},{3,2},{4,3},{5,4},{6,5},{7,6},{9,8},{10,9},{11,10},{12... | collective-permute-start | bytes 1572872 | tf_op jit(solution)/shard_map/ppermute | solution.py:22
  662.3 313.1 %reduce-scatter.11.cloned.1.call-start = ((), (), s32[]{:S(2)}) async-start(), calls=%async_computation.11 | async-start | bytes 5242880 | tf_op jit(solution)/shard_map/reduce_scatter | solution.py:80
  671.5 87.9 %collective-permute-start.18 = (bf16[1024,1024]{1,0:T(8,128)(2,1)}, bf16[1024,1024]{1,0:T(8,128)(2,1)}, u32[]{:S(2)}, u32[]{:S(2)}) collective-permute-start(bf16[1024,1024]{1,0:T(8,128)(2,1)} %dynamic-slice_bitcast_fusion.3), channel_id=1, source_target_pairs={{0,1},{1,0},{2,3},{3,2},{4,5},{5,4},{6,7},{7,6},{8,9},{9,8},{10,11... | collective-permute-start | bytes 6291464 | tf_op jit(solution)/shard_map/ppermute | solution.py:27
  695.6 67.6 %collective-permute-start.24 = (bf16[512,2048]{1,0:T(8,128)(2,1)}, bf16[512,2048]{1,0:T(8,128)(2,1)}, u32[]{:S(2)}, u32[]{:S(2)}) collective-permute-start(bf16[512,2048]{1,0:T(8,128)(2,1)} %dynamic-slice_bitcast_fusion.2), channel_id=1, source_target_pairs={{0,1},{1,0},{2,3},{3,2},{4,5},{5,4},{6,7},{7,6},{8,9},{9,8},{10,11... | collective-permute-start | bytes 6291464 | tf_op jit(solution)/shard_map/ppermute | solution.py:27
  720.8 49.3 %collective-permute-start.6 = (bf16[1024,1024]{1,0:T(8,128)(2,1)}, bf16[1024,1024]{1,0:T(8,128)(2,1)}, u32[]{:S(2)}, u32[]{:S(2)}) collective-permute-start(bf16[1024,1024]{1,0:T(8,128)(2,1)} %dynamic-slice_bitcast_fusion.5), channel_id=1, source_target_pairs={{0,1},{1,0},{2,3},{3,2},{4,5},{5,4},{6,7},{7,6},{8,9},{9,8},{10,11... | collective-permute-start | bytes 6291464 | tf_op jit(solution)/shard_map/ppermute | solution.py:27
  731.1 44.4 %collective-permute-start.12 = (bf16[1024,1024]{1,0:T(8,128)(2,1)}, bf16[1024,1024]{1,0:T(8,128)(2,1)}, u32[]{:S(2)}, u32[]{:S(2)}) collective-permute-start(bf16[1024,1024]{1,0:T(8,128)(2,1)} %dynamic-slice_bitcast_fusion.4), channel_id=1, source_target_pairs={{0,1},{1,0},{2,3},{3,2},{4,5},{5,4},{6,7},{7,6},{8,9},{9,8},{10,11... | collective-permute-start | bytes 6291464 | tf_op jit(solution)/shard_map/ppermute | solution.py:27
  759.4 164.2 %collective-permute-start.35 = (bf16[1024,1024]{1,0:T(8,128)(2,1)}, bf16[1024,1024]{1,0:T(8,128)(2,1)}, u32[]{:S(2)}, u32[]{:S(2)}) collective-permute-start(bf16[1024,1024]{1,0:T(8,128)(2,1)} %maximum_select_fusion.10), channel_id=1, source_target_pairs={{0,1},{1,0},{2,3},{3,2},{4,5},{5,4},{6,7},{7,6},{8,9},{9,8},{10,11... | collective-permute-start | bytes 6291464 | tf_op jit(solution)/shard_map/ppermute | solution.py:27
  763.1 28.4 %collective-permute-start.19 = (bf16[512,1024]{1,0:T(8,128)(2,1)S(1)}, bf16[512,1024]{1,0:T(8,128)(2,1)S(1)}, u32[]{:S(2)}, u32[]{:S(2)}) collective-permute-start(bf16[512,1024]{1,0:T(8,128)(2,1)S(1)} %fusion.61), channel_id=1, source_target_pairs={{0,4},{1,5},{2,6},{3,7},{4,0},{5,1},{6,2},{7,3},{8,12},{9,13},{10,... | collective-permute-start | bytes 3145736 | tf_op jit(solution)/shard_map/ppermute | solution.py:27
  770.1 26.6 %collective-permute-start.25 = (bf16[256,2048]{1,0:T(8,128)(2,1)S(1)}, bf16[256,2048]{1,0:T(8,128)(2,1)S(1)}, u32[]{:S(2)}, u32[]{:S(2)}) collective-permute-start(bf16[256,2048]{1,0:T(8,128)(2,1)S(1)} %fusion.62), channel_id=1, source_target_pairs={{0,2},{1,3},{2,0},{3,1},{4,6},{5,7},{6,4},{7,5},{8,10},{9,11},{10,... | collective-permute-start | bytes 3145736 | tf_op jit(solution)/shard_map/ppermute | solution.py:27
  775.5 38.5 %collective-permute-start.7 = (bf16[512,1024]{1,0:T(8,128)(2,1)S(1)}, bf16[512,1024]{1,0:T(8,128)(2,1)S(1)}, u32[]{:S(2)}, u32[]{:S(2)}) collective-permute-start(bf16[512,1024]{1,0:T(8,128)(2,1)S(1)} %fusion.59), channel_id=1, source_target_pairs={{0,4},{1,5},{2,6},{3,7},{4,0},{5,1},{6,2},{7,3},{8,12},{9,13},{10,... | collective-permute-start | bytes 3145736 | tf_op jit(solution)/shard_map/ppermute | solution.py:27
  791.6 27.6 %collective-permute-start.13 = (bf16[512,1024]{1,0:T(8,128)(2,1)S(1)}, bf16[512,1024]{1,0:T(8,128)(2,1)S(1)}, u32[]{:S(2)}, u32[]{:S(2)}) collective-permute-start(bf16[512,1024]{1,0:T(8,128)(2,1)S(1)} %fusion.60), channel_id=1, source_target_pairs={{0,2},{1,3},{2,0},{3,1},{4,6},{5,7},{6,4},{7,5},{8,10},{9,11},{10,... | collective-permute-start | bytes 3145736 | tf_op jit(solution)/shard_map/ppermute | solution.py:27
  796.7 33.7 %collective-permute-start.20 = (bf16[256,1024]{1,0:T(8,128)(2,1)S(1)}, bf16[256,1024]{1,0:T(8,128)(2,1)S(1)}, u32[]{:S(2)}, u32[]{:S(2)}) collective-permute-start(bf16[256,1024]{1,0:T(8,128)(2,1)S(1)} %fusion.73), channel_id=1, source_target_pairs={{0,2},{1,3},{2,0},{3,1},{4,6},{5,7},{6,4},{7,5},{8,10},{9,11},{10,... | collective-permute-start | bytes 1572872 | tf_op jit(solution)/shard_map/ppermute | solution.py:27
  814.0 17.6 %collective-permute-start.26 = (bf16[128,2048]{1,0:T(8,128)(2,1)S(1)}, bf16[128,2048]{1,0:T(8,128)(2,1)S(1)}, u32[]{:S(2)}, u32[]{:S(2)}) collective-permute-start(bf16[128,2048]{1,0:T(8,128)(2,1)S(1)} %fusion.74), channel_id=1, source_target_pairs={{0,4},{1,5},{2,6},{3,7},{4,0},{5,1},{6,2},{7,3},{8,12},{9,13},{10,... | collective-permute-start | bytes 1572872 | tf_op jit(solution)/shard_map/ppermute | solution.py:27
  819.2 22.5 %collective-permute-start.8 = (bf16[256,1024]{1,0:T(8,128)(2,1)S(1)}, bf16[256,1024]{1,0:T(8,128)(2,1)S(1)}, u32[]{:S(2)}, u32[]{:S(2)}) collective-permute-start(bf16[256,1024]{1,0:T(8,128)(2,1)S(1)} %fusion.71), channel_id=1, source_target_pairs={{0,2},{1,3},{2,0},{3,1},{4,6},{5,7},{6,4},{7,5},{8,10},{9,11},{10,... | collective-permute-start | bytes 1572872 | tf_op jit(solution)/shard_map/ppermute | solution.py:27
  830.5 24.3 %collective-permute-start.14 = (bf16[256,1024]{1,0:T(8,128)(2,1)S(1)}, bf16[256,1024]{1,0:T(8,128)(2,1)S(1)}, u32[]{:S(2)}, u32[]{:S(2)}) collective-permute-start(bf16[256,1024]{1,0:T(8,128)(2,1)S(1)} %fusion.72), channel_id=1, source_target_pairs={{0,4},{1,5},{2,6},{3,7},{4,0},{5,1},{6,2},{7,3},{8,12},{9,13},{10,... | collective-permute-start | bytes 1572872 | tf_op jit(solution)/shard_map/ppermute | solution.py:27
  831.6 20.9 %collective-permute-start.21 = (bf16[256,1024]{1,0:T(8,128)(2,1)S(1)}, bf16[256,1024]{1,0:T(8,128)(2,1)S(1)}, u32[]{:S(2)}, u32[]{:S(2)}) collective-permute-start(bf16[256,1024]{1,0:T(8,128)(2,1)S(1)} %fusion.68), channel_id=1, source_target_pairs={{0,2},{1,3},{2,0},{3,1},{4,6},{5,7},{6,4},{7,5},{8,10},{9,11},{10,... | collective-permute-start | bytes 1572872 | tf_op jit(solution)/shard_map/ppermute | solution.py:27
  841.7 13.7 %collective-permute-start.27 = (bf16[128,2048]{1,0:T(8,128)(2,1)S(1)}, bf16[128,2048]{1,0:T(8,128)(2,1)S(1)}, u32[]{:S(2)}, u32[]{:S(2)}) collective-permute-start(bf16[128,2048]{1,0:T(8,128)(2,1)S(1)} %fusion.67), channel_id=1, source_target_pairs={{0,4},{1,5},{2,6},{3,7},{4,0},{5,1},{6,2},{7,3},{8,12},{9,13},{10,... | collective-permute-start | bytes 1572872 | tf_op jit(solution)/shard_map/ppermute | solution.py:27
  852.5 14.8 %collective-permute-start.9 = (bf16[256,1024]{1,0:T(8,128)(2,1)S(1)}, bf16[256,1024]{1,0:T(8,128)(2,1)S(1)}, u32[]{:S(2)}, u32[]{:S(2)}) collective-permute-start(bf16[256,1024]{1,0:T(8,128)(2,1)S(1)} %fusion.70), channel_id=1, source_target_pairs={{0,2},{1,3},{2,0},{3,1},{4,6},{5,7},{6,4},{7,5},{8,10},{9,11},{10,... | collective-permute-start | bytes 1572872 | tf_op jit(solution)/shard_map/ppermute | solution.py:27
  854.7 36.2 %collective-permute-start.22 = (bf16[512,1024]{1,0:T(8,128)(2,1)S(1)}, bf16[512,1024]{1,0:T(8,128)(2,1)S(1)}, u32[]{:S(2)}, u32[]{:S(2)}) collective-permute-start(bf16[512,1024]{1,0:T(8,128)(2,1)S(1)} %maximum_select_fusion.14), channel_id=1, source_target_pairs={{0,4},{1,5},{2,6},{3,7},{4,0},{5,1},{6,2},{7,3},{8,12},{9,13},{10,... | collective-permute-start | bytes 3145736 | tf_op jit(solution)/shard_map/ppermute | solution.py:27
  855.4 34.8 %collective-permute-start.15 = (bf16[256,1024]{1,0:T(8,128)(2,1)S(1)}, bf16[256,1024]{1,0:T(8,128)(2,1)S(1)}, u32[]{:S(2)}, u32[]{:S(2)}) collective-permute-start(bf16[256,1024]{1,0:T(8,128)(2,1)S(1)} %fusion.69), channel_id=1, source_target_pairs={{0,4},{1,5},{2,6},{3,7},{4,0},{5,1},{6,2},{7,3},{8,12},{9,13},{10,... | collective-permute-start | bytes 1572872 | tf_op jit(solution)/shard_map/ppermute | solution.py:27
  857.3 36.6 %collective-permute-start.28 = (bf16[256,2048]{1,0:T(8,128)(2,1)S(1)}, bf16[256,2048]{1,0:T(8,128)(2,1)S(1)}, u32[]{:S(2)}, u32[]{:S(2)}) collective-permute-start(bf16[256,2048]{1,0:T(8,128)(2,1)S(1)} %maximum_select_fusion.15), channel_id=1, source_target_pairs={{0,2},{1,3},{2,0},{3,1},{4,6},{5,7},{6,4},{7,5},{8,10},{9,11},{10,... | collective-permute-start | bytes 3145736 | tf_op jit(solution)/shard_map/ppermute | solution.py:27
  867.3 62.1 %collective-permute-start.41 = (bf16[512,2048]{1,0:T(8,128)(2,1)}, bf16[512,2048]{1,0:T(8,128)(2,1)}, u32[]{:S(2)}, u32[]{:S(2)}) collective-permute-start(bf16[512,2048]{1,0:T(8,128)(2,1)} %maximum_select_fusion.11), channel_id=1, source_target_pairs={{0,1},{1,0},{2,3},{3,2},{4,5},{5,4},{6,7},{7,6},{8,9},{9,8},{10,11... | collective-permute-start | bytes 6291464 | tf_op jit(solution)/shard_map/ppermute | solution.py:27
  890.2 23.2 %collective-permute-start.10 = (bf16[512,1024]{1,0:T(8,128)(2,1)S(1)}, bf16[512,1024]{1,0:T(8,128)(2,1)S(1)}, u32[]{:S(2)}, u32[]{:S(2)}) collective-permute-start(bf16[512,1024]{1,0:T(8,128)(2,1)S(1)} %maximum_select_fusion.12), channel_id=1, source_target_pairs={{0,4},{1,5},{2,6},{3,7},{4,0},{5,1},{6,2},{7,3},{8,12},{9,13},{10,... | collective-permute-start | bytes 3145736 | tf_op jit(solution)/shard_map/ppermute | solution.py:27
  891.0 28.3 %collective-permute-start.16 = (bf16[512,1024]{1,0:T(8,128)(2,1)S(1)}, bf16[512,1024]{1,0:T(8,128)(2,1)}, u32[]{:S(2)}, u32[]{:S(2)}) collective-permute-start(bf16[512,1024]{1,0:T(8,128)(2,1)S(1)} %maximum_select_fusion.13), channel_id=1, source_target_pairs={{0,2},{1,3},{2,0},{3,1},{4,6},{5,7},{6,4},{7,5},{8,10},{9,11},{10,... | collective-permute-start | bytes 3145736 | tf_op jit(solution)/shard_map/ppermute | solution.py:27
  894.0 53.3 %collective-permute-start.23 = (bf16[1024,1024]{1,0:T(8,128)(2,1)}, bf16[1024,1024]{1,0:T(8,128)(2,1)}, u32[]{:S(2)}, u32[]{:S(2)}) collective-permute-start(bf16[1024,1024]{1,0:T(8,128)(2,1)} %maximum_select_fusion.8), channel_id=1, source_target_pairs={{0,1},{1,0},{2,3},{3,2},{4,5},{5,4},{6,7},{7,6},{8,9},{9,8},{10,11... | collective-permute-start | bytes 6291464 | tf_op jit(solution)/shard_map/ppermute | solution.py:27
  914.4 39.1 %collective-permute-start.29 = (bf16[512,2048]{1,0:T(8,128)(2,1)}, bf16[512,2048]{1,0:T(8,128)(2,1)}, u32[]{:S(2)}, u32[]{:S(2)}) collective-permute-start(bf16[512,2048]{1,0:T(8,128)(2,1)} %maximum_select_fusion.9), channel_id=1, source_target_pairs={{0,1},{1,0},{2,3},{3,2},{4,5},{5,4},{6,7},{7,6},{8,9},{9,8},{10,11... | collective-permute-start | bytes 6291464 | tf_op jit(solution)/shard_map/ppermute | solution.py:27
  919.3 41.1 %collective-permute-start.11 = (bf16[1024,1024]{1,0:T(8,128)(2,1)}, bf16[1024,1024]{1,0:T(8,128)(2,1)}, u32[]{:S(2)}, u32[]{:S(2)}) collective-permute-start(bf16[1024,1024]{1,0:T(8,128)(2,1)} %maximum_select_fusion.6), channel_id=1, source_target_pairs={{0,1},{1,0},{2,3},{3,2},{4,5},{5,4},{6,7},{7,6},{8,9},{9,8},{10,11... | collective-permute-start | bytes 6291464 | tf_op jit(solution)/shard_map/ppermute | solution.py:27
  923.6 41.0 %collective-permute-start.17 = (bf16[1024,1024]{1,0:T(8,128)(2,1)}, bf16[1024,1024]{1,0:T(8,128)(2,1)}, u32[]{:S(2)}, u32[]{:S(2)}) collective-permute-start(bf16[1024,1024]{1,0:T(8,128)(2,1)} %maximum_select_fusion.7), channel_id=1, source_target_pairs={{0,1},{1,0},{2,3},{3,2},{4,5},{5,4},{6,7},{7,6},{8,9},{9,8},{10,11... | collective-permute-start | bytes 6291464 | tf_op jit(solution)/shard_map/ppermute | solution.py:27
  (101 other events, 1552.0 us)
Sparse Core Ops, SparseCore 0:
  9.6 83.8 all-gather.4
  178.3 84.0 reduce-scatter.4
  265.0 81.2 all-gather.6
  347.8 79.2 all-gather.8
  453.7 75.8 reduce-scatter.6
  533.4 81.2 all-gather.10
  662.5 82.4 reduce-scatter.8
  759.5 81.3 reduce-scatter.10

commit v2 on v1

v2 whole, which is shorter than its diff:
```python
from functools import partial

import jax
import jax.numpy as jnp
from jax import lax
from jax.experimental import pallas as pl
from jax.experimental.pallas import tpu as pltpu
from jax.sharding import PartitionSpec as P

KD = 256
VD = 512
EPSILON = 1e-05
BF = jnp.bfloat16
F32 = jnp.float32


def after(value, *others):
    return lax.optimization_barrier((value, *others))[0]


def shifted(value, by):
    length = lax.axis_size("tok")
    pairs = [(i, i + by) for i in range(length) if 0 <= i + by < length]
    return lax.ppermute(value, "tok", pairs)


def swapped(value, axis, mask):
    return lax.ppermute(value, axis, [(i, i ^ mask) for i in range(lax.axis_size(axis))])


def my_bit(axis, bit):
    return (lax.axis_index(axis) >> bit) & 1


def joined(value, other, first, axis):
    return jnp.where(
        first,
        jnp.concatenate([value, other], axis=axis),
        jnp.concatenate([other, value], axis=axis),
    )


def bit_orders():
    bits = lax.axis_size("tok").bit_length() - 1
    first = list(range(bits))
    second = [0, 2, 1] if bits == 3 else first[bits // 2 :] + first[: bits // 2]
    return first, second


def halves(value, axis, bit, dim):
    shape = value.shape
    pieces = value.reshape(*shape[:dim], 2, shape[dim] // 2, *shape[dim + 1 :])
    mine = my_bit(axis, bit)
    keep = lax.dynamic_index_in_dim(pieces, mine, dim, keepdims=False)
    give = lax.dynamic_index_in_dim(pieces, 1 - mine, dim, keepdims=False)
    return keep, give


def own_piece(value, order, dim=0):
    for bit in order:
        value = halves(value, "tok", bit, dim)[0]
    return value


def scatter_sum(value, order, dim=0, waits=()):
    values = []
    for place, bit in enumerate(order):
        keep, give = halves(value, "tok", bit, dim)
        if place == 1 and waits:
            give = after(give, *waits)
        value = keep.astype(F32) + swapped(give.astype(BF), "tok", 1 << bit).astype(F32)
        values.append(value)
    return values


def gather_back(value, order, dim=0):
    for bit in order[::-1]:
        other = swapped(value, "tok", 1 << bit)
        value = joined(value, other, my_bit("tok", bit) == 0, dim)
    return value


def in_order(pieces, order):
    bits, shape = len(order), pieces.shape
    pieces = pieces.reshape(*[2] * bits, *shape[1:])
    pieces = pieces.transpose(*[bits - 1 - bit for bit in order], bits, bits + 1)
    return pieces.reshape(shape[0] * shape[1], shape[2]).astype(F32)


def far_swap(first, second):
    rows = first.shape[0]
    both = jnp.concatenate([first, second.reshape(-1, first.shape[1])], axis=0)
    both = swapped(both, "head", lax.axis_size("head") // 2)
    return both[:rows], both[rows:].reshape(second.shape)


def side_bits():
    return range(lax.axis_size("head").bit_length() - 2)


def gather_side(value):
    for bit in side_bits():
        other = swapped(value, "head", 1 << bit)
        value = joined(value, other, my_bit("head", bit) == 0, 1)
    return value


def scatter_side(value):
    for bit in list(side_bits())[::-1]:
        keep, give = halves(value, "head", bit, 1)
        value = keep.astype(F32) + swapped(give.astype(BF), "head", 1 << bit).astype(F32)
    return value[:, 0]


def sum_side(value):
    for bit in side_bits():
        value = value + swapped(value, "head", 1 << bit)
    return value


TILE = 256
EXTRA = 16
CHUNK = 512
VMEM_LIMIT = 58 << 20


def dot(left, right):
    return jnp.dot(left, right, preferred_element_type=F32)


def dot_nt(left, right):
    return lax.dot_general(left, right, (((1,), (1,)), ((), ())), preferred_element_type=F32)


def dot_tn(left, right):
    return lax.dot_general(left, right, (((0,), (0,)), ((), ())), preferred_element_type=F32)


def tiles(columns):
    return pl.BlockSpec((TILE, columns), lambda i: (i, 0))


def whole(*shape):
    zeros = (0,) * len(shape)
    return pl.BlockSpec(shape, lambda i: zeros, pipeline_mode=pl.Buffered(1))


def held(*shape):
    zeros = (0,) * len(shape)
    return pl.BlockSpec(shape, lambda i: zeros)


SCALARS = pl.BlockSpec(memory_space=pltpu.SMEM)


def call(kernel, rows, in_specs, outs, out_specs, scratch=()):
    return pl.pallas_call(
        kernel,
        grid=(rows // TILE,),
        in_specs=in_specs,
        out_specs=out_specs,
        out_shape=[jax.ShapeDtypeStruct(shape, dtype) for shape, dtype in outs],
        scratch_shapes=list(scratch),
        cost_estimate=pl.CostEstimate(flops=0, bytes_accessed=0, transcendentals=0),
        compiler_params=pltpu.CompilerParams(vmem_limit_bytes=VMEM_LIMIT),
    )


def turned(value, cosine, sine):
    half_dim = KD // 2
    front, back = value[:, :half_dim], value[:, half_dim:]
    return jnp.concatenate([front * cosine - back * sine, back * cosine + front * sine], axis=1)


def tile_decay(log_decay, behind, docs_col, docs_row, pads_row):
    rows = lax.broadcasted_iota(jnp.int32, (TILE, 1), 0)
    cols = lax.broadcasted_iota(jnp.int32, (1, TILE), 1)
    allowed = (docs_col == docs_row) & (rows + behind >= cols) & (pads_row > 0)
    rise = jnp.exp(rows.astype(F32) * log_decay)
    fall = jnp.exp((behind - cols).astype(F32) * log_decay)
    return jnp.where(allowed, rise * fall, 0.0)


def send_state(docs, acc, sum_out):
    sum_out[:, :KD, :] = acc[...].astype(BF)
    sum_out[:, KD:, :] = jnp.full((acc.shape[0], EXTRA, VD), docs[0].astype(F32), F32).astype(BF)


def lanes(shards):
    return jnp.concatenate([shards[i] for i in range(shards.shape[0])], axis=1)


def vector_of(rows, index):
    return rows[3 * index : 3 * index + 1] + rows[3 * index + 1 : 3 * index + 2] + rows[
        3 * index + 2 : 3 * index + 3
    ]


def entry_kernel(x, one, two, three, four, out):
    rows = x.shape[0]
    out[:rows] = x[...]
    pieces = []
    for vector in (one, two, three, four):
        value = vector[...]
        for _ in range(3):
            piece = value.astype(BF)
            pieces.append(piece.astype(F32))
            value = value - piece.astype(F32)
    pieces.append(jnp.zeros((EXTRA - len(pieces), x.shape[1]), F32))
    out[rows:] = jnp.concatenate(pieces, axis=0).astype(BF)


def project_kernel(
    heads, docs, x, vec, wq, wk, wv, cos, sin, end, ln_out, q_out, k_out, v_out, stat_out,
    sum_out, acc
):
    step = pl.program_id(0)
    rows = lanes(x).astype(F32)
    vectors = lanes(vec).astype(F32)
    mean = jnp.mean(rows, axis=1, keepdims=True)
    scale = lax.rsqrt(jnp.mean(rows * rows, axis=1, keepdims=True) - mean * mean + EPSILON)
    low = ((rows - mean) * scale * vector_of(vectors, 0) + vector_of(vectors, 1)).astype(BF)
    ln_out[...] = low
    stat_out[...] = jnp.concatenate([mean, scale], axis=1)
    values = dot(low, wv[...]).astype(BF)
    v_out[...] = values
    queries = dot(low, wq[...])
    keys = dot(low, wk[...])
    cosine, sine = cos[...], sin[...]

    @pl.when(step == 0)
    def _():
        acc[...] = jnp.zeros_like(acc)

    for h in range(heads):
        mine = slice(h * KD, (h + 1) * KD)
        q_out[:, mine] = turned(queries[:, mine], cosine, sine).astype(BF)
        key = (turned(keys[:, mine], cosine, sine) * KD ** (-0.5)).astype(BF)
        k_out[:, mine] = key
        key_end = (key.astype(F32) * end[:, h : h + 1]).astype(BF)
        acc[h] += dot_tn(key_end, values[:, h * VD : (h + 1) * VD])

    @pl.when(step == pl.num_programs(0) - 1)
    def _():
        send_state(docs, acc, sum_out)


def inner_kernel(heads, decay, low, wg, q, k, v, dcol, drow, prow, gate_out, inner_out):
    step = pl.program_id(0)
    gate_out[...] = dot(low[...], wg[...])
    docs_col = dcol[...]

    def turn(j, totals):
        at = pl.ds(pl.multiple_of(j * TILE, TILE), TILE)
        sums = []
        for h in range(heads):
            mine = slice(h * KD, (h + 1) * KD)
            wide = slice(h * VD, (h + 1) * VD)
            factor = tile_decay(decay[h], (step - j) * TILE, docs_col, drow[:, at], prow[:, at])
            weights = (dot_nt(q[:, mine], k[at, mine]) * factor).astype(BF)
            sums.append(totals[h] + dot(weights, v[at, wide]))
        return tuple(sums)

    zeros = tuple(jnp.zeros((TILE, VD), F32) for _ in range(heads))
    totals = lax.fori_loop(0, step + 1, turn, zeros)
    for h in range(heads):
        inner_out[:, h * VD : (h + 1) * VD] = totals[h]


def joined_state(decay, rows, one, two, three, link_two, link_three):
    states = []
    for h in range(one.shape[0]):
        far = jnp.exp(jnp.full((1, 1), rows, F32) * decay[h])
        states.append(
            (
                one[h, :KD].astype(F32)
                + two[h, :KD].astype(F32) * (link_two * far)
                + three[h, :KD].astype(F32) * (link_three * far * far)
            ).astype(BF)
        )
    return states


def doc_in(payload):
    return payload[0, KD : KD + 1, 0:1].astype(F32)


def mix_kernel(
    heads, rows, decay, inner, q, one, two, three, gate, dcol, pcol, wo, group_out, scale_out,
    gated_out, part_out, state_out, carry_out
):
    step = pl.program_id(0)
    before = doc_in(one)

    @pl.when(step == 0)
    def _():
        link_two = (doc_in(two) == before).astype(F32)
        link_three = (doc_in(three) == before).astype(F32)
        states = joined_state(decay, rows, one, two, three, link_two, link_three)
        for h in range(heads):
            state_out[h] = states[h]

    same = (dcol[...].astype(F32) == before).astype(F32)
    place = (step * TILE + 1 + lax.broadcasted_iota(jnp.int32, (TILE, 1), 0)).astype(F32)
    for h in range(heads):
        mine = slice(h * KD, (h + 1) * KD)
        wide = slice(h * VD, (h + 1) * VD)
        carry = same * jnp.exp(place * decay[h])
        carry_out[:, h : h + 1] = carry
        carried = (q[:, mine].astype(F32) * carry).astype(BF)
        mixed = inner[:, wide] + dot(carried, state_out[h])
        mean = jnp.mean(mixed, axis=1, keepdims=True)
        scale = lax.rsqrt(jnp.mean(mixed * mixed, axis=1, keepdims=True) - mean * mean + 1.0)
        grouped = (mixed - mean) * scale
        group_out[:, wide] = grouped
        scale_out[:, h : h + 1] = scale
        gate_h = gate[:, wide]
        gated_out[:, wide] = (pcol[...] * gate_h * jax.nn.sigmoid(gate_h) * grouped).astype(BF)
    part = dot(gated_out[...], wo[...]).astype(BF)
    sides, width = part_out.shape[1], part_out.shape[4]
    for side in range(sides):
        for f in range(2):
            first = (f * sides + side) * width
            part_out[0, side, f] = part[:, first : first + width]


def gate_kernel(heads, grad, wo, gate, group, scale, pcol, dgate_out, mix_out):
    sides = grad.shape[1]
    rows = jnp.concatenate(
        [grad[0, side, f] for f in range(2) for side in range(sides)], axis=1
    )
    passed = dot_nt(rows, wo[...]) * pcol[...]
    for h in range(heads):
        wide = slice(h * VD, (h + 1) * VD)
        gate_h, grouped = gate[:, wide], group[:, wide]
        squash = jax.nn.sigmoid(gate_h)
        upstream = passed[:, wide]
        dgate_out[:, wide] = (
            upstream * grouped * (squash + gate_h * squash * (1.0 - squash))
        ).astype(BF)
        grad_group = upstream * gate_h * squash
        mean = jnp.mean(grad_group, axis=1, keepdims=True)
        cross = jnp.mean(grad_group * grouped, axis=1, keepdims=True)
        mix_out[:, wide] = (scale[:, h : h + 1] * (grad_group - mean - grouped * cross)).astype(BF)


def outer_kernel(gated, grad, out):
    rows = jnp.concatenate([grad[0, 0, 0], grad[1, 0, 0]], axis=0)
    out[...] = dot_tn(gated[...], rows).astype(BF)


def back_kernel(
    heads, docs, decay, mix, q, k, v, carry, state, dcol, drow, prow, cos, sin, dq_out, dk_out,
    dv_out, sum_out, acc
):
    step = pl.program_id(0)

    @pl.when(step == 0)
    def _():
        acc[...] = jnp.zeros_like(acc)
        dk_out[...] = jnp.zeros_like(dk_out)
        dv_out[...] = jnp.zeros_like(dv_out)

    docs_col = dcol[...]

    def turn(j, totals):
        at = pl.ds(pl.multiple_of(j * TILE, TILE), TILE)
        sums = []
        for h in range(heads):
            mine = slice(h * KD, (h + 1) * KD)
            wide = slice(h * VD, (h + 1) * VD)
            query, grad_mixed, key = q[:, mine], mix[:, wide], k[at, mine]
            factor = tile_decay(decay[h], (step - j) * TILE, docs_col, drow[:, at], prow[:, at])
            weights = (dot_nt(query, key) * factor).astype(BF)
            grads = (dot_nt(grad_mixed, v[at, wide]) * factor).astype(BF)
            dk_out[at, mine] += dot_tn(grads, query)
            dv_out[at, wide] += dot_tn(weights, grad_mixed)
            sums.append(totals[h] + dot(grads, key))
        return tuple(sums)

    zeros = tuple(jnp.zeros((TILE, KD), F32) for _ in range(heads))
    totals = lax.fori_loop(0, step + 1, turn, zeros)
    for h in range(heads):
        mine = slice(h * KD, (h + 1) * KD)
        wide = slice(h * VD, (h + 1) * VD)
        lift = carry[:, h : h + 1]
        total = totals[h] + lift * dot_nt(mix[:, wide], state[h])
        dq_out[:, mine] = turned(total, cos[...], -sin[...]).astype(BF)
        acc[h] += dot_tn((q[:, mine].astype(F32) * lift).astype(BF), mix[:, wide])

    @pl.when(step == pl.num_programs(0) - 1)
    def _():
        send_state(docs, acc, sum_out)


def finish_kernel(
    heads, size, docs, decay, dk_in, dv_in, k, v, end, one, two, three, dq, dgate, wq, wk, wv, wg,
    cos, sin, x, stat, vec, dk_out, dv_out, part_out, rows_out, cols_out, state
):
    step = pl.program_id(0)

    @pl.when(step == 0)
    def _():
        last = docs[0].astype(F32)
        link_two = (doc_in(one) == last).astype(F32)
        link_three = (doc_in(two) == last).astype(F32)
        states = joined_state(decay, size, one, two, three, link_two, link_three)
        for h in range(heads):
            state[h] = states[h]

    cosine, sine = cos[...], -sin[...]
    for h in range(heads):
        mine = slice(h * KD, (h + 1) * KD)
        wide = slice(h * VD, (h + 1) * VD)
        lift = end[:, h : h + 1]
        grad_key = dk_in[:, mine] + lift * dot_nt(v[:, wide], state[h])
        dk_out[:, mine] = (turned(grad_key, cosine, sine) * KD ** (-0.5)).astype(BF)
        key_end = (k[:, mine].astype(F32) * lift).astype(BF)
        dv_out[:, wide] = (dv_in[:, wide] + dot(key_end, state[h])).astype(BF)
    part = (
        dot_nt(dq[...], wq[...])
        + dot_nt(dk_out[...], wk[...])
        + dot_nt(dv_out[...], wv[...])
        + dot_nt(dgate[...], wg[...])
    )
    count, width = part_out.shape[0], part_out.shape[2]
    for shard in range(count):
        part_out[shard] = part[:, shard * width : (shard + 1) * width].astype(BF)
    normed = (lanes(x).astype(F32) - stat[:, 0:1]) * stat[:, 1:2]
    scaled = part * vec[0:1, :]
    ones = jnp.ones((8, scaled.shape[1]), BF)
    rows_out[0, 0:8] = dot_nt(ones, scaled.astype(BF))
    rows_out[0, 8:16] = dot_nt(ones, (scaled * normed).astype(BF))
    sums = jnp.concatenate(
        [jnp.sum(part * normed, axis=0, keepdims=True), jnp.sum(part, axis=0, keepdims=True)],
        axis=0,
    )

    @pl.when(step == 0)
    def _():
        cols_out[...] = jnp.zeros_like(cols_out)

    cols_out[...] += sums


def feed_kernel(
    chunks, x, grads, vec, up_near, up_far, down_near, down_far, ln_out, grad_out, act_out,
    dup_out, part_out, stat_out, rows_out, cols_out, acc
):
    step = pl.program_id(0)
    count = x.shape[1]
    steps = count // TILE

    def at_rows(r):
        return pl.ds(pl.multiple_of(r * TILE, TILE), TILE)

    @pl.when(step == 0)
    def _():
        def start(r, carry):
            at = at_rows(r)
            rows = jnp.concatenate([x[i, at, :] for i in range(x.shape[0])], axis=1).astype(F32)
            mean = jnp.mean(rows, axis=1, keepdims=True)
            scale = lax.rsqrt(jnp.mean(rows * rows, axis=1, keepdims=True) - mean * mean + EPSILON)
            stat_out[at, :] = jnp.concatenate([mean, scale], axis=1)
            ln_out[at, :] = ((rows - mean) * scale * vec[2:3, :] + vec[3:4, :]).astype(BF)
            grad_out[at, :] = jnp.concatenate(
                [grads[i, at, :] for i in range(grads.shape[0])], axis=1
            )
            acc[at, :] = jnp.zeros((TILE, acc.shape[1]), F32)
            return carry

        lax.fori_loop(0, steps, start, 0)

    def units(up, down):
        def turn(r, carry):
            at = at_rows(r)
            lifted = dot(ln_out[at, :], up[...])
            share = 0.5 * (1.0 + lax.erf(lifted * 0.5**0.5))
            act_out[at, :] = (lifted * share).astype(BF)
            slope = share + lifted * jnp.exp(-0.5 * lifted * lifted) * 0.3989422804014327
            lowered = (slope * dot_nt(grad_out[at, :], down[...])).astype(BF)
            dup_out[at, :] = lowered
            acc[at, :] += dot_nt(lowered, up[...])
            return carry

        lax.fori_loop(0, steps, turn, 0)

    @pl.when(step < chunks)
    def _():
        units(up_near, down_near)

    @pl.when(step >= chunks)
    def _():
        units(up_far, down_far)

    @pl.when(step == pl.num_programs(0) - 1)
    def _():
        cols_out[...] = jnp.zeros_like(cols_out)
        sides, width = part_out.shape[1], part_out.shape[3]

        def finish(r, carry):
            at = at_rows(r)
            part = acc[at, :]
            for f in range(2):
                for side in range(sides):
                    first = (f * sides + side) * width
                    part_out[f, side, at, :] = part[:, first : first + width].astype(BF)
            rows = jnp.concatenate([x[i, at, :] for i in range(x.shape[0])], axis=1).astype(F32)
            normed = (rows - stat_out[at, 0:1]) * stat_out[at, 1:2]
            scaled = part * vec[2:3, :]
            rows_out[at, :] = jnp.concatenate(
                [
                    jnp.sum(scaled, axis=1, keepdims=True),
                    jnp.sum(scaled * normed, axis=1, keepdims=True),
                ],
                axis=1,
            )
            cols_out[...] += jnp.concatenate(
                [
                    jnp.sum(part * normed, axis=0, keepdims=True),
                    jnp.sum(part, axis=0, keepdims=True),
                ],
                axis=0,
            )
            return carry

        lax.fori_loop(0, steps, finish, 0)


def lower_kernel(act, down_near, down_far, out):
    units = down_near.shape[0]
    part = (dot(act[:, :units], down_near[...]) + dot(act[:, units:], down_far[...])).astype(BF)
    sides, width = out.shape[1], out.shape[3]
    for f in range(2):
        for side in range(sides):
            first = (f * sides + side) * width
            out[f, side] = part[:, first : first + width]


def weight_kernel(left, *rights):
    out = rights[-1]
    first = 0
    for right in rights[:-1]:
        width = right.shape[1]
        out[:, first : first + width] = dot_tn(left[...], right[...]).astype(BF)
        first += width


def weight_grad(left, *rights):
    rows, columns = left.shape
    width = sum(right.shape[1] for right in rights)
    return pl.pallas_call(
        weight_kernel,
        grid=(columns // CHUNK,),
        in_specs=[pl.BlockSpec((rows, CHUNK), lambda i: (0, i))]
        + [whole(*right.shape) for right in rights],
        out_specs=pl.BlockSpec((CHUNK, width), lambda i: (i, 0)),
        out_shape=jax.ShapeDtypeStruct((columns, width), BF),
        cost_estimate=pl.CostEstimate(flops=0, bytes_accessed=0, transcendentals=0),
        compiler_params=pltpu.CompilerParams(vmem_limit_bytes=VMEM_LIMIT),
    )(left, *rights)


def body(
    tokens,
    mix_gain,
    mix_bias,
    query_weight,
    key_weight,
    value_weight,
    gate_weight,
    output_weight,
    feed_gain,
    feed_bias,
    up_weight,
    down_weight,
    doc_ids,
    pad_mask,
    out_grad,
):
    row_count, width = tokens.shape
    heads_here = query_weight.shape[1] // KD
    shards = lax.axis_size("head")
    full_width = width * shards
    sides = shards // 2
    spread = lax.axis_index("head") // sides
    side = lax.axis_index("head") % sides
    half_rows = row_count // 2
    block = lax.axis_index("tok")

    packed = pl.pallas_call(
        entry_kernel,
        out_shape=jax.ShapeDtypeStruct((row_count + EXTRA, width), BF),
        compiler_params=pltpu.CompilerParams(vmem_limit_bytes=VMEM_LIMIT),
    )(tokens, mix_gain[None], mix_bias[None], feed_gain[None], feed_bias[None])
    rows_raw = lax.all_gather(packed, "head", axis=0)
    vector_rows = rows_raw[:, row_count:, :].astype(F32)
    vectors = (vector_rows[:, 0:12:3] + vector_rows[:, 1:12:3] + vector_rows[:, 2:12:3]).transpose(
        1, 0, 2
    )
    side_vectors = lax.dynamic_index_in_dim(
        vectors.reshape(4, 2, sides, width), side, 2, keepdims=False
    )
    vectors = vectors.reshape(4, full_width)

    order_one, order_two = bit_orders()
    up_piece, down_piece = own_piece(up_weight, order_one), own_piece(down_weight, order_two)
    late_up, late_down, late_grad, _ = lax.optimization_barrier(
        (up_piece, down_piece, out_grad, rows_raw)
    )
    up_seen, down_seen = far_swap(late_up, late_down)
    grad_keep, grad_give = halves(late_grad, "head", shards.bit_length() - 2, 0)
    side_grads = joined(
        grad_keep[None], swapped(grad_give, "head", sides)[None], spread == 0, 0
    )
    grad_rows = gather_side(side_grads[:, None]).reshape(shards, half_rows, width)
    up_other = gather_back(up_seen, order_one)
    down_other = gather_back(down_seen, order_two)

    first_head = lax.axis_index("head") * heads_here
    log_decay = jnp.log(
        1.0 - 2.0 ** (-5.0 - (first_head + jnp.arange(heads_here, dtype=jnp.int32)).astype(F32))
    )
    position = jnp.arange(row_count, dtype=jnp.int32)
    frequency = 10000.0 ** (-2.0 * jnp.arange(KD // 2, dtype=jnp.int32).astype(F32) / KD)
    angles = (block * row_count + position).astype(F32)[:, None] * frequency[None, :]
    cosine, sine = jnp.cos(angles), jnp.sin(angles)
    padding = pad_mask.astype(F32)
    last_doc = doc_ids[row_count - 1]

    end_factor = (padding * (doc_ids == last_doc).astype(F32))[:, None] * jnp.exp(
        (row_count - 1 - position).astype(F32)[:, None] * log_decay[None, :]
    )

    docs_col, docs_row = doc_ids[:, None], doc_ids[None, :]
    pads_col, pads_row = padding[:, None], padding[None, :]
    inner_width, value_width = heads_here * KD, heads_here * VD
    states = pltpu.VMEM((heads_here, KD, VD), F32)
    state_shape = (heads_here, KD, VD)
    sent_shape = (heads_here, KD + EXTRA, VD)
    shard_tiles = pl.BlockSpec((shards, TILE, width), lambda i: (0, i, 0))
    per_half = half_rows // TILE
    split_tiles = pl.BlockSpec(
        (1, sides, 2, TILE, width), lambda i: (i // per_half, 0, 0, i % per_half, 0)
    )
    last_docs = doc_ids[row_count - 1 :]
    rows_first, query_rot, key_rot, values, stats, summary = call(
        partial(project_kernel, heads_here),
        row_count,
        [
            SCALARS,
            shard_tiles,
            pl.BlockSpec((shards, EXTRA, width), lambda i: (0, row_count // EXTRA, 0)),
            whole(full_width, inner_width),
            whole(full_width, inner_width),
            whole(full_width, value_width),
            tiles(KD // 2),
            tiles(KD // 2),
            tiles(heads_here),
        ],
        [
            ((row_count, full_width), BF),
            ((row_count, inner_width), BF),
            ((row_count, inner_width), BF),
            ((row_count, value_width), BF),
            ((row_count, 2), F32),
            (sent_shape, BF),
        ],
        [
            tiles(full_width),
            tiles(inner_width),
            tiles(inner_width),
            tiles(value_width),
            tiles(2),
            held(*sent_shape),
        ],
        [states],
    )(
        last_docs,
        rows_raw,
        rows_raw,
        query_weight,
        key_weight,
        value_weight,
        cosine,
        sine,
        end_factor,
    )
    one_back, two_back, three_back = (shifted(summary, by) for by in (1, 2, 3))
    gate_pre, inner_part = call(
        partial(inner_kernel, heads_here),
        row_count,
        [
            SCALARS,
            tiles(full_width),
            whole(full_width, value_width),
            tiles(inner_width),
            whole(row_count, inner_width),
            whole(row_count, value_width),
            tiles(1),
            whole(1, row_count),
            whole(1, row_count),
        ],
        [((row_count, value_width), F32)] * 2,
        [tiles(value_width)] * 2,
    )(
        log_decay,
        rows_first,
        gate_weight,
        query_rot,
        key_rot,
        values,
        docs_col,
        docs_row,
        pads_row,
    )
    flat_group, group_scale, gated, mix_part, state_low, carry_factor = call(
        partial(mix_kernel, heads_here, row_count),
        row_count,
        [
            SCALARS,
            tiles(value_width),
            tiles(inner_width),
            whole(*sent_shape),
            whole(*sent_shape),
            whole(*sent_shape),
            tiles(value_width),
            tiles(1),
            tiles(1),
            whole(value_width, full_width),
        ],
        [
            ((row_count, value_width), F32),
            ((row_count, heads_here), F32),
            ((row_count, value_width), BF),
            ((2, sides, 2, half_rows, width), BF),
            (state_shape, BF),
            ((row_count, heads_here), F32),
        ],
        [
            tiles(value_width),
            tiles(heads_here),
            tiles(value_width),
            split_tiles,
            held(*state_shape),
            tiles(heads_here),
        ],
    )(
        after(log_decay, side_grads),
        inner_part,
        query_rot,
        one_back,
        two_back,
        three_back,
        gate_pre,
        docs_col,
        pads_col,
        output_weight,
    )
    mix_part = after(mix_part, up_seen, down_seen)
    side_tokens = lax.dynamic_index_in_dim(
        lax.dynamic_slice_in_dim(rows_raw, spread * half_rows, half_rows, axis=1).reshape(
            2, sides, half_rows, width
        ),
        side,
        1,
        keepdims=False,
    )
    mixed_sum = lax.psum_scatter(
        mix_part.reshape(shards, 2, half_rows, width), "head", scatter_dimension=0
    )
    hidden = side_tokens.astype(F32) + mixed_sum.astype(F32)
    hidden_rows = gather_side(hidden.astype(BF)[:, None]).reshape(shards, half_rows, width)
    units = up_weight.shape[1]
    chunks = units // CHUNK
    rows_second, grad_plain, act_low, grad_up, feed_part, stats_second, row_second, cols_second = (
        pl.pallas_call(
            partial(feed_kernel, chunks),
            grid=(2 * chunks,),
            in_specs=[
                whole(shards, half_rows, width),
                whole(shards, half_rows, width),
                whole(4, full_width),
                pl.BlockSpec((full_width, CHUNK), lambda i: (0, jnp.minimum(i, chunks - 1))),
                pl.BlockSpec((full_width, CHUNK), lambda i: (0, jnp.maximum(i - chunks, 0))),
                pl.BlockSpec((CHUNK, full_width), lambda i: (jnp.minimum(i, chunks - 1), 0)),
                pl.BlockSpec((CHUNK, full_width), lambda i: (jnp.maximum(i - chunks, 0), 0)),
            ],
            out_specs=[
                held(half_rows, full_width),
                held(half_rows, full_width),
                pl.BlockSpec((half_rows, CHUNK), lambda i: (0, i)),
                pl.BlockSpec((half_rows, CHUNK), lambda i: (0, i)),
                held(2, sides, half_rows, width),
                held(half_rows, 2),
                held(half_rows, 2),
                held(2, full_width),
            ],
            out_shape=[
                jax.ShapeDtypeStruct((half_rows, full_width), BF),
                jax.ShapeDtypeStruct((half_rows, full_width), BF),
                jax.ShapeDtypeStruct((half_rows, 2 * units), BF),
                jax.ShapeDtypeStruct((half_rows, 2 * units), BF),
                jax.ShapeDtypeStruct((2, sides, half_rows, width), BF),
                jax.ShapeDtypeStruct((half_rows, 2), F32),
                jax.ShapeDtypeStruct((half_rows, 2), F32),
                jax.ShapeDtypeStruct((2, full_width), F32),
            ],
            scratch_shapes=[pltpu.VMEM((half_rows, full_width), F32)],
            cost_estimate=pl.CostEstimate(flops=0, bytes_accessed=0, transcendentals=0),
            compiler_params=pltpu.CompilerParams(vmem_limit_bytes=VMEM_LIMIT),
        )(hidden_rows, grad_rows, vectors, up_weight, up_other, down_weight, down_other)
    )
    grad_ln2 = scatter_side(feed_part)
    row_second = sum_side(row_second) / full_width
    norm_second = (hidden - stats_second[None, :, 0:1]) * stats_second[None, :, 1:2]
    grad_hidden = side_grads.astype(F32) + stats_second[None, :, 1:2] * (
        grad_ln2 * side_vectors[2][:, None, :]
        - row_second[None, :, 0:1]
        - norm_second * row_second[None, :, 1:2]
    )
    grad_branch = lax.all_gather(grad_hidden.astype(BF), "head", axis=0).reshape(
        2, sides, 2, half_rows, width
    )

    down_part = pl.pallas_call(
        lower_kernel,
        grid=(half_rows // TILE,),
        in_specs=[tiles(2 * units), whole(units, full_width), whole(units, full_width)],
        out_specs=pl.BlockSpec((2, sides, TILE, width), lambda i: (0, 0, i, 0)),
        out_shape=jax.ShapeDtypeStruct((2, sides, half_rows, width), BF),
        cost_estimate=pl.CostEstimate(flops=0, bytes_accessed=0, transcendentals=0),
        compiler_params=pltpu.CompilerParams(vmem_limit_bytes=VMEM_LIMIT),
    )(act_low, down_weight, down_other)

    branch = grad_hidden.astype(BF)
    grad_down = weight_grad(after(act_low, branch), grad_plain)
    grad_down = grad_down.reshape(2, units, full_width)
    grad_upw = weight_grad(rows_second, after(grad_up, branch))
    down_sum = scatter_sum(grad_down, order_one, 1)
    up_sum = scatter_sum(grad_upw, order_two)

    grad_outw = pl.pallas_call(
        outer_kernel,
        grid=(shards,),
        in_specs=[
            whole(row_count, value_width),
            pl.BlockSpec((2, 1, 1, half_rows, width), lambda i: (0, i % sides, i // sides, 0, 0)),
        ],
        out_specs=pl.BlockSpec((value_width, width), lambda i: (0, i)),
        out_shape=jax.ShapeDtypeStruct((value_width, full_width), BF),
        cost_estimate=pl.CostEstimate(flops=0, bytes_accessed=0, transcendentals=0),
        compiler_params=pltpu.CompilerParams(vmem_limit_bytes=VMEM_LIMIT),
    )(after(gated, down_sum[1], up_sum[1]), grad_branch)
    outw_sum = scatter_sum(grad_outw, order_one)
    dgate, grad_mixed = call(
        partial(gate_kernel, heads_here),
        row_count,
        [
            split_tiles,
            whole(value_width, full_width),
            tiles(value_width),
            tiles(value_width),
            tiles(heads_here),
            tiles(1),
        ],
        [((row_count, value_width), BF), ((row_count, value_width), BF)],
        [tiles(value_width), tiles(value_width)],
    )(
        grad_branch,
        output_weight,
        gate_pre,
        flat_group,
        group_scale,
        after(pads_col, grad_outw),
    )
    up_last, down_last = up_sum[-1], down_sum[-1]
    up_far, down_far = far_swap(up_last[:, units:].astype(BF), down_last[1].astype(BF))
    down_near = down_last[0] + down_far.astype(F32)
    up_near = up_last[:, :units] + up_far.astype(F32)
    grad_gw = weight_grad(rows_first, dgate)
    dq, dk_part, dv_part, grad_state = call(
        partial(back_kernel, heads_here),
        row_count,
        [
            SCALARS,
            SCALARS,
            tiles(value_width),
            tiles(inner_width),
            whole(row_count, inner_width),
            whole(row_count, value_width),
            tiles(heads_here),
            whole(*state_shape),
            tiles(1),
            whole(1, row_count),
            whole(1, row_count),
            tiles(KD // 2),
            tiles(KD // 2),
        ],
        [
            ((row_count, inner_width), BF),
            ((row_count, inner_width), F32),
            ((row_count, value_width), F32),
            (sent_shape, BF),
        ],
        [
            tiles(inner_width),
            held(row_count, inner_width),
            held(row_count, value_width),
            held(*sent_shape),
        ],
        [states],
    )(
        last_docs,
        after(log_decay, down_last, up_last, outw_sum[0], down_part),
        grad_mixed,
        query_rot,
        key_rot,
        values,
        carry_factor,
        state_low,
        docs_col,
        docs_row,
        pads_row,
        cosine,
        sine,
    )
    gw_sum = scatter_sum(grad_gw, order_two)
    one_on, two_on, three_on = (shifted(grad_state, -by) for by in (1, 2, 3))
    dk, dv, last_part, row_sums, column_first = call(
        partial(finish_kernel, heads_here, row_count),
        row_count,
        [
            SCALARS,
            SCALARS,
            tiles(inner_width),
            tiles(value_width),
            tiles(inner_width),
            tiles(value_width),
            tiles(heads_here),
            whole(*sent_shape),
            whole(*sent_shape),
            whole(*sent_shape),
            tiles(inner_width),
            tiles(value_width),
            whole(full_width, inner_width),
            whole(full_width, inner_width),
            whole(full_width, value_width),
            whole(full_width, value_width),
            tiles(KD // 2),
            tiles(KD // 2),
            shard_tiles,
            tiles(2),
            whole(4, full_width),
        ],
        [
            ((row_count, inner_width), BF),
            ((row_count, value_width), BF),
            ((shards, row_count + EXTRA, width), BF),
            ((row_count // TILE, 16, TILE), F32),
            ((2, full_width), F32),
        ],
        [
            tiles(inner_width),
            tiles(value_width),
            shard_tiles,
            pl.BlockSpec((1, 16, TILE), lambda i: (i, 0, 0)),
            held(2, full_width),
        ],
        [pltpu.VMEM(state_shape, BF)],
    )(
        last_docs,
        after(log_decay, down_near, up_near, outw_sum[1], gw_sum[0]),
        dk_part,
        dv_part,
        key_rot,
        values,
        end_factor,
        one_on,
        two_on,
        three_on,
        dq,
        dgate,
        query_weight,
        key_weight,
        value_weight,
        gate_weight,
        cosine,
        sine,
        rows_raw,
        stats,
        vectors,
    )
    count = row_count // TILE
    line = jnp.concatenate([row_sums[:, 0], row_sums[:, 8]], axis=0)
    line = jnp.pad(line, ((0, EXTRA - 2 * count - 4), (0, width - TILE)))
    columns = jnp.concatenate([column_first, cols_second]).reshape(4, shards, width)
    extra = jnp.concatenate(
        [jnp.broadcast_to(line[None], (shards, *line.shape)), columns.transpose(1, 0, 2)], axis=1
    )
    last_part = lax.dynamic_update_slice_in_dim(last_part, extra.astype(BF), row_count, axis=1)
    last_sum = lax.psum_scatter(last_part, "head", scatter_dimension=0).astype(F32)
    grad_ln1 = last_sum[:row_count]
    sums_first = last_sum[row_count:, :TILE] / full_width
    sums_first = jnp.stack(
        [sums_first[:count].reshape(row_count), sums_first[count : 2 * count].reshape(row_count)],
        axis=1,
    )
    columns = lax.psum(last_sum[row_count + EXTRA - 4 :], "tok")
    grad_vw = weight_grad(rows_first, dv)
    grad_qkw = weight_grad(rows_first, dq, dk)

    down_back = gather_back(down_near.astype(BF), order_one)
    up_back = gather_back(up_near.astype(BF), order_two)
    grad_down, grad_upw = down_back.astype(F32), up_back.astype(F32)
    waits = (outw_sum[-1], gw_sum[-1], down_back, up_back)
    vw_sum = scatter_sum(grad_vw, order_one, 0, waits)[-1].astype(BF)
    qkw_sum = scatter_sum(grad_qkw, order_two, 0, waits)[-1].astype(BF)
    grad_outw = gather_back(outw_sum[-1].astype(BF), order_one).astype(F32)
    grad_gw = gather_back(gw_sum[-1].astype(BF), order_two).astype(F32)
    pieces = after(jnp.stack([vw_sum, qkw_sum]), grad_outw, grad_gw, grad_down, grad_upw)
    pieces = lax.all_gather(pieces, "tok", axis=0)
    grad_vw = in_order(pieces[:, 0], order_one)
    grad_qkw = in_order(pieces[:, 1], order_two)
    grad_qw, grad_kw = grad_qkw[:, :inner_width], grad_qkw[:, inner_width:]

    late_down_part = after(down_part, last_sum)
    result = (hidden + scatter_side(late_down_part)).astype(BF)
    result_keep = lax.dynamic_index_in_dim(result, spread, 0, keepdims=False)
    result_give = lax.dynamic_index_in_dim(result, 1 - spread, 0, keepdims=False)
    layer_out = joined(result_keep, swapped(result_give, "head", sides), spread == 0, 0)

    norm_first = (tokens.astype(F32) - stats[:, 0:1]) * stats[:, 1:2]
    branch_rows = lax.dynamic_index_in_dim(
        lax.dynamic_index_in_dim(grad_branch, side, 1, keepdims=False), spread, 1, keepdims=False
    ).reshape(row_count, width)
    tokens_grad = branch_rows.astype(F32) + stats[:, 1:2] * (
        grad_ln1 * mix_gain - sums_first[:, 0:1] - norm_first * sums_first[:, 1:2]
    )
    return (
        layer_out,
        tokens_grad,
        columns[0],
        columns[1],
        grad_qw,
        grad_kw,
        grad_vw,
        grad_gw,
        grad_outw,
        columns[2],
        columns[3],
        grad_upw,
        grad_down,
    )


def solution(mesh):
    rows = P("tok", "head")
    columns = P(None, "head")
    return jax.shard_map(
        body,
        mesh=mesh,
        in_specs=(
            rows,
            P("head"),
            P("head"),
            columns,
            columns,
            columns,
            columns,
            P("head", None),
            P("head"),
            P("head"),
            columns,
            P("head", None),
            P("tok"),
            P("tok"),
            rows,
        ),
        out_specs=(
            rows,
            rows,
            P("head"),
            P("head"),
            columns,
            columns,
            columns,
            columns,
            P("head", None),
            P("head"),
            P("head"),
            columns,
            P("head", None),
        ),
        check_vma=False,
    )
```

time: 1010 us -> 874 us (0.87)
  Pallas kernels: 0 us -> 202 us
  matrix products: 189 us -> 0 us
  waiting for transfers between devices: 464 us -> 364 us
  blocking collectives: 57.8 us -> 12.4 us
  starting transfers between devices: 54.6 us -> 67.3 us
    pallas_call x0 -> x15, Pallas kernels: none -> 202 us  [the longest x5 42.2 us: weight_grad(): pl.pallas_call(weight_kernel, grid=(columns // CHUNK,), in_specs=[pl.Bloc...]
    dot_general x32 -> x0, matrix products: 189 us -> none  [the longest x1 18.2 us: body(): jnp.einsum('nd,fd->nf', grad_rows, down_weight, preferred_element_type=F32)]
    all_gather x4 -> x3, waiting for transfers between devices: 182 us -> 84.4 us  [the longest x1 77.7 us: body(): rows_raw = lax.all_gather(packed, 'head', axis=0)]
    ppermute x36 -> x45, waiting for transfers between devices: 144 us -> 231 us  [swapped(): lax.ppermute(value, axis, [(i, i ^ mask) for i in range(lax.axis_size(axi...]
    reduce_scatter x4 -> x2, waiting for transfers between devices: 126 us -> 48.3 us  [the longest x1 48.3 us: body(): lax.psum_scatter(mix_part.reshape(shards, 2, half_rows, width), 'head', s...]
    unnamed x205 -> x80, local copies, waits for them, and re-layouts: 40.9 us -> 4.88 us
    psum x3 -> x1, blocking collectives: 33.6 us -> 12.4 us  [body(): columns = lax.psum(last_sum[row_count + EXTRA - 4:], 'tok')]
    add x12 -> x20, other arithmetic: 21.4 us -> 41.7 us  [the longest x16 35.6 us: scatter_sum(): keep.astype(F32) + swapped(give.astype(BF), 'tok', 1 << bit).astype(F32)]
  transfers between devices with their start and end apart: 50 -> 56, of which waited for: 22 -> 23; matrix products, arithmetic and copies ran while one was open for 29% -> 20% of each run, Pallas kernels for 0% -> 19%
where the time goes in v2:
time: 874 us; the launch traced here: 868 us
  waiting for transfers between devices  364 us (42%)
  Pallas kernels  202 us (23%)
  other arithmetic  135 us (15%)
  local copies, waits for them, and re-layouts  72.5 us (8%)
  starting transfers between devices  67.3 us (8%)
  between operations  15.1 us (2%)
  blocking collectives  12.4 us (1%)
    ppermute x45, waiting for transfers between devices, swapped(): lax.ppermute(value, axis, [(i, i ^ mask) for i in range(lax.axis_size(axi...  231 us
    all_gather x1, waiting for transfers between devices, body(): rows_raw = lax.all_gather(packed, 'head', axis=0)  77.7 us
    reduce_scatter x1, waiting for transfers between devices, body(): lax.psum_scatter(mix_part.reshape(shards, 2, half_rows, width), 'head', s...  48.3 us
    select_n x18, other arithmetic, joined(): jnp.where(first, jnp.concatenate([value, other], axis=axis), jnp.concaten...  42.9 us
    pallas_call x5, Pallas kernels, weight_grad(): pl.pallas_call(weight_kernel, grid=(columns // CHUNK,), in_specs=[pl.Bloc...  42.2 us
    ppermute x45, starting transfers between devices, swapped(): lax.ppermute(value, axis, [(i, i ^ mask) for i in range(lax.axis_size(axi...  40.7 us
    add x16, other arithmetic, scatter_sum(): keep.astype(F32) + swapped(give.astype(BF), 'tok', 1 << bit).astype(F32)  35.6 us
    pallas_call x1, Pallas kernels, body(): call(partial(finish_kernel, heads_here, row_count), row_count, [SCALARS,...  27.2 us
  transfers between devices with their start and end apart: 56, of which 23 were waited for; matrix products, arithmetic and copies ran while one was open for 20% of the time, Pallas kernels for 19%

profile of v2, /device:TPU:0, one launch (start us, length us, event | category | flops | bytes accessed | tf_op | source)
XLA Modules:
  0.0 868.0 jit_solution(17367230588560867964)
XLA Ops:
  17.0 77.7 %all-gather.8.cloned.1.call-done = bf16[4160,512]{1,0:T(8,128)(2,1)} async-done(((bf16[1040,512]{1,0:T(8,128)(2,1)}), bf16[4160,512]{1,0:T(8,128)(2,1)}) %all-gather.8.cloned.1.call-update) | async-done | bytes 4259856 | tf_op jit(solution)/shard_map/all_gather | solution.py:596
  101.4 19.2 %shard_map.247 = (bf16[1024,2048]{1,0:T(8,128)(2,1)}, bf16[1024,512]{1,0:T(8,128)(2,1)}, bf16[1024,512]{1,0:T(8,128)(2,1)}, bf16[1024,1024]{1,0:T(8,128)(2,1)}, ...) custom-call(s32[1]{0:T(128)} %slice.117.docs, bf16[4,1040,512]{2,1,0:T(8,128)(2,1)} %bitcast.287, ...), custom_call_target="tpu_custom_call" | custom-call | tf_op jit(solution)/shard_map/pallas_call | solution.py:647
  122.0 4.9 collective-permute-start.2
  126.9 4.3 collective-permute-start.3
  133.2 18.1 %shard_map.248 = (f32[1024,1024]{1,0:T(8,128)}, f32[1024,1024]{1,0:T(8,128)}) custom-call(f32[2]{0:T(128)} %copy-done.36, bf16[1024,2048]{1,0:T(8,128)(2,1)} %get-tuple-element.63.low.left, bf16[2048,1024]{1,0:T(8,128)(2,1)} %wg.3, bf16[1024,512]{1,0:T(8,128)(2,1)} %get-tuple-element.64.q, bf16[1024,512]{1,0:T(8,128)(2,1)} %get-tuple-element.65.k, ...), custom_call_target="tpu_custom_call" | custom-call | tf_op jit(solution)/shard_map/pallas_call | solution.py:690
  151.3 14.0 %collective-permute-done = bf16[512,512]{1,0:T(8,128)(2,1)S(1)} collective-permute-done((bf16[512,512]{1,0:T(8,128)(2,1)S(1)}, bf16[512,512]{1,0:T(8,128)(2,1)S(1)}, u32[]{:S(2)}, u32[]{:S(2)}) %collective-permute-start) | collective-permute-done | bytes 524320 | tf_op jit(solution)/shard_map/ppermute | solution.py:28
  166.1 14.1 %shard_map.249 = (f32[1024,1024]{1,0:T(8,128)}, f32[1024,2]{1,0:T(8,128)}, bf16[1024,1024]{1,0:T(8,128)(2,1)}, bf16[2,2,2,512,512]{4,3,2,1,0:T(8,128)(2,1)}, bf1...) custom-call(f32[2]{0:T(128)} %copy-done.36, f32[1024,1024]{1,0:T(8,128)} %get-tuple-element.67.inner, ...), custom_call_target="tpu_custom_call" | custom-call | tf_op jit(solution)/shard_map/pallas_call | solution.py:717
  183.9 10.9 %collective-permute-done.7 = bf16[256,1024]{1,0:T(8,128)(2,1)} collective-permute-done((bf16[256,1024]{1,0:T(8,128)(2,1)S(1)}, bf16[256,1024]{1,0:T(8,128)(2,1)}, u32[]{:S(2)}, u32[]{:S(2)}) %collective-permute-start.7) | collective-permute-done | bytes 524320 | tf_op jit(solution)/shard_map/ppermute | solution.py:28
  201.2 19.7 %collective-permute-done.8 = bf16[512,1024]{1,0:T(8,128)(2,1)} collective-permute-done((bf16[512,1024]{1,0:T(8,128)(2,1)S(1)}, bf16[512,1024]{1,0:T(8,128)(2,1)}, u32[]{:S(2)}, u32[]{:S(2)}) %collective-permute-start.8) | collective-permute-done | bytes 1048608 | tf_op jit(solution)/shard_map/ppermute | solution.py:28
  231.4 48.3 %reduce-scatter.3.cloned.1.call-done = bf16[1,2,512,512]{3,2,1,0:T(8,128)(2,1)} async-done(((bf16[4,2,512,512]{3,2,1,0:T(8,128)(2,1)}), bf16[1,2,512,512]{3,2,1,0:T(8,128)(2,1)}) %reduce-scatter.3.cloned.1.call-update) | async-done | bytes 1048592 | tf_op jit(solution)/shard_map/reduce_scatter | solution.py:769
  284.7 5.6 maximum_select_fusion.up_far
  290.3 6.2 maximum_select_fusion.1.down_far
  296.5 9.5 %collective-permute-done.5 = bf16[2,1,512,512]{3,2,0,1:T(8,128)(2,1)S(1)} collective-permute-done((bf16[2,1,512,512]{3,2,0,1:T(8,128)(2,1)S(1)}, bf16[2,1,512,512]{3,2,0,1:T(8,128)(2,1)S(1)}, u32[]{:S(2)}, u32[]{:S(2)}) %collective-permute-start.5) | collective-permute-done | bytes 1048608 | tf_op jit(solution)/shard_map/ppermute | solution.py:28
  307.8 27.0 %shard_map.250 = (bf16[512,2048]{1,0:T(8,128)(2,1)}, bf16[512,2048]{1,0:T(8,128)(2,1)}, bf16[512,2048]{1,0:T(8,128)(2,1)}, bf16[512,2048]{1,0:T(8,128)(2,1)}, bf...) custom-call(bf16[4,512,512]{2,1,0:T(8,128)(2,1)} %bitcast.332, ...), custom_call_target="tpu_custom_call" | custom-call | tf_op jit(solution)/shard_map/pallas_call | solution.py:777
  339.3 26.3 %collective-permute-done.14 = f32[512,2]{1,0:T(8,128)S(1)} collective-permute-done((f32[512,2]{1,0:T(8,128)}, f32[512,2]{1,0:T(8,128)S(1)}, u32[]{:S(2)}, u32[]{:S(2)}) %collective-permute-start.14) | collective-permute-done | bytes 4128 | tf_op jit(solution)/shard_map/ppermute | solution.py:28
  367.0 8.5 shard_map.252
  375.4 4.7 dynamic-slice_bitcast_fusion.1
  380.2 8.4 shard_map.253
  388.7 4.9 dynamic-slice_bitcast_fusion
  397.5 11.1 %reduce-scatter.5.cloned.1.call-start = ((), (), s32[]{:S(2)}) async-start(), calls=%async_computation.4 | async-start | bytes 5324800 | tf_op jit(solution)/shard_map/reduce_scatter | solution.py:1002
  408.6 5.4 convert_add_fusion.1
  416.0 5.4 convert_add_fusion
  423.3 38.9 %collective-permute-done.16 = bf16[2,256,2048]{2,1,0:T(8,128)(2,1)} collective-permute-done((bf16[2,256,2048]{2,1,0:T(8,128)(2,1)S(1)}, bf16[2,256,2048]{2,1,0:T(8,128)(2,1)}, u32[]{:S(2)}, u32[]{:S(2)}) %collective-permute-start.16) | collective-permute-done | bytes 2097184 | tf_op jit(solution)/shard_map/ppermute | solution.py:28
  472.9 6.7 all-gather.6.cloned.1.call-done
  479.6 8.5 shard_map.254
  495.7 11.7 %shard_map.255 = (bf16[1024,1024]{1,0:T(8,128)(2,1)}, bf16[1024,1024]{1,0:T(8,128)(2,1)}) custom-call(bf16[2,2,2,512,512]{4,3,2,1,0:T(8,128)(2,1)} %bitcast.303, bf16[1024,2048]{1,0:T(8,128)(2,1)} %wo.3, f32[1024,1024]{1,0:T(8,128)} %get-tuple-element.69.gate, f32[1024,1024]{1,0:T(8,128)} %get-tuple-element.85.group, f32[1024,2]{1,0:T(8,128)} %get-tuple-element.86.scale, ...), custom_call_target="tpu_custom_call" | custom-call | tf_op jit(solution)/shard_map/pallas_call | solution.py:856
  507.5 8.4 shard_map.256
  528.0 9.8 %shard_map.251 = bf16[2,2,512,512]{3,2,1,0:T(8,128)(2,1)} custom-call(bf16[512,2048]{1,0:T(8,128)(2,1)} %get-tuple-element.78.act.left, bf16[1024,2048]{1,0:T(8,128)(2,1)} %down_near.3, bf16[1024,2048]{1,0:T(8,128)(2,1)} %maximum_select_fusion.1.down_far), custom_call_target="tpu_custom_call" | custom-call | tf_op jit(solution)/shard_map/pallas_call | solution.py:826
  537.9 4.4 convert_add_fusion.5
  542.3 22.2 %shard_map.257 = (bf16[1024,512]{1,0:T(8,128)(2,1)}, f32[1024,512]{1,0:T(8,128)}, f32[1024,1024]{1,0:T(8,128)}, bf16[2,272,512]{2,1,0:T(8,128)(2,1)}) custom-call(s32[1]{0:T(128)} %slice.117.docs, f32[2]{0:T(128)} %copy-done.36, bf16[1024,1024]{1,0:T(8,128)(2,1)} %get-tuple-element.91.mix, bf16[1024,512]{1,0:T(8,128)(2,1)} %get-tuple-element.64.q, ...), custom_call_target="tpu_custom_call" | custom-call | tf_op jit(solution)/shard_map/pallas_call | solution.py:882
  586.9 27.5 %collective-permute-done.23 = bf16[256,2048]{1,0:T(8,128)(2,1)} collective-permute-done((bf16[256,2048]{1,0:T(8,128)(2,1)}, bf16[256,2048]{1,0:T(8,128)(2,1)}, u32[]{:S(2)}, u32[]{:S(2)}) %collective-permute-start.23) | collective-permute-done | bytes 1048608 | tf_op jit(solution)/shard_map/ppermute | solution.py:28
  618.2 27.2 %shard_map.258 = (bf16[1024,512]{1,0:T(8,128)(2,1)}, bf16[1024,1024]{1,0:T(8,128)(2,1)}, bf16[4,1040,512]{2,1,0:T(8,128)(2,1)}, f32[4,16,256]{2,1,0:T(8,128)}, f32[2,2048]{1,0:T(2,128)}) custom-call(s32[1]{0:T(128)} %slice.117.docs, f32[2]{0:T(128)} %copy-done.36, f32[1024,512]{1,0:T(8,128)} %get-tuple-element.94.dk_in, ...), custom_call_target="tpu_custom_call" | custom-call | tf_op jit(solution)/shard_map/pallas_call | solution.py:930
  655.9 8.4 shard_map.260
  672.1 4.8 collective-permute-done.35
  685.6 7.0 collective-permute-done.31
  694.6 8.5 shard_map.259
  715.4 6.0 fusion.41
  721.4 6.1 fusion.40
  739.8 19.4 %collective-permute-done.43 = bf16[512,1024]{1,0:T(8,128)(2,1)S(1)} collective-permute-done((bf16[512,1024]{1,0:T(8,128)(2,1)S(1)}, bf16[512,1024]{1,0:T(8,128)(2,1)S(1)}, u32[]{:S(2)}, u32[]{:S(2)}) %collective-permute-start.43) | collective-permute-done | bytes 1048608 | tf_op jit(solution)/shard_map/ppermute | solution.py:28
  762.5 10.5 %collective-permute-done.44 = bf16[256,1024]{1,0:T(8,128)(2,1)S(1)} collective-permute-done((bf16[256,1024]{1,0:T(8,128)(2,1)S(1)}, bf16[256,1024]{1,0:T(8,128)(2,1)S(1)}, u32[]{:S(2)}, u32[]{:S(2)}) %collective-permute-start.44) | collective-permute-done | bytes 524320 | tf_op jit(solution)/shard_map/ppermute | solution.py:28
  776.3 6.0 fusion
  782.3 6.4 fusion.1
  788.7 4.0 fusion.44
  799.4 12.4 %psum.7 = f32[4,512]{1,0:T(4,128)S(1)} all-reduce(f32[4,512]{1,0:T(4,128)S(1)} %slice_bitcast_fusion.2), channel_id=1, replica_groups=mesh['head'=4,'tok'=8] {'tok'}, use_global_device_ids=true, to_apply=%region_2.3 | all-reduce | flops 2048 | bytes 16384 | tf_op jit(solution)/shard_map/psum | solution.py:1009
  811.9 5.5 collective-permute-done.28
  824.1 19.3 %collective-permute-done.29 = bf16[512,512]{1,0:T(8,128)(2,1)S(1)} collective-permute-done((bf16[512,512]{1,0:T(8,128)(2,1)S(1)}, bf16[512,512]{1,0:T(8,128)(2,1)S(1)}, u32[]{:S(2)}, u32[]{:S(2)}) %collective-permute-start.29) | collective-permute-done | bytes 524320 | tf_op jit(solution)/shard_map/ppermute | solution.py:28
  851.5 4.4 fusion.43
  857.0 4.2 copy.118
  (294 shorter events, 200.3 us)
Async XLA Ops:
  7.2 87.6 %all-gather.8.cloned.1.call-start = ((), (), s32[]{:S(2)}) async-start(), calls=%async_computation.5 | async-start | bytes 5324800 | tf_op jit(solution)/shard_map/all_gather | solution.py:596
  9.6 270.1 %reduce-scatter.3.cloned.1.call-start = ((), (), s32[]{:S(2)}) async-start(), calls=%async_computation.2 | async-start | bytes 5242880 | tf_op jit(solution)/shard_map/reduce_scatter | solution.py:769
  96.0 84.2 %collective-permute-start.4 = (bf16[512,1024]{1,0:T(8,128)(2,1)}, bf16[512,1024]{1,0:T(8,128)(2,1)S(1)}, u32[]{:S(2)}, u32[]{:S(2)}) collective-permute-start(bf16[512,1024]{1,0:T(8,128)(2,1)} %pad_maximum_fusion), channel_id=1, source_target_pairs={{0,16},{8,24},{16,0},{24,8},{1,17},{9,25},{17,1},{25,9},{2,18},{10... | collective-permute-start | bytes 3145736 | tf_op jit(solution)/shard_map/ppermute | solution.py:28
  98.2 67.1 %collective-permute-start = (bf16[512,512]{1,0:T(8,128)(2,1)S(1)}, bf16[512,512]{1,0:T(8,128)(2,1)S(1)}, u32[]{:S(2)}, u32[]{:S(2)}) collective-permute-start(bf16[512,512]{1,0:T(8,128)(2,1)S(1)} %get-tuple-element.132), channel_id=1, source_target_pairs={{0,16},{8,24},{16,0},{24,8},{1,17},{9,25},{17,1},{25,9},{2,18},{10... | collective-permute-start | bytes 1572872 | tf_op jit(solution)/shard_map/ppermute | solution.py:28
  120.7 44.6 %collective-permute-start.1 = (bf16[2,272,512]{2,1,0:T(8,128)(2,1)}, bf16[2,272,512]{2,1,0:T(8,128)(2,1)S(1)}, u32[]{:S(2)}, u32[]{:S(2)}) collective-permute-start(bf16[2,272,512]{2,1,0:T(8,128)(2,1)} %get-tuple-element.68), channel_id=1, source_target_pairs={{0,1},{1,2},{2,3},{3,4},{4,5},{5,6},{6,7},{8,9},{9,10},{10,11},{11... | collective-permute-start | bytes 1671176 | tf_op jit(solution)/shard_map/ppermute | solution.py:24
  122.0 43.3 %collective-permute-start.2 = (bf16[2,272,512]{2,1,0:T(8,128)(2,1)}, bf16[2,272,512]{2,1,0:T(8,128)(2,1)}, u32[]{:S(2)}, u32[]{:S(2)}) collective-permute-start(bf16[2,272,512]{2,1,0:T(8,128)(2,1)} %get-tuple-element.68), channel_id=1, source_target_pairs={{0,2},{1,3},{2,4},{3,5},{4,6},{5,7},{8,10},{9,11},{10,12},{11,13},... | collective-permute-start | bytes 1671176 | tf_op jit(solution)/shard_map/ppermute | solution.py:24
  126.9 38.5 %collective-permute-start.3 = (bf16[2,272,512]{2,1,0:T(8,128)(2,1)}, bf16[2,272,512]{2,1,0:T(8,128)(2,1)}, u32[]{:S(2)}, u32[]{:S(2)}) collective-permute-start(bf16[2,272,512]{2,1,0:T(8,128)(2,1)} %get-tuple-element.68), channel_id=1, source_target_pairs={{0,3},{1,4},{2,5},{3,6},{4,7},{8,11},{9,12},{10,13},{11,14},{12,15... | collective-permute-start | bytes 1671176 | tf_op jit(solution)/shard_map/ppermute | solution.py:24
  180.5 299.1 %all-gather.6.cloned.1.call-start = ((), (), s32[]{:S(2)}) async-start(), calls=%async_computation.3 | async-start | bytes 5242880 | tf_op jit(solution)/shard_map/all_gather | solution.py:822
  196.5 24.4 %collective-permute-start.8 = (bf16[512,1024]{1,0:T(8,128)(2,1)S(1)}, bf16[512,1024]{1,0:T(8,128)(2,1)}, u32[]{:S(2)}, u32[]{:S(2)}) collective-permute-start(bf16[512,1024]{1,0:T(8,128)(2,1)S(1)} %maximum_select_fusion.16), channel_id=1, source_target_pairs={{0,2},{1,3},{2,0},{3,1},{4,6},{5,7},{6,4},{7,5},{8,10},{9,11},{10,... | collective-permute-start | bytes 3145736 | tf_op jit(solution)/shard_map/ppermute | solution.py:28
  199.6 25.2 %collective-permute-start.11 = (bf16[256,2048]{1,0:T(8,128)(2,1)S(1)}, bf16[256,2048]{1,0:T(8,128)(2,1)S(1)}, u32[]{:S(2)}, u32[]{:S(2)}) collective-permute-start(bf16[256,2048]{1,0:T(8,128)(2,1)S(1)} %maximum_select_fusion.17), channel_id=1, source_target_pairs={{0,4},{1,5},{2,6},{3,7},{4,0},{5,1},{6,2},{7,3},{8,12},{9,13},{10,... | collective-permute-start | bytes 3145736 | tf_op jit(solution)/shard_map/ppermute | solution.py:28
  224.8 59.9 %collective-permute-start.9 = (bf16[1024,1024]{1,0:T(8,128)(2,1)}, bf16[1024,1024]{1,0:T(8,128)(2,1)}, u32[]{:S(2)}, u32[]{:S(2)}) collective-permute-start(bf16[1024,1024]{1,0:T(8,128)(2,1)} %maximum_select_fusion.8), channel_id=1, source_target_pairs={{0,1},{1,0},{2,3},{3,2},{4,5},{5,4},{6,7},{7,6},{8,9},{9,8},{10,11... | collective-permute-start | bytes 6291464 | tf_op jit(solution)/shard_map/ppermute | solution.py:28
  227.2 63.1 %collective-permute-start.12 = (bf16[512,2048]{1,0:T(8,128)(2,1)}, bf16[512,2048]{1,0:T(8,128)(2,1)}, u32[]{:S(2)}, u32[]{:S(2)}) collective-permute-start(bf16[512,2048]{1,0:T(8,128)(2,1)} %maximum_select_fusion.9), channel_id=1, source_target_pairs={{0,1},{1,0},{2,3},{3,2},{4,5},{5,4},{6,7},{7,6},{8,9},{9,8},{10,11... | collective-permute-start | bytes 6291464 | tf_op jit(solution)/shard_map/ppermute | solution.py:28
  227.9 53.4 %collective-permute-start.6 = (bf16[2,1,512,512]{3,2,0,1:T(8,128)(2,1)S(1)}, bf16[2,1,512,512]{3,2,0,1:T(8,128)(2,1)}, u32[]{:S(2)}, u32[]{:S(2)}) collective-permute-start(bf16[2,1,512,512]{3,2,0,1:T(8,128)(2,1)S(1)} %maximum_select_fusion.15), channel_id=1, source_target_pairs={{0,8},{8,0},{16,24},{24,16},{1,9},{9,1},{17,25},{25,17},{2,10},{10... | collective-permute-start | bytes 3145736 | tf_op jit(solution)/shard_map/ppermute | solution.py:28
  281.2 24.8 %collective-permute-start.5 = (bf16[2,1,512,512]{3,2,0,1:T(8,128)(2,1)S(1)}, bf16[2,1,512,512]{3,2,0,1:T(8,128)(2,1)S(1)}, u32[]{:S(2)}, u32[]{:S(2)}) collective-permute-start(bf16[2,1,512,512]{3,2,0,1:T(8,128)(2,1)S(1)} %fusion.3), channel_id=1, source_target_pairs={{0,8},{8,0},{16,24},{24,16},{1,9},{9,1},{17,25},{25,17},{2,10},{10... | collective-permute-start | bytes 3145736 | tf_op jit(solution)/shard_map/ppermute | solution.py:28
  336.2 30.8 %collective-permute-start.13 = (bf16[2,1,512,512]{3,2,0,1:T(8,128)(2,1)S(1)}, bf16[2,1,512,512]{3,2,0,1:T(8,128)(2,1)}, u32[]{:S(2)}, u32[]{:S(2)}) collective-permute-start(bf16[2,1,512,512]{3,2,0,1:T(8,128)(2,1)S(1)} %constant_dynamic-slice_fusion.3), channel_id=1, source_target_pairs={{0,8},{8,0},{16,24},{24,16},{1,9},{9,1},{17,25},{25,17},{2,10},{10... | collective-permute-start | bytes 3145736 | tf_op jit(solution)/shard_map/ppermute | solution.py:28
  337.2 28.4 %collective-permute-start.14 = (f32[512,2]{1,0:T(8,128)}, f32[512,2]{1,0:T(8,128)S(1)}, u32[]{:S(2)}, u32[]{:S(2)}) collective-permute-start(f32[512,2]{1,0:T(8,128)} %get-tuple-element.77), channel_id=1, source_target_pairs={{0,8},{8,0},{16,24},{24,16},{1,9},{9,1},{17,25},{25,17},{2,10},{10... | collective-permute-start | bytes 12296 | tf_op jit(solution)/shard_map/ppermute | solution.py:28
  380.2 28.4 %collective-permute-start.15 = (bf16[2,512,2048]{2,1,0:T(8,128)(2,1)}, bf16[2,512,2048]{2,1,0:T(8,128)(2,1)}, u32[]{:S(2)}, u32[]{:S(2)}) collective-permute-start(bf16[2,512,2048]{2,1,0:T(8,128)(2,1)} %dynamic-slice_bitcast_fusion.1), channel_id=1, source_target_pairs={{0,1},{1,0},{2,3},{3,2},{4,5},{5,4},{6,7},{7,6},{8,9},{9,8},{10,11... | collective-permute-start | bytes 12582920 | tf_op jit(solution)/shard_map/ppermute | solution.py:28
  393.6 22.4 %collective-permute-start.18 = (bf16[1024,2048]{1,0:T(8,128)(2,1)}, bf16[1024,2048]{1,0:T(8,128)(2,1)}, u32[]{:S(2)}, u32[]{:S(2)}) collective-permute-start(bf16[1024,2048]{1,0:T(8,128)(2,1)} %dynamic-slice_bitcast_fusion), channel_id=1, source_target_pairs={{0,1},{1,0},{2,3},{3,2},{4,5},{5,4},{6,7},{7,6},{8,9},{9,8},{10,11... | collective-permute-start | bytes 12582920 | tf_op jit(solution)/shard_map/ppermute | solution.py:28
  397.5 391.2 %reduce-scatter.5.cloned.1.call-start = ((), (), s32[]{:S(2)}) async-start(), calls=%async_computation.4 | async-start | bytes 5324800 | tf_op jit(solution)/shard_map/reduce_scatter | solution.py:1002
  414.4 47.8 %collective-permute-start.16 = (bf16[2,256,2048]{2,1,0:T(8,128)(2,1)S(1)}, bf16[2,256,2048]{2,1,0:T(8,128)(2,1)}, u32[]{:S(2)}, u32[]{:S(2)}) collective-permute-start(bf16[2,256,2048]{2,1,0:T(8,128)(2,1)S(1)} %fusion.11), channel_id=1, source_target_pairs={{0,2},{1,3},{2,0},{3,1},{4,6},{5,7},{6,4},{7,5},{8,10},{9,11},{10,... | collective-permute-start | bytes 6291464 | tf_op jit(solution)/shard_map/ppermute | solution.py:28
  421.7 48.6 %collective-permute-start.19 = (bf16[512,2048]{1,0:T(8,128)(2,1)S(1)}, bf16[512,2048]{1,0:T(8,128)(2,1)S(1)}, u32[]{:S(2)}, u32[]{:S(2)}) collective-permute-start(bf16[512,2048]{1,0:T(8,128)(2,1)S(1)} %fusion.12), channel_id=1, source_target_pairs={{0,4},{1,5},{2,6},{3,7},{4,0},{5,1},{6,2},{7,3},{8,12},{9,13},{10,... | collective-permute-start | bytes 6291464 | tf_op jit(solution)/shard_map/ppermute | solution.py:28
  465.7 53.7 %collective-permute-start.17 = (bf16[2,128,2048]{2,1,0:T(8,128)(2,1)}, bf16[2,128,2048]{2,1,0:T(8,128)(2,1)}, u32[]{:S(2)}, u32[]{:S(2)}) collective-permute-start(bf16[2,128,2048]{2,1,0:T(8,128)(2,1)} %fusion.28), channel_id=1, source_target_pairs={{0,4},{1,5},{2,6},{3,7},{4,0},{5,1},{6,2},{7,3},{8,12},{9,13},{10,... | collective-permute-start | bytes 3145736 | tf_op jit(solution)/shard_map/ppermute | solution.py:28
  491.4 46.5 %collective-permute-start.22 = (bf16[512,2048]{1,0:T(8,128)(2,1)}, bf16[512,2048]{1,0:T(8,128)(2,1)}, u32[]{:S(2)}, u32[]{:S(2)}) collective-permute-start(bf16[512,2048]{1,0:T(8,128)(2,1)} %dynamic-slice_bitcast_fusion.7), channel_id=1, source_target_pairs={{0,1},{1,0},{2,3},{3,2},{4,5},{5,4},{6,7},{7,6},{8,9},{9,8},{10,11... | collective-permute-start | bytes 6291464 | tf_op jit(solution)/shard_map/ppermute | solution.py:28
  493.1 29.5 %collective-permute-start.20 = (bf16[256,2048]{1,0:T(8,128)(2,1)S(1)}, bf16[256,2048]{1,0:T(8,128)(2,1)}, u32[]{:S(2)}, u32[]{:S(2)}) collective-permute-start(bf16[256,2048]{1,0:T(8,128)(2,1)S(1)} %fusion.25), channel_id=1, source_target_pairs={{0,2},{1,3},{2,0},{3,1},{4,6},{5,7},{6,4},{7,5},{8,10},{9,11},{10,... | collective-permute-start | bytes 3145736 | tf_op jit(solution)/shard_map/ppermute | solution.py:28
  519.1 58.4 %collective-permute-start.24 = (bf16[1024,1024]{1,0:T(8,128)(2,1)}, bf16[1024,1024]{1,0:T(8,128)(2,1)}, u32[]{:S(2)}, u32[]{:S(2)}) collective-permute-start(bf16[1024,1024]{1,0:T(8,128)(2,1)} %dynamic-slice_bitcast_fusion.6), channel_id=1, source_target_pairs={{0,1},{1,0},{2,3},{3,2},{4,5},{5,4},{6,7},{7,6},{8,9},{9,8},{10,11... | collective-permute-start | bytes 6291464 | tf_op jit(solution)/shard_map/ppermute | solution.py:28
  527.1 47.5 %collective-permute-start.21 = (bf16[512,1024]{1,0:T(8,128)(2,1)}, bf16[512,1024]{1,0:T(8,128)(2,1)}, u32[]{:S(2)}, u32[]{:S(2)}) collective-permute-start(bf16[512,1024]{1,0:T(8,128)(2,1)} %pad_maximum_fusion.1), channel_id=1, source_target_pairs={{0,16},{8,24},{16,0},{24,8},{1,17},{9,25},{17,1},{25,9},{2,18},{10... | collective-permute-start | bytes 3145736 | tf_op jit(solution)/shard_map/ppermute | solution.py:28
  564.6 51.3 %collective-permute-start.25 = (bf16[2,272,512]{2,1,0:T(8,128)(2,1)}, bf16[2,272,512]{2,1,0:T(8,128)(2,1)}, u32[]{:S(2)}, u32[]{:S(2)}) collective-permute-start(bf16[2,272,512]{2,1,0:T(8,128)(2,1)} %get-tuple-element.96), channel_id=1, source_target_pairs={{1,0},{2,1},{3,2},{4,3},{5,4},{6,5},{7,6},{9,8},{10,9},{11,10},{12... | collective-permute-start | bytes 1671176 | tf_op jit(solution)/shard_map/ppermute | solution.py:24
  566.0 52.2 %collective-permute-start.26 = (bf16[2,272,512]{2,1,0:T(8,128)(2,1)}, bf16[2,272,512]{2,1,0:T(8,128)(2,1)}, u32[]{:S(2)}, u32[]{:S(2)}) collective-permute-start(bf16[2,272,512]{2,1,0:T(8,128)(2,1)} %get-tuple-element.96), channel_id=1, source_target_pairs={{2,0},{3,1},{4,2},{5,3},{6,4},{7,5},{10,8},{11,9},{12,10},{13,11},... | collective-permute-start | bytes 1671176 | tf_op jit(solution)/shard_map/ppermute | solution.py:24
  567.3 50.9 %collective-permute-start.27 = (bf16[2,272,512]{2,1,0:T(8,128)(2,1)}, bf16[2,272,512]{2,1,0:T(8,128)(2,1)}, u32[]{:S(2)}, u32[]{:S(2)}) collective-permute-start(bf16[2,272,512]{2,1,0:T(8,128)(2,1)} %get-tuple-element.96), channel_id=1, source_target_pairs={{3,0},{4,1},{5,2},{6,3},{7,4},{11,8},{12,9},{13,10},{14,11},{15,12... | collective-permute-start | bytes 1671176 | tf_op jit(solution)/shard_map/ppermute | solution.py:24
  574.6 39.8 %collective-permute-start.23 = (bf16[256,2048]{1,0:T(8,128)(2,1)}, bf16[256,2048]{1,0:T(8,128)(2,1)}, u32[]{:S(2)}, u32[]{:S(2)}) collective-permute-start(bf16[256,2048]{1,0:T(8,128)(2,1)} %fusion.26), channel_id=1, source_target_pairs={{0,2},{1,3},{2,0},{3,1},{4,6},{5,7},{6,4},{7,5},{8,10},{9,11},{10,... | collective-permute-start | bytes 3145736 | tf_op jit(solution)/shard_map/ppermute | solution.py:28
  583.8 65.2 %collective-permute-start.34 = (bf16[128,2048]{1,0:T(8,128)(2,1)}, bf16[128,2048]{1,0:T(8,128)(2,1)}, u32[]{:S(2)}, u32[]{:S(2)}) collective-permute-start(bf16[128,2048]{1,0:T(8,128)(2,1)} %fusion.29), channel_id=1, source_target_pairs={{0,4},{1,5},{2,6},{3,7},{4,0},{5,1},{6,2},{7,3},{8,12},{9,13},{10,... | collective-permute-start | bytes 1572872 | tf_op jit(solution)/shard_map/ppermute | solution.py:28
  614.4 38.0 %collective-permute-start.37 = (bf16[256,1024]{1,0:T(8,128)(2,1)}, bf16[256,1024]{1,0:T(8,128)(2,1)}, u32[]{:S(2)}, u32[]{:S(2)}) collective-permute-start(bf16[256,1024]{1,0:T(8,128)(2,1)} %get-tuple-element.127), channel_id=1, source_target_pairs={{0,2},{1,3},{2,0},{3,1},{4,6},{5,7},{6,4},{7,5},{8,10},{9,11},{10,... | collective-permute-start | bytes 1572872 | tf_op jit(solution)/shard_map/ppermute | solution.py:28
  615.9 54.4 %collective-permute-start.32 = (bf16[512,1024]{1,0:T(8,128)(2,1)}, bf16[512,1024]{1,0:T(8,128)(2,1)}, u32[]{:S(2)}, u32[]{:S(2)}) collective-permute-start(bf16[512,1024]{1,0:T(8,128)(2,1)} %fusion.27), channel_id=1, source_target_pairs={{0,4},{1,5},{2,6},{3,7},{4,0},{5,1},{6,2},{7,3},{8,12},{9,13},{10,... | collective-permute-start | bytes 3145736 | tf_op jit(solution)/shard_map/ppermute | solution.py:28
  648.6 196.3 %all-gather.10.cloned.1.call-start = ((), (), s32[]{:S(2)}) async-start(), calls=%async_computation.6 | async-start | bytes 9437184 | tf_op jit(solution)/shard_map/all_gather | solution.py:1022
  650.9 26.0 %collective-permute-start.35 = (bf16[256,2048]{1,0:T(8,128)(2,1)S(1)}, bf16[256,2048]{1,0:T(8,128)(2,1)}, u32[]{:S(2)}, u32[]{:S(2)}) collective-permute-start(bf16[256,2048]{1,0:T(8,128)(2,1)S(1)} %maximum_select_fusion.19), channel_id=1, source_target_pairs={{0,2},{1,3},{2,0},{3,1},{4,6},{5,7},{6,4},{7,5},{8,10},{9,11},{10,... | collective-permute-start | bytes 3145736 | tf_op jit(solution)/shard_map/ppermute | solution.py:28
  655.5 26.0 %collective-permute-start.38 = (bf16[512,1024]{1,0:T(8,128)(2,1)}, bf16[512,1024]{1,0:T(8,128)(2,1)}, u32[]{:S(2)}, u32[]{:S(2)}) collective-permute-start(bf16[512,1024]{1,0:T(8,128)(2,1)} %maximum_select_fusion.20), channel_id=1, source_target_pairs={{0,4},{1,5},{2,6},{3,7},{4,0},{5,1},{6,2},{7,3},{8,12},{9,13},{10,... | collective-permute-start | bytes 3145736 | tf_op jit(solution)/shard_map/ppermute | solution.py:28
  667.5 43.9 %collective-permute-start.42 = (bf16[1024,1024]{1,0:T(8,128)(2,1)}, bf16[1024,1024]{1,0:T(8,128)(2,1)}, u32[]{:S(2)}, u32[]{:S(2)}) collective-permute-start(bf16[1024,1024]{1,0:T(8,128)(2,1)} %dynamic-slice_bitcast_fusion.3), channel_id=1, source_target_pairs={{0,1},{1,0},{2,3},{3,2},{4,5},{5,4},{6,7},{7,6},{8,9},{9,8},{10,11... | collective-permute-start | bytes 6291464 | tf_op jit(solution)/shard_map/ppermute | solution.py:28
  668.5 24.1 %collective-permute-start.31 = (bf16[128,2048]{1,0:T(8,128)(2,1)S(1)}, bf16[128,2048]{1,0:T(8,128)(2,1)S(1)}, u32[]{:S(2)}, u32[]{:S(2)}) collective-permute-start(bf16[128,2048]{1,0:T(8,128)(2,1)S(1)} %fusion.33), channel_id=1, source_target_pairs={{0,4},{1,5},{2,6},{3,7},{4,0},{5,1},{6,2},{7,3},{8,12},{9,13},{10,... | collective-permute-start | bytes 1572872 | tf_op jit(solution)/shard_map/ppermute | solution.py:28
  679.4 35.9 %collective-permute-start.36 = (bf16[512,2048]{1,0:T(8,128)(2,1)S(1)}, bf16[512,2048]{1,0:T(8,128)(2,1)}, u32[]{:S(2)}, u32[]{:S(2)}) collective-permute-start(bf16[512,2048]{1,0:T(8,128)(2,1)S(1)} %maximum_select_fusion.10), channel_id=1, source_target_pairs={{0,1},{1,0},{2,3},{3,2},{4,5},{5,4},{6,7},{7,6},{8,9},{9,8},{10,11... | collective-permute-start | bytes 6291464 | tf_op jit(solution)/shard_map/ppermute | solution.py:28
  684.8 36.5 %collective-permute-start.39 = (bf16[1024,1024]{1,0:T(8,128)(2,1)S(1)}, bf16[1024,1024]{1,0:T(8,128)(2,1)}, u32[]{:S(2)}, u32[]{:S(2)}) collective-permute-start(bf16[1024,1024]{1,0:T(8,128)(2,1)S(1)} %maximum_select_fusion.11), channel_id=1, source_target_pairs={{0,1},{1,0},{2,3},{3,2},{4,5},{5,4},{6,7},{7,6},{8,9},{9,8},{10,11... | collective-permute-start | bytes 6291464 | tf_op jit(solution)/shard_map/ppermute | solution.py:28
  708.9 26.0 %collective-permute-start.46 = (bf16[256,2048]{1,0:T(8,128)(2,1)S(1)}, bf16[256,2048]{1,0:T(8,128)(2,1)S(1)}, u32[]{:S(2)}, u32[]{:S(2)}) collective-permute-start(bf16[256,2048]{1,0:T(8,128)(2,1)S(1)} %maximum_select_fusion.21), channel_id=1, source_target_pairs={{0,2},{1,3},{2,0},{3,1},{4,6},{5,7},{6,4},{7,5},{8,10},{9,11},{10,... | collective-permute-start | bytes 3145736 | tf_op jit(solution)/shard_map/ppermute | solution.py:28
  711.4 26.1 %collective-permute-start.49 = (bf16[512,1024]{1,0:T(8,128)(2,1)S(1)}, bf16[512,1024]{1,0:T(8,128)(2,1)S(1)}, u32[]{:S(2)}, u32[]{:S(2)}) collective-permute-start(bf16[512,1024]{1,0:T(8,128)(2,1)S(1)} %maximum_select_fusion.22), channel_id=1, source_target_pairs={{0,4},{1,5},{2,6},{3,7},{4,0},{5,1},{6,2},{7,3},{8,12},{9,13},{10,... | collective-permute-start | bytes 3145736 | tf_op jit(solution)/shard_map/ppermute | solution.py:28
  727.5 31.7 %collective-permute-start.43 = (bf16[512,1024]{1,0:T(8,128)(2,1)S(1)}, bf16[512,1024]{1,0:T(8,128)(2,1)S(1)}, u32[]{:S(2)}, u32[]{:S(2)}) collective-permute-start(bf16[512,1024]{1,0:T(8,128)(2,1)S(1)} %dynamic-slice_bitcast_fusion.2), channel_id=1, source_target_pairs={{0,4},{1,5},{2,6},{3,7},{4,0},{5,1},{6,2},{7,3},{8,12},{9,13},{10,... | collective-permute-start | bytes 3145736 | tf_op jit(solution)/shard_map/ppermute | solution.py:28
  729.4 32.0 %collective-permute-start.40 = (bf16[512,1024]{1,0:T(8,128)(2,1)S(1)}, bf16[512,1024]{1,0:T(8,128)(2,1)S(1)}, u32[]{:S(2)}, u32[]{:S(2)}) collective-permute-start(bf16[512,1024]{1,0:T(8,128)(2,1)S(1)} %dynamic-slice_bitcast_fusion.4), channel_id=1, source_target_pairs={{0,2},{1,3},{2,0},{3,1},{4,6},{5,7},{6,4},{7,5},{8,10},{9,11},{10,... | collective-permute-start | bytes 3145736 | tf_op jit(solution)/shard_map/ppermute | solution.py:28
  735.9 40.4 %collective-permute-start.47 = (bf16[512,2048]{1,0:T(8,128)(2,1)S(1)}, bf16[512,2048]{1,0:T(8,128)(2,1)}, u32[]{:S(2)}, u32[]{:S(2)}) collective-permute-start(bf16[512,2048]{1,0:T(8,128)(2,1)S(1)} %maximum_select_fusion.12), channel_id=1, source_target_pairs={{0,1},{1,0},{2,3},{3,2},{4,5},{5,4},{6,7},{7,6},{8,9},{9,8},{10,11... | collective-permute-start | bytes 6291464 | tf_op jit(solution)/shard_map/ppermute | solution.py:28
  739.8 42.5 %collective-permute-start.50 = (bf16[1024,1024]{1,0:T(8,128)(2,1)}, bf16[1024,1024]{1,0:T(8,128)(2,1)}, u32[]{:S(2)}, u32[]{:S(2)}) collective-permute-start(bf16[1024,1024]{1,0:T(8,128)(2,1)} %maximum_select_fusion.13), channel_id=1, source_target_pairs={{0,1},{1,0},{2,3},{3,2},{4,5},{5,4},{6,7},{7,6},{8,9},{9,8},{10,11... | collective-permute-start | bytes 6291464 | tf_op jit(solution)/shard_map/ppermute | solution.py:28
  793.7 23.6 %collective-permute-start.28 = (bf16[2,1,512,512]{3,2,1,0:T(8,128)(2,1)}, bf16[2,1,512,512]{3,2,1,0:T(8,128)(2,1)}, u32[]{:S(2)}, u32[]{:S(2)}) collective-permute-start(bf16[2,1,512,512]{3,2,1,0:T(8,128)(2,1)} %constant_dynamic-slice_fusion.1), channel_id=1, source_target_pairs={{0,8},{8,0},{16,24},{24,16},{1,9},{9,1},{17,25},{25,17},{2,10},{10... | collective-permute-start | bytes 3145736 | tf_op jit(solution)/shard_map/ppermute | solution.py:28
  819.7 23.7 %collective-permute-start.29 = (bf16[512,512]{1,0:T(8,128)(2,1)S(1)}, bf16[512,512]{1,0:T(8,128)(2,1)S(1)}, u32[]{:S(2)}, u32[]{:S(2)}) collective-permute-start(bf16[512,512]{1,0:T(8,128)(2,1)S(1)} %get-tuple-element.126), channel_id=1, source_target_pairs={{0,16},{8,24},{16,0},{24,8},{1,17},{9,25},{17,1},{25,9},{2,18},{10... | collective-permute-start | bytes 1572872 | tf_op jit(solution)/shard_map/ppermute | solution.py:28
  (46 other events, 779.0 us)
Sparse Core Ops, SparseCore 0:
  10.2 84.5 all-gather.7
  180.6 99.0 reduce-scatter.2
  397.6 81.9 all-gather.5
  648.7 76.9 reduce-scatter.4
  788.8 51.9 all-gather.9

commit v3 on v2

--- a/solution.py
+++ b/solution.py
@@ -62,36 +62,15 @@
     return value
 
 
-def scatter_sum(value, order, dim=0, waits=()):
-    values = []
-    for place, bit in enumerate(order):
-        keep, give = halves(value, "tok", bit, dim)
-        if place == 1 and waits:
-            give = after(give, *waits)
-        value = keep.astype(F32) + swapped(give.astype(BF), "tok", 1 << bit).astype(F32)
-        values.append(value)
-    return values
-
-
-def gather_back(value, order, dim=0):
+def gather_back(value, order):
     for bit in order[::-1]:
         other = swapped(value, "tok", 1 << bit)
-        value = joined(value, other, my_bit("tok", bit) == 0, dim)
+        value = joined(value, other, my_bit("tok", bit) == 0, 0)
     return value
 
 
-def in_order(pieces, order):
-    bits, shape = len(order), pieces.shape
-    pieces = pieces.reshape(*[2] * bits, *shape[1:])
-    pieces = pieces.transpose(*[bits - 1 - bit for bit in order], bits, bits + 1)
-    return pieces.reshape(shape[0] * shape[1], shape[2]).astype(F32)
-
-
-def far_swap(first, second):
-    rows = first.shape[0]
-    both = jnp.concatenate([first, second.reshape(-1, first.shape[1])], axis=0)
-    both = swapped(both, "head", lax.axis_size("head") // 2)
-    return both[:rows], both[rows:].reshape(second.shape)
+def far_swap(*values):
+    return [swapped(value, "head", lax.axis_size("head") // 2) for value in values]
 
 
 def side_bits():
@@ -105,6 +84,14 @@
     return value
 
 
+def scatter_side_start(value):
+    for bit in list(side_bits())[:0:-1]:
+        keep, give = halves(value, "head", bit, 1)
+        value = keep.astype(F32) + swapped(give.astype(BF), "head", 1 << bit).astype(F32)
+    give = halves(value, "head", 0, 1)[1]
+    return value, swapped(give.astype(BF), "head", 1)
+
+
 def scatter_side(value):
     for bit in list(side_bits())[::-1]:
         keep, give = halves(value, "head", bit, 1)
@@ -153,7 +140,7 @@
 SCALARS = pl.BlockSpec(memory_space=pltpu.SMEM)
 
 
-def call(kernel, rows, in_specs, outs, out_specs, scratch=()):
+def call(kernel, rows, in_specs, outs, out_specs, scratch=(), flops=0):
     return pl.pallas_call(
         kernel,
         grid=(rows // TILE,),
@@ -161,7 +148,7 @@
         out_specs=out_specs,
         out_shape=[jax.ShapeDtypeStruct(shape, dtype) for shape, dtype in outs],
         scratch_shapes=list(scratch),
-        cost_estimate=pl.CostEstimate(flops=0, bytes_accessed=0, transcendentals=0),
+        cost_estimate=pl.CostEstimate(flops=flops, bytes_accessed=0, transcendentals=0),
         compiler_params=pltpu.CompilerParams(vmem_limit_bytes=VMEM_LIMIT),
     )
 
@@ -342,11 +329,6 @@
         mean = jnp.mean(grad_group, axis=1, keepdims=True)
         cross = jnp.mean(grad_group * grouped, axis=1, keepdims=True)
         mix_out[:, wide] = (scale[:, h : h + 1] * (grad_group - mean - grouped * cross)).astype(BF)
-
-
-def outer_kernel(gated, grad, out):
-    rows = jnp.concatenate([grad[0, 0, 0], grad[1, 0, 0]], axis=0)
-    out[...] = dot_tn(gated[...], rows).astype(BF)
 
 
 def back_kernel(
@@ -527,6 +509,18 @@
         lax.fori_loop(0, steps, finish, 0)
 
 
+def branch_kernel(full, mine, keep, other, hidden, grads, gain, stat, near, far, out):
+    total_rows = (near[...] + far[...]) * (1.0 / full)
+    upstream = keep[0, 0].astype(F32) + other[0, 0].astype(F32)
+    scale = stat[:, 1:2]
+    normed = (hidden[0] - stat[:, 0:1]) * scale
+    out[0] = (
+        grads[0].astype(F32)
+        + scale
+        * (upstream * gain[0] - total_rows[:, 0:1] - normed * total_rows[:, 1:2])
+    ).astype(BF)
+
+
 def lower_kernel(act, down_near, down_far, out):
     units = down_near.shape[0]
     part = (dot(act[:, :units], down_near[...]) + dot(act[:, units:], down_far[...])).astype(BF)
@@ -537,28 +531,225 @@
             out[f, side] = part[:, first : first + width]
 
 
-def weight_kernel(left, *rights):
-    out = rights[-1]
-    first = 0
-    for right in rights[:-1]:
-        width = right.shape[1]
-        out[:, first : first + width] = dot_tn(left[...], right[...]).astype(BF)
-        first += width
-
-
-def weight_grad(left, *rights):
+def prefetched(kernel, grid, in_specs, out_specs, outs):
+    return pl.pallas_call(
+        kernel,
+        grid_spec=pltpu.PrefetchScalarGridSpec(
+            num_scalar_prefetch=1, grid=grid, in_specs=in_specs, out_specs=out_specs
+        ),
+        out_shape=[jax.ShapeDtypeStruct(shape, dtype) for shape, dtype in outs],
+        cost_estimate=pl.CostEstimate(flops=0, bytes_accessed=0, transcendentals=0),
+        compiler_params=pltpu.CompilerParams(vmem_limit_bytes=VMEM_LIMIT),
+    )
+
+
+def bit_value(bit):
+    return my_bit("tok", bit)[None].astype(jnp.int32)
+
+
+def split_source(groups, rows, block):
+    per_half = rows // (2 * block)
+    count = groups * per_half
+
+    def source(i, mine):
+        keeps = (i >= count).astype(jnp.int32)
+        half = jnp.where(keeps == 1, mine[0], 1 - mine[0])
+        j = i - keeps * count
+        return (j // per_half) * (2 * per_half) + half * per_half + j % per_half
+
+    give = lambda i, mine: (jnp.minimum(i, count - 1), 0)
+    keep = lambda i, mine: (jnp.maximum(i - count, 0), 0)
+    return count, source, give, keep
+
+
+def weight_kernel(count, mine, left, *refs):
+    give, keep = refs[-2:]
+
+    def fill(out):
+        first = 0
+        for right in refs[:-2]:
+            width = right.shape[1]
+            out[:, first : first + width] = dot_tn(left[...], right[...]).astype(BF)
+            first += width
+
+    @pl.when(pl.program_id(0) < count)
+    def _():
+        fill(give)
+
+    @pl.when(pl.program_id(0) >= count)
+    def _():
+        fill(keep)
+
+
+def weight_grad(bit, groups, left, *rights):
     rows, columns = left.shape
     width = sum(right.shape[1] for right in rights)
+    block = min(CHUNK, columns // groups // 2)
+    count, source, give, keep = split_source(groups, columns // groups, block)
+    half = (columns // 2, width)
+    return prefetched(
+        partial(weight_kernel, count),
+        (2 * count,),
+        [pl.BlockSpec((rows, block), lambda i, mine: (0, source(i, mine)))]
+        + [
+            pl.BlockSpec(right.shape, lambda i, mine: (0, 0), pipeline_mode=pl.Buffered(1))
+            for right in rights
+        ],
+        [pl.BlockSpec((block, width), give), pl.BlockSpec((block, width), keep)],
+        [(half, BF), (half, BF)],
+    )(bit_value(bit), left, *rights)
+
+
+def turned_place(i, order):
+    place = 0
+    for k, bit in enumerate(order):
+        place = place + (((i >> (len(order) - 1 - k)) & 1) << bit)
+    return place
+
+
+def outer_kernel(mine, gated, grad, give, keep):
+    part = dot_tn(gated[...], jnp.concatenate([grad[0, 0, 0], grad[1, 0, 0]], axis=0)).astype(BF)
+    half = give.shape[0]
+
+    @pl.when(mine[0] == 0)
+    def _():
+        keep[...] = part[:half]
+        give[...] = part[half:]
+
+    @pl.when(mine[0] == 1)
+    def _():
+        keep[...] = part[half:]
+        give[...] = part[:half]
+
+
+def fold_kernel(count, mine, one, two, give, keep):
+    total = (one[...].astype(F32) + two[...].astype(F32)).astype(BF)
+
+    @pl.when(pl.program_id(0) < count)
+    def _():
+        give[...] = total
+
+    @pl.when(pl.program_id(0) >= count)
+    def _():
+        keep[...] = total
+
+
+def fold(bit, groups, one, two):
+    rows, columns = one.shape
+    block = min(CHUNK // 2, rows // groups // 2)
+    count, source, give, keep = split_source(groups, rows // groups, block)
+    spec = pl.BlockSpec((block, columns), lambda i, mine: (source(i, mine), 0))
+    half = (rows // 2, columns)
+    return prefetched(
+        partial(fold_kernel, count),
+        (2 * count,),
+        [spec, spec],
+        [pl.BlockSpec((block, columns), give), pl.BlockSpec((block, columns), keep)],
+        [(half, BF), (half, BF)],
+    )(bit_value(bit), one, two)
+
+
+def scatter_rest(give, keep, order, groups=1, waits=None):
+    values, others = [], []
+    for place, bit in enumerate(order):
+        if waits and place in waits:
+            give = after(give, *waits[place])
+        other = swapped(give, "tok", 1 << bit)
+        others.append(other)
+        if place + 1 < len(order):
+            give, keep = fold(order[place + 1], groups, keep, other)
+            values.append(give)
+        else:
+            values.append((keep, other))
+    return values, others
+
+
+def total(pair):
+    return pair[0].astype(F32) + pair[1].astype(F32)
+
+
+def spread_kernel(per_half, mine, near, other, out):
+    here = pl.program_id(0) // per_half == mine[0]
+
+    @pl.when(here)
+    def _():
+        out[...] = near[...].astype(out.dtype)
+
+    @pl.when(jnp.logical_not(here))
+    def _():
+        out[...] = other[...].astype(out.dtype)
+
+
+def gather_one(value, bit):
+    return joined(value, swapped(value, "tok", 1 << bit), my_bit("tok", bit) == 0, 0)
+
+
+def gather_wide(value, order):
+    for bit in order[:0:-1]:
+        value = gather_one(value, bit)
+    bit = order[0]
+    other = swapped(value, "tok", 1 << bit)
+    rows, columns = value.shape
+    block = min(CHUNK // 2, rows)
+    per_half = rows // block
+
+    def spec(mirror):
+        def index(i, mine):
+            half = 1 - mine[0] if mirror else mine[0]
+            return (jnp.clip(i - half * per_half, 0, per_half - 1), 0)
+
+        return pl.BlockSpec((block, columns), index)
+
+    return prefetched(
+        partial(spread_kernel, per_half),
+        (2 * per_half,),
+        [spec(False), spec(True)],
+        [pl.BlockSpec((block, columns), lambda i, mine: (i, 0))],
+        [((2 * rows, columns), F32)],
+    )(bit_value(bit), value, other)[0], value
+
+
+def order_kernel(split, first, second, one_out, two_out, *rest):
+    rows, columns = one_out.shape[0], first.shape[2]
+    for i in range(first.shape[1] // rows):
+        at = slice(i * columns, (i + 1) * columns)
+        one_out[:, at] = first[0, i * rows : (i + 1) * rows].astype(F32)
+    if rest:
+        two_out[...] = second[0, :, :split].astype(F32)
+        rest[0][...] = second[0, :, split:].astype(F32)
+    else:
+        two_out[...] = second[0].astype(F32)
+
+
+def packed_pieces(first, second):
+    columns = second.shape[1]
+    parts = [first[:, i : i + columns] for i in range(0, first.shape[1], columns)]
+    return jnp.concatenate([*parts, second], axis=0)
+
+
+def in_order(pieces, first, order_one, order_two, split=None):
+    count, rows, columns = pieces.shape
+    half = rows // 2
+
+    def spec(order, which):
+        return pl.BlockSpec(
+            (1, half, columns), lambda i: (turned_place(i, order), which, 0)
+        )
+
+    shapes = [first]
+    if split:
+        shapes += [(half, split), (half, columns - split)]
+    else:
+        shapes += [(half, columns)]
     return pl.pallas_call(
-        weight_kernel,
-        grid=(columns // CHUNK,),
-        in_specs=[pl.BlockSpec((rows, CHUNK), lambda i: (0, i))]
-        + [whole(*right.shape) for right in rights],
-        out_specs=pl.BlockSpec((CHUNK, width), lambda i: (i, 0)),
-        out_shape=jax.ShapeDtypeStruct((columns, width), BF),
+        partial(order_kernel, split),
+        grid=(count,),
+        in_specs=[spec(order_one, 0), spec(order_two, 1)],
+        out_specs=[pl.BlockSpec(shape, lambda i: (i, 0)) for shape in shapes],
+        out_shape=[jax.ShapeDtypeStruct((count * high, wide), F32) for high, wide in shapes],
         cost_estimate=pl.CostEstimate(flops=0, bytes_accessed=0, transcendentals=0),
         compiler_params=pltpu.CompilerParams(vmem_limit_bytes=VMEM_LIMIT),
-    )(left, *rights)
+    )(pieces, pieces)
 
 
 def body(
@@ -604,18 +795,11 @@
     vectors = vectors.reshape(4, full_width)
 
     order_one, order_two = bit_orders()
+    late_grad = after(out_grad, rows_raw)
+    grad_keep, grad_give = halves(late_grad, "head", shards.bit_length() - 2, 0)
+    grad_seen = swapped(grad_give, "head", sides)
     up_piece, down_piece = own_piece(up_weight, order_one), own_piece(down_weight, order_two)
-    late_up, late_down, late_grad, _ = lax.optimization_barrier(
-        (up_piece, down_piece, out_grad, rows_raw)
-    )
-    up_seen, down_seen = far_swap(late_up, late_down)
-    grad_keep, grad_give = halves(late_grad, "head", shards.bit_length() - 2, 0)
-    side_grads = joined(
-        grad_keep[None], swapped(grad_give, "head", sides)[None], spread == 0, 0
-    )
-    grad_rows = gather_side(side_grads[:, None]).reshape(shards, half_rows, width)
-    up_other = gather_back(up_seen, order_one)
-    down_other = gather_back(down_seen, order_two)
+    both_pieces = jnp.concatenate([up_piece, down_piece.reshape(up_piece.shape)], axis=0)
 
     first_head = lax.axis_index("head") * heads_here
     log_decay = jnp.log(
@@ -687,6 +871,14 @@
         end_factor,
     )
     one_back, two_back, three_back = (shifted(summary, by) for by in (1, 2, 3))
+    grad_seen = after(grad_seen, summary)
+    side_grads = joined(grad_keep[None], grad_seen[None], spread == 0, 0)
+    grad_rows = gather_side(side_grads[:, None]).reshape(shards, half_rows, width)
+    (both_seen,) = far_swap(after(both_pieces, grad_seen))
+    up_seen = both_seen[: up_piece.shape[0]]
+    down_seen = both_seen[up_piece.shape[0] :].reshape(down_piece.shape)
+    up_other = gather_back(up_seen, order_one)
+    down_other = gather_back(down_seen, order_two)
     gate_pre, inner_part = call(
         partial(inner_kernel, heads_here),
         row_count,
@@ -704,7 +896,7 @@
         [((row_count, value_width), F32)] * 2,
         [tiles(value_width)] * 2,
     )(
-        log_decay,
+        after(log_decay, side_grads),
         rows_first,
         gate_weight,
         query_rot,
@@ -746,7 +938,7 @@
             tiles(heads_here),
         ],
     )(
-        after(log_decay, side_grads),
+        log_decay,
         inner_part,
         query_rot,
         one_back,
@@ -757,7 +949,7 @@
         pads_col,
         output_weight,
     )
-    mix_part = after(mix_part, up_seen, down_seen)
+    mix_part = after(mix_part, grad_rows, both_seen)
     side_tokens = lax.dynamic_index_in_dim(
         lax.dynamic_slice_in_dim(rows_raw, spread * half_rows, half_rows, axis=1).reshape(
             2, sides, half_rows, width
@@ -769,7 +961,7 @@
     mixed_sum = lax.psum_scatter(
         mix_part.reshape(shards, 2, half_rows, width), "head", scatter_dimension=0
     )
-    hidden = side_tokens.astype(F32) + mixed_sum.astype(F32)
+    hidden = lax.optimization_barrier(side_tokens.astype(F32) + mixed_sum.astype(F32))
     hidden_rows = gather_side(hidden.astype(BF)[:, None]).reshape(shards, half_rows, width)
     units = up_weight.shape[1]
     chunks = units // CHUNK
@@ -811,15 +1003,42 @@
             compiler_params=pltpu.CompilerParams(vmem_limit_bytes=VMEM_LIMIT),
         )(hidden_rows, grad_rows, vectors, up_weight, up_other, down_weight, down_other)
     )
-    grad_ln2 = scatter_side(feed_part)
-    row_second = sum_side(row_second) / full_width
-    norm_second = (hidden - stats_second[None, :, 0:1]) * stats_second[None, :, 1:2]
-    grad_hidden = side_grads.astype(F32) + stats_second[None, :, 1:2] * (
-        grad_ln2 * side_vectors[2][:, None, :]
-        - row_second[None, :, 0:1]
-        - norm_second * row_second[None, :, 1:2]
-    )
-    grad_branch = lax.all_gather(grad_hidden.astype(BF), "head", axis=0).reshape(
+    feed_value, feed_seen = scatter_side_start(feed_part)
+    for bit in list(side_bits())[:0:-1]:
+        row_second = row_second + swapped(row_second, "head", 1 << bit)
+    row_seen = swapped(row_second, "head", 1)
+    down_give, down_keep = weight_grad(order_one[0], 2, act_low, grad_plain)
+    up_give, up_keep = weight_grad(order_two[0], 1, rows_second, grad_up)
+    row_seen = after(row_seen, down_give, up_give)
+    half_block = pl.BlockSpec((1, TILE, width), lambda f, i, mine: (f, i, 0))
+    row_block = pl.BlockSpec((TILE, 2), lambda f, i, mine: (i, 0))
+    (branch,) = prefetched(
+        partial(branch_kernel, full_width),
+        (2, half_rows // TILE),
+        [
+            pl.BlockSpec((1, 1, TILE, width), lambda f, i, mine: (f, mine[0], i, 0)),
+            pl.BlockSpec((1, 1, TILE, width), lambda f, i, mine: (f, 0, i, 0)),
+            half_block,
+            half_block,
+            pl.BlockSpec((1, 1, width), lambda f, i, mine: (f, 0, 0)),
+            row_block,
+            row_block,
+            row_block,
+        ],
+        [half_block],
+        [((2, half_rows, width), BF)],
+    )(
+        my_bit("head", 0)[None].astype(jnp.int32),
+        feed_value,
+        feed_seen[:, None] if feed_seen.ndim == 3 else feed_seen,
+        hidden,
+        side_grads,
+        side_vectors[2][:, None, :],
+        stats_second,
+        row_second,
+        row_seen,
+    )
+    grad_branch = lax.all_gather(branch, "head", axis=0).reshape(
         2, sides, 2, half_rows, width
     )
 
@@ -831,28 +1050,13 @@
         out_shape=jax.ShapeDtypeStruct((2, sides, half_rows, width), BF),
         cost_estimate=pl.CostEstimate(flops=0, bytes_accessed=0, transcendentals=0),
         compiler_params=pltpu.CompilerParams(vmem_limit_bytes=VMEM_LIMIT),
-    )(act_low, down_weight, down_other)
-
-    branch = grad_hidden.astype(BF)
-    grad_down = weight_grad(after(act_low, branch), grad_plain)
-    grad_down = grad_down.reshape(2, units, full_width)
-    grad_upw = weight_grad(rows_second, after(grad_up, branch))
-    down_sum = scatter_sum(grad_down, order_one, 1)
-    up_sum = scatter_sum(grad_upw, order_two)
-
-    grad_outw = pl.pallas_call(
-        outer_kernel,
-        grid=(shards,),
-        in_specs=[
-            whole(row_count, value_width),
-            pl.BlockSpec((2, 1, 1, half_rows, width), lambda i: (0, i % sides, i // sides, 0, 0)),
-        ],
-        out_specs=pl.BlockSpec((value_width, width), lambda i: (0, i)),
-        out_shape=jax.ShapeDtypeStruct((value_width, full_width), BF),
-        cost_estimate=pl.CostEstimate(flops=0, bytes_accessed=0, transcendentals=0),
-        compiler_params=pltpu.CompilerParams(vmem_limit_bytes=VMEM_LIMIT),
-    )(after(gated, down_sum[1], up_sum[1]), grad_branch)
-    outw_sum = scatter_sum(grad_outw, order_one)
+    )(after(act_low, branch), down_weight, down_other)
+
+    down_sum, _ = scatter_rest(
+        down_give, down_keep, order_one, 2, {0: (branch,), len(order_one) - 1: (down_part,)}
+    )
+    up_sum, _ = scatter_rest(up_give, up_keep, order_two, 1, {0: (branch,)})
+
     dgate, grad_mixed = call(
         partial(gate_kernel, heads_here),
         row_count,
@@ -872,13 +1076,16 @@
         gate_pre,
         flat_group,
         group_scale,
-        after(pads_col, grad_outw),
-    )
-    up_last, down_last = up_sum[-1], down_sum[-1]
-    up_far, down_far = far_swap(up_last[:, units:].astype(BF), down_last[1].astype(BF))
-    down_near = down_last[0] + down_far.astype(F32)
-    up_near = up_last[:, :units] + up_far.astype(F32)
-    grad_gw = weight_grad(rows_first, dgate)
+        pads_col,
+    )
+    half_down = down_sum[-1][0].shape[0] // 2
+    up_pair = lax.optimization_barrier((*up_sum[-1], dgate))[:2]
+    down_pair = lax.optimization_barrier((*down_sum[-1], dgate))[:2]
+    up_give = total([part[:, units:] for part in up_pair]).astype(BF)
+    down_give = total([part[half_down:] for part in down_pair]).astype(BF)
+    up_far, down_far = far_swap(up_give, down_give)
+    up_near = total([part[:, :units] for part in up_pair]) + up_far.astype(F32)
+    down_near = total([part[:half_down] for part in down_pair]) + down_far.astype(F32)
     dq, dk_part, dv_part, grad_state = call(
         partial(back_kernel, heads_here),
         row_count,
@@ -910,9 +1117,10 @@
             held(*sent_shape),
         ],
         [states],
+        10 * row_count * full_width * value_width,
     )(
         last_docs,
-        after(log_decay, down_last, up_last, outw_sum[0], down_part),
+        after(log_decay, down_part, up_give, down_give),
         grad_mixed,
         query_rot,
         key_rot,
@@ -925,7 +1133,24 @@
         cosine,
         sine,
     )
-    gw_sum = scatter_sum(grad_gw, order_two)
+    width_out = (value_width // 2, full_width)
+    outw_give, outw_keep = prefetched(
+        outer_kernel,
+        (shards,),
+        [
+            pl.BlockSpec(
+                (row_count, value_width), lambda i, mine: (0, 0), pipeline_mode=pl.Buffered(1)
+            ),
+            pl.BlockSpec(
+                (2, 1, 1, half_rows, width), lambda i, mine: (0, i % sides, i // sides, 0, 0)
+            ),
+        ],
+        [pl.BlockSpec((value_width // 2, width), lambda i, mine: (0, i))] * 2,
+        [(width_out, BF), (width_out, BF)],
+    )(bit_value(order_one[0]), after(gated, dq), grad_branch)
+    outw_sum, outw_seen = scatter_rest(outw_give, outw_keep, order_one)
+    gw_give, gw_keep = weight_grad(order_two[0], 1, rows_first, after(dgate, dq))
+    gw_sum, gw_seen = scatter_rest(gw_give, gw_keep, order_two)
     one_on, two_on, three_on = (shifted(grad_state, -by) for by in (1, 2, 3))
     dk, dv, last_part, row_sums, column_first = call(
         partial(finish_kernel, heads_here, row_count),
@@ -968,9 +1193,10 @@
             held(2, full_width),
         ],
         [pltpu.VMEM(state_shape, BF)],
+        12 * row_count * full_width * value_width,
     )(
         last_docs,
-        after(log_decay, down_near, up_near, outw_sum[1], gw_sum[0]),
+        after(log_decay, outw_sum[0], gw_give),
         dk_part,
         dv_part,
         key_rot,
@@ -999,6 +1225,12 @@
         [jnp.broadcast_to(line[None], (shards, *line.shape)), columns.transpose(1, 0, 2)], axis=1
     )
     last_part = lax.dynamic_update_slice_in_dim(last_part, extra.astype(BF), row_count, axis=1)
+    down_low, up_low = down_near.astype(BF), up_near.astype(BF)
+    down_next = swapped(down_low, "tok", 1 << order_one[-1])
+    up_next = swapped(up_low, "tok", 1 << order_two[-1])
+    last_part = after(last_part, down_far, up_far, outw_seen[1], gw_seen[0])
+    down_back = joined(down_low, down_next, my_bit("tok", order_one[-1]) == 0, 0)
+    up_back = joined(up_low, up_next, my_bit("tok", order_two[-1]) == 0, 0)
     last_sum = lax.psum_scatter(last_part, "head", scatter_dimension=0).astype(F32)
     grad_ln1 = last_sum[:row_count]
     sums_first = last_sum[row_count:, :TILE] / full_width
@@ -1007,28 +1239,28 @@
         axis=1,
     )
     columns = lax.psum(last_sum[row_count + EXTRA - 4 :], "tok")
-    grad_vw = weight_grad(rows_first, dv)
-    grad_qkw = weight_grad(rows_first, dq, dk)
-
-    down_back = gather_back(down_near.astype(BF), order_one)
-    up_back = gather_back(up_near.astype(BF), order_two)
-    grad_down, grad_upw = down_back.astype(F32), up_back.astype(F32)
-    waits = (outw_sum[-1], gw_sum[-1], down_back, up_back)
-    vw_sum = scatter_sum(grad_vw, order_one, 0, waits)[-1].astype(BF)
-    qkw_sum = scatter_sum(grad_qkw, order_two, 0, waits)[-1].astype(BF)
-    grad_outw = gather_back(outw_sum[-1].astype(BF), order_one).astype(F32)
-    grad_gw = gather_back(gw_sum[-1].astype(BF), order_two).astype(F32)
-    pieces = after(jnp.stack([vw_sum, qkw_sum]), grad_outw, grad_gw, grad_down, grad_upw)
-    pieces = lax.all_gather(pieces, "tok", axis=0)
-    grad_vw = in_order(pieces[:, 0], order_one)
-    grad_qkw = in_order(pieces[:, 1], order_two)
-    grad_qw, grad_kw = grad_qkw[:, :inner_width], grad_qkw[:, inner_width:]
-
-    late_down_part = after(down_part, last_sum)
-    result = (hidden + scatter_side(late_down_part)).astype(BF)
+    result = (hidden + scatter_side(after(down_part, last_sum))).astype(BF)
     result_keep = lax.dynamic_index_in_dim(result, spread, 0, keepdims=False)
     result_give = lax.dynamic_index_in_dim(result, 1 - spread, 0, keepdims=False)
     layer_out = joined(result_keep, swapped(result_give, "head", sides), spread == 0, 0)
+
+    vw_give, vw_keep = weight_grad(order_one[0], 1, rows_first, dv)
+    qkw_give, qkw_keep = weight_grad(order_two[0], 1, rows_first, dq, dk)
+    grad_down, down_back = gather_wide(down_back, order_one[:-1])
+    grad_upw, up_back = gather_wide(up_back, order_two[:-1])
+    outw_low, gw_low = total(outw_sum[-1]).astype(BF), total(gw_sum[-1]).astype(BF)
+    waits = {1: (gw_sum[0],), 2: (outw_sum[1], gw_sum[1])}
+    vw_sum, _ = scatter_rest(vw_give, vw_keep, order_one, 1, waits)
+    qkw_sum, _ = scatter_rest(qkw_give, qkw_keep, order_two, 1, waits)
+    gates = (last_sum, vw_sum[0], qkw_sum[0], down_back, up_back)
+    middle = lax.all_gather(after(packed_pieces(outw_low, gw_low), *gates), "tok", axis=0)
+    grad_outw, grad_gw = in_order(middle, outw_low.shape, order_one, order_two)
+    vw_low, qkw_low = total(vw_sum[-1]).astype(BF), total(qkw_sum[-1]).astype(BF)
+    pieces = after(packed_pieces(vw_low, qkw_low), grad_down, grad_upw, middle, result)
+    pieces = lax.all_gather(pieces, "tok", axis=0)
+    grad_vw, grad_qw, grad_kw = in_order(
+        pieces, vw_low.shape, order_one, order_two, inner_width
+    )
 
     norm_first = (tokens.astype(F32) - stats[:, 0:1]) * stats[:, 1:2]
     branch_rows = lax.dynamic_index_in_dim(

time: 874 us -> 805 us (0.921)
  Pallas kernels: 202 us -> 298 us
  other arithmetic: 135 us -> 57.1 us
  waiting for transfers between devices: 364 us -> 313 us
  local copies, waits for them, and re-layouts: 72.5 us -> 32.6 us
    pallas_call x6 -> x23, Pallas kernels: 50.7 us -> 146 us  [the longest x12 53.4 us: fold(): prefetched(partial(fold_kernel, count), (2 * count,), [spec, spec], [pl.B...]
    ppermute x45 -> x40, waiting for transfers between devices: 231 us -> 191 us  [swapped(): lax.ppermute(value, axis, [(i, i ^ mask) for i in range(lax.axis_size(axi...]
    add x18 -> x1, other arithmetic: 38.8 us -> 1.86 us  [body(): side_tokens.astype(F32) + mixed_sum.astype(F32)]
    convert_element_type x9, other arithmetic: 33.7 us -> 9.93 us  [the longest x2 3.05 us: body(): down_low, up_low = (down_near.astype(BF), up_near.astype(BF))]
    squeeze x10 -> x2, local copies, waits for them, and re-layouts: 23.9 us -> 2.39 us  [halves(): give = lax.dynamic_index_in_dim(pieces, 1 - mine, dim, keepdims=False)]
    reduce_scatter x1, waiting for transfers between devices: 48.3 us -> 27.6 us  [body(): lax.psum_scatter(mix_part.reshape(shards, 2, half_rows, width), 'head', s...]
    select_n x18 -> x15, other arithmetic: 42.9 us -> 27.8 us  [joined(): jnp.where(first, jnp.concatenate([value, other], axis=axis), jnp.concaten...]
    convert_element_type x14 -> x0, local copies, waits for them, and re-layouts: 14.2 us -> none  [the longest x10 7.79 us: scatter_sum(): give.astype(BF)]
  transfers between devices with their start and end apart: 56 -> 52, of which waited for: 23 -> 22; matrix products, arithmetic and copies ran while one was open for 20% -> 9% of each run, Pallas kernels for 19% -> 28%
where the time goes in v3:
time: 805 us; the launch traced here: 794 us
  waiting for transfers between devices  313 us (39%)
  Pallas kernels  298 us (37%)
  starting transfers between devices  65.3 us (8%)
  other arithmetic  57.1 us (7%)
  local copies, waits for them, and re-layouts  32.6 us (4%)
  between operations  15.4 us (2%)
  blocking collectives  13.5 us (2%)
    ppermute x40, waiting for transfers between devices, swapped(): lax.ppermute(value, axis, [(i, i ^ mask) for i in range(lax.axis_size(axi...  191 us
    all_gather x1, waiting for transfers between devices, body(): rows_raw = lax.all_gather(packed, 'head', axis=0)  80.8 us
    pallas_call x12, Pallas kernels, fold(): prefetched(partial(fold_kernel, count), (2 * count,), [spec, spec], [pl.B...  53.4 us
    ppermute x40, starting transfers between devices, swapped(): lax.ppermute(value, axis, [(i, i ^ mask) for i in range(lax.axis_size(axi...  50.5 us
    pallas_call x5, Pallas kernels, weight_grad(): prefetched(partial(weight_kernel, count), (2 * count,), [pl.BlockSpec((ro...  45 us
    select_n x15, other arithmetic, joined(): jnp.where(first, jnp.concatenate([value, other], axis=axis), jnp.concaten...  27.8 us
    reduce_scatter x1, waiting for transfers between devices, body(): lax.psum_scatter(mix_part.reshape(shards, 2, half_rows, width), 'head', s...  27.6 us
    pallas_call x1, Pallas kernels, body(): call(partial(finish_kernel, heads_here, row_count), row_count, [SCALARS,...  27.2 us
  transfers between devices with their start and end apart: 52, of which 22 were waited for; matrix products, arithmetic and copies ran while one was open for 9% of the time, Pallas kernels for 28%

profile of v3, /device:TPU:0, one launch (start us, length us, event | category | flops | bytes accessed | tf_op | source)
XLA Modules:
  0.0 794.5 jit_solution(16290102464588689237)
XLA Ops:
  14.0 80.8 %all-gather.9.cloned.1.call-done = bf16[4160,512]{1,0:T(8,128)(2,1)} async-done(((bf16[1040,512]{1,0:T(8,128)(2,1)}), bf16[4160,512]{1,0:T(8,128)(2,1)}) %all-gather.9.cloned.1.call-update) | async-done | bytes 4259856 | tf_op jit(solution)/shard_map/all_gather | solution.py:787
  102.2 19.2 %shard_map.247 = (bf16[1024,2048]{1,0:T(8,128)(2,1)}, bf16[1024,512]{1,0:T(8,128)(2,1)}, bf16[1024,512]{1,0:T(8,128)(2,1)}, bf16[1024,1024]{1,0:T(8,128)(2,1)}, ...) custom-call(s32[1]{0:T(128)} %slice.102.docs, bf16[4,1040,512]{2,1,0:T(8,128)(2,1)} %bitcast.106, ...), custom_call_target="tpu_custom_call" | custom-call | tf_op jit(solution)/shard_map/pallas_call | solution.py:831
  139.2 18.0 %shard_map.248 = (f32[1024,1024]{1,0:T(8,128)}, f32[1024,1024]{1,0:T(8,128)}) custom-call(f32[2]{0:T(128)} %copy-done.34, bf16[1024,2048]{1,0:T(8,128)(2,1)} %get-tuple-element.117.low.left, bf16[2048,1024]{1,0:T(8,128)(2,1)} %wg.3, bf16[1024,512]{1,0:T(8,128)(2,1)} %get-tuple-element.118.q, bf16[1024,512]{1,0:T(8,128)(2,1)} %get-tuple-element.119.k, ...), custom_call_target="tpu_custom_call" | custom-call | tf_op jit(solution)/shard_map/pallas_call | solution.py:882
  157.2 14.0 %shard_map.249 = (f32[1024,1024]{1,0:T(8,128)}, f32[1024,2]{1,0:T(8,128)}, bf16[1024,1024]{1,0:T(8,128)(2,1)}, bf16[2,2,2,512,512]{4,3,2,1,0:T(8,128)(2,1)}, bf1...) custom-call(f32[2]{0:T(128)} %copy-done.34, f32[1024,1024]{1,0:T(8,128)} %get-tuple-element.121.inner, ...), custom_call_target="tpu_custom_call" | custom-call | tf_op jit(solution)/shard_map/pallas_call | solution.py:909
  175.2 5.8 collective-permute-start.7
  181.3 11.2 %collective-permute-done.7 = bf16[256,1024]{1,0:T(8,128)(2,1)S(1)} collective-permute-done((bf16[256,1024]{1,0:T(8,128)(2,1)S(1)}, bf16[256,1024]{1,0:T(8,128)(2,1)S(1)}, u32[]{:S(2)}, u32[]{:S(2)}) %collective-permute-start.7) | collective-permute-done | bytes 524320 | tf_op jit(solution)/shard_map/ppermute | solution.py:28
  195.3 21.8 %collective-permute-done.8 = bf16[512,1024]{1,0:T(8,128)(2,1)} collective-permute-done((bf16[512,1024]{1,0:T(8,128)(2,1)S(1)}, bf16[512,1024]{1,0:T(8,128)(2,1)}, u32[]{:S(2)}, u32[]{:S(2)}) %collective-permute-start.8) | collective-permute-done | bytes 1048608 | tf_op jit(solution)/shard_map/ppermute | solution.py:28
  226.7 27.6 %reduce-scatter.3.cloned.1.call-done = bf16[1,2,512,512]{3,2,1,0:T(8,128)(2,1)} async-done(((bf16[4,2,512,512]{3,2,1,0:T(8,128)(2,1)}), bf16[1,2,512,512]{3,2,1,0:T(8,128)(2,1)}) %reduce-scatter.3.cloned.1.call-update) | async-done | bytes 1048592 | tf_op jit(solution)/shard_map/reduce_scatter | solution.py:961
  258.4 4.8 maximum_select_fusion.up_far
  263.2 6.1 maximum_select_fusion.1.down_far
  269.2 12.0 %collective-permute-done.6 = bf16[2,1,512,512]{3,2,0,1:T(8,128)(2,1)S(1)} collective-permute-done((bf16[2,1,512,512]{3,2,0,1:T(8,128)(2,1)S(1)}, bf16[2,1,512,512]{3,2,0,1:T(8,128)(2,1)S(1)}, u32[]{:S(2)}, u32[]{:S(2)}) %collective-permute-start.6) | collective-permute-done | bytes 1048608 | tf_op jit(solution)/shard_map/ppermute | solution.py:28
  283.1 27.0 %shard_map.250 = (bf16[512,2048]{1,0:T(8,128)(2,1)}, bf16[512,2048]{1,0:T(8,128)(2,1)}, bf16[512,2048]{1,0:T(8,128)(2,1)}, bf16[512,2048]{1,0:T(8,128)(2,1)}, bf...) custom-call(bf16[4,512,512]{2,1,0:T(8,128)(2,1)} %bitcast.117, ...), custom_call_target="tpu_custom_call" | custom-call | tf_op jit(solution)/shard_map/pallas_call | solution.py:969
  314.8 9.3 %shard_map.251 = (bf16[1024,2048]{1,0:T(8,128)(2,1)}, bf16[1024,2048]{1,0:T(8,128)(2,1)}) custom-call(s32[1]{0:T(128)} %bitcast.34.mine, bf16[512,2048]{1,0:T(8,128)(2,1)} %get-tuple-element.136.left.act, bf16[512,2048]{1,0:T(8,128)(2,1)} %get-tuple-element.130.refs_0_), custom_call_target="tpu_custom_call" | custom-call | tf_op jit(solution)/shard_map/pallas_call | solution.py:590
  324.1 9.2 %shard_map.252 = (bf16[1024,2048]{1,0:T(8,128)(2,1)}, bf16[1024,2048]{1,0:T(8,128)(2,1)}) custom-call(s32[1]{0:T(128)} %bitcast.34.mine, bf16[512,2048]{1,0:T(8,128)(2,1)} %get-tuple-element.132.left, bf16[512,2048]{1,0:T(8,128)(2,1)} %get-tuple-element.133.refs_0_), custom_call_target="tpu_custom_call" | custom-call | tf_op jit(solution)/shard_map/pallas_call | solution.py:590
  333.3 7.9 collective-permute-done.14.far
  342.3 4.9 shard_map.253
  347.8 6.9 collective-permute-done.15.two
  354.7 7.2 shard_map.255
  363.5 6.7 shard_map.258
  371.6 9.5 %shard_map.254 = bf16[2,2,512,512]{3,2,1,0:T(8,128)(2,1)} custom-call(bf16[512,2048]{1,0:T(8,128)(2,1)} %get-tuple-element.136.left.act, bf16[1024,2048]{1,0:T(8,128)(2,1)} %down_near.3, bf16[1024,2048]{1,0:T(8,128)(2,1)} %maximum_select_fusion.1.down_far), custom_call_target="tpu_custom_call" | custom-call | tf_op jit(solution)/shard_map/pallas_call | solution.py:1045
  381.1 28.8 %collective-permute-done.16.two = bf16[512,2048]{1,0:T(8,128)(2,1)S(1)} collective-permute-done((bf16[512,2048]{1,0:T(8,128)(2,1)}, bf16[512,2048]{1,0:T(8,128)(2,1)S(1)}, u32[]{:S(2)}, u32[]{:S(2)}) %collective-permute-start.16) | collective-permute-done | bytes 2097184 | tf_op jit(solution)/shard_map/ppermute | solution.py:28
  419.3 4.8 shard_map.259
  424.4 4.8 all-gather.11.cloned.1.call-done
  429.2 11.9 %shard_map.257 = (bf16[1024,1024]{1,0:T(8,128)(2,1)}, bf16[1024,1024]{1,0:T(8,128)(2,1)}) custom-call(bf16[2,2,2,512,512]{4,3,2,1,0:T(8,128)(2,1)} %bitcast.112, bf16[1024,2048]{1,0:T(8,128)(2,1)} %wo.3, f32[1024,1024]{1,0:T(8,128)} %get-tuple-element.122.gate, f32[1024,1024]{1,0:T(8,128)} %get-tuple-element.144.group, f32[1024,2]{1,0:T(8,128)} %get-tuple-element.145.scale, ...), custom_call_target="tpu_custom_call" | custom-call | tf_op jit(solution)/shard_map/pallas_call | solution.py:1060
  441.1 7.2 collective-permute-done.20
  450.4 22.2 %shard_map.260 = (bf16[1024,512]{1,0:T(8,128)(2,1)}, f32[1024,512]{1,0:T(8,128)}, f32[1024,1024]{1,0:T(8,128)}, bf16[2,272,512]{2,1,0:T(8,128)(2,1)}) custom-call(s32[1]{0:T(128)} %slice.102.docs, f32[2]{0:T(128)} %copy-done.34, bf16[1024,1024]{1,0:T(8,128)(2,1)} %get-tuple-element.159.mix, bf16[1024,512]{1,0:T(8,128)(2,1)} %get-tuple-element.118.q, ...), custom_call_target="tpu_custom_call" | custom-call | flops 21474836480 | tf_op jit(solution)/shard_map/pallas_call | solution.py:1089
  472.6 8.8 %shard_map.261 = (bf16[512,2048]{1,0:T(8,128)(2,1)}, bf16[512,2048]{1,0:T(8,128)(2,1)}) custom-call(s32[1]{0:T(128)} %bitcast.34.mine, bf16[1024,1024]{1,0:T(8,128)(2,1)} %get-tuple-element.163.gated, bf16[2,2,2,512,512]{4,3,2,1,0:T(8,128)(2,1)} %bitcast.113), custom_call_target="tpu_custom_call" | custom-call | tf_op jit(solution)/shard_map/pallas_call | solution.py:1137
  488.2 9.0 %shard_map.263 = (bf16[1024,1024]{1,0:T(8,128)(2,1)}, bf16[1024,1024]{1,0:T(8,128)(2,1)}) custom-call(s32[1]{0:T(128)} %bitcast.34.mine, bf16[1024,2048]{1,0:T(8,128)(2,1)} %get-tuple-element.117.low.left, bf16[1024,1024]{1,0:T(8,128)(2,1)} %get-tuple-element.167.refs_0_.dgate), custom_call_target="tpu_custom_call" | custom-call | tf_op jit(solution)/shard_map/pallas_call | solution.py:590
  503.4 6.3 collective-permute-done.23.two
  512.2 27.2 %shard_map.264 = (bf16[1024,512]{1,0:T(8,128)(2,1)}, bf16[1024,1024]{1,0:T(8,128)(2,1)}, bf16[4,1040,512]{2,1,0:T(8,128)(2,1)}, f32[4,16,256]{2,1,0:T(8,128)}, f32[2,2048]{1,0:T(2,128)}) custom-call(s32[1]{0:T(128)} %slice.102.docs, f32[2]{0:T(128)} %copy-done.34, f32[1024,512]{1,0:T(8,128)} %get-tuple-element.170.dk_in, ...), custom_call_target="tpu_custom_call" | custom-call | flops 25769803776 | tf_op jit(solution)/shard_map/pallas_call | solution.py:1155
  548.7 5.5 collective-permute-start.38
  560.6 6.0 collective-permute-done.38
  567.0 5.1 shard_map.267
  574.6 8.7 %shard_map.271 = (bf16[1024,1024]{1,0:T(8,128)(2,1)}, bf16[1024,1024]{1,0:T(8,128)(2,1)}) custom-call(s32[1]{0:T(128)} %bitcast.34.mine, bf16[1024,2048]{1,0:T(8,128)(2,1)} %get-tuple-element.117.low.left, bf16[1024,512]{1,0:T(8,128)(2,1)} %get-tuple-element.162.dq.refs_0_, bf16[1024,512]{1,0:T(8,128)(2,1)} %get-tuple-element.195.refs_1_), custom_call_target="tpu_custom_call" | custom-call | tf_op jit(solution)/shard_map/pallas_call | solution.py:590
  583.3 8.8 %shard_map.265 = (bf16[1024,1024]{1,0:T(8,128)(2,1)}, bf16[1024,1024]{1,0:T(8,128)(2,1)}) custom-call(s32[1]{0:T(128)} %bitcast.34.mine, bf16[1024,2048]{1,0:T(8,128)(2,1)} %get-tuple-element.117.low.left, bf16[1024,1024]{1,0:T(8,128)(2,1)} %get-tuple-element.180.refs_0_), custom_call_target="tpu_custom_call" | custom-call | tf_op jit(solution)/shard_map/pallas_call | solution.py:590
  597.2 4.5 maximum_select_fusion.6.near
  601.8 9.8 %collective-permute-done.33.two = bf16[512,1024]{1,0:T(8,128)(2,1)} collective-permute-done((bf16[512,1024]{1,0:T(8,128)(2,1)}, bf16[512,1024]{1,0:T(8,128)(2,1)}, u32[]{:S(2)}, u32[]{:S(2)}) %collective-permute-start.33) | collective-permute-done | bytes 1048608 | tf_op jit(solution)/shard_map/ppermute | solution.py:28
  614.5 8.1 %collective-permute-done.44 = bf16[128,2048]{1,0:T(8,128)(2,1)S(1)} collective-permute-done((bf16[128,2048]{1,0:T(8,128)(2,1)}, bf16[128,2048]{1,0:T(8,128)(2,1)S(1)}, u32[]{:S(2)}, u32[]{:S(2)}) %collective-permute-start.44) | collective-permute-done | bytes 524320 | tf_op jit(solution)/shard_map/ppermute | solution.py:28
  622.7 5.4 collective-permute-done.45
  629.4 4.8 shard_map.272
  634.2 4.9 shard_map.266
  646.3 34.9 %collective-permute-done.36.two = bf16[512,1024]{1,0:T(8,128)(2,1)} collective-permute-done((bf16[512,1024]{1,0:T(8,128)(2,1)}, bf16[512,1024]{1,0:T(8,128)(2,1)}, u32[]{:S(2)}, u32[]{:S(2)}) %collective-permute-start.36) | collective-permute-done | bytes 1048608 | tf_op jit(solution)/shard_map/ppermute | solution.py:28
  692.0 6.4 shard_map.274
  698.5 7.7 shard_map.275
  724.2 13.5 %psum.7 = f32[4,512]{1,0:T(4,128)S(1)} all-reduce(f32[4,512]{1,0:T(4,128)S(1)} %slice_bitcast_fusion.1), channel_id=1, replica_groups=mesh['head'=4,'tok'=8] {'tok'}, use_global_device_ids=true, to_apply=%region_2.3 | all-reduce | flops 2048 | bytes 16384 | tf_op jit(solution)/shard_map/psum | solution.py:1241
  744.0 19.5 %collective-permute-done.30 = bf16[512,512]{1,0:T(8,128)(2,1)S(1)} collective-permute-done((bf16[512,512]{1,0:T(8,128)(2,1)S(1)}, bf16[512,512]{1,0:T(8,128)(2,1)S(1)}, u32[]{:S(2)}, u32[]{:S(2)}) %collective-permute-start.30) | collective-permute-done | bytes 524320 | tf_op jit(solution)/shard_map/ppermute | solution.py:28
  765.0 10.1 %shard_map.277 = (f32[1024,2048]{1,0:T(8,128)}, f32[2048,1024]{1,0:T(8,128)}) custom-call(bf16[8,512,1024]{2,1,0:T(8,128)(2,1)} %bitcast.102, bf16[8,512,1024]{2,1,0:T(8,128)(2,1)} %bitcast.103), custom_call_target="tpu_custom_call" | custom-call | tf_op jit(solution)/shard_map/pallas_call | solution.py:744
  777.1 10.1 %shard_map.276 = (f32[2048,1024]{1,0:T(8,128)}, f32[2048,512]{1,0:T(8,128)}, f32[2048,512]{1,0:T(8,128)}) custom-call(bf16[8,512,1024]{2,1,0:T(8,128)(2,1)} %bitcast.104, bf16[8,512,1024]{2,1,0:T(8,128)(2,1)} %bitcast.105), custom_call_target="tpu_custom_call" | custom-call | tf_op jit(solution)/shard_map/pallas_call | solution.py:744
  (247 shorter events, 164.7 us)
Async XLA Ops:
  7.2 87.6 %all-gather.9.cloned.1.call-start = ((), (), s32[]{:S(2)}) async-start(), calls=%async_computation.4 | async-start | bytes 5324800 | tf_op jit(solution)/shard_map/all_gather | solution.py:787
  9.6 244.6 %reduce-scatter.3.cloned.1.call-start = ((), (), s32[]{:S(2)}) async-start(), calls=%async_computation.2 | async-start | bytes 5242880 | tf_op jit(solution)/shard_map/reduce_scatter | solution.py:961
  96.0 25.5 %collective-permute-start = (bf16[512,512]{1,0:T(8,128)(2,1)S(1)}, bf16[512,512]{1,0:T(8,128)(2,1)S(1)}, u32[]{:S(2)}, u32[]{:S(2)}) collective-permute-start(bf16[512,512]{1,0:T(8,128)(2,1)S(1)} %get-tuple-element.222), channel_id=1, source_target_pairs={{0,16},{8,24},{16,0},{24,8},{1,17},{9,25},{17,1},{25,9},{2,18},{10... | collective-permute-start | bytes 1572872 | tf_op jit(solution)/shard_map/ppermute | solution.py:28
  121.7 49.6 %collective-permute-start.4 = (bf16[2,1,512,512]{3,2,0,1:T(8,128)(2,1)S(1)}, bf16[2,1,512,512]{3,2,0,1:T(8,128)(2,1)}, u32[]{:S(2)}, u32[]{:S(2)}) collective-permute-start(bf16[2,1,512,512]{3,2,0,1:T(8,128)(2,1)S(1)} %maximum_select_fusion.9), channel_id=1, source_target_pairs={{0,8},{8,0},{16,24},{24,16},{1,9},{9,1},{17,25},{25,17},{2,10},{10... | collective-permute-start | bytes 3145736 | tf_op jit(solution)/shard_map/ppermute | solution.py:28
  123.6 51.2 %collective-permute-start.5 = (bf16[512,1024]{1,0:T(8,128)(2,1)}, bf16[512,1024]{1,0:T(8,128)(2,1)S(1)}, u32[]{:S(2)}, u32[]{:S(2)}) collective-permute-start(bf16[512,1024]{1,0:T(8,128)(2,1)} %pad_maximum_fusion), channel_id=1, source_target_pairs={{0,16},{8,24},{16,0},{24,8},{1,17},{9,25},{17,1},{25,9},{2,18},{10... | collective-permute-start | bytes 3145736 | tf_op jit(solution)/shard_map/ppermute | solution.py:28
  125.5 31.7 %collective-permute-start.1 = (bf16[2,272,512]{2,1,0:T(8,128)(2,1)}, bf16[2,272,512]{2,1,0:T(8,128)(2,1)}, u32[]{:S(2)}, u32[]{:S(2)}) collective-permute-start(bf16[2,272,512]{2,1,0:T(8,128)(2,1)} %get-tuple-element.114), channel_id=1, source_target_pairs={{0,1},{1,2},{2,3},{3,4},{4,5},{5,6},{6,7},{8,9},{9,10},{10,11},{11... | collective-permute-start | bytes 1671176 | tf_op jit(solution)/shard_map/ppermute | solution.py:24
  127.7 29.6 %collective-permute-start.2 = (bf16[2,272,512]{2,1,0:T(8,128)(2,1)}, bf16[2,272,512]{2,1,0:T(8,128)(2,1)}, u32[]{:S(2)}, u32[]{:S(2)}) collective-permute-start(bf16[2,272,512]{2,1,0:T(8,128)(2,1)} %get-tuple-element.114), channel_id=1, source_target_pairs={{0,2},{1,3},{2,4},{3,5},{4,6},{5,7},{8,10},{9,11},{10,12},{11,13},... | collective-permute-start | bytes 1671176 | tf_op jit(solution)/shard_map/ppermute | solution.py:24
  131.7 25.5 %collective-permute-start.3 = (bf16[2,272,512]{2,1,0:T(8,128)(2,1)}, bf16[2,272,512]{2,1,0:T(8,128)(2,1)}, u32[]{:S(2)}, u32[]{:S(2)}) collective-permute-start(bf16[2,272,512]{2,1,0:T(8,128)(2,1)} %get-tuple-element.114), channel_id=1, source_target_pairs={{0,3},{1,4},{2,5},{3,6},{4,7},{8,11},{9,12},{10,13},{11,14},{12,15... | collective-permute-start | bytes 1671176 | tf_op jit(solution)/shard_map/ppermute | solution.py:24
  174.7 254.4 %all-gather.11.cloned.1.call-start = ((), (), s32[]{:S(2)}) async-start(), calls=%async_computation.5 | async-start | bytes 5242880 | tf_op jit(solution)/shard_map/all_gather | solution.py:1041
  175.2 17.3 %collective-permute-start.7 = (bf16[256,1024]{1,0:T(8,128)(2,1)S(1)}, bf16[256,1024]{1,0:T(8,128)(2,1)S(1)}, u32[]{:S(2)}, u32[]{:S(2)}) collective-permute-start(bf16[256,1024]{1,0:T(8,128)(2,1)S(1)} %get-tuple-element.220), channel_id=1, source_target_pairs={{0,4},{1,5},{2,6},{3,7},{4,0},{5,1},{6,2},{7,3},{8,12},{9,13},{10,... | collective-permute-start | bytes 1572872 | tf_op jit(solution)/shard_map/ppermute | solution.py:28
  193.0 24.1 %collective-permute-start.8 = (bf16[512,1024]{1,0:T(8,128)(2,1)S(1)}, bf16[512,1024]{1,0:T(8,128)(2,1)}, u32[]{:S(2)}, u32[]{:S(2)}) collective-permute-start(bf16[512,1024]{1,0:T(8,128)(2,1)S(1)} %maximum_select_fusion.10), channel_id=1, source_target_pairs={{0,2},{1,3},{2,0},{3,1},{4,6},{5,7},{6,4},{7,5},{8,10},{9,11},{10,... | collective-permute-start | bytes 3145736 | tf_op jit(solution)/shard_map/ppermute | solution.py:28
  193.3 26.4 %collective-permute-start.11 = (bf16[256,2048]{1,0:T(8,128)(2,1)S(1)}, bf16[256,2048]{1,0:T(8,128)(2,1)S(1)}, u32[]{:S(2)}, u32[]{:S(2)}) collective-permute-start(bf16[256,2048]{1,0:T(8,128)(2,1)S(1)} %maximum_select_fusion.11), channel_id=1, source_target_pairs={{0,4},{1,5},{2,6},{3,7},{4,0},{5,1},{6,2},{7,3},{8,12},{9,13},{10,... | collective-permute-start | bytes 3145736 | tf_op jit(solution)/shard_map/ppermute | solution.py:28
  219.7 38.8 %collective-permute-start.9 = (bf16[1024,1024]{1,0:T(8,128)(2,1)S(1)}, bf16[1024,1024]{1,0:T(8,128)(2,1)}, u32[]{:S(2)}, u32[]{:S(2)}) collective-permute-start(bf16[1024,1024]{1,0:T(8,128)(2,1)S(1)} %maximum_select_fusion.4), channel_id=1, source_target_pairs={{0,1},{1,0},{2,3},{3,2},{4,5},{5,4},{6,7},{7,6},{8,9},{9,8},{10,11... | collective-permute-start | bytes 6291464 | tf_op jit(solution)/shard_map/ppermute | solution.py:28
  222.1 41.0 %collective-permute-start.12 = (bf16[512,2048]{1,0:T(8,128)(2,1)}, bf16[512,2048]{1,0:T(8,128)(2,1)}, u32[]{:S(2)}, u32[]{:S(2)}) collective-permute-start(bf16[512,2048]{1,0:T(8,128)(2,1)} %maximum_select_fusion.5), channel_id=1, source_target_pairs={{0,1},{1,0},{2,3},{3,2},{4,5},{5,4},{6,7},{7,6},{8,9},{9,8},{10,11... | collective-permute-start | bytes 6291464 | tf_op jit(solution)/shard_map/ppermute | solution.py:28
  256.2 25.0 %collective-permute-start.6 = (bf16[2,1,512,512]{3,2,0,1:T(8,128)(2,1)S(1)}, bf16[2,1,512,512]{3,2,0,1:T(8,128)(2,1)S(1)}, u32[]{:S(2)}, u32[]{:S(2)}) collective-permute-start(bf16[2,1,512,512]{3,2,0,1:T(8,128)(2,1)S(1)} %convert_bitcast_fusion), channel_id=1, source_target_pairs={{0,8},{8,0},{16,24},{24,16},{1,9},{9,1},{17,25},{25,17},{2,10},{10... | collective-permute-start | bytes 3145736 | tf_op jit(solution)/shard_map/ppermute | solution.py:28
  311.4 29.8 %collective-permute-start.13 = (bf16[2,1,512,512]{3,2,1,0:T(8,128)(2,1)S(1)}, bf16[2,1,512,512]{3,2,1,0:T(8,128)(2,1)S(1)}, u32[]{:S(2)}, u32[]{:S(2)}) collective-permute-start(bf16[2,1,512,512]{3,2,1,0:T(8,128)(2,1)S(1)} %constant_dynamic-slice_fusion.3), channel_id=1, source_target_pairs={{0,8},{8,0},{16,24},{24,16},{1,9},{9,1},{17,25},{25,17},{2,10},{10... | collective-permute-start | bytes 3145736 | tf_op jit(solution)/shard_map/ppermute | solution.py:28
  313.0 28.2 %collective-permute-start.14 = (f32[512,2]{1,0:T(8,128)S(1)}, f32[512,2]{1,0:T(8,128)S(1)}, u32[]{:S(2)}, u32[]{:S(2)}) collective-permute-start(f32[512,2]{1,0:T(8,128)S(1)} %copy-done.27), channel_id=1, source_target_pairs={{0,8},{8,0},{16,24},{24,16},{1,9},{9,1},{17,25},{25,17},{2,10},{10... | collective-permute-start | bytes 12296 | tf_op jit(solution)/shard_map/ppermute | solution.py:28
  347.2 16.3 %collective-permute-start.18 = (bf16[1024,2048]{1,0:T(8,128)(2,1)}, bf16[1024,2048]{1,0:T(8,128)(2,1)}, u32[]{:S(2)}, u32[]{:S(2)}) collective-permute-start(bf16[1024,2048]{1,0:T(8,128)(2,1)} %get-tuple-element.150), channel_id=1, source_target_pairs={{0,1},{1,0},{2,3},{3,2},{4,5},{5,4},{6,7},{7,6},{8,9},{9,8},{10,11... | collective-permute-start | bytes 12582920 | tf_op jit(solution)/shard_map/ppermute | solution.py:28
  347.7 291.3 %reduce-scatter.5.cloned.1.call-start = ((), (), s32[]{:S(2)}) async-start(), calls=%async_computation.3 | async-start | bytes 5324800 | tf_op jit(solution)/shard_map/reduce_scatter | solution.py:1234
  361.9 47.9 %collective-permute-start.16 = (bf16[512,2048]{1,0:T(8,128)(2,1)}, bf16[512,2048]{1,0:T(8,128)(2,1)S(1)}, u32[]{:S(2)}, u32[]{:S(2)}) collective-permute-start(bf16[512,2048]{1,0:T(8,128)(2,1)} %get-tuple-element.141), channel_id=1, source_target_pairs={{0,4},{1,5},{2,6},{3,7},{4,0},{5,1},{6,2},{7,3},{8,12},{9,13},{10,... | collective-permute-start | bytes 6291464 | tf_op jit(solution)/shard_map/ppermute | solution.py:28
  370.2 47.8 %collective-permute-start.19 = (bf16[512,2048]{1,0:T(8,128)(2,1)}, bf16[512,2048]{1,0:T(8,128)(2,1)S(1)}, u32[]{:S(2)}, u32[]{:S(2)}) collective-permute-start(bf16[512,2048]{1,0:T(8,128)(2,1)} %get-tuple-element.152), channel_id=1, source_target_pairs={{0,2},{1,3},{2,0},{3,1},{4,6},{5,7},{6,4},{7,5},{8,10},{9,11},{10,... | collective-permute-start | bytes 6291464 | tf_op jit(solution)/shard_map/ppermute | solution.py:28
  415.3 25.8 %collective-permute-start.17 = (bf16[256,2048]{1,0:T(8,128)(2,1)}, bf16[256,2048]{1,0:T(8,128)(2,1)S(1)}, u32[]{:S(2)}, u32[]{:S(2)}) collective-permute-start(bf16[256,2048]{1,0:T(8,128)(2,1)} %get-tuple-element.143), channel_id=1, source_target_pairs={{0,2},{1,3},{2,0},{3,1},{4,6},{5,7},{6,4},{7,5},{8,10},{9,11},{10,... | collective-permute-start | bytes 3145736 | tf_op jit(solution)/shard_map/ppermute | solution.py:28
  424.1 24.2 %collective-permute-start.20 = (bf16[256,2048]{1,0:T(8,128)(2,1)}, bf16[256,2048]{1,0:T(8,128)(2,1)S(1)}, u32[]{:S(2)}, u32[]{:S(2)}) collective-permute-start(bf16[256,2048]{1,0:T(8,128)(2,1)} %get-tuple-element.155), channel_id=1, source_target_pairs={{0,4},{1,5},{2,6},{3,7},{4,0},{5,1},{6,2},{7,3},{8,12},{9,13},{10,... | collective-permute-start | bytes 3145736 | tf_op jit(solution)/shard_map/ppermute | solution.py:28
  481.4 15.9 %collective-permute-start.21 = (bf16[512,2048]{1,0:T(8,128)(2,1)}, bf16[512,2048]{1,0:T(8,128)(2,1)S(1)}, u32[]{:S(2)}, u32[]{:S(2)}) collective-permute-start(bf16[512,2048]{1,0:T(8,128)(2,1)} %get-tuple-element.165), channel_id=1, source_target_pairs={{0,1},{1,0},{2,3},{3,2},{4,5},{5,4},{6,7},{7,6},{8,9},{9,8},{10,11... | collective-permute-start | bytes 6291464 | tf_op jit(solution)/shard_map/ppermute | solution.py:28
  481.4 21.2 %collective-permute-start.22 = (bf16[2,272,512]{2,1,0:T(8,128)(2,1)}, bf16[2,272,512]{2,1,0:T(8,128)(2,1)}, u32[]{:S(2)}, u32[]{:S(2)}) collective-permute-start(bf16[2,272,512]{2,1,0:T(8,128)(2,1)} %get-tuple-element.172), channel_id=1, source_target_pairs={{1,0},{2,1},{3,2},{4,3},{5,4},{6,5},{7,6},{9,8},{10,9},{11,10},{12... | collective-permute-start | bytes 1671176 | tf_op jit(solution)/shard_map/ppermute | solution.py:24
  482.7 27.1 %collective-permute-start.23 = (bf16[2,272,512]{2,1,0:T(8,128)(2,1)}, bf16[2,272,512]{2,1,0:T(8,128)(2,1)}, u32[]{:S(2)}, u32[]{:S(2)}) collective-permute-start(bf16[2,272,512]{2,1,0:T(8,128)(2,1)} %get-tuple-element.172), channel_id=1, source_target_pairs={{2,0},{3,1},{4,2},{5,3},{6,4},{7,5},{10,8},{11,9},{12,10},{13,11},... | collective-permute-start | bytes 1671176 | tf_op jit(solution)/shard_map/ppermute | solution.py:24
  484.0 28.2 %collective-permute-start.24 = (bf16[2,272,512]{2,1,0:T(8,128)(2,1)}, bf16[2,272,512]{2,1,0:T(8,128)(2,1)}, u32[]{:S(2)}, u32[]{:S(2)}) collective-permute-start(bf16[2,272,512]{2,1,0:T(8,128)(2,1)} %get-tuple-element.172), channel_id=1, source_target_pairs={{3,0},{4,1},{5,2},{6,3},{7,4},{11,8},{12,9},{13,10},{14,11},{15,12... | collective-permute-start | bytes 1671176 | tf_op jit(solution)/shard_map/ppermute | solution.py:24
  485.3 57.2 %collective-permute-start.25 = (bf16[128,2048]{1,0:T(8,128)(2,1)}, bf16[128,2048]{1,0:T(8,128)(2,1)}, u32[]{:S(2)}, u32[]{:S(2)}) collective-permute-start(bf16[128,2048]{1,0:T(8,128)(2,1)} %add_convert_fusion.6), channel_id=1, source_target_pairs={{0,16},{8,24},{16,0},{24,8},{1,17},{9,25},{17,1},{25,9},{2,18},{10... | collective-permute-start | bytes 1572872 | tf_op jit(solution)/shard_map/ppermute | solution.py:28
  497.2 45.3 %collective-permute-start.26 = (bf16[256,1024]{1,0:T(8,128)(2,1)}, bf16[256,1024]{1,0:T(8,128)(2,1)}, u32[]{:S(2)}, u32[]{:S(2)}) collective-permute-start(bf16[256,1024]{1,0:T(8,128)(2,1)} %add_convert_fusion.7), channel_id=1, source_target_pairs={{0,16},{8,24},{16,0},{24,8},{1,17},{9,25},{17,1},{25,9},{2,18},{10... | collective-permute-start | bytes 1572872 | tf_op jit(solution)/shard_map/ppermute | solution.py:28
  502.6 39.9 %collective-permute-start.28 = (bf16[1024,1024]{1,0:T(8,128)(2,1)}, bf16[1024,1024]{1,0:T(8,128)(2,1)S(1)}, u32[]{:S(2)}, u32[]{:S(2)}) collective-permute-start(bf16[1024,1024]{1,0:T(8,128)(2,1)} %get-tuple-element.168), channel_id=1, source_target_pairs={{0,1},{1,0},{2,3},{3,2},{4,5},{5,4},{6,7},{7,6},{8,9},{9,8},{10,11... | collective-permute-start | bytes 6291464 | tf_op jit(solution)/shard_map/ppermute | solution.py:28
  509.7 32.8 %collective-permute-start.27 = (bf16[256,2048]{1,0:T(8,128)(2,1)}, bf16[256,2048]{1,0:T(8,128)(2,1)S(1)}, u32[]{:S(2)}, u32[]{:S(2)}) collective-permute-start(bf16[256,2048]{1,0:T(8,128)(2,1)} %get-tuple-element.166), channel_id=1, source_target_pairs={{0,2},{1,3},{2,0},{3,1},{4,6},{5,7},{6,4},{7,5},{8,10},{9,11},{10,... | collective-permute-start | bytes 3145736 | tf_op jit(solution)/shard_map/ppermute | solution.py:28
  544.2 176.3 %all-gather.13.cloned.1.call-start = ((), (), s32[]{:S(2)}) async-start(), calls=%async_computation.6 | async-start | bytes 9437184 | tf_op jit(solution)/shard_map/all_gather | solution.py:1256
  548.7 17.8 %collective-permute-start.38 = (bf16[128,2048]{1,0:T(8,128)(2,1)S(1)}, bf16[128,2048]{1,0:T(8,128)(2,1)S(1)}, u32[]{:S(2)}, u32[]{:S(2)}) collective-permute-start(bf16[128,2048]{1,0:T(8,128)(2,1)S(1)} %add_convert_fusion.3), channel_id=1, source_target_pairs={{0,4},{1,5},{2,6},{3,7},{4,0},{5,1},{6,2},{7,3},{8,12},{9,13},{10,... | collective-permute-start | bytes 1572872 | tf_op jit(solution)/shard_map/ppermute | solution.py:28
  556.5 38.8 %collective-permute-start.42 = (bf16[512,1024]{1,0:T(8,128)(2,1)S(1)}, bf16[512,1024]{1,0:T(8,128)(2,1)S(1)}, u32[]{:S(2)}, u32[]{:S(2)}) collective-permute-start(bf16[512,1024]{1,0:T(8,128)(2,1)S(1)} %maximum_select_fusion.14), channel_id=1, source_target_pairs={{0,4},{1,5},{2,6},{3,7},{4,0},{5,1},{6,2},{7,3},{8,12},{9,13},{10,... | collective-permute-start | bytes 3145736 | tf_op jit(solution)/shard_map/ppermute | solution.py:28
  566.8 30.5 %collective-permute-start.39 = (bf16[256,2048]{1,0:T(8,128)(2,1)S(1)}, bf16[256,2048]{1,0:T(8,128)(2,1)}, u32[]{:S(2)}, u32[]{:S(2)}) collective-permute-start(bf16[256,2048]{1,0:T(8,128)(2,1)S(1)} %maximum_select_fusion.13), channel_id=1, source_target_pairs={{0,2},{1,3},{2,0},{3,1},{4,6},{5,7},{6,4},{7,5},{8,10},{9,11},{10,... | collective-permute-start | bytes 3145736 | tf_op jit(solution)/shard_map/ppermute | solution.py:28
  572.1 39.5 %collective-permute-start.33 = (bf16[512,1024]{1,0:T(8,128)(2,1)}, bf16[512,1024]{1,0:T(8,128)(2,1)}, u32[]{:S(2)}, u32[]{:S(2)}) collective-permute-start(bf16[512,1024]{1,0:T(8,128)(2,1)} %get-tuple-element.186), channel_id=1, source_target_pairs={{0,4},{1,5},{2,6},{3,7},{4,0},{5,1},{6,2},{7,3},{8,12},{9,13},{10,... | collective-permute-start | bytes 3145736 | tf_op jit(solution)/shard_map/ppermute | solution.py:28
  583.3 46.1 %collective-permute-start.35 = (bf16[1024,1024]{1,0:T(8,128)(2,1)}, bf16[1024,1024]{1,0:T(8,128)(2,1)}, u32[]{:S(2)}, u32[]{:S(2)}) collective-permute-start(bf16[1024,1024]{1,0:T(8,128)(2,1)} %get-tuple-element.197), channel_id=1, source_target_pairs={{0,1},{1,0},{2,3},{3,2},{4,5},{5,4},{6,7},{7,6},{8,9},{9,8},{10,11... | collective-permute-start | bytes 6291464 | tf_op jit(solution)/shard_map/ppermute | solution.py:28
  592.1 42.1 %collective-permute-start.31 = (bf16[1024,1024]{1,0:T(8,128)(2,1)}, bf16[1024,1024]{1,0:T(8,128)(2,1)}, u32[]{:S(2)}, u32[]{:S(2)}) collective-permute-start(bf16[1024,1024]{1,0:T(8,128)(2,1)} %get-tuple-element.182), channel_id=1, source_target_pairs={{0,1},{1,0},{2,3},{3,2},{4,5},{5,4},{6,7},{7,6},{8,9},{9,8},{10,11... | collective-permute-start | bytes 6291464 | tf_op jit(solution)/shard_map/ppermute | solution.py:28
  595.3 27.2 %collective-permute-start.44 = (bf16[128,2048]{1,0:T(8,128)(2,1)}, bf16[128,2048]{1,0:T(8,128)(2,1)S(1)}, u32[]{:S(2)}, u32[]{:S(2)}) collective-permute-start(bf16[128,2048]{1,0:T(8,128)(2,1)} %get-tuple-element.191), channel_id=1, source_target_pairs={{0,4},{1,5},{2,6},{3,7},{4,0},{5,1},{6,2},{7,3},{8,12},{9,13},{10,... | collective-permute-start | bytes 1572872 | tf_op jit(solution)/shard_map/ppermute | solution.py:28
  642.9 134.2 %all-gather.15.cloned.1.call-start = ((), (), s32[]{:S(2)}) async-start(), calls=%async_computation.7 | async-start | bytes 9437184 | tf_op jit(solution)/shard_map/all_gather | solution.py:1260
  642.9 49.1 %collective-permute-start.40 = (bf16[512,2048]{1,0:T(8,128)(2,1)}, bf16[512,2048]{1,0:T(8,128)(2,1)}, u32[]{:S(2)}, u32[]{:S(2)}) collective-permute-start(bf16[512,2048]{1,0:T(8,128)(2,1)} %maximum_select_fusion.6.near), channel_id=1, source_target_pairs={{0,1},{1,0},{2,3},{3,2},{4,5},{5,4},{6,7},{7,6},{8,9},{9,8},{10,11... | collective-permute-start | bytes 6291464 | tf_op jit(solution)/shard_map/ppermute | solution.py:28
  644.0 54.5 %collective-permute-start.43 = (bf16[1024,1024]{1,0:T(8,128)(2,1)S(1)}, bf16[1024,1024]{1,0:T(8,128)(2,1)}, u32[]{:S(2)}, u32[]{:S(2)}) collective-permute-start(bf16[1024,1024]{1,0:T(8,128)(2,1)S(1)} %maximum_select_fusion.7.near), channel_id=1, source_target_pairs={{0,1},{1,0},{2,3},{3,2},{4,5},{5,4},{6,7},{7,6},{8,9},{9,8},{10,11... | collective-permute-start | bytes 6291464 | tf_op jit(solution)/shard_map/ppermute | solution.py:28
  644.1 37.1 %collective-permute-start.36 = (bf16[512,1024]{1,0:T(8,128)(2,1)}, bf16[512,1024]{1,0:T(8,128)(2,1)}, u32[]{:S(2)}, u32[]{:S(2)}) collective-permute-start(bf16[512,1024]{1,0:T(8,128)(2,1)} %get-tuple-element.200), channel_id=1, source_target_pairs={{0,4},{1,5},{2,6},{3,7},{4,0},{5,1},{6,2},{7,3},{8,12},{9,13},{10,... | collective-permute-start | bytes 3145736 | tf_op jit(solution)/shard_map/ppermute | solution.py:28
  645.8 41.0 %collective-permute-start.32 = (bf16[512,1024]{1,0:T(8,128)(2,1)}, bf16[512,1024]{1,0:T(8,128)(2,1)S(1)}, u32[]{:S(2)}, u32[]{:S(2)}) collective-permute-start(bf16[512,1024]{1,0:T(8,128)(2,1)} %get-tuple-element.187), channel_id=1, source_target_pairs={{0,2},{1,3},{2,0},{3,1},{4,6},{5,7},{6,4},{7,5},{8,10},{9,11},{10,... | collective-permute-start | bytes 3145736 | tf_op jit(solution)/shard_map/ppermute | solution.py:28
  684.7 25.7 %collective-permute-start.37 = (bf16[256,1024]{1,0:T(8,128)(2,1)}, bf16[256,1024]{1,0:T(8,128)(2,1)}, u32[]{:S(2)}, u32[]{:S(2)}) collective-permute-start(bf16[256,1024]{1,0:T(8,128)(2,1)} %get-tuple-element.203), channel_id=1, source_target_pairs={{0,2},{1,3},{2,0},{3,1},{4,6},{5,7},{6,4},{7,5},{8,10},{9,11},{10,... | collective-permute-start | bytes 1572872 | tf_op jit(solution)/shard_map/ppermute | solution.py:28
  685.8 31.7 %collective-permute-start.29 = (bf16[2,1,512,512]{3,2,1,0:T(8,128)(2,1)}, bf16[2,1,512,512]{3,2,1,0:T(8,128)(2,1)}, u32[]{:S(2)}, u32[]{:S(2)}) collective-permute-start(bf16[2,1,512,512]{3,2,1,0:T(8,128)(2,1)} %constant_dynamic-slice_fusion.1), channel_id=1, source_target_pairs={{0,8},{8,0},{16,24},{24,16},{1,9},{9,1},{17,25},{25,17},{2,10},{10... | collective-permute-start | bytes 3145736 | tf_op jit(solution)/shard_map/ppermute | solution.py:28
  690.6 25.6 %collective-permute-start.34 = (bf16[256,1024]{1,0:T(8,128)(2,1)}, bf16[256,1024]{1,0:T(8,128)(2,1)S(1)}, u32[]{:S(2)}, u32[]{:S(2)}) collective-permute-start(bf16[256,1024]{1,0:T(8,128)(2,1)} %get-tuple-element.194), channel_id=1, source_target_pairs={{0,4},{1,5},{2,6},{3,7},{4,0},{5,1},{6,2},{7,3},{8,12},{9,13},{10,... | collective-permute-start | bytes 1572872 | tf_op jit(solution)/shard_map/ppermute | solution.py:28
  739.0 24.6 %collective-permute-start.30 = (bf16[512,512]{1,0:T(8,128)(2,1)S(1)}, bf16[512,512]{1,0:T(8,128)(2,1)S(1)}, u32[]{:S(2)}, u32[]{:S(2)}) collective-permute-start(bf16[512,512]{1,0:T(8,128)(2,1)S(1)} %get-tuple-element.218), channel_id=1, source_target_pairs={{0,16},{8,24},{16,0},{24,8},{1,17},{9,25},{17,1},{25,9},{2,18},{10... | collective-permute-start | bytes 1572872 | tf_op jit(solution)/shard_map/ppermute | solution.py:28
  (39 other events, 424.2 us)
Sparse Core Ops, SparseCore 0:
  10.2 84.5 all-gather.8
  174.9 79.3 reduce-scatter.2
  347.9 81.2 all-gather.10
  542.7 82.8 reduce-scatter.4
  643.0 77.1 all-gather.12
  722.5 54.4 all-gather.14

commit v4 on v3

--- a/solution.py
+++ b/solution.py
@@ -81,7 +81,7 @@
     for bit in side_bits():
         other = swapped(value, "head", 1 << bit)
         value = joined(value, other, my_bit("head", bit) == 0, 1)
-    return value
+    return value, other
 
 
 def scatter_side_start(value):
@@ -490,13 +490,9 @@
             rows = jnp.concatenate([x[i, at, :] for i in range(x.shape[0])], axis=1).astype(F32)
             normed = (rows - stat_out[at, 0:1]) * stat_out[at, 1:2]
             scaled = part * vec[2:3, :]
-            rows_out[at, :] = jnp.concatenate(
-                [
-                    jnp.sum(scaled, axis=1, keepdims=True),
-                    jnp.sum(scaled * normed, axis=1, keepdims=True),
-                ],
-                axis=1,
-            )
+            ones = jnp.ones((8, scaled.shape[1]), BF)
+            rows_out[r, 0:8] = dot_nt(ones, scaled.astype(BF))
+            rows_out[r, 8:16] = dot_nt(ones, (scaled * normed).astype(BF))
             cols_out[...] += jnp.concatenate(
                 [
                     jnp.sum(part * normed, axis=0, keepdims=True),
@@ -510,14 +506,17 @@
 
 
 def branch_kernel(full, mine, keep, other, hidden, grads, gain, stat, near, far, out):
-    total_rows = (near[...] + far[...]) * (1.0 / full)
+    sums = (near[0] + far[0]) * (1.0 / full)
+    one, two = (
+        sums[at : at + 8].T[:, 0:1] for at in (0, 8)
+    )
     upstream = keep[0, 0].astype(F32) + other[0, 0].astype(F32)
     scale = stat[:, 1:2]
     normed = (hidden[0] - stat[:, 0:1]) * scale
     out[0] = (
         grads[0].astype(F32)
         + scale
-        * (upstream * gain[0] - total_rows[:, 0:1] - normed * total_rows[:, 1:2])
+        * (upstream * gain[0] - one - normed * two)
     ).astype(BF)
 
 
@@ -531,14 +530,14 @@
             out[f, side] = part[:, first : first + width]
 
 
-def prefetched(kernel, grid, in_specs, out_specs, outs):
+def prefetched(kernel, grid, in_specs, out_specs, outs, flops=0):
     return pl.pallas_call(
         kernel,
         grid_spec=pltpu.PrefetchScalarGridSpec(
             num_scalar_prefetch=1, grid=grid, in_specs=in_specs, out_specs=out_specs
         ),
         out_shape=[jax.ShapeDtypeStruct(shape, dtype) for shape, dtype in outs],
-        cost_estimate=pl.CostEstimate(flops=0, bytes_accessed=0, transcendentals=0),
+        cost_estimate=pl.CostEstimate(flops=flops, bytes_accessed=0, transcendentals=0),
         compiler_params=pltpu.CompilerParams(vmem_limit_bytes=VMEM_LIMIT),
     )
 
@@ -597,6 +596,7 @@
         ],
         [pl.BlockSpec((block, width), give), pl.BlockSpec((block, width), keep)],
         [(half, BF), (half, BF)],
+        4 * rows * columns * width,
     )(bit_value(bit), left, *rights)
 
 
@@ -655,6 +655,8 @@
         if waits and place in waits:
             give = after(give, *waits[place])
         other = swapped(give, "tok", 1 << bit)
+        if waits and ("seen", place) in waits:
+            other = after(other, *waits["seen", place])
         others.append(other)
         if place + 1 < len(order):
             give, keep = fold(order[place + 1], groups, keep, other)
@@ -709,47 +711,48 @@
     )(bit_value(bit), value, other)[0], value
 
 
-def order_kernel(split, first, second, one_out, two_out, *rest):
-    rows, columns = one_out.shape[0], first.shape[2]
-    for i in range(first.shape[1] // rows):
-        at = slice(i * columns, (i + 1) * columns)
-        one_out[:, at] = first[0, i * rows : (i + 1) * rows].astype(F32)
-    if rest:
-        two_out[...] = second[0, :, :split].astype(F32)
-        rest[0][...] = second[0, :, split:].astype(F32)
-    else:
-        two_out[...] = second[0].astype(F32)
-
-
-def packed_pieces(first, second):
-    columns = second.shape[1]
+def order_kernel(plan, *refs):
+    outs = list(refs[len(plan) :])
+    for part, count in zip(refs, plan, strict=False):
+        if count == 1:
+            out = outs.pop(0)
+            rows, columns = out.shape[0], part.shape[2]
+            for i in range(part.shape[1] // rows):
+                at = slice(i * columns, (i + 1) * columns)
+                out[:, at] = part[0, i * rows : (i + 1) * rows].astype(F32)
+            continue
+        first = 0
+        for _ in range(count):
+            out = outs.pop(0)
+            out[...] = part[0, :, first : first + out.shape[1]].astype(F32)
+            first += out.shape[1]
+
+
+def packed_pieces(first, *others):
+    columns = others[0].shape[1]
     parts = [first[:, i : i + columns] for i in range(0, first.shape[1], columns)]
-    return jnp.concatenate([*parts, second], axis=0)
-
-
-def in_order(pieces, first, order_one, order_two, split=None):
+    return jnp.concatenate([*parts, *others], axis=0)
+
+
+def in_order(pieces, plan):
     count, rows, columns = pieces.shape
-    half = rows // 2
-
-    def spec(order, which):
+    part = rows // len(plan)
+
+    def spec(which, order):
         return pl.BlockSpec(
-            (1, half, columns), lambda i: (turned_place(i, order), which, 0)
+            (1, part, columns), lambda i: (turned_place(i, order), which, 0)
         )
 
-    shapes = [first]
-    if split:
-        shapes += [(half, split), (half, columns - split)]
-    else:
-        shapes += [(half, columns)]
+    shapes = [shape for _, parts in plan for shape in parts]
     return pl.pallas_call(
-        partial(order_kernel, split),
+        partial(order_kernel, [len(parts) for _, parts in plan]),
         grid=(count,),
-        in_specs=[spec(order_one, 0), spec(order_two, 1)],
+        in_specs=[spec(which, order) for which, (order, _) in enumerate(plan)],
         out_specs=[pl.BlockSpec(shape, lambda i: (i, 0)) for shape in shapes],
         out_shape=[jax.ShapeDtypeStruct((count * high, wide), F32) for high, wide in shapes],
         cost_estimate=pl.CostEstimate(flops=0, bytes_accessed=0, transcendentals=0),
         compiler_params=pltpu.CompilerParams(vmem_limit_bytes=VMEM_LIMIT),
-    )(pieces, pieces)
+    )(*[pieces] * len(plan))
 
 
 def body(
@@ -795,12 +798,6 @@
     vectors = vectors.reshape(4, full_width)
 
     order_one, order_two = bit_orders()
-    late_grad = after(out_grad, rows_raw)
-    grad_keep, grad_give = halves(late_grad, "head", shards.bit_length() - 2, 0)
-    grad_seen = swapped(grad_give, "head", sides)
-    up_piece, down_piece = own_piece(up_weight, order_one), own_piece(down_weight, order_two)
-    both_pieces = jnp.concatenate([up_piece, down_piece.reshape(up_piece.shape)], axis=0)
-
     first_head = lax.axis_index("head") * heads_here
     log_decay = jnp.log(
         1.0 - 2.0 ** (-5.0 - (first_head + jnp.arange(heads_here, dtype=jnp.int32)).astype(F32))
@@ -815,6 +812,12 @@
     end_factor = (padding * (doc_ids == last_doc).astype(F32))[:, None] * jnp.exp(
         (row_count - 1 - position).astype(F32)[:, None] * log_decay[None, :]
     )
+
+    late_grad = after(out_grad, rows_raw, cosine, sine, end_factor)
+    grad_keep, grad_give = halves(late_grad, "head", shards.bit_length() - 2, 0)
+    grad_seen = swapped(grad_give, "head", sides)
+    up_piece, down_piece = own_piece(up_weight, order_one), own_piece(down_weight, order_two)
+    both_pieces = jnp.concatenate([up_piece, down_piece.reshape(up_piece.shape)], axis=0)
 
     docs_col, docs_row = doc_ids[:, None], doc_ids[None, :]
     pads_col, pads_row = padding[:, None], padding[None, :]
@@ -873,7 +876,8 @@
     one_back, two_back, three_back = (shifted(summary, by) for by in (1, 2, 3))
     grad_seen = after(grad_seen, summary)
     side_grads = joined(grad_keep[None], grad_seen[None], spread == 0, 0)
-    grad_rows = gather_side(side_grads[:, None]).reshape(shards, half_rows, width)
+    grad_rows, grads_last = gather_side(side_grads[:, None])
+    grad_rows = grad_rows.reshape(shards, half_rows, width)
     (both_seen,) = far_swap(after(both_pieces, grad_seen))
     up_seen = both_seen[: up_piece.shape[0]]
     down_seen = both_seen[up_piece.shape[0] :].reshape(down_piece.shape)
@@ -949,7 +953,7 @@
         pads_col,
         output_weight,
     )
-    mix_part = after(mix_part, grad_rows, both_seen)
+    mix_part = after(mix_part, grads_last, both_seen)
     side_tokens = lax.dynamic_index_in_dim(
         lax.dynamic_slice_in_dim(rows_raw, spread * half_rows, half_rows, axis=1).reshape(
             2, sides, half_rows, width
@@ -962,7 +966,7 @@
         mix_part.reshape(shards, 2, half_rows, width), "head", scatter_dimension=0
     )
     hidden = lax.optimization_barrier(side_tokens.astype(F32) + mixed_sum.astype(F32))
-    hidden_rows = gather_side(hidden.astype(BF)[:, None]).reshape(shards, half_rows, width)
+    hidden_rows = gather_side(hidden.astype(BF)[:, None])[0].reshape(shards, half_rows, width)
     units = up_weight.shape[1]
     chunks = units // CHUNK
     rows_second, grad_plain, act_low, grad_up, feed_part, stats_second, row_second, cols_second = (
@@ -985,7 +989,7 @@
                 pl.BlockSpec((half_rows, CHUNK), lambda i: (0, i)),
                 held(2, sides, half_rows, width),
                 held(half_rows, 2),
-                held(half_rows, 2),
+                held(half_rows // TILE, 16, TILE),
                 held(2, full_width),
             ],
             out_shape=[
@@ -995,7 +999,7 @@
                 jax.ShapeDtypeStruct((half_rows, 2 * units), BF),
                 jax.ShapeDtypeStruct((2, sides, half_rows, width), BF),
                 jax.ShapeDtypeStruct((half_rows, 2), F32),
-                jax.ShapeDtypeStruct((half_rows, 2), F32),
+                jax.ShapeDtypeStruct((half_rows // TILE, 16, TILE), F32),
                 jax.ShapeDtypeStruct((2, full_width), F32),
             ],
             scratch_shapes=[pltpu.VMEM((half_rows, full_width), F32)],
@@ -1012,6 +1016,7 @@
     row_seen = after(row_seen, down_give, up_give)
     half_block = pl.BlockSpec((1, TILE, width), lambda f, i, mine: (f, i, 0))
     row_block = pl.BlockSpec((TILE, 2), lambda f, i, mine: (i, 0))
+    sum_block = pl.BlockSpec((1, 16, TILE), lambda f, i, mine: (i, 0, 0))
     (branch,) = prefetched(
         partial(branch_kernel, full_width),
         (2, half_rows // TILE),
@@ -1022,8 +1027,8 @@
             half_block,
             pl.BlockSpec((1, 1, width), lambda f, i, mine: (f, 0, 0)),
             row_block,
-            row_block,
-            row_block,
+            sum_block,
+            sum_block,
         ],
         [half_block],
         [((2, half_rows, width), BF)],
@@ -1052,10 +1057,12 @@
         compiler_params=pltpu.CompilerParams(vmem_limit_bytes=VMEM_LIMIT),
     )(after(act_low, branch), down_weight, down_other)
 
-    down_sum, _ = scatter_rest(
-        down_give, down_keep, order_one, 2, {0: (branch,), len(order_one) - 1: (down_part,)}
-    )
-    up_sum, _ = scatter_rest(up_give, up_keep, order_two, 1, {0: (branch,)})
+    down_sum, down_seen_all = scatter_rest(
+        down_give, down_keep, order_one, 2, {0: (branch,), ("seen", 1): (down_part,)}
+    )
+    up_sum, up_seen_all = scatter_rest(
+        up_give, up_keep, order_two, 1, {0: (branch,), ("seen", 1): (down_part,)}
+    )
 
     dgate, grad_mixed = call(
         partial(gate_kernel, heads_here),
@@ -1076,16 +1083,13 @@
         gate_pre,
         flat_group,
         group_scale,
-        pads_col,
+        after(pads_col, down_sum[1], up_sum[1]),
     )
     half_down = down_sum[-1][0].shape[0] // 2
     up_pair = lax.optimization_barrier((*up_sum[-1], dgate))[:2]
     down_pair = lax.optimization_barrier((*down_sum[-1], dgate))[:2]
     up_give = total([part[:, units:] for part in up_pair]).astype(BF)
     down_give = total([part[half_down:] for part in down_pair]).astype(BF)
-    up_far, down_far = far_swap(up_give, down_give)
-    up_near = total([part[:, :units] for part in up_pair]) + up_far.astype(F32)
-    down_near = total([part[:half_down] for part in down_pair]) + down_far.astype(F32)
     dq, dk_part, dv_part, grad_state = call(
         partial(back_kernel, heads_here),
         row_count,
@@ -1147,11 +1151,22 @@
         ],
         [pl.BlockSpec((value_width // 2, width), lambda i, mine: (0, i))] * 2,
         [(width_out, BF), (width_out, BF)],
-    )(bit_value(order_one[0]), after(gated, dq), grad_branch)
+        4 * row_count * value_width * full_width,
+    )(bit_value(order_one[0]), after(gated, dq, up_give, down_give), grad_branch)
     outw_sum, outw_seen = scatter_rest(outw_give, outw_keep, order_one)
     gw_give, gw_keep = weight_grad(order_two[0], 1, rows_first, after(dgate, dq))
     gw_sum, gw_seen = scatter_rest(gw_give, gw_keep, order_two)
     one_on, two_on, three_on = (shifted(grad_state, -by) for by in (1, 2, 3))
+    up_far, down_far = far_swap(up_give, down_give)
+    up_far, down_far = after(up_far, gw_give, outw_give), after(down_far, gw_give, outw_give)
+    up_near = total([part[:, :units] for part in up_pair]) + up_far.astype(F32)
+    down_near = total([part[:half_down] for part in down_pair]) + down_far.astype(F32)
+    down_low, up_low = down_near.astype(BF), up_near.astype(BF)
+    feed_pieces = after(packed_pieces(down_low, up_low), one_on, two_on, three_on)
+    feed_pieces = lax.all_gather(feed_pieces, "tok", axis=0)
+    grad_down, grad_upw = in_order(
+        feed_pieces, ((order_one, [down_low.shape]), (order_two, [up_low.shape]))
+    )
     dk, dv, last_part, row_sums, column_first = call(
         partial(finish_kernel, heads_here, row_count),
         row_count,
@@ -1196,7 +1211,7 @@
         12 * row_count * full_width * value_width,
     )(
         last_docs,
-        after(log_decay, outw_sum[0], gw_give),
+        after(log_decay, up_near, down_near),
         dk_part,
         dv_part,
         key_rot,
@@ -1225,12 +1240,9 @@
         [jnp.broadcast_to(line[None], (shards, *line.shape)), columns.transpose(1, 0, 2)], axis=1
     )
     last_part = lax.dynamic_update_slice_in_dim(last_part, extra.astype(BF), row_count, axis=1)
-    down_low, up_low = down_near.astype(BF), up_near.astype(BF)
-    down_next = swapped(down_low, "tok", 1 << order_one[-1])
-    up_next = swapped(up_low, "tok", 1 << order_two[-1])
-    last_part = after(last_part, down_far, up_far, outw_seen[1], gw_seen[0])
-    down_back = joined(down_low, down_next, my_bit("tok", order_one[-1]) == 0, 0)
-    up_back = joined(up_low, up_next, my_bit("tok", order_two[-1]) == 0, 0)
+    vw_give, vw_keep = weight_grad(order_one[0], 1, rows_first, dv)
+    qkw_give, qkw_keep = weight_grad(order_two[0], 1, rows_first, dq, dk)
+    last_part = after(last_part, feed_pieces, vw_give, qkw_give, outw_sum[0], gw_seen[0])
     last_sum = lax.psum_scatter(last_part, "head", scatter_dimension=0).astype(F32)
     grad_ln1 = last_sum[:row_count]
     sums_first = last_sum[row_count:, :TILE] / full_width
@@ -1244,22 +1256,22 @@
     result_give = lax.dynamic_index_in_dim(result, 1 - spread, 0, keepdims=False)
     layer_out = joined(result_keep, swapped(result_give, "head", sides), spread == 0, 0)
 
-    vw_give, vw_keep = weight_grad(order_one[0], 1, rows_first, dv)
-    qkw_give, qkw_keep = weight_grad(order_two[0], 1, rows_first, dq, dk)
-    grad_down, down_back = gather_wide(down_back, order_one[:-1])
-    grad_upw, up_back = gather_wide(up_back, order_two[:-1])
     outw_low, gw_low = total(outw_sum[-1]).astype(BF), total(gw_sum[-1]).astype(BF)
     waits = {1: (gw_sum[0],), 2: (outw_sum[1], gw_sum[1])}
     vw_sum, _ = scatter_rest(vw_give, vw_keep, order_one, 1, waits)
     qkw_sum, _ = scatter_rest(qkw_give, qkw_keep, order_two, 1, waits)
-    gates = (last_sum, vw_sum[0], qkw_sum[0], down_back, up_back)
-    middle = lax.all_gather(after(packed_pieces(outw_low, gw_low), *gates), "tok", axis=0)
-    grad_outw, grad_gw = in_order(middle, outw_low.shape, order_one, order_two)
     vw_low, qkw_low = total(vw_sum[-1]).astype(BF), total(qkw_sum[-1]).astype(BF)
-    pieces = after(packed_pieces(vw_low, qkw_low), grad_down, grad_upw, middle, result)
+    pieces = packed_pieces(outw_low, gw_low, vw_low, qkw_low)
     pieces = lax.all_gather(pieces, "tok", axis=0)
-    grad_vw, grad_qw, grad_kw = in_order(
-        pieces, vw_low.shape, order_one, order_two, inner_width
+    high = qkw_low.shape[0]
+    grad_outw, grad_gw, grad_vw, grad_qw, grad_kw = in_order(
+        pieces,
+        (
+            (order_one, [outw_low.shape]),
+            (order_two, [gw_low.shape]),
+            (order_one, [vw_low.shape]),
+            (order_two, [(high, inner_width), (high, inner_width)]),
+        ),
     )
 
     norm_first = (tokens.astype(F32) - stats[:, 0:1]) * stats[:, 1:2]

time: 805 us -> 758 us (0.942)
  waiting for transfers between devices: 313 us -> 293 us
  other arithmetic: 57.1 us -> 46.4 us
  starting transfers between devices: 65.3 us -> 55.2 us
    ppermute x40 -> x34, waiting for transfers between devices: 191 us -> 157 us  [swapped(): lax.ppermute(value, axis, [(i, i ^ mask) for i in range(lax.axis_size(axi...]
    all_gather x1, waiting for transfers between devices: 1.96 us -> 25.2 us  [body(): pieces = lax.all_gather(pieces, 'tok', axis=0)]
    ppermute x40 -> x34, starting transfers between devices: 50.5 us -> 40.5 us  [swapped(): lax.ppermute(value, axis, [(i, i ^ mask) for i in range(lax.axis_size(axi...]
    pallas_call x4 -> x2, Pallas kernels: 34.3 us -> 28.4 us  [in_order(): pl.pallas_call(partial(order_kernel, [len(parts) for _, parts in plan]),...]
    select_n x15 -> x10, other arithmetic: 27.8 us -> 22.8 us  [joined(): jnp.where(first, jnp.concatenate([value, other], axis=axis), jnp.concaten...]
  transfers between devices with their start and end apart: 52 -> 46, of which waited for: 22 -> 23; matrix products, arithmetic and copies ran while one was open for 9% -> 9% of each run, Pallas kernels for 28% -> 32%
where the time goes in v4:
time: 758 us; the launch traced here: 748 us
  waiting for transfers between devices  293 us (39%)
  Pallas kernels  291 us (38%)
  starting transfers between devices  55.2 us (7%)
  other arithmetic  46.4 us (6%)
  local copies, waits for them, and re-layouts  34.9 us (5%)
  between operations  15.1 us (2%)
  blocking collectives  12.8 us (2%)
    ppermute x34, waiting for transfers between devices, swapped(): lax.ppermute(value, axis, [(i, i ^ mask) for i in range(lax.axis_size(axi...  157 us
    all_gather x1, waiting for transfers between devices, body(): rows_raw = lax.all_gather(packed, 'head', axis=0)  77.2 us
    pallas_call x12, Pallas kernels, fold(): prefetched(partial(fold_kernel, count), (2 * count,), [spec, spec], [pl.B...  52.7 us
    pallas_call x5, Pallas kernels, weight_grad(): prefetched(partial(weight_kernel, count), (2 * count,), [pl.BlockSpec((ro...  44.9 us
    ppermute x34, starting transfers between devices, swapped(): lax.ppermute(value, axis, [(i, i ^ mask) for i in range(lax.axis_size(axi...  40.5 us
    pallas_call x2, Pallas kernels, in_order(): pl.pallas_call(partial(order_kernel, [len(parts) for _, parts in plan]),...  28.4 us
    pallas_call x1, Pallas kernels, body(): call(partial(finish_kernel, heads_here, row_count), row_count, [SCALARS,...  27.2 us
    pallas_call x1, Pallas kernels, body(): pl.pallas_call(partial(feed_kernel, chunks), grid=(2 * chunks,), in_specs...  26.9 us
  transfers between devices with their start and end apart: 46, of which 23 were waited for; matrix products, arithmetic and copies ran while one was open for 9% of the time, Pallas kernels for 32%

profile of v4, /device:TPU:0, one launch (start us, length us, event | category | flops | bytes accessed | tf_op | source)
XLA Modules:
  0.0 748.3 jit_solution(4891732169518286810)
XLA Ops:
  17.5 77.2 %all-gather.9.cloned.1.call-done = bf16[4160,512]{1,0:T(8,128)(2,1)} async-done(((bf16[1040,512]{1,0:T(8,128)(2,1)}), bf16[4160,512]{1,0:T(8,128)(2,1)}) %all-gather.9.cloned.1.call-update) | async-done | bytes 4259856 | tf_op jit(solution)/shard_map/all_gather | solution.py:790
  98.8 19.2 %shard_map.247 = (bf16[1024,2048]{1,0:T(8,128)(2,1)}, bf16[1024,512]{1,0:T(8,128)(2,1)}, bf16[1024,512]{1,0:T(8,128)(2,1)}, bf16[1024,1024]{1,0:T(8,128)(2,1)}, ...) custom-call(s32[1]{0:T(128)} %slice.108.docs, bf16[4,1040,512]{2,1,0:T(8,128)(2,1)} %bitcast.109, ...), custom_call_target="tpu_custom_call" | custom-call | tf_op jit(solution)/shard_map/pallas_call | solution.py:834
  125.0 4.2 collective-permute-start.2
  135.9 18.0 %shard_map.248 = (f32[1024,1024]{1,0:T(8,128)}, f32[1024,1024]{1,0:T(8,128)}) custom-call(f32[2]{0:T(128)} %copy-done.34, bf16[1024,2048]{1,0:T(8,128)(2,1)} %get-tuple-element.122.low.left, bf16[2048,1024]{1,0:T(8,128)(2,1)} %wg.3, bf16[1024,512]{1,0:T(8,128)(2,1)} %get-tuple-element.123.q, bf16[1024,512]{1,0:T(8,128)(2,1)} %get-tuple-element.124.k, ...), custom_call_target="tpu_custom_call" | custom-call | tf_op jit(solution)/shard_map/pallas_call | solution.py:886
  154.0 14.1 %shard_map.249 = (f32[1024,1024]{1,0:T(8,128)}, f32[1024,2]{1,0:T(8,128)}, bf16[1024,1024]{1,0:T(8,128)(2,1)}, bf16[2,2,2,512,512]{4,3,2,1,0:T(8,128)(2,1)}, bf1...) custom-call(f32[2]{0:T(128)} %copy-done.34, f32[1024,1024]{1,0:T(8,128)} %get-tuple-element.126.inner, ...), custom_call_target="tpu_custom_call" | custom-call | tf_op jit(solution)/shard_map/pallas_call | solution.py:913
  171.5 4.1 collective-permute-start.7
  175.6 8.6 %collective-permute-done.10 = bf16[128,2048]{1,0:T(8,128)(2,1)} collective-permute-done((bf16[128,2048]{1,0:T(8,128)(2,1)S(1)}, bf16[128,2048]{1,0:T(8,128)(2,1)}, u32[]{:S(2)}, u32[]{:S(2)}) %collective-permute-start.10) | collective-permute-done | bytes 524320 | tf_op jit(solution)/shard_map/ppermute | solution.py:28
  190.6 20.9 %collective-permute-done.11 = bf16[256,2048]{1,0:T(8,128)(2,1)} collective-permute-done((bf16[256,2048]{1,0:T(8,128)(2,1)S(1)}, bf16[256,2048]{1,0:T(8,128)(2,1)}, u32[]{:S(2)}, u32[]{:S(2)}) %collective-permute-start.11) | collective-permute-done | bytes 1048608 | tf_op jit(solution)/shard_map/ppermute | solution.py:28
  221.6 24.9 %reduce-scatter.3.cloned.1.call-done = bf16[1,2,512,512]{3,2,1,0:T(8,128)(2,1)} async-done(((bf16[4,2,512,512]{3,2,1,0:T(8,128)(2,1)}), bf16[1,2,512,512]{3,2,1,0:T(8,128)(2,1)}) %reduce-scatter.3.cloned.1.call-update) | async-done | bytes 1048592 | tf_op jit(solution)/shard_map/reduce_scatter | solution.py:965
  250.7 5.2 maximum_select_fusion.1.down_far
  255.9 5.5 maximum_select_fusion.up_far
  261.4 12.1 %collective-permute-done.6 = bf16[2,1,512,512]{3,2,0,1:T(8,128)(2,1)S(1)} collective-permute-done((bf16[2,1,512,512]{3,2,0,1:T(8,128)(2,1)S(1)}, bf16[2,1,512,512]{3,2,0,1:T(8,128)(2,1)S(1)}, u32[]{:S(2)}, u32[]{:S(2)}) %collective-permute-start.6) | collective-permute-done | bytes 1048608 | tf_op jit(solution)/shard_map/ppermute | solution.py:28
  277.2 26.9 %shard_map.250 = (bf16[512,2048]{1,0:T(8,128)(2,1)}, bf16[512,2048]{1,0:T(8,128)(2,1)}, bf16[512,2048]{1,0:T(8,128)(2,1)}, bf16[512,2048]{1,0:T(8,128)(2,1)}, bf...) custom-call(bf16[4,512,512]{2,1,0:T(8,128)(2,1)} %bitcast.116, ...), custom_call_target="tpu_custom_call" | custom-call | tf_op jit(solution)/shard_map/pallas_call | solution.py:973
  307.6 9.3 %shard_map.251 = (bf16[1024,2048]{1,0:T(8,128)(2,1)}, bf16[1024,2048]{1,0:T(8,128)(2,1)}) custom-call(s32[1]{0:T(128)} %bitcast.34.mine, bf16[512,2048]{1,0:T(8,128)(2,1)} %get-tuple-element.141.left.act, bf16[512,2048]{1,0:T(8,128)(2,1)} %get-tuple-element.135.refs_0_), custom_call_target="tpu_custom_call" | custom-call | flops 8589934592 | tf_op jit(solution)/shard_map/pallas_call | solution.py:589
  316.9 9.2 %shard_map.252 = (bf16[1024,2048]{1,0:T(8,128)(2,1)}, bf16[1024,2048]{1,0:T(8,128)(2,1)}) custom-call(s32[1]{0:T(128)} %bitcast.34.mine, bf16[512,2048]{1,0:T(8,128)(2,1)} %get-tuple-element.137.left, bf16[512,2048]{1,0:T(8,128)(2,1)} %get-tuple-element.138.refs_0_), custom_call_target="tpu_custom_call" | custom-call | flops 8589934592 | tf_op jit(solution)/shard_map/pallas_call | solution.py:589
  326.1 4.8 collective-permute-done.13.other
  331.9 5.1 shard_map.253
  337.5 6.9 collective-permute-done.15.two
  344.4 7.4 shard_map.255
  353.4 6.7 shard_map.257
  361.5 9.5 %shard_map.254 = bf16[2,2,512,512]{3,2,1,0:T(8,128)(2,1)} custom-call(bf16[512,2048]{1,0:T(8,128)(2,1)} %get-tuple-element.141.left.act, bf16[1024,2048]{1,0:T(8,128)(2,1)} %down_near.3, bf16[1024,2048]{1,0:T(8,128)(2,1)} %maximum_select_fusion.1.down_far), custom_call_target="tpu_custom_call" | custom-call | tf_op jit(solution)/shard_map/pallas_call | solution.py:1050
  371.0 28.7 %collective-permute-done.16.two = bf16[512,2048]{1,0:T(8,128)(2,1)S(1)} collective-permute-done((bf16[512,2048]{1,0:T(8,128)(2,1)}, bf16[512,2048]{1,0:T(8,128)(2,1)S(1)}, u32[]{:S(2)}, u32[]{:S(2)}) %collective-permute-start.16) | collective-permute-done | bytes 2097184 | tf_op jit(solution)/shard_map/ppermute | solution.py:28
  401.1 4.1 shard_map.256
  409.3 4.8 shard_map.258
  418.8 11.9 %shard_map.259 = (bf16[1024,1024]{1,0:T(8,128)(2,1)}, bf16[1024,1024]{1,0:T(8,128)(2,1)}) custom-call(bf16[2,2,2,512,512]{4,3,2,1,0:T(8,128)(2,1)} %bitcast.118, bf16[1024,2048]{1,0:T(8,128)(2,1)} %wo.3, f32[1024,1024]{1,0:T(8,128)} %get-tuple-element.127.gate, f32[1024,1024]{1,0:T(8,128)} %get-tuple-element.149.group, f32[1024,2]{1,0:T(8,128)} %get-tuple-element.150.scale, ...), custom_call_target="tpu_custom_call" | custom-call | tf_op jit(solution)/shard_map/pallas_call | solution.py:1067
  432.7 5.5 collective-permute-done.21
  440.6 22.2 %shard_map.260 = (bf16[1024,512]{1,0:T(8,128)(2,1)}, f32[1024,512]{1,0:T(8,128)}, f32[1024,1024]{1,0:T(8,128)}, bf16[2,272,512]{2,1,0:T(8,128)(2,1)}) custom-call(s32[1]{0:T(128)} %slice.108.docs, f32[2]{0:T(128)} %copy-done.34, bf16[1024,1024]{1,0:T(8,128)(2,1)} %get-tuple-element.165.mix, bf16[1024,512]{1,0:T(8,128)(2,1)} %get-tuple-element.123.q, ...), custom_call_target="tpu_custom_call" | custom-call | flops 21474836480 | tf_op jit(solution)/shard_map/pallas_call | solution.py:1093
  466.7 9.0 %shard_map.262 = (bf16[512,2048]{1,0:T(8,128)(2,1)}, bf16[512,2048]{1,0:T(8,128)(2,1)}) custom-call(s32[1]{0:T(128)} %bitcast.34.mine, bf16[1024,1024]{1,0:T(8,128)(2,1)} %get-tuple-element.172.gated, bf16[2,2,2,512,512]{4,3,2,1,0:T(8,128)(2,1)} %bitcast.119), custom_call_target="tpu_custom_call" | custom-call | flops 8589934592 | tf_op jit(solution)/shard_map/pallas_call | solution.py:1141
  475.7 8.8 %shard_map.261 = (bf16[1024,1024]{1,0:T(8,128)(2,1)}, bf16[1024,1024]{1,0:T(8,128)(2,1)}) custom-call(s32[1]{0:T(128)} %bitcast.34.mine, bf16[1024,2048]{1,0:T(8,128)(2,1)} %get-tuple-element.122.low.left, bf16[1024,1024]{1,0:T(8,128)(2,1)} %get-tuple-element.169.refs_0_.dgate), custom_call_target="tpu_custom_call" | custom-call | flops 8589934592 | tf_op jit(solution)/shard_map/pallas_call | solution.py:589
  491.9 27.2 %shard_map.263 = (bf16[1024,512]{1,0:T(8,128)(2,1)}, bf16[1024,1024]{1,0:T(8,128)(2,1)}, bf16[4,1040,512]{2,1,0:T(8,128)(2,1)}, f32[4,16,256]{2,1,0:T(8,128)}, f32[2,2048]{1,0:T(2,128)}) custom-call(s32[1]{0:T(128)} %slice.108.docs, f32[2]{0:T(128)} %copy-done.34, f32[1024,512]{1,0:T(8,128)} %get-tuple-element.177.dk_in, ...), custom_call_target="tpu_custom_call" | custom-call | flops 25769803776 | tf_op jit(solution)/shard_map/pallas_call | solution.py:1170
  522.2 8.9 %shard_map.265 = (bf16[1024,1024]{1,0:T(8,128)(2,1)}, bf16[1024,1024]{1,0:T(8,128)(2,1)}) custom-call(s32[1]{0:T(128)} %bitcast.34.mine, bf16[1024,2048]{1,0:T(8,128)(2,1)} %get-tuple-element.122.low.left, bf16[1024,512]{1,0:T(8,128)(2,1)} %get-tuple-element.168.dq.refs_0_, bf16[1024,512]{1,0:T(8,128)(2,1)} %get-tuple-element.188.refs_1_), custom_call_target="tpu_custom_call" | custom-call | flops 8589934592 | tf_op jit(solution)/shard_map/pallas_call | solution.py:589
  531.1 8.8 %shard_map.264 = (bf16[1024,1024]{1,0:T(8,128)(2,1)}, bf16[1024,1024]{1,0:T(8,128)(2,1)}) custom-call(s32[1]{0:T(128)} %bitcast.34.mine, bf16[1024,2048]{1,0:T(8,128)(2,1)} %get-tuple-element.122.low.left, bf16[1024,1024]{1,0:T(8,128)(2,1)} %get-tuple-element.186.refs_0_), custom_call_target="tpu_custom_call" | custom-call | flops 8589934592 | tf_op jit(solution)/shard_map/pallas_call | solution.py:589
  539.9 4.1 shard_map.266
  543.9 4.4 all-gather.13.cloned.1.call-done
  552.8 5.0 shard_map.268
  559.1 4.8 shard_map.270
  564.1 13.0 %collective-permute-done.30.two = bf16[256,2048]{1,0:T(8,128)(2,1)} collective-permute-done((bf16[256,2048]{1,0:T(8,128)(2,1)}, bf16[256,2048]{1,0:T(8,128)(2,1)}, u32[]{:S(2)}, u32[]{:S(2)}) %collective-permute-start.30) | collective-permute-done | bytes 1048608 | tf_op jit(solution)/shard_map/ppermute | solution.py:28
  581.2 4.8 shard_map.272
  595.4 4.1 collective-permute-done.35.two
  603.2 14.4 %collective-permute-done.38.two = bf16[512,1024]{1,0:T(8,128)(2,1)S(1)} collective-permute-done((bf16[512,1024]{1,0:T(8,128)(2,1)}, bf16[512,1024]{1,0:T(8,128)(2,1)S(1)}, u32[]{:S(2)}, u32[]{:S(2)}) %collective-permute-start.38) | collective-permute-done | bytes 1048608 | tf_op jit(solution)/shard_map/ppermute | solution.py:28
  623.3 4.9 collective-permute-done.36
  628.4 5.9 collective-permute-done.39
  635.9 4.0 fusion.11
  644.1 10.4 %shard_map.275 = (f32[1024,2048]{1,0:T(8,128)}, f32[2048,1024]{1,0:T(8,128)}) custom-call(bf16[8,512,1024]{2,1,0:T(8,128)(2,1)} %bitcast.107, bf16[8,512,1024]{2,1,0:T(8,128)(2,1)} %bitcast.108), custom_call_target="tpu_custom_call" | custom-call | tf_op jit(solution)/shard_map/pallas_call | solution.py:747
  655.9 12.8 %psum.7 = f32[4,512]{1,0:T(4,128)S(1)} all-reduce(f32[4,512]{1,0:T(4,128)S(1)} %slice_bitcast_fusion.1), channel_id=1, replica_groups=mesh['head'=4,'tok'=8] {'tok'}, use_global_device_ids=true, to_apply=%region_2.3 | all-reduce | flops 2048 | bytes 16384 | tf_op jit(solution)/shard_map/psum | solution.py:1253
  674.1 22.5 %collective-permute-done.29 = bf16[512,512]{1,0:T(8,128)(2,1)S(1)} collective-permute-done((bf16[512,512]{1,0:T(8,128)(2,1)S(1)}, bf16[512,512]{1,0:T(8,128)(2,1)S(1)}, u32[]{:S(2)}, u32[]{:S(2)}) %collective-permute-start.29) | collective-permute-done | bytes 524320 | tf_op jit(solution)/shard_map/ppermute | solution.py:28
  698.0 25.2 %all-gather.15.cloned.1.call-done = bf16[8192,1024]{1,0:T(8,128)(2,1)} async-done(((bf16[1024,1024]{1,0:T(8,128)(2,1)}), bf16[8192,1024]{1,0:T(8,128)(2,1)}) %all-gather.15.cloned.1.call-update) | async-done | bytes 16777232 | tf_op jit(solution)/shard_map/all_gather | solution.py:1265
  723.2 17.9 %shard_map.274 = (f32[1024,2048]{1,0:T(8,128)}, f32[2048,1024]{1,0:T(8,128)}, f32[2048,1024]{1,0:T(8,128)}, f32[2048,512]{1,0:T(8,128)}, f32[2048,512]{1,0:T(8,128)}) custom-call(bf16[8,1024,1024]{2,1,0:T(8,128)(2,1)} %bitcast.103, bf16[8,1024,1024]{2,1,0:T(8,128)(2,1)} %bitcast.104, bf16[8,1024,1024]{2,1,0:T(8,128)(2,1)} %bitcast.105, ...), custom_call_target="tpu_custom_call" | custom-call | tf_op jit(solution)/shard_map/pallas_call | solution.py:747
  (231 shorter events, 135.5 us)
Async XLA Ops:
  7.2 87.6 %all-gather.9.cloned.1.call-start = ((), (), s32[]{:S(2)}) async-start(), calls=%async_computation.4 | async-start | bytes 5324800 | tf_op jit(solution)/shard_map/all_gather | solution.py:790
  9.6 236.9 %reduce-scatter.3.cloned.1.call-start = ((), (), s32[]{:S(2)}) async-start(), calls=%async_computation.2 | async-start | bytes 5242880 | tf_op jit(solution)/shard_map/reduce_scatter | solution.py:965
  12.1 82.6 %copy-start.21 = (bf16[1024,512]{1,0:T(8,128)(2,1)S(1)}, bf16[1024,512]{1,0:T(8,128)(2,1)}, u32[]{:S(2)}) copy-start(bf16[1024,512]{1,0:T(8,128)(2,1)} %param.29) | copy-start | bytes 3145732
  12.4 85.2 %copy-start.34 = (f32[2]{0:T(128)}, f32[2]{0:T(128)S(1)}, u32[]{:S(2)}) copy-start(f32[2]{0:T(128)S(1)} %subtract_log_fusion.decay) | copy-start | bytes 28
  94.8 24.3 %collective-permute-start = (bf16[512,512]{1,0:T(8,128)(2,1)S(1)}, bf16[512,512]{1,0:T(8,128)(2,1)S(1)}, u32[]{:S(2)}, u32[]{:S(2)}) collective-permute-start(bf16[512,512]{1,0:T(8,128)(2,1)S(1)} %get-tuple-element.232), channel_id=1, source_target_pairs={{0,16},{8,24},{16,0},{24,8},{1,17},{9,25},{17,1},{25,9},{2,18},{10... | collective-permute-start | bytes 1572872 | tf_op jit(solution)/shard_map/ppermute | solution.py:28
  119.2 48.9 %collective-permute-start.4 = (bf16[2,1,512,512]{3,2,0,1:T(8,128)(2,1)S(1)}, bf16[2,1,512,512]{3,2,0,1:T(8,128)(2,1)S(1)}, u32[]{:S(2)}, u32[]{:S(2)}) collective-permute-start(bf16[2,1,512,512]{3,2,0,1:T(8,128)(2,1)S(1)} %maximum_select_fusion.7), channel_id=1, source_target_pairs={{0,8},{8,0},{16,24},{24,16},{1,9},{9,1},{17,25},{25,17},{2,10},{10... | collective-permute-start | bytes 3145736 | tf_op jit(solution)/shard_map/ppermute | solution.py:28
  119.3 48.9 %collective-permute-start.5 = (bf16[512,1024]{1,0:T(8,128)(2,1)}, bf16[512,1024]{1,0:T(8,128)(2,1)}, u32[]{:S(2)}, u32[]{:S(2)}) collective-permute-start(bf16[512,1024]{1,0:T(8,128)(2,1)} %pad_maximum_fusion), channel_id=1, source_target_pairs={{0,16},{8,24},{16,0},{24,8},{1,17},{9,25},{17,1},{25,9},{2,18},{10... | collective-permute-start | bytes 3145736 | tf_op jit(solution)/shard_map/ppermute | solution.py:28
  122.3 31.7 %collective-permute-start.3 = (bf16[2,272,512]{2,1,0:T(8,128)(2,1)}, bf16[2,272,512]{2,1,0:T(8,128)(2,1)}, u32[]{:S(2)}, u32[]{:S(2)}) collective-permute-start(bf16[2,272,512]{2,1,0:T(8,128)(2,1)} %get-tuple-element.119), channel_id=1, source_target_pairs={{0,3},{1,4},{2,5},{3,6},{4,7},{8,11},{9,12},{10,13},{11,14},{12,15... | collective-permute-start | bytes 1671176 | tf_op jit(solution)/shard_map/ppermute | solution.py:24
  125.0 29.0 %collective-permute-start.2 = (bf16[2,272,512]{2,1,0:T(8,128)(2,1)}, bf16[2,272,512]{2,1,0:T(8,128)(2,1)}, u32[]{:S(2)}, u32[]{:S(2)}) collective-permute-start(bf16[2,272,512]{2,1,0:T(8,128)(2,1)} %get-tuple-element.119), channel_id=1, source_target_pairs={{0,2},{1,3},{2,4},{3,5},{4,6},{5,7},{8,10},{9,11},{10,12},{11,13},... | collective-permute-start | bytes 1671176 | tf_op jit(solution)/shard_map/ppermute | solution.py:24
  129.2 24.8 %collective-permute-start.1 = (bf16[2,272,512]{2,1,0:T(8,128)(2,1)}, bf16[2,272,512]{2,1,0:T(8,128)(2,1)}, u32[]{:S(2)}, u32[]{:S(2)}) collective-permute-start(bf16[2,272,512]{2,1,0:T(8,128)(2,1)} %get-tuple-element.119), channel_id=1, source_target_pairs={{0,1},{1,2},{2,3},{3,4},{4,5},{5,6},{6,7},{8,9},{9,10},{10,11},{11... | collective-permute-start | bytes 1671176 | tf_op jit(solution)/shard_map/ppermute | solution.py:24
  169.1 249.7 %all-gather.11.cloned.1.call-start = ((), (), s32[]{:S(2)}) async-start(), calls=%async_computation.5 | async-start | bytes 5242880 | tf_op jit(solution)/shard_map/all_gather | solution.py:1046
  170.7 13.5 %collective-permute-start.10 = (bf16[128,2048]{1,0:T(8,128)(2,1)S(1)}, bf16[128,2048]{1,0:T(8,128)(2,1)}, u32[]{:S(2)}, u32[]{:S(2)}) collective-permute-start(bf16[128,2048]{1,0:T(8,128)(2,1)S(1)} %reshape.210), channel_id=1, source_target_pairs={{0,2},{1,3},{2,0},{3,1},{4,6},{5,7},{6,4},{7,5},{8,10},{9,11},{10,... | collective-permute-start | bytes 1572872 | tf_op jit(solution)/shard_map/ppermute | solution.py:28
  171.5 15.7 %collective-permute-start.7 = (bf16[256,1024]{1,0:T(8,128)(2,1)S(1)}, bf16[256,1024]{1,0:T(8,128)(2,1)}, u32[]{:S(2)}, u32[]{:S(2)}) collective-permute-start(bf16[256,1024]{1,0:T(8,128)(2,1)S(1)} %get-tuple-element.230), channel_id=1, source_target_pairs={{0,4},{1,5},{2,6},{3,7},{4,0},{5,1},{6,2},{7,3},{8,12},{9,13},{10,... | collective-permute-start | bytes 1572872 | tf_op jit(solution)/shard_map/ppermute | solution.py:28
  185.8 25.7 %collective-permute-start.11 = (bf16[256,2048]{1,0:T(8,128)(2,1)S(1)}, bf16[256,2048]{1,0:T(8,128)(2,1)}, u32[]{:S(2)}, u32[]{:S(2)}) collective-permute-start(bf16[256,2048]{1,0:T(8,128)(2,1)S(1)} %maximum_select_fusion.9), channel_id=1, source_target_pairs={{0,4},{1,5},{2,6},{3,7},{4,0},{5,1},{6,2},{7,3},{8,12},{9,13},{10,... | collective-permute-start | bytes 3145736 | tf_op jit(solution)/shard_map/ppermute | solution.py:28
  188.8 26.4 %collective-permute-start.8 = (bf16[512,1024]{1,0:T(8,128)(2,1)S(1)}, bf16[512,1024]{1,0:T(8,128)(2,1)S(1)}, u32[]{:S(2)}, u32[]{:S(2)}) collective-permute-start(bf16[512,1024]{1,0:T(8,128)(2,1)S(1)} %maximum_select_fusion.8), channel_id=1, source_target_pairs={{0,2},{1,3},{2,0},{3,1},{4,6},{5,7},{6,4},{7,5},{8,10},{9,11},{10,... | collective-permute-start | bytes 3145736 | tf_op jit(solution)/shard_map/ppermute | solution.py:28
  214.5 36.2 %collective-permute-start.12 = (bf16[512,2048]{1,0:T(8,128)(2,1)S(1)}, bf16[512,2048]{1,0:T(8,128)(2,1)}, u32[]{:S(2)}, u32[]{:S(2)}) collective-permute-start(bf16[512,2048]{1,0:T(8,128)(2,1)S(1)} %maximum_select_fusion.5), channel_id=1, source_target_pairs={{0,1},{1,0},{2,3},{3,2},{4,5},{5,4},{6,7},{7,6},{8,9},{9,8},{10,11... | collective-permute-start | bytes 6291464 | tf_op jit(solution)/shard_map/ppermute | solution.py:28
  217.6 38.3 %collective-permute-start.9 = (bf16[1024,1024]{1,0:T(8,128)(2,1)}, bf16[1024,1024]{1,0:T(8,128)(2,1)}, u32[]{:S(2)}, u32[]{:S(2)}) collective-permute-start(bf16[1024,1024]{1,0:T(8,128)(2,1)} %maximum_select_fusion.4), channel_id=1, source_target_pairs={{0,1},{1,0},{2,3},{3,2},{4,5},{5,4},{6,7},{7,6},{8,9},{9,8},{10,11... | collective-permute-start | bytes 6291464 | tf_op jit(solution)/shard_map/ppermute | solution.py:28
  248.5 25.0 %collective-permute-start.6 = (bf16[2,1,512,512]{3,2,0,1:T(8,128)(2,1)S(1)}, bf16[2,1,512,512]{3,2,0,1:T(8,128)(2,1)S(1)}, u32[]{:S(2)}, u32[]{:S(2)}) collective-permute-start(bf16[2,1,512,512]{3,2,0,1:T(8,128)(2,1)S(1)} %convert_bitcast_fusion), channel_id=1, source_target_pairs={{0,8},{8,0},{16,24},{24,16},{1,9},{9,1},{17,25},{25,17},{2,10},{10... | collective-permute-start | bytes 3145736 | tf_op jit(solution)/shard_map/ppermute | solution.py:28
  304.2 22.0 %collective-permute-start.14 = (f32[2,16,256]{2,1,0:T(8,128)}, f32[2,16,256]{2,1,0:T(8,128)S(1)}, u32[]{:S(2)}, u32[]{:S(2)}) collective-permute-start(f32[2,16,256]{2,1,0:T(8,128)} %get-tuple-element.134.near), channel_id=1, source_target_pairs={{0,8},{8,0},{16,24},{24,16},{1,9},{9,1},{17,25},{25,17},{2,10},{10... | collective-permute-start | bytes 98312 | tf_op jit(solution)/shard_map/ppermute | solution.py:28
  307.0 23.9 %collective-permute-start.13 = (bf16[2,1,512,512]{3,2,1,0:T(8,128)(2,1)S(1)}, bf16[2,1,512,512]{3,2,1,0:T(8,128)(2,1)S(1)}, u32[]{:S(2)}, u32[]{:S(2)}) collective-permute-start(bf16[2,1,512,512]{3,2,1,0:T(8,128)(2,1)S(1)} %constant_dynamic-slice_fusion.3), channel_id=1, source_target_pairs={{0,8},{8,0},{16,24},{24,16},{1,9},{9,1},{17,25},{25,17},{2,10},{10... | collective-permute-start | bytes 3145736 | tf_op jit(solution)/shard_map/ppermute | solution.py:28
  336.9 7.5 %collective-permute-start.15 = (bf16[1024,2048]{1,0:T(8,128)(2,1)}, bf16[1024,2048]{1,0:T(8,128)(2,1)}, u32[]{:S(2)}, u32[]{:S(2)}) collective-permute-start(bf16[1024,2048]{1,0:T(8,128)(2,1)} %get-tuple-element.143), channel_id=1, source_target_pairs={{0,1},{1,0},{2,3},{3,2},{4,5},{5,4},{6,7},{7,6},{8,9},{9,8},{10,11... | collective-permute-start | bytes 12582920 | tf_op jit(solution)/shard_map/ppermute | solution.py:28
  336.9 16.4 %collective-permute-start.18 = (bf16[1024,2048]{1,0:T(8,128)(2,1)}, bf16[1024,2048]{1,0:T(8,128)(2,1)}, u32[]{:S(2)}, u32[]{:S(2)}) collective-permute-start(bf16[1024,2048]{1,0:T(8,128)(2,1)} %get-tuple-element.152), channel_id=1, source_target_pairs={{0,1},{1,0},{2,3},{3,2},{4,5},{5,4},{6,7},{7,6},{8,9},{9,8},{10,11... | collective-permute-start | bytes 12582920 | tf_op jit(solution)/shard_map/ppermute | solution.py:28
  337.5 210.9 %all-gather.13.cloned.1.call-start = ((), (), s32[]{:S(2)}) async-start(), calls=%async_computation.6 | async-start | bytes 9437184 | tf_op jit(solution)/shard_map/all_gather | solution.py:1166
  351.8 47.9 %collective-permute-start.16 = (bf16[512,2048]{1,0:T(8,128)(2,1)}, bf16[512,2048]{1,0:T(8,128)(2,1)S(1)}, u32[]{:S(2)}, u32[]{:S(2)}) collective-permute-start(bf16[512,2048]{1,0:T(8,128)(2,1)} %get-tuple-element.145), channel_id=1, source_target_pairs={{0,4},{1,5},{2,6},{3,7},{4,0},{5,1},{6,2},{7,3},{8,12},{9,13},{10,... | collective-permute-start | bytes 6291464 | tf_op jit(solution)/shard_map/ppermute | solution.py:28
  360.1 47.9 %collective-permute-start.19 = (bf16[512,2048]{1,0:T(8,128)(2,1)}, bf16[512,2048]{1,0:T(8,128)(2,1)S(1)}, u32[]{:S(2)}, u32[]{:S(2)}) collective-permute-start(bf16[512,2048]{1,0:T(8,128)(2,1)} %get-tuple-element.154), channel_id=1, source_target_pairs={{0,2},{1,3},{2,0},{3,1},{4,6},{5,7},{6,4},{7,5},{8,10},{9,11},{10,... | collective-permute-start | bytes 6291464 | tf_op jit(solution)/shard_map/ppermute | solution.py:28
  405.1 25.6 %collective-permute-start.17 = (bf16[256,2048]{1,0:T(8,128)(2,1)}, bf16[256,2048]{1,0:T(8,128)(2,1)S(1)}, u32[]{:S(2)}, u32[]{:S(2)}) collective-permute-start(bf16[256,2048]{1,0:T(8,128)(2,1)} %get-tuple-element.148), channel_id=1, source_target_pairs={{0,2},{1,3},{2,0},{3,1},{4,6},{5,7},{6,4},{7,5},{8,10},{9,11},{10,... | collective-permute-start | bytes 3145736 | tf_op jit(solution)/shard_map/ppermute | solution.py:28
  414.1 24.1 %collective-permute-start.21 = (bf16[256,2048]{1,0:T(8,128)(2,1)}, bf16[256,2048]{1,0:T(8,128)(2,1)S(1)}, u32[]{:S(2)}, u32[]{:S(2)}) collective-permute-start(bf16[256,2048]{1,0:T(8,128)(2,1)} %get-tuple-element.156), channel_id=1, source_target_pairs={{0,4},{1,5},{2,6},{3,7},{4,0},{5,1},{6,2},{7,3},{8,12},{9,13},{10,... | collective-permute-start | bytes 3145736 | tf_op jit(solution)/shard_map/ppermute | solution.py:28
  430.9 54.9 %collective-permute-start.20 = (bf16[256,1024]{1,0:T(8,128)(2,1)S(1)}, bf16[256,1024]{1,0:T(8,128)(2,1)}, u32[]{:S(2)}, u32[]{:S(2)}) collective-permute-start(bf16[256,1024]{1,0:T(8,128)(2,1)S(1)} %add_convert_fusion.5), channel_id=1, source_target_pairs={{0,16},{8,24},{16,0},{24,8},{1,17},{9,25},{17,1},{25,9},{2,18},{10... | collective-permute-start | bytes 1572872 | tf_op jit(solution)/shard_map/ppermute | solution.py:28
  438.3 46.2 %collective-permute-start.22 = (bf16[128,2048]{1,0:T(8,128)(2,1)S(1)}, bf16[128,2048]{1,0:T(8,128)(2,1)}, u32[]{:S(2)}, u32[]{:S(2)}) collective-permute-start(bf16[128,2048]{1,0:T(8,128)(2,1)S(1)} %add_convert_fusion.4), channel_id=1, source_target_pairs={{0,16},{8,24},{16,0},{24,8},{1,17},{9,25},{17,1},{25,9},{2,18},{10... | collective-permute-start | bytes 1572872 | tf_op jit(solution)/shard_map/ppermute | solution.py:28
  462.8 25.4 %collective-permute-start.25 = (bf16[2,272,512]{2,1,0:T(8,128)(2,1)}, bf16[2,272,512]{2,1,0:T(8,128)(2,1)}, u32[]{:S(2)}, u32[]{:S(2)}) collective-permute-start(bf16[2,272,512]{2,1,0:T(8,128)(2,1)} %get-tuple-element.179), channel_id=1, source_target_pairs={{3,0},{4,1},{5,2},{6,3},{7,4},{11,8},{12,9},{13,10},{14,11},{15,12... | collective-permute-start | bytes 1671176 | tf_op jit(solution)/shard_map/ppermute | solution.py:24
  464.1 24.1 %collective-permute-start.24 = (bf16[2,272,512]{2,1,0:T(8,128)(2,1)}, bf16[2,272,512]{2,1,0:T(8,128)(2,1)}, u32[]{:S(2)}, u32[]{:S(2)}) collective-permute-start(bf16[2,272,512]{2,1,0:T(8,128)(2,1)} %get-tuple-element.179), channel_id=1, source_target_pairs={{2,0},{3,1},{4,2},{5,3},{6,4},{7,5},{10,8},{11,9},{12,10},{13,11},... | collective-permute-start | bytes 1671176 | tf_op jit(solution)/shard_map/ppermute | solution.py:24
  465.4 22.9 %collective-permute-start.23 = (bf16[2,272,512]{2,1,0:T(8,128)(2,1)}, bf16[2,272,512]{2,1,0:T(8,128)(2,1)}, u32[]{:S(2)}, u32[]{:S(2)}) collective-permute-start(bf16[2,272,512]{2,1,0:T(8,128)(2,1)} %get-tuple-element.179), channel_id=1, source_target_pairs={{1,0},{2,1},{3,2},{4,3},{5,4},{6,5},{7,6},{9,8},{10,9},{11,10},{12... | collective-permute-start | bytes 1671176 | tf_op jit(solution)/shard_map/ppermute | solution.py:24
  488.3 147.6 %reduce-scatter.5.cloned.1.call-start = ((), (), s32[]{:S(2)}) async-start(), calls=%async_computation.3 | async-start | bytes 5324800 | tf_op jit(solution)/shard_map/reduce_scatter | solution.py:1246
  488.3 51.5 %collective-permute-start.26 = (bf16[512,2048]{1,0:T(8,128)(2,1)}, bf16[512,2048]{1,0:T(8,128)(2,1)}, u32[]{:S(2)}, u32[]{:S(2)}) collective-permute-start(bf16[512,2048]{1,0:T(8,128)(2,1)} %get-tuple-element.173), channel_id=1, source_target_pairs={{0,1},{1,0},{2,3},{3,2},{4,5},{5,4},{6,7},{7,6},{8,9},{9,8},{10,11... | collective-permute-start | bytes 6291464 | tf_op jit(solution)/shard_map/ppermute | solution.py:28
  491.8 52.1 %collective-permute-start.27 = (bf16[1024,1024]{1,0:T(8,128)(2,1)}, bf16[1024,1024]{1,0:T(8,128)(2,1)S(1)}, u32[]{:S(2)}, u32[]{:S(2)}) collective-permute-start(bf16[1024,1024]{1,0:T(8,128)(2,1)} %get-tuple-element.170), channel_id=1, source_target_pairs={{0,1},{1,0},{2,3},{3,2},{4,5},{5,4},{6,7},{7,6},{8,9},{9,8},{10,11... | collective-permute-start | bytes 6291464 | tf_op jit(solution)/shard_map/ppermute | solution.py:28
  548.4 174.9 %all-gather.15.cloned.1.call-start = ((), (), s32[]{:S(2)}) async-start(), calls=%async_computation.7 | async-start | bytes 18874368 | tf_op jit(solution)/shard_map/all_gather | solution.py:1265
  548.4 9.4 %collective-permute-start.34 = (bf16[1024,1024]{1,0:T(8,128)(2,1)}, bf16[1024,1024]{1,0:T(8,128)(2,1)S(1)}, u32[]{:S(2)}, u32[]{:S(2)}) collective-permute-start(bf16[1024,1024]{1,0:T(8,128)(2,1)} %get-tuple-element.187), channel_id=1, source_target_pairs={{0,1},{1,0},{2,3},{3,2},{4,5},{5,4},{6,7},{7,6},{8,9},{9,8},{10,11... | collective-permute-start | bytes 6291464 | tf_op jit(solution)/shard_map/ppermute | solution.py:28
  548.8 31.2 %collective-permute-start.37 = (bf16[1024,1024]{1,0:T(8,128)(2,1)}, bf16[1024,1024]{1,0:T(8,128)(2,1)S(1)}, u32[]{:S(2)}, u32[]{:S(2)}) collective-permute-start(bf16[1024,1024]{1,0:T(8,128)(2,1)} %get-tuple-element.189), channel_id=1, source_target_pairs={{0,1},{1,0},{2,3},{3,2},{4,5},{5,4},{6,7},{7,6},{8,9},{9,8},{10,11... | collective-permute-start | bytes 6291464 | tf_op jit(solution)/shard_map/ppermute | solution.py:28
  549.0 28.1 %collective-permute-start.30 = (bf16[256,2048]{1,0:T(8,128)(2,1)}, bf16[256,2048]{1,0:T(8,128)(2,1)}, u32[]{:S(2)}, u32[]{:S(2)}) collective-permute-start(bf16[256,2048]{1,0:T(8,128)(2,1)} %get-tuple-element.191), channel_id=1, source_target_pairs={{0,2},{1,3},{2,0},{3,1},{4,6},{5,7},{6,4},{7,5},{8,10},{9,11},{10,... | collective-permute-start | bytes 3145736 | tf_op jit(solution)/shard_map/ppermute | solution.py:28
  557.8 30.2 %collective-permute-start.32 = (bf16[512,1024]{1,0:T(8,128)(2,1)}, bf16[512,1024]{1,0:T(8,128)(2,1)S(1)}, u32[]{:S(2)}, u32[]{:S(2)}) collective-permute-start(bf16[512,1024]{1,0:T(8,128)(2,1)} %get-tuple-element.199), channel_id=1, source_target_pairs={{0,4},{1,5},{2,6},{3,7},{4,0},{5,1},{6,2},{7,3},{8,12},{9,13},{10,... | collective-permute-start | bytes 3145736 | tf_op jit(solution)/shard_map/ppermute | solution.py:28
  563.9 35.6 %collective-permute-start.35 = (bf16[512,1024]{1,0:T(8,128)(2,1)}, bf16[512,1024]{1,0:T(8,128)(2,1)S(1)}, u32[]{:S(2)}, u32[]{:S(2)}) collective-permute-start(bf16[512,1024]{1,0:T(8,128)(2,1)} %get-tuple-element.205), channel_id=1, source_target_pairs={{0,2},{1,3},{2,0},{3,1},{4,6},{5,7},{6,4},{7,5},{8,10},{9,11},{10,... | collective-permute-start | bytes 3145736 | tf_op jit(solution)/shard_map/ppermute | solution.py:28
  579.9 15.3 %collective-permute-start.31 = (bf16[128,2048]{1,0:T(8,128)(2,1)}, bf16[128,2048]{1,0:T(8,128)(2,1)S(1)}, u32[]{:S(2)}, u32[]{:S(2)}) collective-permute-start(bf16[128,2048]{1,0:T(8,128)(2,1)} %get-tuple-element.196), channel_id=1, source_target_pairs={{0,4},{1,5},{2,6},{3,7},{4,0},{5,1},{6,2},{7,3},{8,12},{9,13},{10,... | collective-permute-start | bytes 1572872 | tf_op jit(solution)/shard_map/ppermute | solution.py:28
  586.0 31.7 %collective-permute-start.38 = (bf16[512,1024]{1,0:T(8,128)(2,1)}, bf16[512,1024]{1,0:T(8,128)(2,1)S(1)}, u32[]{:S(2)}, u32[]{:S(2)}) collective-permute-start(bf16[512,1024]{1,0:T(8,128)(2,1)} %get-tuple-element.212), channel_id=1, source_target_pairs={{0,4},{1,5},{2,6},{3,7},{4,0},{5,1},{6,2},{7,3},{8,12},{9,13},{10,... | collective-permute-start | bytes 3145736 | tf_op jit(solution)/shard_map/ppermute | solution.py:28
  591.7 31.4 %collective-permute-start.33 = (bf16[256,1024]{1,0:T(8,128)(2,1)}, bf16[256,1024]{1,0:T(8,128)(2,1)S(1)}, u32[]{:S(2)}, u32[]{:S(2)}) collective-permute-start(bf16[256,1024]{1,0:T(8,128)(2,1)} %get-tuple-element.201), channel_id=1, source_target_pairs={{0,2},{1,3},{2,0},{3,1},{4,6},{5,7},{6,4},{7,5},{8,10},{9,11},{10,... | collective-permute-start | bytes 1572872 | tf_op jit(solution)/shard_map/ppermute | solution.py:28
  603.2 25.1 %collective-permute-start.36 = (bf16[256,1024]{1,0:T(8,128)(2,1)}, bf16[256,1024]{1,0:T(8,128)(2,1)S(1)}, u32[]{:S(2)}, u32[]{:S(2)}) collective-permute-start(bf16[256,1024]{1,0:T(8,128)(2,1)} %get-tuple-element.208), channel_id=1, source_target_pairs={{0,4},{1,5},{2,6},{3,7},{4,0},{5,1},{6,2},{7,3},{8,12},{9,13},{10,... | collective-permute-start | bytes 1572872 | tf_op jit(solution)/shard_map/ppermute | solution.py:28
  621.5 12.8 %collective-permute-start.39 = (bf16[256,1024]{1,0:T(8,128)(2,1)}, bf16[256,1024]{1,0:T(8,128)(2,1)S(1)}, u32[]{:S(2)}, u32[]{:S(2)}) collective-permute-start(bf16[256,1024]{1,0:T(8,128)(2,1)} %get-tuple-element.215), channel_id=1, source_target_pairs={{0,2},{1,3},{2,0},{3,1},{4,6},{5,7},{6,4},{7,5},{8,10},{9,11},{10,... | collective-permute-start | bytes 1572872 | tf_op jit(solution)/shard_map/ppermute | solution.py:28
  640.9 27.8 %collective-permute-start.28 = (bf16[2,1,512,512]{3,2,1,0:T(8,128)(2,1)}, bf16[2,1,512,512]{3,2,1,0:T(8,128)(2,1)}, u32[]{:S(2)}, u32[]{:S(2)}) collective-permute-start(bf16[2,1,512,512]{3,2,1,0:T(8,128)(2,1)} %constant_dynamic-slice_fusion.1), channel_id=1, source_target_pairs={{0,8},{8,0},{16,24},{24,16},{1,9},{9,1},{17,25},{25,17},{2,10},{10... | collective-permute-start | bytes 3145736 | tf_op jit(solution)/shard_map/ppermute | solution.py:28
  671.0 25.6 %collective-permute-start.29 = (bf16[512,512]{1,0:T(8,128)(2,1)S(1)}, bf16[512,512]{1,0:T(8,128)(2,1)S(1)}, u32[]{:S(2)}, u32[]{:S(2)}) collective-permute-start(bf16[512,512]{1,0:T(8,128)(2,1)S(1)} %get-tuple-element.228), channel_id=1, source_target_pairs={{0,16},{8,24},{16,0},{24,8},{1,17},{9,25},{17,1},{25,9},{2,18},{10... | collective-permute-start | bytes 1572872 | tf_op jit(solution)/shard_map/ppermute | solution.py:28
  (33 other events, 204.1 us)
Sparse Core Ops, SparseCore 0:
  10.2 84.5 all-gather.8
  168.3 78.1 reduce-scatter.2
  337.6 81.1 all-gather.10
  488.4 59.9 all-gather.12
  551.2 77.8 reduce-scatter.4
  636.0 87.2 all-gather.14

commit v5 on v4

--- a/solution.py
+++ b/solution.py
@@ -108,6 +108,7 @@
 TILE = 256
 EXTRA = 16
 CHUNK = 512
+WIDE = 512
 VMEM_LIMIT = 58 << 20
 
 
@@ -161,7 +162,7 @@
 
 def tile_decay(log_decay, behind, docs_col, docs_row, pads_row):
     rows = lax.broadcasted_iota(jnp.int32, (TILE, 1), 0)
-    cols = lax.broadcasted_iota(jnp.int32, (1, TILE), 1)
+    cols = lax.broadcasted_iota(jnp.int32, (1, WIDE), 1)
     allowed = (docs_col == docs_row) & (rows + behind >= cols) & (pads_row > 0)
     rise = jnp.exp(rows.astype(F32) * log_decay)
     fall = jnp.exp((behind - cols).astype(F32) * log_decay)
@@ -238,18 +239,18 @@
     docs_col = dcol[...]
 
     def turn(j, totals):
-        at = pl.ds(pl.multiple_of(j * TILE, TILE), TILE)
+        at = pl.ds(pl.multiple_of(j * WIDE, WIDE), WIDE)
         sums = []
         for h in range(heads):
             mine = slice(h * KD, (h + 1) * KD)
             wide = slice(h * VD, (h + 1) * VD)
-            factor = tile_decay(decay[h], (step - j) * TILE, docs_col, drow[:, at], prow[:, at])
+            factor = tile_decay(decay[h], step * TILE - j * WIDE, docs_col, drow[:, at], prow[:, at])
             weights = (dot_nt(q[:, mine], k[at, mine]) * factor).astype(BF)
             sums.append(totals[h] + dot(weights, v[at, wide]))
         return tuple(sums)
 
     zeros = tuple(jnp.zeros((TILE, VD), F32) for _ in range(heads))
-    totals = lax.fori_loop(0, step + 1, turn, zeros)
+    totals = lax.fori_loop(0, step * TILE // WIDE + 1, turn, zeros)
     for h in range(heads):
         inner_out[:, h * VD : (h + 1) * VD] = totals[h]
 
@@ -346,13 +347,13 @@
     docs_col = dcol[...]
 
     def turn(j, totals):
-        at = pl.ds(pl.multiple_of(j * TILE, TILE), TILE)
+        at = pl.ds(pl.multiple_of(j * WIDE, WIDE), WIDE)
         sums = []
         for h in range(heads):
             mine = slice(h * KD, (h + 1) * KD)
             wide = slice(h * VD, (h + 1) * VD)
             query, grad_mixed, key = q[:, mine], mix[:, wide], k[at, mine]
-            factor = tile_decay(decay[h], (step - j) * TILE, docs_col, drow[:, at], prow[:, at])
+            factor = tile_decay(decay[h], step * TILE - j * WIDE, docs_col, drow[:, at], prow[:, at])
             weights = (dot_nt(query, key) * factor).astype(BF)
             grads = (dot_nt(grad_mixed, v[at, wide]) * factor).astype(BF)
             dk_out[at, mine] += dot_tn(grads, query)
@@ -361,7 +362,7 @@
         return tuple(sums)
 
     zeros = tuple(jnp.zeros((TILE, KD), F32) for _ in range(heads))
-    totals = lax.fori_loop(0, step + 1, turn, zeros)
+    totals = lax.fori_loop(0, step * TILE // WIDE + 1, turn, zeros)
     for h in range(heads):
         mine = slice(h * KD, (h + 1) * KD)
         wide = slice(h * VD, (h + 1) * VD)

time: 758 us -> 755 us (level)
  transfers between devices with their start and end apart: 46 -> 46, of which waited for: 23 -> 23; matrix products, arithmetic and copies ran while one was open for 9% -> 9% of each run, Pallas kernels for 32% -> 31%
where the time goes in v5:
time: 755 us; the launch traced here: 745 us
  waiting for transfers between devices  292 us (39%)
  Pallas kernels  287 us (38%)
  starting transfers between devices  57.8 us (8%)
  other arithmetic  46.5 us (6%)
  local copies, waits for them, and re-layouts  34 us (5%)
  between operations  15.3 us (2%)
  blocking collectives  12.8 us (2%)
    ppermute x34, waiting for transfers between devices, swapped(): lax.ppermute(value, axis, [(i, i ^ mask) for i in range(lax.axis_size(axi...  155 us
    all_gather x1, waiting for transfers between devices, body(): rows_raw = lax.all_gather(packed, 'head', axis=0)  77.2 us
    pallas_call x12, Pallas kernels, fold(): prefetched(partial(fold_kernel, count), (2 * count,), [spec, spec], [pl.B...  52.5 us
    pallas_call x5, Pallas kernels, weight_grad(): prefetched(partial(weight_kernel, count), (2 * count,), [pl.BlockSpec((ro...  44.8 us
    ppermute x34, starting transfers between devices, swapped(): lax.ppermute(value, axis, [(i, i ^ mask) for i in range(lax.axis_size(axi...  42.9 us
    pallas_call x2, Pallas kernels, in_order(): pl.pallas_call(partial(order_kernel, [len(parts) for _, parts in plan]),...  28.4 us
    pallas_call x1, Pallas kernels, body(): call(partial(finish_kernel, heads_here, row_count), row_count, [SCALARS,...  27.2 us
    pallas_call x1, Pallas kernels, body(): pl.pallas_call(partial(feed_kernel, chunks), grid=(2 * chunks,), in_specs...  26.9 us
  transfers between devices with their start and end apart: 46, of which 23 were waited for; matrix products, arithmetic and copies ran while one was open for 9% of the time, Pallas kernels for 31%

profile of v5, /device:TPU:0, one launch (start us, length us, event | category | flops | bytes accessed | tf_op | source)
XLA Modules:
  0.0 745.2 jit_solution(1425655960395763997)
XLA Ops:
  17.5 77.2 %all-gather.9.cloned.1.call-done = bf16[4160,512]{1,0:T(8,128)(2,1)} async-done(((bf16[1040,512]{1,0:T(8,128)(2,1)}), bf16[4160,512]{1,0:T(8,128)(2,1)}) %all-gather.9.cloned.1.call-update) | async-done | bytes 4259856 | tf_op jit(solution)/shard_map/all_gather | solution.py:791
  98.8 19.2 %shard_map.247 = (bf16[1024,2048]{1,0:T(8,128)(2,1)}, bf16[1024,512]{1,0:T(8,128)(2,1)}, bf16[1024,512]{1,0:T(8,128)(2,1)}, bf16[1024,1024]{1,0:T(8,128)(2,1)}, ...) custom-call(s32[1]{0:T(128)} %slice.108.docs, bf16[4,1040,512]{2,1,0:T(8,128)(2,1)} %bitcast.109, ...), custom_call_target="tpu_custom_call" | custom-call | tf_op jit(solution)/shard_map/pallas_call | solution.py:835
  125.0 4.2 collective-permute-start.2
  135.9 16.7 %shard_map.248 = (f32[1024,1024]{1,0:T(8,128)}, f32[1024,1024]{1,0:T(8,128)}) custom-call(f32[2]{0:T(128)} %copy-done.34, bf16[1024,2048]{1,0:T(8,128)(2,1)} %get-tuple-element.122.low.left, bf16[2048,1024]{1,0:T(8,128)(2,1)} %wg.3, bf16[1024,512]{1,0:T(8,128)(2,1)} %get-tuple-element.123.q, bf16[1024,512]{1,0:T(8,128)(2,1)} %get-tuple-element.124.k, ...), custom_call_target="tpu_custom_call" | custom-call | tf_op jit(solution)/shard_map/pallas_call | solution.py:887
  152.7 14.1 %shard_map.249 = (f32[1024,1024]{1,0:T(8,128)}, f32[1024,2]{1,0:T(8,128)}, bf16[1024,1024]{1,0:T(8,128)(2,1)}, bf16[2,2,2,512,512]{4,3,2,1,0:T(8,128)(2,1)}, bf1...) custom-call(f32[2]{0:T(128)} %copy-done.34, f32[1024,1024]{1,0:T(8,128)} %get-tuple-element.126.inner, ...), custom_call_target="tpu_custom_call" | custom-call | tf_op jit(solution)/shard_map/pallas_call | solution.py:914
  171.7 4.1 collective-permute-start.7
  175.8 7.3 collective-permute-done.10
  190.7 19.0 %collective-permute-done.11 = bf16[256,2048]{1,0:T(8,128)(2,1)} collective-permute-done((bf16[256,2048]{1,0:T(8,128)(2,1)S(1)}, bf16[256,2048]{1,0:T(8,128)(2,1)}, u32[]{:S(2)}, u32[]{:S(2)}) %collective-permute-start.11) | collective-permute-done | bytes 1048608 | tf_op jit(solution)/shard_map/ppermute | solution.py:28
  220.5 26.1 %reduce-scatter.3.cloned.1.call-done = bf16[1,2,512,512]{3,2,1,0:T(8,128)(2,1)} async-done(((bf16[4,2,512,512]{3,2,1,0:T(8,128)(2,1)}), bf16[1,2,512,512]{3,2,1,0:T(8,128)(2,1)}) %reduce-scatter.3.cloned.1.call-update) | async-done | bytes 1048592 | tf_op jit(solution)/shard_map/reduce_scatter | solution.py:966
  250.7 5.2 maximum_select_fusion.1.down_far
  255.9 5.5 maximum_select_fusion.up_far
  261.4 12.2 %collective-permute-done.6 = bf16[2,1,512,512]{3,2,0,1:T(8,128)(2,1)S(1)} collective-permute-done((bf16[2,1,512,512]{3,2,0,1:T(8,128)(2,1)S(1)}, bf16[2,1,512,512]{3,2,0,1:T(8,128)(2,1)S(1)}, u32[]{:S(2)}, u32[]{:S(2)}) %collective-permute-start.6) | collective-permute-done | bytes 1048608 | tf_op jit(solution)/shard_map/ppermute | solution.py:28
  277.2 26.9 %shard_map.250 = (bf16[512,2048]{1,0:T(8,128)(2,1)}, bf16[512,2048]{1,0:T(8,128)(2,1)}, bf16[512,2048]{1,0:T(8,128)(2,1)}, bf16[512,2048]{1,0:T(8,128)(2,1)}, bf...) custom-call(bf16[4,512,512]{2,1,0:T(8,128)(2,1)} %bitcast.116, ...), custom_call_target="tpu_custom_call" | custom-call | tf_op jit(solution)/shard_map/pallas_call | solution.py:974
  307.6 9.3 %shard_map.251 = (bf16[1024,2048]{1,0:T(8,128)(2,1)}, bf16[1024,2048]{1,0:T(8,128)(2,1)}) custom-call(s32[1]{0:T(128)} %bitcast.34.mine, bf16[512,2048]{1,0:T(8,128)(2,1)} %get-tuple-element.141.left.act, bf16[512,2048]{1,0:T(8,128)(2,1)} %get-tuple-element.135.refs_0_), custom_call_target="tpu_custom_call" | custom-call | flops 8589934592 | tf_op jit(solution)/shard_map/pallas_call | solution.py:590
  316.9 9.2 %shard_map.252 = (bf16[1024,2048]{1,0:T(8,128)(2,1)}, bf16[1024,2048]{1,0:T(8,128)(2,1)}) custom-call(s32[1]{0:T(128)} %bitcast.34.mine, bf16[512,2048]{1,0:T(8,128)(2,1)} %get-tuple-element.137.left, bf16[512,2048]{1,0:T(8,128)(2,1)} %get-tuple-element.138.refs_0_), custom_call_target="tpu_custom_call" | custom-call | flops 8589934592 | tf_op jit(solution)/shard_map/pallas_call | solution.py:590
  326.1 4.8 collective-permute-done.13.other
  331.9 5.1 shard_map.253
  337.5 6.9 collective-permute-done.15.two
  344.4 7.2 shard_map.255
  353.2 6.7 shard_map.257
  361.3 9.5 %shard_map.254 = bf16[2,2,512,512]{3,2,1,0:T(8,128)(2,1)} custom-call(bf16[512,2048]{1,0:T(8,128)(2,1)} %get-tuple-element.141.left.act, bf16[1024,2048]{1,0:T(8,128)(2,1)} %down_near.3, bf16[1024,2048]{1,0:T(8,128)(2,1)} %maximum_select_fusion.1.down_far), custom_call_target="tpu_custom_call" | custom-call | tf_op jit(solution)/shard_map/pallas_call | solution.py:1051
  370.8 28.7 %collective-permute-done.16.two = bf16[512,2048]{1,0:T(8,128)(2,1)S(1)} collective-permute-done((bf16[512,2048]{1,0:T(8,128)(2,1)}, bf16[512,2048]{1,0:T(8,128)(2,1)S(1)}, u32[]{:S(2)}, u32[]{:S(2)}) %collective-permute-start.16) | collective-permute-done | bytes 2097184 | tf_op jit(solution)/shard_map/ppermute | solution.py:28
  400.9 4.1 shard_map.256
  409.1 4.8 shard_map.258
  418.8 11.9 %shard_map.259 = (bf16[1024,1024]{1,0:T(8,128)(2,1)}, bf16[1024,1024]{1,0:T(8,128)(2,1)}) custom-call(bf16[2,2,2,512,512]{4,3,2,1,0:T(8,128)(2,1)} %bitcast.118, bf16[1024,2048]{1,0:T(8,128)(2,1)} %wo.3, f32[1024,1024]{1,0:T(8,128)} %get-tuple-element.127.gate, f32[1024,1024]{1,0:T(8,128)} %get-tuple-element.149.group, f32[1024,2]{1,0:T(8,128)} %get-tuple-element.150.scale, ...), custom_call_target="tpu_custom_call" | custom-call | tf_op jit(solution)/shard_map/pallas_call | solution.py:1068
  432.5 5.5 collective-permute-done.21
  440.4 19.2 %shard_map.260 = (bf16[1024,512]{1,0:T(8,128)(2,1)}, f32[1024,512]{1,0:T(8,128)}, f32[1024,1024]{1,0:T(8,128)}, bf16[2,272,512]{2,1,0:T(8,128)(2,1)}) custom-call(s32[1]{0:T(128)} %slice.108.docs, f32[2]{0:T(128)} %copy-done.34, bf16[1024,1024]{1,0:T(8,128)(2,1)} %get-tuple-element.165.mix, bf16[1024,512]{1,0:T(8,128)(2,1)} %get-tuple-element.123.q, ...), custom_call_target="tpu_custom_call" | custom-call | flops 21474836480 | tf_op jit(solution)/shard_map/pallas_call | solution.py:1094
  463.5 9.1 %shard_map.262 = (bf16[512,2048]{1,0:T(8,128)(2,1)}, bf16[512,2048]{1,0:T(8,128)(2,1)}) custom-call(s32[1]{0:T(128)} %bitcast.34.mine, bf16[1024,1024]{1,0:T(8,128)(2,1)} %get-tuple-element.172.gated, bf16[2,2,2,512,512]{4,3,2,1,0:T(8,128)(2,1)} %bitcast.119), custom_call_target="tpu_custom_call" | custom-call | flops 8589934592 | tf_op jit(solution)/shard_map/pallas_call | solution.py:1142
  472.6 8.8 %shard_map.261 = (bf16[1024,1024]{1,0:T(8,128)(2,1)}, bf16[1024,1024]{1,0:T(8,128)(2,1)}) custom-call(s32[1]{0:T(128)} %bitcast.34.mine, bf16[1024,2048]{1,0:T(8,128)(2,1)} %get-tuple-element.122.low.left, bf16[1024,1024]{1,0:T(8,128)(2,1)} %get-tuple-element.169.refs_0_.dgate), custom_call_target="tpu_custom_call" | custom-call | flops 8589934592 | tf_op jit(solution)/shard_map/pallas_call | solution.py:590
  488.8 27.2 %shard_map.263 = (bf16[1024,512]{1,0:T(8,128)(2,1)}, bf16[1024,1024]{1,0:T(8,128)(2,1)}, bf16[4,1040,512]{2,1,0:T(8,128)(2,1)}, f32[4,16,256]{2,1,0:T(8,128)}, f32[2,2048]{1,0:T(2,128)}) custom-call(s32[1]{0:T(128)} %slice.108.docs, f32[2]{0:T(128)} %copy-done.34, f32[1024,512]{1,0:T(8,128)} %get-tuple-element.177.dk_in, ...), custom_call_target="tpu_custom_call" | custom-call | flops 25769803776 | tf_op jit(solution)/shard_map/pallas_call | solution.py:1171
  519.1 8.7 %shard_map.265 = (bf16[1024,1024]{1,0:T(8,128)(2,1)}, bf16[1024,1024]{1,0:T(8,128)(2,1)}) custom-call(s32[1]{0:T(128)} %bitcast.34.mine, bf16[1024,2048]{1,0:T(8,128)(2,1)} %get-tuple-element.122.low.left, bf16[1024,512]{1,0:T(8,128)(2,1)} %get-tuple-element.168.dq.refs_0_, bf16[1024,512]{1,0:T(8,128)(2,1)} %get-tuple-element.188.refs_1_), custom_call_target="tpu_custom_call" | custom-call | flops 8589934592 | tf_op jit(solution)/shard_map/pallas_call | solution.py:590
  527.8 8.8 %shard_map.264 = (bf16[1024,1024]{1,0:T(8,128)(2,1)}, bf16[1024,1024]{1,0:T(8,128)(2,1)}) custom-call(s32[1]{0:T(128)} %bitcast.34.mine, bf16[1024,2048]{1,0:T(8,128)(2,1)} %get-tuple-element.122.low.left, bf16[1024,1024]{1,0:T(8,128)(2,1)} %get-tuple-element.186.refs_0_), custom_call_target="tpu_custom_call" | custom-call | flops 8589934592 | tf_op jit(solution)/shard_map/pallas_call | solution.py:590
  536.6 4.1 shard_map.266
  540.7 4.3 all-gather.13.cloned.1.call-done
  549.6 5.1 shard_map.268
  556.0 4.8 shard_map.270
  561.0 13.0 %collective-permute-done.30.two = bf16[256,2048]{1,0:T(8,128)(2,1)} collective-permute-done((bf16[256,2048]{1,0:T(8,128)(2,1)}, bf16[256,2048]{1,0:T(8,128)(2,1)}, u32[]{:S(2)}, u32[]{:S(2)}) %collective-permute-start.30) | collective-permute-done | bytes 1048608 | tf_op jit(solution)/shard_map/ppermute | solution.py:28
  578.1 4.8 shard_map.272
  592.3 4.0 collective-permute-done.35.two
  600.1 14.5 %collective-permute-done.38.two = bf16[512,1024]{1,0:T(8,128)(2,1)S(1)} collective-permute-done((bf16[512,1024]{1,0:T(8,128)(2,1)}, bf16[512,1024]{1,0:T(8,128)(2,1)S(1)}, u32[]{:S(2)}, u32[]{:S(2)}) %collective-permute-start.38) | collective-permute-done | bytes 1048608 | tf_op jit(solution)/shard_map/ppermute | solution.py:28
  620.2 4.9 collective-permute-done.36
  625.3 5.9 collective-permute-done.39
  632.8 4.0 fusion.11
  640.8 10.4 %shard_map.275 = (f32[1024,2048]{1,0:T(8,128)}, f32[2048,1024]{1,0:T(8,128)}) custom-call(bf16[8,512,1024]{2,1,0:T(8,128)(2,1)} %bitcast.107, bf16[8,512,1024]{2,1,0:T(8,128)(2,1)} %bitcast.108), custom_call_target="tpu_custom_call" | custom-call | tf_op jit(solution)/shard_map/pallas_call | solution.py:748
  652.7 12.8 %psum.7 = f32[4,512]{1,0:T(4,128)S(1)} all-reduce(f32[4,512]{1,0:T(4,128)S(1)} %slice_bitcast_fusion.1), channel_id=1, replica_groups=mesh['head'=4,'tok'=8] {'tok'}, use_global_device_ids=true, to_apply=%region_2.3 | all-reduce | flops 2048 | bytes 16384 | tf_op jit(solution)/shard_map/psum | solution.py:1254
  670.8 22.5 %collective-permute-done.29 = bf16[512,512]{1,0:T(8,128)(2,1)S(1)} collective-permute-done((bf16[512,512]{1,0:T(8,128)(2,1)S(1)}, bf16[512,512]{1,0:T(8,128)(2,1)S(1)}, u32[]{:S(2)}, u32[]{:S(2)}) %collective-permute-start.29) | collective-permute-done | bytes 524320 | tf_op jit(solution)/shard_map/ppermute | solution.py:28
  694.7 25.2 %all-gather.15.cloned.1.call-done = bf16[8192,1024]{1,0:T(8,128)(2,1)} async-done(((bf16[1024,1024]{1,0:T(8,128)(2,1)}), bf16[8192,1024]{1,0:T(8,128)(2,1)}) %all-gather.15.cloned.1.call-update) | async-done | bytes 16777232 | tf_op jit(solution)/shard_map/all_gather | solution.py:1266
  720.0 17.9 %shard_map.274 = (f32[1024,2048]{1,0:T(8,128)}, f32[2048,1024]{1,0:T(8,128)}, f32[2048,1024]{1,0:T(8,128)}, f32[2048,512]{1,0:T(8,128)}, f32[2048,512]{1,0:T(8,128)}) custom-call(bf16[8,1024,1024]{2,1,0:T(8,128)(2,1)} %bitcast.103, bf16[8,1024,1024]{2,1,0:T(8,128)(2,1)} %bitcast.104, bf16[8,1024,1024]{2,1,0:T(8,128)(2,1)} %bitcast.105, ...), custom_call_target="tpu_custom_call" | custom-call | tf_op jit(solution)/shard_map/pallas_call | solution.py:748
  (231 shorter events, 138.9 us)
Async XLA Ops:
  7.2 87.6 %all-gather.9.cloned.1.call-start = ((), (), s32[]{:S(2)}) async-start(), calls=%async_computation.4 | async-start | bytes 5324800 | tf_op jit(solution)/shard_map/all_gather | solution.py:791
  9.6 236.9 %reduce-scatter.3.cloned.1.call-start = ((), (), s32[]{:S(2)}) async-start(), calls=%async_computation.2 | async-start | bytes 5242880 | tf_op jit(solution)/shard_map/reduce_scatter | solution.py:966
  12.1 82.6 %copy-start.21 = (bf16[1024,512]{1,0:T(8,128)(2,1)S(1)}, bf16[1024,512]{1,0:T(8,128)(2,1)}, u32[]{:S(2)}) copy-start(bf16[1024,512]{1,0:T(8,128)(2,1)} %param.29) | copy-start | bytes 3145732
  12.4 85.2 %copy-start.34 = (f32[2]{0:T(128)}, f32[2]{0:T(128)S(1)}, u32[]{:S(2)}) copy-start(f32[2]{0:T(128)S(1)} %subtract_log_fusion.decay) | copy-start | bytes 28
  94.8 24.3 %collective-permute-start = (bf16[512,512]{1,0:T(8,128)(2,1)S(1)}, bf16[512,512]{1,0:T(8,128)(2,1)S(1)}, u32[]{:S(2)}, u32[]{:S(2)}) collective-permute-start(bf16[512,512]{1,0:T(8,128)(2,1)S(1)} %get-tuple-element.232), channel_id=1, source_target_pairs={{0,16},{8,24},{16,0},{24,8},{1,17},{9,25},{17,1},{25,9},{2,18},{10... | collective-permute-start | bytes 1572872 | tf_op jit(solution)/shard_map/ppermute | solution.py:28
  119.2 47.5 %collective-permute-start.4 = (bf16[2,1,512,512]{3,2,0,1:T(8,128)(2,1)S(1)}, bf16[2,1,512,512]{3,2,0,1:T(8,128)(2,1)S(1)}, u32[]{:S(2)}, u32[]{:S(2)}) collective-permute-start(bf16[2,1,512,512]{3,2,0,1:T(8,128)(2,1)S(1)} %maximum_select_fusion.7), channel_id=1, source_target_pairs={{0,8},{8,0},{16,24},{24,16},{1,9},{9,1},{17,25},{25,17},{2,10},{10... | collective-permute-start | bytes 3145736 | tf_op jit(solution)/shard_map/ppermute | solution.py:28
  119.3 48.9 %collective-permute-start.5 = (bf16[512,1024]{1,0:T(8,128)(2,1)}, bf16[512,1024]{1,0:T(8,128)(2,1)}, u32[]{:S(2)}, u32[]{:S(2)}) collective-permute-start(bf16[512,1024]{1,0:T(8,128)(2,1)} %pad_maximum_fusion), channel_id=1, source_target_pairs={{0,16},{8,24},{16,0},{24,8},{1,17},{9,25},{17,1},{25,9},{2,18},{10... | collective-permute-start | bytes 3145736 | tf_op jit(solution)/shard_map/ppermute | solution.py:28
  122.3 30.4 %collective-permute-start.3 = (bf16[2,272,512]{2,1,0:T(8,128)(2,1)}, bf16[2,272,512]{2,1,0:T(8,128)(2,1)}, u32[]{:S(2)}, u32[]{:S(2)}) collective-permute-start(bf16[2,272,512]{2,1,0:T(8,128)(2,1)} %get-tuple-element.119), channel_id=1, source_target_pairs={{0,3},{1,4},{2,5},{3,6},{4,7},{8,11},{9,12},{10,13},{11,14},{12,15... | collective-permute-start | bytes 1671176 | tf_op jit(solution)/shard_map/ppermute | solution.py:24
  125.0 27.7 %collective-permute-start.2 = (bf16[2,272,512]{2,1,0:T(8,128)(2,1)}, bf16[2,272,512]{2,1,0:T(8,128)(2,1)}, u32[]{:S(2)}, u32[]{:S(2)}) collective-permute-start(bf16[2,272,512]{2,1,0:T(8,128)(2,1)} %get-tuple-element.119), channel_id=1, source_target_pairs={{0,2},{1,3},{2,4},{3,5},{4,6},{5,7},{8,10},{9,11},{10,12},{11,13},... | collective-permute-start | bytes 1671176 | tf_op jit(solution)/shard_map/ppermute | solution.py:24
  129.2 23.5 %collective-permute-start.1 = (bf16[2,272,512]{2,1,0:T(8,128)(2,1)}, bf16[2,272,512]{2,1,0:T(8,128)(2,1)}, u32[]{:S(2)}, u32[]{:S(2)}) collective-permute-start(bf16[2,272,512]{2,1,0:T(8,128)(2,1)} %get-tuple-element.119), channel_id=1, source_target_pairs={{0,1},{1,2},{2,3},{3,4},{4,5},{5,6},{6,7},{8,9},{9,10},{10,11},{11... | collective-permute-start | bytes 1671176 | tf_op jit(solution)/shard_map/ppermute | solution.py:24
  168.2 250.6 %all-gather.11.cloned.1.call-start = ((), (), s32[]{:S(2)}) async-start(), calls=%async_computation.5 | async-start | bytes 5242880 | tf_op jit(solution)/shard_map/all_gather | solution.py:1047
  170.1 13.0 %collective-permute-start.10 = (bf16[128,2048]{1,0:T(8,128)(2,1)S(1)}, bf16[128,2048]{1,0:T(8,128)(2,1)}, u32[]{:S(2)}, u32[]{:S(2)}) collective-permute-start(bf16[128,2048]{1,0:T(8,128)(2,1)S(1)} %reshape.210), channel_id=1, source_target_pairs={{0,2},{1,3},{2,0},{3,1},{4,6},{5,7},{6,4},{7,5},{8,10},{9,11},{10,... | collective-permute-start | bytes 1572872 | tf_op jit(solution)/shard_map/ppermute | solution.py:28
  171.7 15.7 %collective-permute-start.7 = (bf16[256,1024]{1,0:T(8,128)(2,1)S(1)}, bf16[256,1024]{1,0:T(8,128)(2,1)}, u32[]{:S(2)}, u32[]{:S(2)}) collective-permute-start(bf16[256,1024]{1,0:T(8,128)(2,1)S(1)} %get-tuple-element.230), channel_id=1, source_target_pairs={{0,4},{1,5},{2,6},{3,7},{4,0},{5,1},{6,2},{7,3},{8,12},{9,13},{10,... | collective-permute-start | bytes 1572872 | tf_op jit(solution)/shard_map/ppermute | solution.py:28
  184.6 25.1 %collective-permute-start.11 = (bf16[256,2048]{1,0:T(8,128)(2,1)S(1)}, bf16[256,2048]{1,0:T(8,128)(2,1)}, u32[]{:S(2)}, u32[]{:S(2)}) collective-permute-start(bf16[256,2048]{1,0:T(8,128)(2,1)S(1)} %maximum_select_fusion.9), channel_id=1, source_target_pairs={{0,4},{1,5},{2,6},{3,7},{4,0},{5,1},{6,2},{7,3},{8,12},{9,13},{10,... | collective-permute-start | bytes 3145736 | tf_op jit(solution)/shard_map/ppermute | solution.py:28
  189.0 25.1 %collective-permute-start.8 = (bf16[512,1024]{1,0:T(8,128)(2,1)S(1)}, bf16[512,1024]{1,0:T(8,128)(2,1)S(1)}, u32[]{:S(2)}, u32[]{:S(2)}) collective-permute-start(bf16[512,1024]{1,0:T(8,128)(2,1)S(1)} %maximum_select_fusion.8), channel_id=1, source_target_pairs={{0,2},{1,3},{2,0},{3,1},{4,6},{5,7},{6,4},{7,5},{8,10},{9,11},{10,... | collective-permute-start | bytes 3145736 | tf_op jit(solution)/shard_map/ppermute | solution.py:28
  212.8 37.9 %collective-permute-start.12 = (bf16[512,2048]{1,0:T(8,128)(2,1)S(1)}, bf16[512,2048]{1,0:T(8,128)(2,1)}, u32[]{:S(2)}, u32[]{:S(2)}) collective-permute-start(bf16[512,2048]{1,0:T(8,128)(2,1)S(1)} %maximum_select_fusion.5), channel_id=1, source_target_pairs={{0,1},{1,0},{2,3},{3,2},{4,5},{5,4},{6,7},{7,6},{8,9},{9,8},{10,11... | collective-permute-start | bytes 6291464 | tf_op jit(solution)/shard_map/ppermute | solution.py:28
  216.4 39.5 %collective-permute-start.9 = (bf16[1024,1024]{1,0:T(8,128)(2,1)}, bf16[1024,1024]{1,0:T(8,128)(2,1)}, u32[]{:S(2)}, u32[]{:S(2)}) collective-permute-start(bf16[1024,1024]{1,0:T(8,128)(2,1)} %maximum_select_fusion.4), channel_id=1, source_target_pairs={{0,1},{1,0},{2,3},{3,2},{4,5},{5,4},{6,7},{7,6},{8,9},{9,8},{10,11... | collective-permute-start | bytes 6291464 | tf_op jit(solution)/shard_map/ppermute | solution.py:28
  248.5 25.0 %collective-permute-start.6 = (bf16[2,1,512,512]{3,2,0,1:T(8,128)(2,1)S(1)}, bf16[2,1,512,512]{3,2,0,1:T(8,128)(2,1)S(1)}, u32[]{:S(2)}, u32[]{:S(2)}) collective-permute-start(bf16[2,1,512,512]{3,2,0,1:T(8,128)(2,1)S(1)} %convert_bitcast_fusion), channel_id=1, source_target_pairs={{0,8},{8,0},{16,24},{24,16},{1,9},{9,1},{17,25},{25,17},{2,10},{10... | collective-permute-start | bytes 3145736 | tf_op jit(solution)/shard_map/ppermute | solution.py:28
  304.2 22.0 %collective-permute-start.14 = (f32[2,16,256]{2,1,0:T(8,128)}, f32[2,16,256]{2,1,0:T(8,128)S(1)}, u32[]{:S(2)}, u32[]{:S(2)}) collective-permute-start(f32[2,16,256]{2,1,0:T(8,128)} %get-tuple-element.134.near), channel_id=1, source_target_pairs={{0,8},{8,0},{16,24},{24,16},{1,9},{9,1},{17,25},{25,17},{2,10},{10... | collective-permute-start | bytes 98312 | tf_op jit(solution)/shard_map/ppermute | solution.py:28
  307.0 23.9 %collective-permute-start.13 = (bf16[2,1,512,512]{3,2,1,0:T(8,128)(2,1)S(1)}, bf16[2,1,512,512]{3,2,1,0:T(8,128)(2,1)S(1)}, u32[]{:S(2)}, u32[]{:S(2)}) collective-permute-start(bf16[2,1,512,512]{3,2,1,0:T(8,128)(2,1)S(1)} %constant_dynamic-slice_fusion.3), channel_id=1, source_target_pairs={{0,8},{8,0},{16,24},{24,16},{1,9},{9,1},{17,25},{25,17},{2,10},{10... | collective-permute-start | bytes 3145736 | tf_op jit(solution)/shard_map/ppermute | solution.py:28
  336.9 7.5 %collective-permute-start.15 = (bf16[1024,2048]{1,0:T(8,128)(2,1)}, bf16[1024,2048]{1,0:T(8,128)(2,1)}, u32[]{:S(2)}, u32[]{:S(2)}) collective-permute-start(bf16[1024,2048]{1,0:T(8,128)(2,1)} %get-tuple-element.143), channel_id=1, source_target_pairs={{0,1},{1,0},{2,3},{3,2},{4,5},{5,4},{6,7},{7,6},{8,9},{9,8},{10,11... | collective-permute-start | bytes 12582920 | tf_op jit(solution)/shard_map/ppermute | solution.py:28
  336.9 16.2 %collective-permute-start.18 = (bf16[1024,2048]{1,0:T(8,128)(2,1)}, bf16[1024,2048]{1,0:T(8,128)(2,1)}, u32[]{:S(2)}, u32[]{:S(2)}) collective-permute-start(bf16[1024,2048]{1,0:T(8,128)(2,1)} %get-tuple-element.152), channel_id=1, source_target_pairs={{0,1},{1,0},{2,3},{3,2},{4,5},{5,4},{6,7},{7,6},{8,9},{9,8},{10,11... | collective-permute-start | bytes 12582920 | tf_op jit(solution)/shard_map/ppermute | solution.py:28
  337.5 207.6 %all-gather.13.cloned.1.call-start = ((), (), s32[]{:S(2)}) async-start(), calls=%async_computation.6 | async-start | bytes 9437184 | tf_op jit(solution)/shard_map/all_gather | solution.py:1167
  351.6 47.9 %collective-permute-start.16 = (bf16[512,2048]{1,0:T(8,128)(2,1)}, bf16[512,2048]{1,0:T(8,128)(2,1)S(1)}, u32[]{:S(2)}, u32[]{:S(2)}) collective-permute-start(bf16[512,2048]{1,0:T(8,128)(2,1)} %get-tuple-element.145), channel_id=1, source_target_pairs={{0,4},{1,5},{2,6},{3,7},{4,0},{5,1},{6,2},{7,3},{8,12},{9,13},{10,... | collective-permute-start | bytes 6291464 | tf_op jit(solution)/shard_map/ppermute | solution.py:28
  359.9 47.9 %collective-permute-start.19 = (bf16[512,2048]{1,0:T(8,128)(2,1)}, bf16[512,2048]{1,0:T(8,128)(2,1)S(1)}, u32[]{:S(2)}, u32[]{:S(2)}) collective-permute-start(bf16[512,2048]{1,0:T(8,128)(2,1)} %get-tuple-element.154), channel_id=1, source_target_pairs={{0,2},{1,3},{2,0},{3,1},{4,6},{5,7},{6,4},{7,5},{8,10},{9,11},{10,... | collective-permute-start | bytes 6291464 | tf_op jit(solution)/shard_map/ppermute | solution.py:28
  404.9 25.8 %collective-permute-start.17 = (bf16[256,2048]{1,0:T(8,128)(2,1)}, bf16[256,2048]{1,0:T(8,128)(2,1)S(1)}, u32[]{:S(2)}, u32[]{:S(2)}) collective-permute-start(bf16[256,2048]{1,0:T(8,128)(2,1)} %get-tuple-element.148), channel_id=1, source_target_pairs={{0,2},{1,3},{2,0},{3,1},{4,6},{5,7},{6,4},{7,5},{8,10},{9,11},{10,... | collective-permute-start | bytes 3145736 | tf_op jit(solution)/shard_map/ppermute | solution.py:28
  413.9 24.1 %collective-permute-start.21 = (bf16[256,2048]{1,0:T(8,128)(2,1)}, bf16[256,2048]{1,0:T(8,128)(2,1)S(1)}, u32[]{:S(2)}, u32[]{:S(2)}) collective-permute-start(bf16[256,2048]{1,0:T(8,128)(2,1)} %get-tuple-element.156), channel_id=1, source_target_pairs={{0,4},{1,5},{2,6},{3,7},{4,0},{5,1},{6,2},{7,3},{8,12},{9,13},{10,... | collective-permute-start | bytes 3145736 | tf_op jit(solution)/shard_map/ppermute | solution.py:28
  430.9 51.8 %collective-permute-start.20 = (bf16[256,1024]{1,0:T(8,128)(2,1)S(1)}, bf16[256,1024]{1,0:T(8,128)(2,1)}, u32[]{:S(2)}, u32[]{:S(2)}) collective-permute-start(bf16[256,1024]{1,0:T(8,128)(2,1)S(1)} %add_convert_fusion.5), channel_id=1, source_target_pairs={{0,16},{8,24},{16,0},{24,8},{1,17},{9,25},{17,1},{25,9},{2,18},{10... | collective-permute-start | bytes 1572872 | tf_op jit(solution)/shard_map/ppermute | solution.py:28
  438.1 43.3 %collective-permute-start.22 = (bf16[128,2048]{1,0:T(8,128)(2,1)S(1)}, bf16[128,2048]{1,0:T(8,128)(2,1)}, u32[]{:S(2)}, u32[]{:S(2)}) collective-permute-start(bf16[128,2048]{1,0:T(8,128)(2,1)S(1)} %add_convert_fusion.4), channel_id=1, source_target_pairs={{0,16},{8,24},{16,0},{24,8},{1,17},{9,25},{17,1},{25,9},{2,18},{10... | collective-permute-start | bytes 1572872 | tf_op jit(solution)/shard_map/ppermute | solution.py:28
  459.6 25.5 %collective-permute-start.25 = (bf16[2,272,512]{2,1,0:T(8,128)(2,1)}, bf16[2,272,512]{2,1,0:T(8,128)(2,1)}, u32[]{:S(2)}, u32[]{:S(2)}) collective-permute-start(bf16[2,272,512]{2,1,0:T(8,128)(2,1)} %get-tuple-element.179), channel_id=1, source_target_pairs={{3,0},{4,1},{5,2},{6,3},{7,4},{11,8},{12,9},{13,10},{14,11},{15,12... | collective-permute-start | bytes 1671176 | tf_op jit(solution)/shard_map/ppermute | solution.py:24
  460.9 24.2 %collective-permute-start.24 = (bf16[2,272,512]{2,1,0:T(8,128)(2,1)}, bf16[2,272,512]{2,1,0:T(8,128)(2,1)}, u32[]{:S(2)}, u32[]{:S(2)}) collective-permute-start(bf16[2,272,512]{2,1,0:T(8,128)(2,1)} %get-tuple-element.179), channel_id=1, source_target_pairs={{2,0},{3,1},{4,2},{5,3},{6,4},{7,5},{10,8},{11,9},{12,10},{13,11},... | collective-permute-start | bytes 1671176 | tf_op jit(solution)/shard_map/ppermute | solution.py:24
  462.2 22.9 %collective-permute-start.23 = (bf16[2,272,512]{2,1,0:T(8,128)(2,1)}, bf16[2,272,512]{2,1,0:T(8,128)(2,1)}, u32[]{:S(2)}, u32[]{:S(2)}) collective-permute-start(bf16[2,272,512]{2,1,0:T(8,128)(2,1)} %get-tuple-element.179), channel_id=1, source_target_pairs={{1,0},{2,1},{3,2},{4,3},{5,4},{6,5},{7,6},{9,8},{10,9},{11,10},{12... | collective-permute-start | bytes 1671176 | tf_op jit(solution)/shard_map/ppermute | solution.py:24
  485.1 147.7 %reduce-scatter.5.cloned.1.call-start = ((), (), s32[]{:S(2)}) async-start(), calls=%async_computation.3 | async-start | bytes 5324800 | tf_op jit(solution)/shard_map/reduce_scatter | solution.py:1247
  485.2 51.4 %collective-permute-start.26 = (bf16[512,2048]{1,0:T(8,128)(2,1)}, bf16[512,2048]{1,0:T(8,128)(2,1)}, u32[]{:S(2)}, u32[]{:S(2)}) collective-permute-start(bf16[512,2048]{1,0:T(8,128)(2,1)} %get-tuple-element.173), channel_id=1, source_target_pairs={{0,1},{1,0},{2,3},{3,2},{4,5},{5,4},{6,7},{7,6},{8,9},{9,8},{10,11... | collective-permute-start | bytes 6291464 | tf_op jit(solution)/shard_map/ppermute | solution.py:28
  488.7 52.0 %collective-permute-start.27 = (bf16[1024,1024]{1,0:T(8,128)(2,1)}, bf16[1024,1024]{1,0:T(8,128)(2,1)S(1)}, u32[]{:S(2)}, u32[]{:S(2)}) collective-permute-start(bf16[1024,1024]{1,0:T(8,128)(2,1)} %get-tuple-element.170), channel_id=1, source_target_pairs={{0,1},{1,0},{2,3},{3,2},{4,5},{5,4},{6,7},{7,6},{8,9},{9,8},{10,11... | collective-permute-start | bytes 6291464 | tf_op jit(solution)/shard_map/ppermute | solution.py:28
  545.1 174.9 %all-gather.15.cloned.1.call-start = ((), (), s32[]{:S(2)}) async-start(), calls=%async_computation.7 | async-start | bytes 18874368 | tf_op jit(solution)/shard_map/all_gather | solution.py:1266
  545.1 9.6 %collective-permute-start.34 = (bf16[1024,1024]{1,0:T(8,128)(2,1)}, bf16[1024,1024]{1,0:T(8,128)(2,1)S(1)}, u32[]{:S(2)}, u32[]{:S(2)}) collective-permute-start(bf16[1024,1024]{1,0:T(8,128)(2,1)} %get-tuple-element.187), channel_id=1, source_target_pairs={{0,1},{1,0},{2,3},{3,2},{4,5},{5,4},{6,7},{7,6},{8,9},{9,8},{10,11... | collective-permute-start | bytes 6291464 | tf_op jit(solution)/shard_map/ppermute | solution.py:28
  545.4 31.3 %collective-permute-start.37 = (bf16[1024,1024]{1,0:T(8,128)(2,1)}, bf16[1024,1024]{1,0:T(8,128)(2,1)S(1)}, u32[]{:S(2)}, u32[]{:S(2)}) collective-permute-start(bf16[1024,1024]{1,0:T(8,128)(2,1)} %get-tuple-element.189), channel_id=1, source_target_pairs={{0,1},{1,0},{2,3},{3,2},{4,5},{5,4},{6,7},{7,6},{8,9},{9,8},{10,11... | collective-permute-start | bytes 6291464 | tf_op jit(solution)/shard_map/ppermute | solution.py:28
  545.7 28.3 %collective-permute-start.30 = (bf16[256,2048]{1,0:T(8,128)(2,1)}, bf16[256,2048]{1,0:T(8,128)(2,1)}, u32[]{:S(2)}, u32[]{:S(2)}) collective-permute-start(bf16[256,2048]{1,0:T(8,128)(2,1)} %get-tuple-element.191), channel_id=1, source_target_pairs={{0,2},{1,3},{2,0},{3,1},{4,6},{5,7},{6,4},{7,5},{8,10},{9,11},{10,... | collective-permute-start | bytes 3145736 | tf_op jit(solution)/shard_map/ppermute | solution.py:28
  554.7 30.2 %collective-permute-start.32 = (bf16[512,1024]{1,0:T(8,128)(2,1)}, bf16[512,1024]{1,0:T(8,128)(2,1)S(1)}, u32[]{:S(2)}, u32[]{:S(2)}) collective-permute-start(bf16[512,1024]{1,0:T(8,128)(2,1)} %get-tuple-element.199), channel_id=1, source_target_pairs={{0,4},{1,5},{2,6},{3,7},{4,0},{5,1},{6,2},{7,3},{8,12},{9,13},{10,... | collective-permute-start | bytes 3145736 | tf_op jit(solution)/shard_map/ppermute | solution.py:28
  560.8 35.5 %collective-permute-start.35 = (bf16[512,1024]{1,0:T(8,128)(2,1)}, bf16[512,1024]{1,0:T(8,128)(2,1)S(1)}, u32[]{:S(2)}, u32[]{:S(2)}) collective-permute-start(bf16[512,1024]{1,0:T(8,128)(2,1)} %get-tuple-element.205), channel_id=1, source_target_pairs={{0,2},{1,3},{2,0},{3,1},{4,6},{5,7},{6,4},{7,5},{8,10},{9,11},{10,... | collective-permute-start | bytes 3145736 | tf_op jit(solution)/shard_map/ppermute | solution.py:28
  576.8 15.4 %collective-permute-start.31 = (bf16[128,2048]{1,0:T(8,128)(2,1)}, bf16[128,2048]{1,0:T(8,128)(2,1)S(1)}, u32[]{:S(2)}, u32[]{:S(2)}) collective-permute-start(bf16[128,2048]{1,0:T(8,128)(2,1)} %get-tuple-element.196), channel_id=1, source_target_pairs={{0,4},{1,5},{2,6},{3,7},{4,0},{5,1},{6,2},{7,3},{8,12},{9,13},{10,... | collective-permute-start | bytes 1572872 | tf_op jit(solution)/shard_map/ppermute | solution.py:28
  582.9 31.7 %collective-permute-start.38 = (bf16[512,1024]{1,0:T(8,128)(2,1)}, bf16[512,1024]{1,0:T(8,128)(2,1)S(1)}, u32[]{:S(2)}, u32[]{:S(2)}) collective-permute-start(bf16[512,1024]{1,0:T(8,128)(2,1)} %get-tuple-element.212), channel_id=1, source_target_pairs={{0,4},{1,5},{2,6},{3,7},{4,0},{5,1},{6,2},{7,3},{8,12},{9,13},{10,... | collective-permute-start | bytes 3145736 | tf_op jit(solution)/shard_map/ppermute | solution.py:28
  588.6 31.4 %collective-permute-start.33 = (bf16[256,1024]{1,0:T(8,128)(2,1)}, bf16[256,1024]{1,0:T(8,128)(2,1)S(1)}, u32[]{:S(2)}, u32[]{:S(2)}) collective-permute-start(bf16[256,1024]{1,0:T(8,128)(2,1)} %get-tuple-element.201), channel_id=1, source_target_pairs={{0,2},{1,3},{2,0},{3,1},{4,6},{5,7},{6,4},{7,5},{8,10},{9,11},{10,... | collective-permute-start | bytes 1572872 | tf_op jit(solution)/shard_map/ppermute | solution.py:28
  600.0 25.1 %collective-permute-start.36 = (bf16[256,1024]{1,0:T(8,128)(2,1)}, bf16[256,1024]{1,0:T(8,128)(2,1)S(1)}, u32[]{:S(2)}, u32[]{:S(2)}) collective-permute-start(bf16[256,1024]{1,0:T(8,128)(2,1)} %get-tuple-element.208), channel_id=1, source_target_pairs={{0,4},{1,5},{2,6},{3,7},{4,0},{5,1},{6,2},{7,3},{8,12},{9,13},{10,... | collective-permute-start | bytes 1572872 | tf_op jit(solution)/shard_map/ppermute | solution.py:28
  618.4 12.8 %collective-permute-start.39 = (bf16[256,1024]{1,0:T(8,128)(2,1)}, bf16[256,1024]{1,0:T(8,128)(2,1)S(1)}, u32[]{:S(2)}, u32[]{:S(2)}) collective-permute-start(bf16[256,1024]{1,0:T(8,128)(2,1)} %get-tuple-element.215), channel_id=1, source_target_pairs={{0,2},{1,3},{2,0},{3,1},{4,6},{5,7},{6,4},{7,5},{8,10},{9,11},{10,... | collective-permute-start | bytes 1572872 | tf_op jit(solution)/shard_map/ppermute | solution.py:28
  637.8 27.6 %collective-permute-start.28 = (bf16[2,1,512,512]{3,2,1,0:T(8,128)(2,1)}, bf16[2,1,512,512]{3,2,1,0:T(8,128)(2,1)}, u32[]{:S(2)}, u32[]{:S(2)}) collective-permute-start(bf16[2,1,512,512]{3,2,1,0:T(8,128)(2,1)} %constant_dynamic-slice_fusion.1), channel_id=1, source_target_pairs={{0,8},{8,0},{16,24},{24,16},{1,9},{9,1},{17,25},{25,17},{2,10},{10... | collective-permute-start | bytes 3145736 | tf_op jit(solution)/shard_map/ppermute | solution.py:28
  667.7 25.6 %collective-permute-start.29 = (bf16[512,512]{1,0:T(8,128)(2,1)S(1)}, bf16[512,512]{1,0:T(8,128)(2,1)S(1)}, u32[]{:S(2)}, u32[]{:S(2)}) collective-permute-start(bf16[512,512]{1,0:T(8,128)(2,1)S(1)} %get-tuple-element.228), channel_id=1, source_target_pairs={{0,16},{8,24},{16,0},{24,8},{1,17},{9,25},{17,1},{25,9},{2,18},{10... | collective-permute-start | bytes 1572872 | tf_op jit(solution)/shard_map/ppermute | solution.py:28
  (33 other events, 205.6 us)
Sparse Core Ops, SparseCore 0:
  10.2 84.5 all-gather.8
  168.3 78.1 reduce-scatter.2
  337.6 81.1 all-gather.10
  485.3 59.7 all-gather.12
  547.9 77.8 reduce-scatter.4
  632.9 87.0 all-gather.14

commit v6 on v5

--- a/solution.py
+++ b/solution.py
@@ -466,7 +466,7 @@
             acc[at, :] += dot_nt(lowered, up[...])
             return carry
 
-        lax.fori_loop(0, steps, turn, 0)
+        lax.fori_loop(0, steps, turn, 0, unroll=True)
 
     @pl.when(step < chunks)
     def _():

time: 755 us -> 758 us (level)
  Pallas kernels: 287 us -> 295 us
    pallas_call x5, Pallas kernels: 44.8 us -> 53.5 us  [weight_grad(): prefetched(partial(weight_kernel, count), (2 * count,), [pl.BlockSpec((ro...]
  transfers between devices with their start and end apart: 46 -> 46, of which waited for: 23 -> 22; matrix products, arithmetic and copies ran while one was open for 9% -> 9% of each run, Pallas kernels for 31% -> 32%
where the time goes in v6:
time: 758 us; the launch traced here: 748 us
  Pallas kernels  295 us (39%)
  waiting for transfers between devices  287 us (38%)
  starting transfers between devices  57.8 us (8%)
  other arithmetic  46.8 us (6%)
  local copies, waits for them, and re-layouts  34.3 us (5%)
  between operations  15.4 us (2%)
  blocking collectives  12.7 us (2%)
    ppermute x34, waiting for transfers between devices, swapped(): lax.ppermute(value, axis, [(i, i ^ mask) for i in range(lax.axis_size(axi...  150 us
    all_gather x1, waiting for transfers between devices, body(): rows_raw = lax.all_gather(packed, 'head', axis=0)  77.2 us
    pallas_call x5, Pallas kernels, weight_grad(): prefetched(partial(weight_kernel, count), (2 * count,), [pl.BlockSpec((ro...  53.5 us
    pallas_call x12, Pallas kernels, fold(): prefetched(partial(fold_kernel, count), (2 * count,), [spec, spec], [pl.B...  52.4 us
    ppermute x34, starting transfers between devices, swapped(): lax.ppermute(value, axis, [(i, i ^ mask) for i in range(lax.axis_size(axi...  43 us
    pallas_call x2, Pallas kernels, in_order(): pl.pallas_call(partial(order_kernel, [len(parts) for _, parts in plan]),...  28.3 us
    pallas_call x1, Pallas kernels, body(): call(partial(finish_kernel, heads_here, row_count), row_count, [SCALARS,...  27.2 us
    pallas_call x1, Pallas kernels, body(): pl.pallas_call(partial(feed_kernel, chunks), grid=(2 * chunks,), in_specs...  26.2 us
  transfers between devices with their start and end apart: 46, of which 22 were waited for; matrix products, arithmetic and copies ran while one was open for 9% of the time, Pallas kernels for 32%

profile of v6, /device:TPU:0, one launch (start us, length us, event | category | flops | bytes accessed | tf_op | source)
XLA Modules:
  0.0 748.4 jit_solution(14953246320767274047)
XLA Ops:
  17.5 77.2 %all-gather.9.cloned.1.call-done = bf16[4160,512]{1,0:T(8,128)(2,1)} async-done(((bf16[1040,512]{1,0:T(8,128)(2,1)}), bf16[4160,512]{1,0:T(8,128)(2,1)}) %all-gather.9.cloned.1.call-update) | async-done | bytes 4259856 | tf_op jit(solution)/shard_map/all_gather | solution.py:791
  98.8 19.2 %shard_map.247 = (bf16[1024,2048]{1,0:T(8,128)(2,1)}, bf16[1024,512]{1,0:T(8,128)(2,1)}, bf16[1024,512]{1,0:T(8,128)(2,1)}, bf16[1024,1024]{1,0:T(8,128)(2,1)}, ...) custom-call(s32[1]{0:T(128)} %slice.108.docs, bf16[4,1040,512]{2,1,0:T(8,128)(2,1)} %bitcast.109, ...), custom_call_target="tpu_custom_call" | custom-call | tf_op jit(solution)/shard_map/pallas_call | solution.py:835
  125.0 4.2 collective-permute-start.2
  135.9 16.7 %shard_map.248 = (f32[1024,1024]{1,0:T(8,128)}, f32[1024,1024]{1,0:T(8,128)}) custom-call(f32[2]{0:T(128)} %copy-done.34, bf16[1024,2048]{1,0:T(8,128)(2,1)} %get-tuple-element.122.low.left, bf16[2048,1024]{1,0:T(8,128)(2,1)} %wg.3, bf16[1024,512]{1,0:T(8,128)(2,1)} %get-tuple-element.123.q, bf16[1024,512]{1,0:T(8,128)(2,1)} %get-tuple-element.124.k, ...), custom_call_target="tpu_custom_call" | custom-call | tf_op jit(solution)/shard_map/pallas_call | solution.py:887
  152.7 14.1 %shard_map.249 = (f32[1024,1024]{1,0:T(8,128)}, f32[1024,2]{1,0:T(8,128)}, bf16[1024,1024]{1,0:T(8,128)(2,1)}, bf16[2,2,2,512,512]{4,3,2,1,0:T(8,128)(2,1)}, bf1...) custom-call(f32[2]{0:T(128)} %copy-done.34, f32[1024,1024]{1,0:T(8,128)} %get-tuple-element.126.inner, ...), custom_call_target="tpu_custom_call" | custom-call | tf_op jit(solution)/shard_map/pallas_call | solution.py:914
  171.6 4.1 collective-permute-start.7
  175.7 7.3 collective-permute-done.10
  190.6 19.0 %collective-permute-done.11 = bf16[256,2048]{1,0:T(8,128)(2,1)} collective-permute-done((bf16[256,2048]{1,0:T(8,128)(2,1)S(1)}, bf16[256,2048]{1,0:T(8,128)(2,1)}, u32[]{:S(2)}, u32[]{:S(2)}) %collective-permute-start.11) | collective-permute-done | bytes 1048608 | tf_op jit(solution)/shard_map/ppermute | solution.py:28
  220.4 26.1 %reduce-scatter.3.cloned.1.call-done = bf16[1,2,512,512]{3,2,1,0:T(8,128)(2,1)} async-done(((bf16[4,2,512,512]{3,2,1,0:T(8,128)(2,1)}), bf16[1,2,512,512]{3,2,1,0:T(8,128)(2,1)}) %reduce-scatter.3.cloned.1.call-update) | async-done | bytes 1048592 | tf_op jit(solution)/shard_map/reduce_scatter | solution.py:966
  250.7 5.2 maximum_select_fusion.1.down_far
  255.9 5.5 maximum_select_fusion.up_far
  261.4 12.2 %collective-permute-done.6 = bf16[2,1,512,512]{3,2,0,1:T(8,128)(2,1)S(1)} collective-permute-done((bf16[2,1,512,512]{3,2,0,1:T(8,128)(2,1)S(1)}, bf16[2,1,512,512]{3,2,0,1:T(8,128)(2,1)S(1)}, u32[]{:S(2)}, u32[]{:S(2)}) %collective-permute-start.6) | collective-permute-done | bytes 1048608 | tf_op jit(solution)/shard_map/ppermute | solution.py:28
  277.2 26.2 %shard_map.250 = (bf16[512,2048]{1,0:T(8,128)(2,1)}, bf16[512,2048]{1,0:T(8,128)(2,1)}, bf16[512,2048]{1,0:T(8,128)(2,1)}, bf16[512,2048]{1,0:T(8,128)(2,1)}, bf...) custom-call(bf16[4,512,512]{2,1,0:T(8,128)(2,1)} %bitcast.116, ...), custom_call_target="tpu_custom_call" | custom-call | tf_op jit(solution)/shard_map/pallas_call | solution.py:974
  306.9 9.3 %shard_map.251 = (bf16[1024,2048]{1,0:T(8,128)(2,1)}, bf16[1024,2048]{1,0:T(8,128)(2,1)}) custom-call(s32[1]{0:T(128)} %bitcast.34.mine, bf16[512,2048]{1,0:T(8,128)(2,1)} %get-tuple-element.141.left.act, bf16[512,2048]{1,0:T(8,128)(2,1)} %get-tuple-element.135.refs_0_), custom_call_target="tpu_custom_call" | custom-call | flops 8589934592 | tf_op jit(solution)/shard_map/pallas_call | solution.py:590
  316.2 18.0 %shard_map.252 = (bf16[1024,2048]{1,0:T(8,128)(2,1)}, bf16[1024,2048]{1,0:T(8,128)(2,1)}) custom-call(s32[1]{0:T(128)} %bitcast.34.mine, bf16[512,2048]{1,0:T(8,128)(2,1)} %get-tuple-element.137.left, bf16[512,2048]{1,0:T(8,128)(2,1)} %get-tuple-element.138.refs_0_), custom_call_target="tpu_custom_call" | custom-call | flops 8589934592 | tf_op jit(solution)/shard_map/pallas_call | solution.py:590
  335.1 5.1 shard_map.253
  340.8 6.9 collective-permute-done.15.two
  347.7 7.1 shard_map.255
  356.3 6.7 shard_map.257
  364.5 9.5 %shard_map.254 = bf16[2,2,512,512]{3,2,1,0:T(8,128)(2,1)} custom-call(bf16[512,2048]{1,0:T(8,128)(2,1)} %get-tuple-element.141.left.act, bf16[1024,2048]{1,0:T(8,128)(2,1)} %down_near.3, bf16[1024,2048]{1,0:T(8,128)(2,1)} %maximum_select_fusion.1.down_far), custom_call_target="tpu_custom_call" | custom-call | tf_op jit(solution)/shard_map/pallas_call | solution.py:1051
  374.0 28.7 %collective-permute-done.16.two = bf16[512,2048]{1,0:T(8,128)(2,1)S(1)} collective-permute-done((bf16[512,2048]{1,0:T(8,128)(2,1)}, bf16[512,2048]{1,0:T(8,128)(2,1)S(1)}, u32[]{:S(2)}, u32[]{:S(2)}) %collective-permute-start.16) | collective-permute-done | bytes 2097184 | tf_op jit(solution)/shard_map/ppermute | solution.py:28
  404.0 4.1 shard_map.256
  412.2 4.8 shard_map.258
  422.2 11.9 %shard_map.259 = (bf16[1024,1024]{1,0:T(8,128)(2,1)}, bf16[1024,1024]{1,0:T(8,128)(2,1)}) custom-call(bf16[2,2,2,512,512]{4,3,2,1,0:T(8,128)(2,1)} %bitcast.118, bf16[1024,2048]{1,0:T(8,128)(2,1)} %wo.3, f32[1024,1024]{1,0:T(8,128)} %get-tuple-element.127.gate, f32[1024,1024]{1,0:T(8,128)} %get-tuple-element.149.group, f32[1024,2]{1,0:T(8,128)} %get-tuple-element.150.scale, ...), custom_call_target="tpu_custom_call" | custom-call | tf_op jit(solution)/shard_map/pallas_call | solution.py:1068
  436.2 4.9 collective-permute-done.21
  444.1 19.2 %shard_map.260 = (bf16[1024,512]{1,0:T(8,128)(2,1)}, f32[1024,512]{1,0:T(8,128)}, f32[1024,1024]{1,0:T(8,128)}, bf16[2,272,512]{2,1,0:T(8,128)(2,1)}) custom-call(s32[1]{0:T(128)} %slice.108.docs, f32[2]{0:T(128)} %copy-done.34, bf16[1024,1024]{1,0:T(8,128)(2,1)} %get-tuple-element.165.mix, bf16[1024,512]{1,0:T(8,128)(2,1)} %get-tuple-element.123.q, ...), custom_call_target="tpu_custom_call" | custom-call | flops 21474836480 | tf_op jit(solution)/shard_map/pallas_call | solution.py:1094
  467.2 9.1 %shard_map.262 = (bf16[512,2048]{1,0:T(8,128)(2,1)}, bf16[512,2048]{1,0:T(8,128)(2,1)}) custom-call(s32[1]{0:T(128)} %bitcast.34.mine, bf16[1024,1024]{1,0:T(8,128)(2,1)} %get-tuple-element.172.gated, bf16[2,2,2,512,512]{4,3,2,1,0:T(8,128)(2,1)} %bitcast.119), custom_call_target="tpu_custom_call" | custom-call | flops 8589934592 | tf_op jit(solution)/shard_map/pallas_call | solution.py:1142
  476.3 8.8 %shard_map.261 = (bf16[1024,1024]{1,0:T(8,128)(2,1)}, bf16[1024,1024]{1,0:T(8,128)(2,1)}) custom-call(s32[1]{0:T(128)} %bitcast.34.mine, bf16[1024,2048]{1,0:T(8,128)(2,1)} %get-tuple-element.122.low.left, bf16[1024,1024]{1,0:T(8,128)(2,1)} %get-tuple-element.169.refs_0_.dgate), custom_call_target="tpu_custom_call" | custom-call | flops 8589934592 | tf_op jit(solution)/shard_map/pallas_call | solution.py:590
  492.4 27.2 %shard_map.263 = (bf16[1024,512]{1,0:T(8,128)(2,1)}, bf16[1024,1024]{1,0:T(8,128)(2,1)}, bf16[4,1040,512]{2,1,0:T(8,128)(2,1)}, f32[4,16,256]{2,1,0:T(8,128)}, f32[2,2048]{1,0:T(2,128)}) custom-call(s32[1]{0:T(128)} %slice.108.docs, f32[2]{0:T(128)} %copy-done.34, f32[1024,512]{1,0:T(8,128)} %get-tuple-element.177.dk_in, ...), custom_call_target="tpu_custom_call" | custom-call | flops 25769803776 | tf_op jit(solution)/shard_map/pallas_call | solution.py:1171
  522.8 8.7 %shard_map.265 = (bf16[1024,1024]{1,0:T(8,128)(2,1)}, bf16[1024,1024]{1,0:T(8,128)(2,1)}) custom-call(s32[1]{0:T(128)} %bitcast.34.mine, bf16[1024,2048]{1,0:T(8,128)(2,1)} %get-tuple-element.122.low.left, bf16[1024,512]{1,0:T(8,128)(2,1)} %get-tuple-element.168.dq.refs_0_, bf16[1024,512]{1,0:T(8,128)(2,1)} %get-tuple-element.188.refs_1_), custom_call_target="tpu_custom_call" | custom-call | flops 8589934592 | tf_op jit(solution)/shard_map/pallas_call | solution.py:590
  531.5 8.8 %shard_map.264 = (bf16[1024,1024]{1,0:T(8,128)(2,1)}, bf16[1024,1024]{1,0:T(8,128)(2,1)}) custom-call(s32[1]{0:T(128)} %bitcast.34.mine, bf16[1024,2048]{1,0:T(8,128)(2,1)} %get-tuple-element.122.low.left, bf16[1024,1024]{1,0:T(8,128)(2,1)} %get-tuple-element.186.refs_0_), custom_call_target="tpu_custom_call" | custom-call | flops 8589934592 | tf_op jit(solution)/shard_map/pallas_call | solution.py:590
  540.3 4.2 shard_map.266
  544.4 4.0 all-gather.13.cloned.1.call-done
  549.1 4.2 collective-permute-start.30
  553.4 5.1 shard_map.268
  559.8 4.8 shard_map.270
  564.6 13.1 %collective-permute-done.30.two = bf16[256,2048]{1,0:T(8,128)(2,1)} collective-permute-done((bf16[256,2048]{1,0:T(8,128)(2,1)}, bf16[256,2048]{1,0:T(8,128)(2,1)}, u32[]{:S(2)}, u32[]{:S(2)}) %collective-permute-start.30) | collective-permute-done | bytes 1048608 | tf_op jit(solution)/shard_map/ppermute | solution.py:28
  581.8 4.8 shard_map.272
  596.0 4.0 collective-permute-done.35.two
  603.9 14.5 %collective-permute-done.38.two = bf16[512,1024]{1,0:T(8,128)(2,1)S(1)} collective-permute-done((bf16[512,1024]{1,0:T(8,128)(2,1)}, bf16[512,1024]{1,0:T(8,128)(2,1)S(1)}, u32[]{:S(2)}, u32[]{:S(2)}) %collective-permute-start.38) | collective-permute-done | bytes 1048608 | tf_op jit(solution)/shard_map/ppermute | solution.py:28
  623.9 5.0 collective-permute-done.36
  629.1 5.9 collective-permute-done.39
  636.5 4.2 fusion.11
  644.0 10.4 %shard_map.275 = (f32[1024,2048]{1,0:T(8,128)}, f32[2048,1024]{1,0:T(8,128)}) custom-call(bf16[8,512,1024]{2,1,0:T(8,128)(2,1)} %bitcast.107, bf16[8,512,1024]{2,1,0:T(8,128)(2,1)} %bitcast.108), custom_call_target="tpu_custom_call" | custom-call | tf_op jit(solution)/shard_map/pallas_call | solution.py:748
  655.9 12.7 %psum.7 = f32[4,512]{1,0:T(4,128)S(1)} all-reduce(f32[4,512]{1,0:T(4,128)S(1)} %slice_bitcast_fusion.1), channel_id=1, replica_groups=mesh['head'=4,'tok'=8] {'tok'}, use_global_device_ids=true, to_apply=%region_2.3 | all-reduce | flops 2048 | bytes 16384 | tf_op jit(solution)/shard_map/psum | solution.py:1254
  674.1 22.4 %collective-permute-done.29 = bf16[512,512]{1,0:T(8,128)(2,1)S(1)} collective-permute-done((bf16[512,512]{1,0:T(8,128)(2,1)S(1)}, bf16[512,512]{1,0:T(8,128)(2,1)S(1)}, u32[]{:S(2)}, u32[]{:S(2)}) %collective-permute-start.29) | collective-permute-done | bytes 524320 | tf_op jit(solution)/shard_map/ppermute | solution.py:28
  698.0 25.2 %all-gather.15.cloned.1.call-done = bf16[8192,1024]{1,0:T(8,128)(2,1)} async-done(((bf16[1024,1024]{1,0:T(8,128)(2,1)}), bf16[8192,1024]{1,0:T(8,128)(2,1)}) %all-gather.15.cloned.1.call-update) | async-done | bytes 16777232 | tf_op jit(solution)/shard_map/all_gather | solution.py:1266
  723.2 17.9 %shard_map.274 = (f32[1024,2048]{1,0:T(8,128)}, f32[2048,1024]{1,0:T(8,128)}, f32[2048,1024]{1,0:T(8,128)}, f32[2048,512]{1,0:T(8,128)}, f32[2048,512]{1,0:T(8,128)}) custom-call(bf16[8,1024,1024]{2,1,0:T(8,128)(2,1)} %bitcast.103, bf16[8,1024,1024]{2,1,0:T(8,128)(2,1)} %bitcast.104, bf16[8,1024,1024]{2,1,0:T(8,128)(2,1)} %bitcast.105, ...), custom_call_target="tpu_custom_call" | custom-call | tf_op jit(solution)/shard_map/pallas_call | solution.py:748
  (231 shorter events, 135.2 us)
Async XLA Ops:
  7.2 87.6 %all-gather.9.cloned.1.call-start = ((), (), s32[]{:S(2)}) async-start(), calls=%async_computation.4 | async-start | bytes 5324800 | tf_op jit(solution)/shard_map/all_gather | solution.py:791
  9.6 236.9 %reduce-scatter.3.cloned.1.call-start = ((), (), s32[]{:S(2)}) async-start(), calls=%async_computation.2 | async-start | bytes 5242880 | tf_op jit(solution)/shard_map/reduce_scatter | solution.py:966
  12.1 82.6 %copy-start.21 = (bf16[1024,512]{1,0:T(8,128)(2,1)S(1)}, bf16[1024,512]{1,0:T(8,128)(2,1)}, u32[]{:S(2)}) copy-start(bf16[1024,512]{1,0:T(8,128)(2,1)} %param.29) | copy-start | bytes 3145732
  12.4 85.2 %copy-start.34 = (f32[2]{0:T(128)}, f32[2]{0:T(128)S(1)}, u32[]{:S(2)}) copy-start(f32[2]{0:T(128)S(1)} %subtract_log_fusion.decay) | copy-start | bytes 28
  94.8 24.3 %collective-permute-start = (bf16[512,512]{1,0:T(8,128)(2,1)S(1)}, bf16[512,512]{1,0:T(8,128)(2,1)S(1)}, u32[]{:S(2)}, u32[]{:S(2)}) collective-permute-start(bf16[512,512]{1,0:T(8,128)(2,1)S(1)} %get-tuple-element.232), channel_id=1, source_target_pairs={{0,16},{8,24},{16,0},{24,8},{1,17},{9,25},{17,1},{25,9},{2,18},{10... | collective-permute-start | bytes 1572872 | tf_op jit(solution)/shard_map/ppermute | solution.py:28
  119.2 47.5 %collective-permute-start.4 = (bf16[2,1,512,512]{3,2,0,1:T(8,128)(2,1)S(1)}, bf16[2,1,512,512]{3,2,0,1:T(8,128)(2,1)S(1)}, u32[]{:S(2)}, u32[]{:S(2)}) collective-permute-start(bf16[2,1,512,512]{3,2,0,1:T(8,128)(2,1)S(1)} %maximum_select_fusion.7), channel_id=1, source_target_pairs={{0,8},{8,0},{16,24},{24,16},{1,9},{9,1},{17,25},{25,17},{2,10},{10... | collective-permute-start | bytes 3145736 | tf_op jit(solution)/shard_map/ppermute | solution.py:28
  119.3 48.9 %collective-permute-start.5 = (bf16[512,1024]{1,0:T(8,128)(2,1)}, bf16[512,1024]{1,0:T(8,128)(2,1)}, u32[]{:S(2)}, u32[]{:S(2)}) collective-permute-start(bf16[512,1024]{1,0:T(8,128)(2,1)} %pad_maximum_fusion), channel_id=1, source_target_pairs={{0,16},{8,24},{16,0},{24,8},{1,17},{9,25},{17,1},{25,9},{2,18},{10... | collective-permute-start | bytes 3145736 | tf_op jit(solution)/shard_map/ppermute | solution.py:28
  122.3 30.4 %collective-permute-start.3 = (bf16[2,272,512]{2,1,0:T(8,128)(2,1)}, bf16[2,272,512]{2,1,0:T(8,128)(2,1)}, u32[]{:S(2)}, u32[]{:S(2)}) collective-permute-start(bf16[2,272,512]{2,1,0:T(8,128)(2,1)} %get-tuple-element.119), channel_id=1, source_target_pairs={{0,3},{1,4},{2,5},{3,6},{4,7},{8,11},{9,12},{10,13},{11,14},{12,15... | collective-permute-start | bytes 1671176 | tf_op jit(solution)/shard_map/ppermute | solution.py:24
  125.0 27.7 %collective-permute-start.2 = (bf16[2,272,512]{2,1,0:T(8,128)(2,1)}, bf16[2,272,512]{2,1,0:T(8,128)(2,1)}, u32[]{:S(2)}, u32[]{:S(2)}) collective-permute-start(bf16[2,272,512]{2,1,0:T(8,128)(2,1)} %get-tuple-element.119), channel_id=1, source_target_pairs={{0,2},{1,3},{2,4},{3,5},{4,6},{5,7},{8,10},{9,11},{10,12},{11,13},... | collective-permute-start | bytes 1671176 | tf_op jit(solution)/shard_map/ppermute | solution.py:24
  129.2 23.5 %collective-permute-start.1 = (bf16[2,272,512]{2,1,0:T(8,128)(2,1)}, bf16[2,272,512]{2,1,0:T(8,128)(2,1)}, u32[]{:S(2)}, u32[]{:S(2)}) collective-permute-start(bf16[2,272,512]{2,1,0:T(8,128)(2,1)} %get-tuple-element.119), channel_id=1, source_target_pairs={{0,1},{1,2},{2,3},{3,4},{4,5},{5,6},{6,7},{8,9},{9,10},{10,11},{11... | collective-permute-start | bytes 1671176 | tf_op jit(solution)/shard_map/ppermute | solution.py:24
  168.2 253.9 %all-gather.11.cloned.1.call-start = ((), (), s32[]{:S(2)}) async-start(), calls=%async_computation.5 | async-start | bytes 5242880 | tf_op jit(solution)/shard_map/all_gather | solution.py:1047
  170.0 13.0 %collective-permute-start.10 = (bf16[128,2048]{1,0:T(8,128)(2,1)S(1)}, bf16[128,2048]{1,0:T(8,128)(2,1)}, u32[]{:S(2)}, u32[]{:S(2)}) collective-permute-start(bf16[128,2048]{1,0:T(8,128)(2,1)S(1)} %reshape.210), channel_id=1, source_target_pairs={{0,2},{1,3},{2,0},{3,1},{4,6},{5,7},{6,4},{7,5},{8,10},{9,11},{10,... | collective-permute-start | bytes 1572872 | tf_op jit(solution)/shard_map/ppermute | solution.py:28
  171.6 15.7 %collective-permute-start.7 = (bf16[256,1024]{1,0:T(8,128)(2,1)S(1)}, bf16[256,1024]{1,0:T(8,128)(2,1)}, u32[]{:S(2)}, u32[]{:S(2)}) collective-permute-start(bf16[256,1024]{1,0:T(8,128)(2,1)S(1)} %get-tuple-element.230), channel_id=1, source_target_pairs={{0,4},{1,5},{2,6},{3,7},{4,0},{5,1},{6,2},{7,3},{8,12},{9,13},{10,... | collective-permute-start | bytes 1572872 | tf_op jit(solution)/shard_map/ppermute | solution.py:28
  184.5 25.1 %collective-permute-start.11 = (bf16[256,2048]{1,0:T(8,128)(2,1)S(1)}, bf16[256,2048]{1,0:T(8,128)(2,1)}, u32[]{:S(2)}, u32[]{:S(2)}) collective-permute-start(bf16[256,2048]{1,0:T(8,128)(2,1)S(1)} %maximum_select_fusion.9), channel_id=1, source_target_pairs={{0,4},{1,5},{2,6},{3,7},{4,0},{5,1},{6,2},{7,3},{8,12},{9,13},{10,... | collective-permute-start | bytes 3145736 | tf_op jit(solution)/shard_map/ppermute | solution.py:28
  188.9 25.1 %collective-permute-start.8 = (bf16[512,1024]{1,0:T(8,128)(2,1)S(1)}, bf16[512,1024]{1,0:T(8,128)(2,1)S(1)}, u32[]{:S(2)}, u32[]{:S(2)}) collective-permute-start(bf16[512,1024]{1,0:T(8,128)(2,1)S(1)} %maximum_select_fusion.8), channel_id=1, source_target_pairs={{0,2},{1,3},{2,0},{3,1},{4,6},{5,7},{6,4},{7,5},{8,10},{9,11},{10,... | collective-permute-start | bytes 3145736 | tf_op jit(solution)/shard_map/ppermute | solution.py:28
  212.7 38.0 %collective-permute-start.12 = (bf16[512,2048]{1,0:T(8,128)(2,1)S(1)}, bf16[512,2048]{1,0:T(8,128)(2,1)}, u32[]{:S(2)}, u32[]{:S(2)}) collective-permute-start(bf16[512,2048]{1,0:T(8,128)(2,1)S(1)} %maximum_select_fusion.5), channel_id=1, source_target_pairs={{0,1},{1,0},{2,3},{3,2},{4,5},{5,4},{6,7},{7,6},{8,9},{9,8},{10,11... | collective-permute-start | bytes 6291464 | tf_op jit(solution)/shard_map/ppermute | solution.py:28
  216.3 39.6 %collective-permute-start.9 = (bf16[1024,1024]{1,0:T(8,128)(2,1)}, bf16[1024,1024]{1,0:T(8,128)(2,1)}, u32[]{:S(2)}, u32[]{:S(2)}) collective-permute-start(bf16[1024,1024]{1,0:T(8,128)(2,1)} %maximum_select_fusion.4), channel_id=1, source_target_pairs={{0,1},{1,0},{2,3},{3,2},{4,5},{5,4},{6,7},{7,6},{8,9},{9,8},{10,11... | collective-permute-start | bytes 6291464 | tf_op jit(solution)/shard_map/ppermute | solution.py:28
  248.5 25.0 %collective-permute-start.6 = (bf16[2,1,512,512]{3,2,0,1:T(8,128)(2,1)S(1)}, bf16[2,1,512,512]{3,2,0,1:T(8,128)(2,1)S(1)}, u32[]{:S(2)}, u32[]{:S(2)}) collective-permute-start(bf16[2,1,512,512]{3,2,0,1:T(8,128)(2,1)S(1)} %convert_bitcast_fusion), channel_id=1, source_target_pairs={{0,8},{8,0},{16,24},{24,16},{1,9},{9,1},{17,25},{25,17},{2,10},{10... | collective-permute-start | bytes 3145736 | tf_op jit(solution)/shard_map/ppermute | solution.py:28
  303.4 30.7 %collective-permute-start.14 = (f32[2,16,256]{2,1,0:T(8,128)}, f32[2,16,256]{2,1,0:T(8,128)S(1)}, u32[]{:S(2)}, u32[]{:S(2)}) collective-permute-start(f32[2,16,256]{2,1,0:T(8,128)} %get-tuple-element.134.near), channel_id=1, source_target_pairs={{0,8},{8,0},{16,24},{24,16},{1,9},{9,1},{17,25},{25,17},{2,10},{10... | collective-permute-start | bytes 98312 | tf_op jit(solution)/shard_map/ppermute | solution.py:28
  306.3 27.9 %collective-permute-start.13 = (bf16[2,1,512,512]{3,2,1,0:T(8,128)(2,1)S(1)}, bf16[2,1,512,512]{3,2,1,0:T(8,128)(2,1)S(1)}, u32[]{:S(2)}, u32[]{:S(2)}) collective-permute-start(bf16[2,1,512,512]{3,2,1,0:T(8,128)(2,1)S(1)} %constant_dynamic-slice_fusion.3), channel_id=1, source_target_pairs={{0,8},{8,0},{16,24},{24,16},{1,9},{9,1},{17,25},{25,17},{2,10},{10... | collective-permute-start | bytes 3145736 | tf_op jit(solution)/shard_map/ppermute | solution.py:28
  340.2 7.5 %collective-permute-start.15 = (bf16[1024,2048]{1,0:T(8,128)(2,1)}, bf16[1024,2048]{1,0:T(8,128)(2,1)}, u32[]{:S(2)}, u32[]{:S(2)}) collective-permute-start(bf16[1024,2048]{1,0:T(8,128)(2,1)} %get-tuple-element.143), channel_id=1, source_target_pairs={{0,1},{1,0},{2,3},{3,2},{4,5},{5,4},{6,7},{7,6},{8,9},{9,8},{10,11... | collective-permute-start | bytes 12582920 | tf_op jit(solution)/shard_map/ppermute | solution.py:28
  340.2 16.1 %collective-permute-start.18 = (bf16[1024,2048]{1,0:T(8,128)(2,1)}, bf16[1024,2048]{1,0:T(8,128)(2,1)}, u32[]{:S(2)}, u32[]{:S(2)}) collective-permute-start(bf16[1024,2048]{1,0:T(8,128)(2,1)} %get-tuple-element.152), channel_id=1, source_target_pairs={{0,1},{1,0},{2,3},{3,2},{4,5},{5,4},{6,7},{7,6},{8,9},{9,8},{10,11... | collective-permute-start | bytes 12582920 | tf_op jit(solution)/shard_map/ppermute | solution.py:28
  340.7 207.7 %all-gather.13.cloned.1.call-start = ((), (), s32[]{:S(2)}) async-start(), calls=%async_computation.6 | async-start | bytes 9437184 | tf_op jit(solution)/shard_map/all_gather | solution.py:1167
  354.8 47.9 %collective-permute-start.16 = (bf16[512,2048]{1,0:T(8,128)(2,1)}, bf16[512,2048]{1,0:T(8,128)(2,1)S(1)}, u32[]{:S(2)}, u32[]{:S(2)}) collective-permute-start(bf16[512,2048]{1,0:T(8,128)(2,1)} %get-tuple-element.145), channel_id=1, source_target_pairs={{0,4},{1,5},{2,6},{3,7},{4,0},{5,1},{6,2},{7,3},{8,12},{9,13},{10,... | collective-permute-start | bytes 6291464 | tf_op jit(solution)/shard_map/ppermute | solution.py:28
  363.1 47.9 %collective-permute-start.19 = (bf16[512,2048]{1,0:T(8,128)(2,1)}, bf16[512,2048]{1,0:T(8,128)(2,1)S(1)}, u32[]{:S(2)}, u32[]{:S(2)}) collective-permute-start(bf16[512,2048]{1,0:T(8,128)(2,1)} %get-tuple-element.154), channel_id=1, source_target_pairs={{0,2},{1,3},{2,0},{3,1},{4,6},{5,7},{6,4},{7,5},{8,10},{9,11},{10,... | collective-permute-start | bytes 6291464 | tf_op jit(solution)/shard_map/ppermute | solution.py:28
  408.1 26.0 %collective-permute-start.17 = (bf16[256,2048]{1,0:T(8,128)(2,1)}, bf16[256,2048]{1,0:T(8,128)(2,1)S(1)}, u32[]{:S(2)}, u32[]{:S(2)}) collective-permute-start(bf16[256,2048]{1,0:T(8,128)(2,1)} %get-tuple-element.148), channel_id=1, source_target_pairs={{0,2},{1,3},{2,0},{3,1},{4,6},{5,7},{6,4},{7,5},{8,10},{9,11},{10,... | collective-permute-start | bytes 3145736 | tf_op jit(solution)/shard_map/ppermute | solution.py:28
  417.0 24.1 %collective-permute-start.21 = (bf16[256,2048]{1,0:T(8,128)(2,1)}, bf16[256,2048]{1,0:T(8,128)(2,1)S(1)}, u32[]{:S(2)}, u32[]{:S(2)}) collective-permute-start(bf16[256,2048]{1,0:T(8,128)(2,1)} %get-tuple-element.156), channel_id=1, source_target_pairs={{0,4},{1,5},{2,6},{3,7},{4,0},{5,1},{6,2},{7,3},{8,12},{9,13},{10,... | collective-permute-start | bytes 3145736 | tf_op jit(solution)/shard_map/ppermute | solution.py:28
  434.3 52.1 %collective-permute-start.20 = (bf16[256,1024]{1,0:T(8,128)(2,1)S(1)}, bf16[256,1024]{1,0:T(8,128)(2,1)}, u32[]{:S(2)}, u32[]{:S(2)}) collective-permute-start(bf16[256,1024]{1,0:T(8,128)(2,1)S(1)} %add_convert_fusion.5), channel_id=1, source_target_pairs={{0,16},{8,24},{16,0},{24,8},{1,17},{9,25},{17,1},{25,9},{2,18},{10... | collective-permute-start | bytes 1572872 | tf_op jit(solution)/shard_map/ppermute | solution.py:28
  441.3 43.8 %collective-permute-start.22 = (bf16[128,2048]{1,0:T(8,128)(2,1)S(1)}, bf16[128,2048]{1,0:T(8,128)(2,1)}, u32[]{:S(2)}, u32[]{:S(2)}) collective-permute-start(bf16[128,2048]{1,0:T(8,128)(2,1)S(1)} %add_convert_fusion.4), channel_id=1, source_target_pairs={{0,16},{8,24},{16,0},{24,8},{1,17},{9,25},{17,1},{25,9},{2,18},{10... | collective-permute-start | bytes 1572872 | tf_op jit(solution)/shard_map/ppermute | solution.py:28
  463.3 25.5 %collective-permute-start.25 = (bf16[2,272,512]{2,1,0:T(8,128)(2,1)}, bf16[2,272,512]{2,1,0:T(8,128)(2,1)}, u32[]{:S(2)}, u32[]{:S(2)}) collective-permute-start(bf16[2,272,512]{2,1,0:T(8,128)(2,1)} %get-tuple-element.179), channel_id=1, source_target_pairs={{3,0},{4,1},{5,2},{6,3},{7,4},{11,8},{12,9},{13,10},{14,11},{15,12... | collective-permute-start | bytes 1671176 | tf_op jit(solution)/shard_map/ppermute | solution.py:24
  464.6 24.2 %collective-permute-start.24 = (bf16[2,272,512]{2,1,0:T(8,128)(2,1)}, bf16[2,272,512]{2,1,0:T(8,128)(2,1)}, u32[]{:S(2)}, u32[]{:S(2)}) collective-permute-start(bf16[2,272,512]{2,1,0:T(8,128)(2,1)} %get-tuple-element.179), channel_id=1, source_target_pairs={{2,0},{3,1},{4,2},{5,3},{6,4},{7,5},{10,8},{11,9},{12,10},{13,11},... | collective-permute-start | bytes 1671176 | tf_op jit(solution)/shard_map/ppermute | solution.py:24
  465.9 22.9 %collective-permute-start.23 = (bf16[2,272,512]{2,1,0:T(8,128)(2,1)}, bf16[2,272,512]{2,1,0:T(8,128)(2,1)}, u32[]{:S(2)}, u32[]{:S(2)}) collective-permute-start(bf16[2,272,512]{2,1,0:T(8,128)(2,1)} %get-tuple-element.179), channel_id=1, source_target_pairs={{1,0},{2,1},{3,2},{4,3},{5,4},{6,5},{7,6},{9,8},{10,9},{11,10},{12... | collective-permute-start | bytes 1671176 | tf_op jit(solution)/shard_map/ppermute | solution.py:24
  488.8 147.7 %reduce-scatter.5.cloned.1.call-start = ((), (), s32[]{:S(2)}) async-start(), calls=%async_computation.3 | async-start | bytes 5324800 | tf_op jit(solution)/shard_map/reduce_scatter | solution.py:1247
  488.9 51.4 %collective-permute-start.26 = (bf16[512,2048]{1,0:T(8,128)(2,1)}, bf16[512,2048]{1,0:T(8,128)(2,1)}, u32[]{:S(2)}, u32[]{:S(2)}) collective-permute-start(bf16[512,2048]{1,0:T(8,128)(2,1)} %get-tuple-element.173), channel_id=1, source_target_pairs={{0,1},{1,0},{2,3},{3,2},{4,5},{5,4},{6,7},{7,6},{8,9},{9,8},{10,11... | collective-permute-start | bytes 6291464 | tf_op jit(solution)/shard_map/ppermute | solution.py:28
  492.4 52.1 %collective-permute-start.27 = (bf16[1024,1024]{1,0:T(8,128)(2,1)}, bf16[1024,1024]{1,0:T(8,128)(2,1)S(1)}, u32[]{:S(2)}, u32[]{:S(2)}) collective-permute-start(bf16[1024,1024]{1,0:T(8,128)(2,1)} %get-tuple-element.170), channel_id=1, source_target_pairs={{0,1},{1,0},{2,3},{3,2},{4,5},{5,4},{6,7},{7,6},{8,9},{9,8},{10,11... | collective-permute-start | bytes 6291464 | tf_op jit(solution)/shard_map/ppermute | solution.py:28
  548.5 174.7 %all-gather.15.cloned.1.call-start = ((), (), s32[]{:S(2)}) async-start(), calls=%async_computation.7 | async-start | bytes 18874368 | tf_op jit(solution)/shard_map/all_gather | solution.py:1266
  548.6 9.9 %collective-permute-start.34 = (bf16[1024,1024]{1,0:T(8,128)(2,1)}, bf16[1024,1024]{1,0:T(8,128)(2,1)S(1)}, u32[]{:S(2)}, u32[]{:S(2)}) collective-permute-start(bf16[1024,1024]{1,0:T(8,128)(2,1)} %get-tuple-element.187), channel_id=1, source_target_pairs={{0,1},{1,0},{2,3},{3,2},{4,5},{5,4},{6,7},{7,6},{8,9},{9,8},{10,11... | collective-permute-start | bytes 6291464 | tf_op jit(solution)/shard_map/ppermute | solution.py:28
  548.9 31.6 %collective-permute-start.37 = (bf16[1024,1024]{1,0:T(8,128)(2,1)}, bf16[1024,1024]{1,0:T(8,128)(2,1)S(1)}, u32[]{:S(2)}, u32[]{:S(2)}) collective-permute-start(bf16[1024,1024]{1,0:T(8,128)(2,1)} %get-tuple-element.189), channel_id=1, source_target_pairs={{0,1},{1,0},{2,3},{3,2},{4,5},{5,4},{6,7},{7,6},{8,9},{9,8},{10,11... | collective-permute-start | bytes 6291464 | tf_op jit(solution)/shard_map/ppermute | solution.py:28
  549.1 28.6 %collective-permute-start.30 = (bf16[256,2048]{1,0:T(8,128)(2,1)}, bf16[256,2048]{1,0:T(8,128)(2,1)}, u32[]{:S(2)}, u32[]{:S(2)}) collective-permute-start(bf16[256,2048]{1,0:T(8,128)(2,1)} %get-tuple-element.191), channel_id=1, source_target_pairs={{0,2},{1,3},{2,0},{3,1},{4,6},{5,7},{6,4},{7,5},{8,10},{9,11},{10,... | collective-permute-start | bytes 3145736 | tf_op jit(solution)/shard_map/ppermute | solution.py:28
  558.4 30.2 %collective-permute-start.32 = (bf16[512,1024]{1,0:T(8,128)(2,1)}, bf16[512,1024]{1,0:T(8,128)(2,1)S(1)}, u32[]{:S(2)}, u32[]{:S(2)}) collective-permute-start(bf16[512,1024]{1,0:T(8,128)(2,1)} %get-tuple-element.199), channel_id=1, source_target_pairs={{0,4},{1,5},{2,6},{3,7},{4,0},{5,1},{6,2},{7,3},{8,12},{9,13},{10,... | collective-permute-start | bytes 3145736 | tf_op jit(solution)/shard_map/ppermute | solution.py:28
  564.5 35.5 %collective-permute-start.35 = (bf16[512,1024]{1,0:T(8,128)(2,1)}, bf16[512,1024]{1,0:T(8,128)(2,1)S(1)}, u32[]{:S(2)}, u32[]{:S(2)}) collective-permute-start(bf16[512,1024]{1,0:T(8,128)(2,1)} %get-tuple-element.205), channel_id=1, source_target_pairs={{0,2},{1,3},{2,0},{3,1},{4,6},{5,7},{6,4},{7,5},{8,10},{9,11},{10,... | collective-permute-start | bytes 3145736 | tf_op jit(solution)/shard_map/ppermute | solution.py:28
  580.5 15.4 %collective-permute-start.31 = (bf16[128,2048]{1,0:T(8,128)(2,1)}, bf16[128,2048]{1,0:T(8,128)(2,1)S(1)}, u32[]{:S(2)}, u32[]{:S(2)}) collective-permute-start(bf16[128,2048]{1,0:T(8,128)(2,1)} %get-tuple-element.196), channel_id=1, source_target_pairs={{0,4},{1,5},{2,6},{3,7},{4,0},{5,1},{6,2},{7,3},{8,12},{9,13},{10,... | collective-permute-start | bytes 1572872 | tf_op jit(solution)/shard_map/ppermute | solution.py:28
  586.6 31.8 %collective-permute-start.38 = (bf16[512,1024]{1,0:T(8,128)(2,1)}, bf16[512,1024]{1,0:T(8,128)(2,1)S(1)}, u32[]{:S(2)}, u32[]{:S(2)}) collective-permute-start(bf16[512,1024]{1,0:T(8,128)(2,1)} %get-tuple-element.212), channel_id=1, source_target_pairs={{0,4},{1,5},{2,6},{3,7},{4,0},{5,1},{6,2},{7,3},{8,12},{9,13},{10,... | collective-permute-start | bytes 3145736 | tf_op jit(solution)/shard_map/ppermute | solution.py:28
  592.3 31.4 %collective-permute-start.33 = (bf16[256,1024]{1,0:T(8,128)(2,1)}, bf16[256,1024]{1,0:T(8,128)(2,1)S(1)}, u32[]{:S(2)}, u32[]{:S(2)}) collective-permute-start(bf16[256,1024]{1,0:T(8,128)(2,1)} %get-tuple-element.201), channel_id=1, source_target_pairs={{0,2},{1,3},{2,0},{3,1},{4,6},{5,7},{6,4},{7,5},{8,10},{9,11},{10,... | collective-permute-start | bytes 1572872 | tf_op jit(solution)/shard_map/ppermute | solution.py:28
  603.8 25.1 %collective-permute-start.36 = (bf16[256,1024]{1,0:T(8,128)(2,1)}, bf16[256,1024]{1,0:T(8,128)(2,1)S(1)}, u32[]{:S(2)}, u32[]{:S(2)}) collective-permute-start(bf16[256,1024]{1,0:T(8,128)(2,1)} %get-tuple-element.208), channel_id=1, source_target_pairs={{0,4},{1,5},{2,6},{3,7},{4,0},{5,1},{6,2},{7,3},{8,12},{9,13},{10,... | collective-permute-start | bytes 1572872 | tf_op jit(solution)/shard_map/ppermute | solution.py:28
  622.1 12.8 %collective-permute-start.39 = (bf16[256,1024]{1,0:T(8,128)(2,1)}, bf16[256,1024]{1,0:T(8,128)(2,1)S(1)}, u32[]{:S(2)}, u32[]{:S(2)}) collective-permute-start(bf16[256,1024]{1,0:T(8,128)(2,1)} %get-tuple-element.215), channel_id=1, source_target_pairs={{0,2},{1,3},{2,0},{3,1},{4,6},{5,7},{6,4},{7,5},{8,10},{9,11},{10,... | collective-permute-start | bytes 1572872 | tf_op jit(solution)/shard_map/ppermute | solution.py:28
  641.8 26.8 %collective-permute-start.28 = (bf16[2,1,512,512]{3,2,1,0:T(8,128)(2,1)}, bf16[2,1,512,512]{3,2,1,0:T(8,128)(2,1)}, u32[]{:S(2)}, u32[]{:S(2)}) collective-permute-start(bf16[2,1,512,512]{3,2,1,0:T(8,128)(2,1)} %constant_dynamic-slice_fusion.1), channel_id=1, source_target_pairs={{0,8},{8,0},{16,24},{24,16},{1,9},{9,1},{17,25},{25,17},{2,10},{10... | collective-permute-start | bytes 3145736 | tf_op jit(solution)/shard_map/ppermute | solution.py:28
  670.9 25.6 %collective-permute-start.29 = (bf16[512,512]{1,0:T(8,128)(2,1)S(1)}, bf16[512,512]{1,0:T(8,128)(2,1)S(1)}, u32[]{:S(2)}, u32[]{:S(2)}) collective-permute-start(bf16[512,512]{1,0:T(8,128)(2,1)S(1)} %get-tuple-element.228), channel_id=1, source_target_pairs={{0,16},{8,24},{16,0},{24,8},{1,17},{9,25},{17,1},{25,9},{2,18},{10... | collective-permute-start | bytes 1572872 | tf_op jit(solution)/shard_map/ppermute | solution.py:28
  (33 other events, 200.5 us)
Sparse Core Ops, SparseCore 0:
  10.2 84.5 all-gather.8
  168.3 78.1 reduce-scatter.2
  340.9 81.2 all-gather.10
  488.9 59.4 all-gather.12
  551.3 77.8 reduce-scatter.4
  636.6 86.5 all-gather.14
